TPU v7x, 32 devices: a whole 2x2x4 slice. The times are simulated.
32 devices in a mesh: gz: 8 (over z, y), gy: 4 (over x, core).
Axes of the slice: x: 2, y: 2, z: 4, core: 2. Of those that a mesh axis runs over, the one named last changes fastest.
Arguments:
- order_param: float32 [32, 128, 512], P('gz', 'gy'), may hold values from 0.2 to 1
- orientation: float32 [32, 128, 512], P('gz', 'gy'), may hold values from -1 to 1
- cell_slot: int32 [32, 128, 512], P('gz', 'gy'), may hold values from 0 to 255, as said below
- tile_grains: int32 [8, 4, 256], P('gz', 'gy'), may hold values from 0 to 4095, as said below
Outputs:
- order_out: float32 [32, 128, 512], P('gz', 'gy')
- orientation_out: float32 [32, 128, 512], P('gz', 'gy')
Inputs may be any that keep to these rules, and one draw needn't show every extreme that they name: `tile_grains`: each tile lists 256 distinct grain ids; every grain is listed by exactly two tiles, which are neighbours along the periodic z dimension and have the same y index. `cell_slot`: every position of a tile's list is used by at least one cell of that tile; the value is constant over aligned blocks of 1 x 2 x 4 cells along z, y, x.
All inputs are finite; a program needn't handle non-finite values.
Results may differ from a plain program's by a relative error of at most 0.0003.
Values sent between devices are 32-bit elements; how exact they have to be, the bound alone decides.
No kernel may reach another device: no remote copies, remote signals or barrier semaphores. Data moves between devices by JAX's collectives and lax.ppermute only.
A program may use at most 128 MiB of HBM per device.

v0:
```python
import jax
import jax.numpy as jnp
from jax import lax
from jax.sharding import PartitionSpec as P

STEPS = 3


DIFFUSE = 0.1
BARRIER = 0.5
PENALTY = 0.05
TORSION = 0.1
TRANSLATE = 2.0
ROTATE = 2.0


def with_halo(array, sides, width, wrap):
    for axis, dim in sides:
        devices, length = (lax.axis_size(axis), array.shape[dim])
        up = [(i, (i + 1) % devices) for i in range(devices if wrap else devices - 1)]
        down = [(j, i) for i, j in up]
        last = lax.slice_in_dim(array, length - width, length, axis=dim)
        initial = lax.slice_in_dim(array, 0, width, axis=dim)
        before = lax.ppermute(last, axis, up)
        after = lax.ppermute(initial, axis, down)
        array = jnp.concatenate([before, array, after], axis=dim)
    return array


def cell_terms(fields, neighbours):
    phase_field = fields[0]
    grain_angle = fields[1]
    laplace = -6.0 * phase_field
    misfit = jnp.zeros_like(phase_field)
    torque = jnp.zeros_like(phase_field)
    for beside in neighbours:
        other_phase = beside[0]
        mismatch = beside[1] - grain_angle
        laplace = laplace + other_phase
        misfit = misfit + (1.0 - jnp.cos(mismatch))
        torque = torque + other_phase * other_phase * jnp.sin(mismatch)
    gradients = [(neighbours[2 * k] - neighbours[2 * k + 1]) * 0.5 for k in range(3)]
    weight = phase_field * misfit
    densities = jnp.stack(
        [
            weight * gradients[0][0],
            weight * gradients[1][0],
            weight * gradients[2][0],
            torque,
            0.5 + phase_field * phase_field,
        ]
    )
    return (densities, laplace, misfit, torque, gradients)


def grain_motion(totals):
    inverse = 1.0 / totals[4]
    return jnp.stack(
        [
            TRANSLATE * totals[0] * inverse,
            TRANSLATE * totals[1] * inverse,
            TRANSLATE * totals[2] * inverse,
            ROTATE * totals[3] * inverse,
        ]
    )


def advance(fields, laplace, misfit, torque, gradients, motion):
    phase_field = fields[0]
    grain_angle = fields[1]
    carried = motion[0] * gradients[0] + motion[1] * gradients[1] + motion[2] * gradients[2]
    next_phase = (
        phase_field
        + DIFFUSE * laplace
        + BARRIER * phase_field * (1.0 - phase_field) * (phase_field - 0.5)
        - PENALTY * phase_field * misfit
        - carried[0]
    )
    next_angle = grain_angle + TORSION * torque + motion[3] - carried[1]
    return jnp.stack([next_phase, next_angle])


def shards(order_param, orientation, cell_slot, tile_grains):
    slot_count = tile_grains.shape[-1]
    grain_ids = tile_grains.reshape(slot_count)
    own_ids = grain_ids.astype(jnp.float32)
    flat_slot = cell_slot.reshape(-1)
    fields = jnp.stack([order_param, orientation])
    for iteration in range(STEPS):
        z_padded = with_halo(fields, (("gz", 1),), 1, True)
        y_padded = with_halo(fields, (("gy", 2),), 1, False)
        neighbours = (
            jnp.roll(fields, -1, axis=3),
            jnp.roll(fields, 1, axis=3),
            y_padded[:, :, 2:],
            y_padded[:, :, :-2],
            z_padded[:, 2:],
            z_padded[:, :-2],
        )
        densities, laplace, misfit, torque, gradients = cell_terms(fields, neighbours)
        partials = jax.vmap(
            lambda values: jax.ops.segment_sum(values, flat_slot, num_segments=slot_count)
        )(densities.reshape(5, -1))
        totals = partials
        packed = jnp.concatenate([partials, own_ids[None, :]], axis=0)[None]
        beside_all = with_halo(packed, (("gz", 0),), 1, True)
        for side in (0, 2):
            matches = (beside_all[side, 5][:, None] == own_ids[None, :]).astype(jnp.float32)
            totals = totals + jnp.dot(
                beside_all[side, :5],
                matches,
                precision=lax.Precision.HIGHEST,
                preferred_element_type=jnp.float32,
            )
        velocity = grain_motion(totals)
        motion = jnp.take(velocity, cell_slot, axis=1)
        fields = advance(fields, laplace, misfit, torque, gradients, motion)
    return (fields[0], fields[1])


def solution(mesh):
    in_specs = (P("gz", "gy", None), P("gz", "gy", None), P("gz", "gy", None), P("gz", "gy", None))
    out_specs = (P("gz", "gy", None), P("gz", "gy", None))
    return jax.shard_map(shards, mesh=mesh, in_specs=in_specs, out_specs=out_specs, check_vma=False)
```

profile of v0, /device:TPU:0, one launch (start us, length us, event | category | flops | bytes accessed | tf_op | source)
XLA Modules:
  0.0 2097.7 jit_solution(17382699104088760735)
XLA Ops:
  2.9 3.0 collective-permute-start.1
  6.9 6.1 collective-permute-start.2
  13.0 1.5 fusion.11
  17.4 1.8 copy.72
  24.4 7.1 multiply_add_fusion.8
  31.5 1.9 stack.108
  33.5 7.1 fusion.81
  40.5 2.0 stack.107
  42.5 2.2 fusion.83
  44.7 2.0 stack.106
  46.6 2.0 stack.105
  48.6 1.9 stack.109
  50.5 5.8 stack.110
  56.3 16.3 copy.57
  72.6 374.4 %scatter_custom_fusion = f32[5,256]{0,1:T(8,128)S(1)} fusion(s32[65536]{0:T(1024)} %bitcast.480, f32[65536,5]{1,0:T(8,128)} %copy.57, f32[]{:T(128)} %constant.10.clone.1), kind=kCustom, calls=%fused_computation.295 | custom fusion | flops 327680 | bytes 5632 | tf_op jit(solution)/shard_map/vmap()/scatter-add | solution.py:102
  447.1 4.8 collective-permute-start.5
  452.0 1.7 compare_and_fusion
  453.6 4.7 collective-permute-done.4
  459.0 215.9 %gather_fusion = f32[65536,4]{1,0:T(8,128)} fusion(f32[4,256]{0,1:T(8,128)S(1)} %copy.60, s32[65536]{0:T(1024)S(1)} %broadcast_clamp_fusion), kind=kCustom, calls=%fused_computation.clone | custom fusion | bytes 2359296 | tf_op jit(solution)/shard_map/jit(_take)/gather | solution.py:116
  675.0 20.4 copy.61
  696.8 1.5 multiply_add_fusion.2
  698.3 2.3 multiply_add_fusion.5
  702.2 3.0 collective-permute-start.7
  706.3 1.9 stack.119
  708.3 2.0 collective-permute-start.9
  711.4 3.1 collective-permute-done.8
  714.5 2.9 collective-permute-done.9
  718.5 7.1 multiply_add_fusion.6
  725.6 2.0 stack.118
  727.5 7.0 fusion.65
  734.5 2.0 stack.117
  736.5 2.0 fusion.67
  738.5 1.9 stack.116
  740.4 2.0 stack.115
  742.4 5.8 stack.120
  748.2 16.3 copy.62
  764.5 374.9 %scatter_custom_fusion.1 = f32[5,256]{0,1:T(8,128)} fusion(s32[65536]{0:T(1024)} %bitcast.481, f32[65536,5]{1,0:T(8,128)} %copy.62, f32[]{:T(128)} %constant.10.clone.1), kind=kCustom, calls=%fused_computation.293 | custom fusion | flops 327680 | bytes 5632 | tf_op jit(solution)/shard_map/vmap()/scatter-add | solution.py:102
  1140.5 2.0 collective-permute-start.10
  1142.5 1.6 collective-permute-done.11
  1144.3 2.5 collective-permute-done.10
  1147.4 236.8 %gather_fusion.1 = f32[65536,4]{1,0:T(8,128)} fusion(f32[4,256]{0,1:T(8,128)S(1)} %copy.65, s32[65536]{0:T(1024)} %copy-done.8), kind=kCustom, calls=%fused_computation.1.clone | custom fusion | bytes 2359296 | tf_op jit(solution)/shard_map/jit(_take)/gather | solution.py:116
  1384.1 20.3 copy.66
  1407.4 2.3 multiply_add_fusion.3
  1411.3 3.6 collective-permute-start.13
  1416.6 1.9 stack.129
  1418.8 1.8 collective-permute-start.15
  1423.9 2.8 collective-permute-done.15
  1428.1 6.0 multiply_add_fusion.4
  1434.1 2.0 stack.128
  1436.1 7.0 fusion.49
  1443.1 2.0 stack.127
  1445.1 2.0 fusion.51
  1447.1 1.9 stack.126
  1449.0 2.0 stack.125
  1451.0 5.8 stack.130
  1456.8 16.3 copy.67
  1473.1 374.3 %scatter_custom_fusion.2 = f32[5,256]{0,1:T(8,128)S(1)} fusion(s32[65536]{0:T(1024)} %bitcast.482, f32[65536,5]{1,0:T(8,128)} %copy.67, f32[]{:T(128)} %constant.10.clone.1), kind=kCustom, calls=%fused_computation.291 | custom fusion | flops 327680 | bytes 5632 | tf_op jit(solution)/shard_map/vmap()/scatter-add | solution.py:102
  1848.6 1.6 collective-permute-start.16
  1850.2 1.6 collective-permute-done.17
  1852.7 2.3 collective-permute-done.16
  1856.1 215.9 %gather_fusion.2 = f32[65536,4]{1,0:T(8,128)} fusion(f32[4,256]{0,1:T(8,128)S(1)} %copy.70, s32[65536]{0:T(1024)S(1)} %copy-done.9), kind=kCustom, calls=%fused_computation.2.clone | custom fusion | bytes 2359296 | tf_op jit(solution)/shard_map/jit(_take)/gather | solution.py:116
  2072.1 20.3 copy.71
  2093.9 1.6 multiply_add_fusion
  2095.5 2.2 fusion.42
  (129 shorter events, 35.9 us)
Async XLA Ops:
  1.6 17.7 collective-permute-start
  2.9 16.4 collective-permute-start.1
  6.9 15.2 collective-permute-start.2
  13.0 9.2 collective-permute-start.3
  15.2 1125.2 %copy-start.20 = (f32[1,256]{1,0:T(1,128)}, f32[1,256]{1,0:T(1,128)S(1)}, u32[]{:S(2)}) copy-start(f32[1,256]{1,0:T(1,128)S(1)} %get-tuple-element.84) | copy-start | bytes 3076
  15.2 1131.7 %copy-start.21 = (f32[1,1,256]{2,1,0:T(1,128)}, f32[1,1,256]{2,1,0:T(1,128)S(1)}, u32[]{:S(2)}) copy-start(f32[1,1,256]{2,1,0:T(1,128)S(1)} %get-tuple-element.85) | copy-start | bytes 3076
  16.3 658.7 %copy-start.8 = (s32[65536]{0:T(1024)}, s32[65536]{0:T(1024)S(1)}, u32[]{:S(2)}) copy-start(s32[65536]{0:T(1024)S(1)} %broadcast_clamp_fusion) | copy-start | bytes 786436
  17.4 657.5 %copy-start.15 = (f32[2,4,32,1]{3,2,1,0:T(8,128)}, f32[2,4,32,1]{3,2,1,0:T(8,128)S(1)}, u32[]{:S(2)}) copy-start(f32[2,4,32,1]{3,2,1,0:T(8,128)S(1)} %get-tuple-element.64) | copy-start | bytes 3076
  17.4 657.5 %copy-start.17 = (f32[2,4,32,1]{3,2,1,0:T(8,128)}, f32[2,4,32,1]{3,2,1,0:T(8,128)S(1)}, u32[]{:S(2)}) copy-start(f32[2,4,32,1]{3,2,1,0:T(8,128)S(1)} %get-tuple-element.65) | copy-start | bytes 3076
  20.7 3.7 copy-start.7
  20.7 35.6 %copy-start.6 = (f32[2,4,33,512]{3,2,1,0:T(8,128)}, f32[2,4,33,512]{3,2,1,0:T(8,128)S(1)}, u32[]{:S(2)}) copy-start(f32[2,4,33,512]{3,2,1,0:T(8,128)S(1)} %get-tuple-element.66) | copy-start | bytes 1622020
  72.6 625.7 %copy-start = (f32[4,32,512]{2,1,0:T(8,128)S(1)}, f32[4,32,512]{2,1,0:T(8,128)}, u32[]{:S(2)}) copy-start(f32[4,32,512]{2,1,0:T(8,128)} %param.6) | copy-start | bytes 786436
  72.6 625.7 %copy-start.1 = (f32[4,32,512]{2,1,0:T(8,128)S(1)}, f32[4,32,512]{2,1,0:T(8,128)}, u32[]{:S(2)}) copy-start(f32[4,32,512]{2,1,0:T(8,128)} %param.7) | copy-start | bytes 786436
  447.1 6.5 collective-permute-start.5
  452.0 6.3 collective-permute-start.4
  675.0 21.8 %copy-start.13 = (f32[2,4,32,512]{3,2,1,0:T(8,128)S(1)}, f32[2,4,32,512]{3,2,1,0:T(8,128)}, u32[]{:S(2)}) copy-start(f32[2,4,32,512]{3,2,1,0:T(8,128)} %slice_subtract_fusion.4) | copy-start | bytes 1572868
  675.0 23.3 %copy-start.16 = (f32[2,4,32,1]{3,2,1,0:T(8,128)S(1)}, f32[2,4,32,1]{3,2,1,0:T(8,128)}, u32[]{:S(2)}) copy-start(f32[2,4,32,1]{3,2,1,0:T(8,128)} %copy-done.15) | copy-start | bytes 3076
  700.7 4.6 copy-start.10
  700.7 5.6 copy-start.12
  700.9 9.4 collective-permute-start.6
  702.2 8.1 collective-permute-start.7
  708.3 6.2 collective-permute-start.8
  708.3 9.0 collective-permute-start.9
  717.5 1.0 copy-start.5
  717.5 429.7 %copy-start.4 = (f32[2,5,32,512]{3,2,1,0:T(8,128)}, f32[2,5,32,512]{3,2,1,0:T(8,128)S(1)}, u32[]{:S(2)}) copy-start(f32[2,5,32,512]{3,2,1,0:T(8,128)S(1)} %get-tuple-element.55) | copy-start | bytes 1966084
  1140.4 3.7 collective-permute-start.11
  1140.5 6.4 collective-permute-start.10
  1147.2 258.7 %copy-start.14 = (f32[2,4,32,512]{3,2,1,0:T(8,128)S(1)}, f32[2,4,32,512]{3,2,1,0:T(8,128)}, u32[]{:S(2)}) copy-start(f32[2,4,32,512]{3,2,1,0:T(8,128)} %slice_subtract_fusion.2) | copy-start | bytes 1572868
  1384.1 23.3 %copy-start.11 = (f32[2,4,32,1]{3,2,1,0:T(8,128)S(1)}, f32[2,4,32,1]{3,2,1,0:T(8,128)}, u32[]{:S(2)}) copy-start(f32[2,4,32,1]{3,2,1,0:T(8,128)} %copy-done.10) | copy-start | bytes 3076
  1409.7 446.4 %copy-start.9 = (s32[65536]{0:T(1024)S(1)}, s32[65536]{0:T(1024)}, u32[]{:S(2)}) copy-start(s32[65536]{0:T(1024)} %copy-done.8) | copy-start | bytes 786436
  1410.0 10.6 collective-permute-start.12
  1411.3 9.3 collective-permute-start.13
  1418.6 5.3 collective-permute-start.14
  1418.8 7.9 collective-permute-start.15
  1426.9 1.0 copy-start.2
  1426.9 1.2 copy-start.3
  1848.2 3.7 collective-permute-start.17
  1848.6 6.3 collective-permute-start.16
  2072.0 20.3 copy-start.19
  2072.1 23.4 %copy-start.18 = (f32[4,32,512]{2,1,0:T(8,128)S(1)}, f32[4,32,512]{2,1,0:T(8,128)}, u32[]{:S(2)}) copy-start(f32[4,32,512]{2,1,0:T(8,128)} %get-tuple-element.8) | copy-start | bytes 786436
where the time goes:
time: 2110 us; the launch traced here: 2100 us
  other arithmetic  1210 us (57%)
  local copies, waits for them, and re-layouts  829 us (39%)
  starting transfers between devices  32.6 us (2%)
  waiting for transfers between devices  23 us (1%)
    scatter-add x3, other arithmetic, shards(): jax.ops.segment_sum(values, flat_slot, num_segments=slot_count)  1120 us
    gather x6, local copies, waits for them, and re-layouts, shards(): motion = jnp.take(velocity, cell_slot, axis=1)  730 us
    another operation x21, local copies, waits for them, and re-layouts, cell_terms(): jnp.stack([weight * gradients[0][0], weight * gradients[1][0], weight * g...  95.5 us
  transfers between devices with their start and end apart: 18, of which 9 were waited for; matrix products, arithmetic and copies ran while one was open for 1% of the time, Pallas kernels for 0%

commit v1 on v0

v1 whole, which is shorter than its diff:
```python
import functools

import jax
import jax.numpy as jnp
from jax import lax
from jax.experimental import pallas as pl
from jax.experimental.pallas import tpu as pltpu
from jax.sharding import PartitionSpec as P

STEPS = 3

DIFFUSE = 0.1
BARRIER = 0.5
PENALTY = 0.05
TORSION = 0.1
TRANSLATE = 2.0
ROTATE = 2.0

ROWS = 2
COLS = 4


def split3(value):
    high = value.astype(jnp.bfloat16)
    rest = value - high.astype(jnp.float32)
    middle = rest.astype(jnp.bfloat16)
    low = (rest - middle.astype(jnp.float32)).astype(jnp.bfloat16)
    return high, middle, low


def exact_dot(value, chooser):
    return sum(jnp.dot(part, chooser, preferred_element_type=jnp.float32) for part in split3(value))


def sin_cos(angle):
    turns = jnp.floor(angle * 0.6366197723675814 + 0.5)
    rest = angle - turns * 1.5703125
    rest = rest - turns * 4.837512969970703125e-4
    rest = rest - turns * 7.54978995489188216e-8
    square = rest * rest
    sine = ((-1.9515295891e-4 * square + 8.3321608736e-3) * square - 1.6666654611e-1) * square * rest + rest
    cosine = ((2.443315711809948e-5 * square - 1.388731625493765e-3) * square + 4.166664568298827e-2) * square * square
    cosine = cosine - 0.5 * square + 1.0
    quarter = turns.astype(jnp.int32)
    odd = (quarter & 1) == 1
    sin_value = jnp.where(odd, cosine, sine)
    cos_value = jnp.where(odd, sine, cosine)
    sin_value = jnp.where((quarter & 2) == 2, -sin_value, sin_value)
    cos_value = jnp.where(((quarter + 1) & 2) == 2, -cos_value, cos_value)
    return sin_value, cos_value


def boundary(fields_ref, below_ref, above_ref, first_ref, last_ref, cz, yb):
    for f in range(2):
        for p in range(ROWS):
            for j in range(COLS):
                below_ref[f, p, j] = fields_ref[f, 0, p, j]
                above_ref[f, p, j] = fields_ref[f, cz - 1, p, j]
        for z in range(cz):
            for j in range(COLS):
                at = (f * cz + z) * COLS + j
                first_ref[at : at + 1, :] = fields_ref[f, z, 0, j, 0:1, :]
                last_ref[at : at + 1, :] = fields_ref[f, z, ROWS - 1, j, yb - 1 : yb, :]


def prepare_kernel(e_ref, q_ref, slot_ref, fields_ref, below_ref, above_ref, first_ref, last_ref, block_ref, rows_ref):
    cz, cy, nx = e_ref.shape
    yb, xb = cy // ROWS, nx // COLS
    row = lax.broadcasted_iota(jnp.int32, (nx, nx), 0)
    col = lax.broadcasted_iota(jnp.int32, (nx, nx), 1)
    chooser = jnp.where(row == COLS * (col % xb) + col // xb, 1.0, 0.0).astype(jnp.bfloat16)
    for f, ref in enumerate((e_ref, q_ref)):
        moved = exact_dot(ref[...].reshape(cz * cy, nx), chooser)
        for j in range(COLS):
            rows_ref[j] = moved[:, j * xb : (j + 1) * xb]
        for z in range(cz):
            for p in range(ROWS):
                for j in range(COLS):
                    fields_ref[f, z, p, j] = rows_ref[j, pl.ds(z * cy + p, yb, stride=ROWS), :]
    slots = slot_ref[...].reshape(cz * cy, nx).astype(jnp.float32).astype(jnp.bfloat16)
    rows_ref[0] = jnp.dot(slots, chooser[:, :xb], preferred_element_type=jnp.float32)
    block_ref[...] = rows_ref[0, pl.ds(0, cz * yb, stride=ROWS), :]
    boundary(fields_ref, below_ref, above_ref, first_ref, last_ref, cz, yb)


def onehot_kernel(block_ref, onehot_ref):
    rows, xb = block_ref.shape
    slots = onehot_ref.shape[1]
    slot = lax.broadcasted_iota(jnp.int32, (slots, xb), 0).astype(jnp.float32)
    for r in range(rows):
        hit = jnp.where(slot == block_ref[r : r + 1, :], 1.0, 0.0).astype(jnp.bfloat16)
        onehot_ref[r // 2, :, (r % 2) * xb : (r % 2 + 1) * xb] = hit


def terms_kernel(
    edge_ref, fields_ref, before_z_ref, after_z_ref, before_y_ref, after_y_ref, onehot_ref, ids_ref,
    message_ref, local_ref, grads_ref,
    all_ref, rim_ref, sums_ref, acc_ref,
):
    _, cz, _, _, yb, xb = fields_ref.shape
    slots = ids_ref.shape[1]
    row = lax.broadcasted_iota(jnp.int32, (yb, xb), 0)

    def fill(put, e, q):
        sin_value, cos_value = sin_cos(q)
        square = e * e
        for k, value in enumerate((e, q, cos_value, sin_value, square * cos_value, square * sin_value)):
            put(k, value)

    for side, ref in enumerate((before_y_ref, after_y_ref)):
        n = cz * COLS
        keep = edge_ref[side] == 0
        e = jnp.where(keep, ref[0:n, :], 0.0)
        q = jnp.where(keep, ref[n : 2 * n, :], 0.0)

        def put(k, value, side=side):
            rim_ref[side, k] = value

        fill(put, e, q)
    for z in range(cz + 2):
        for p in range(ROWS):
            for j in range(COLS):
                if z == 0:
                    e, q = before_z_ref[0, p, j], before_z_ref[1, p, j]
                elif z == cz + 1:
                    e, q = after_z_ref[0, p, j], after_z_ref[1, p, j]
                else:
                    e, q = fields_ref[0, z - 1, p, j], fields_ref[1, z - 1, p, j]

                def put(k, value, z=z, p=p, j=j):
                    all_ref[k, z, p, j] = value

                fill(put, e, q)

    def beside(k, z, p, j):
        x_plus = all_ref[k, z, p, j + 1] if j + 1 < COLS else pltpu.roll(all_ref[k, z, p, 0], xb - 1, 1)
        x_minus = all_ref[k, z, p, j - 1] if j > 0 else pltpu.roll(all_ref[k, z, p, COLS - 1], 1, 1)
        at = (z - 1) * COLS + j
        if p + 1 < ROWS:
            y_plus = all_ref[k, z, p + 1, j]
        else:
            y_plus = jnp.where(
                row == yb - 1, rim_ref[1, k, at : at + 1, :], pltpu.roll(all_ref[k, z, 0, j], yb - 1, 0)
            )
        if p > 0:
            y_minus = all_ref[k, z, p - 1, j]
        else:
            y_minus = jnp.where(
                row == 0, rim_ref[0, k, at : at + 1, :], pltpu.roll(all_ref[k, z, ROWS - 1, j], 1, 0)
            )
        return x_plus, x_minus, y_plus, y_minus, all_ref[k, z + 1, p, j], all_ref[k, z - 1, p, j]

    for z in range(1, cz + 1):
        totals = None
        for p in range(ROWS):
            for j in range(COLS):
                e_side = beside(0, z, p, j)
                q_side = beside(1, z, p, j)
                c_sum, s_sum, a_sum, b_sum = (sum(beside(k, z, p, j)) for k in range(2, 6))
                e, q, c, s = (all_ref[k, z, p, j] for k in range(4))
                misfit = 6.0 - c * c_sum - s * s_sum
                torque = c * b_sum - s * a_sum
                e_grads = [(e_side[2 * d] - e_side[2 * d + 1]) * 0.5 for d in range(3)]
                q_grads = [(q_side[2 * d] - q_side[2 * d + 1]) * 0.5 for d in range(3)]
                laplace = sum(e_side) - 6.0 * e
                weight = e * misfit
                values = [weight * g for g in e_grads] + [torque, 0.5 + e * e]
                totals = values if totals is None else [a + b for a, b in zip(totals, values)]
                local_ref[0, z - 1, p, j] = (
                    e + DIFFUSE * laplace + BARRIER * e * (1.0 - e) * (e - 0.5) - PENALTY * weight
                )
                local_ref[1, z - 1, p, j] = q + TORSION * torque
                for d in range(3):
                    grads_ref[d, z - 1, p, j] = e_grads[d]
                    grads_ref[3 + d, z - 1, p, j] = q_grads[d]
        rows = cz * yb
        for k, value in enumerate(totals):
            for part, piece in enumerate(split3(value)):
                at = (part * 5 + k) * rows + (z - 1) * yb
                sums_ref[at : at + yb, :] = piece.astype(jnp.float32)
    rows = cz * yb
    sums_ref[15 * rows : 16 * rows, :] = jnp.zeros((rows, xb), jnp.float32)
    acc = jnp.zeros((16, slots), jnp.float32)
    for pair in range(rows // 2):
        left = jnp.concatenate(
            [sums_ref[pl.ds(2 * pair + h, 16, stride=rows), :] for h in range(2)], axis=1
        ).astype(jnp.bfloat16)
        acc = acc + lax.dot_general(
            left, onehot_ref[pair], (((1,), (1,)), ((), ())), preferred_element_type=jnp.float32
        )
    acc_ref[...] = acc
    message_ref[0:5, :] = acc_ref[0:5, :] + acc_ref[5:10, :] + acc_ref[10:15, :]
    message_ref[5:6, :] = ids_ref[...]
    message_ref[6:8, :] = jnp.zeros((2, slots), jnp.float32)


def stacked(value):
    return jnp.concatenate([part.astype(jnp.float32) for part in split3(value)], axis=0).astype(jnp.bfloat16)


def unstacked(value):
    return value[0:8] + value[8:16] + value[16:24]


def motion_into(message_ref, before_ref, after_ref, onehot_ref, motion_ref):
    slots = message_ref.shape[1]
    rows = motion_ref.shape[0] // 8
    xb = motion_ref.shape[1]
    totals = message_ref[...]
    own = jnp.broadcast_to(message_ref[5:6, :], (slots, slots))
    for ref in (before_ref, after_ref):
        other = jnp.transpose(jnp.broadcast_to(ref[5:6, :], (slots, slots)))
        matches = jnp.where(other == own, 1.0, 0.0).astype(jnp.bfloat16)
        totals = totals + unstacked(jnp.dot(stacked(ref[...]), matches, preferred_element_type=jnp.float32))
    inverse = 1.0 / totals[4:5, :]
    velocity = stacked(TRANSLATE * totals * inverse)
    for pair in range(rows // 2):
        moved = unstacked(jnp.dot(velocity, onehot_ref[pair], preferred_element_type=jnp.float32))
        for h in range(2):
            motion_ref[pl.ds(2 * pair + h, 8, stride=rows), :] = moved[:, h * xb : (h + 1) * xb]


def advanced(local_ref, grads_ref, motion_ref, z, p, j):
    _, cz, _, _, yb, _ = local_ref.shape
    rows = cz * yb
    vx, vy, vz, turn = (motion_ref[k * rows + z * yb : k * rows + (z + 1) * yb, :] for k in range(4))
    g = [grads_ref[k, z, p, j] for k in range(6)]
    e = local_ref[0, z, p, j] - (vx * g[0] + vy * g[1] + vz * g[2])
    q = local_ref[1, z, p, j] + turn - (vx * g[3] + vy * g[4] + vz * g[5])
    return e, q


def advance_kernel(
    message_ref, before_ref, after_ref, onehot_ref, local_ref, grads_ref,
    fields_ref, below_ref, above_ref, first_ref, last_ref,
    motion_ref,
):
    _, cz, _, _, yb, xb = local_ref.shape
    motion_into(message_ref, before_ref, after_ref, onehot_ref, motion_ref)
    for z in range(cz):
        for p in range(ROWS):
            for j in range(COLS):
                fields_ref[0, z, p, j], fields_ref[1, z, p, j] = advanced(
                    local_ref, grads_ref, motion_ref, z, p, j
                )
    boundary(fields_ref, below_ref, above_ref, first_ref, last_ref, cz, yb)


def finish_kernel(
    message_ref, before_ref, after_ref, onehot_ref, local_ref, grads_ref,
    e_ref, q_ref,
    motion_ref, rows_ref,
):
    _, cz, _, _, yb, xb = local_ref.shape
    nx = COLS * xb
    motion_into(message_ref, before_ref, after_ref, onehot_ref, motion_ref)
    for z in range(cz):
        for p in range(ROWS):
            at = pl.ds(z * ROWS * yb + p, yb, stride=ROWS)
            for j in range(COLS):
                rows_ref[0, j, at, :], rows_ref[1, j, at, :] = advanced(local_ref, grads_ref, motion_ref, z, p, j)
    row = lax.broadcasted_iota(jnp.int32, (nx, nx), 0)
    col = lax.broadcasted_iota(jnp.int32, (nx, nx), 1)
    chooser = jnp.where(col == COLS * (row % xb) + row // xb, 1.0, 0.0).astype(jnp.bfloat16)
    for f, ref in enumerate((e_ref, q_ref)):
        moved = exact_dot(jnp.concatenate([rows_ref[f, j] for j in range(COLS)], axis=1), chooser)
        ref[...] = moved.reshape(ref.shape)


VMEM = pl.BlockSpec(memory_space=pltpu.VMEM)
SMEM = pl.BlockSpec(memory_space=pltpu.SMEM)


def call(kernel, name, outs, scratch=(), scalars=0):
    def run(*args):
        return pl.pallas_call(
            kernel,
            name=name,
            in_specs=[SMEM] * scalars + [VMEM] * (len(args) - scalars),
            out_specs=[VMEM] * len(outs),
            out_shape=[jax.ShapeDtypeStruct(shape, dtype) for shape, dtype in outs],
            scratch_shapes=list(scratch),
            compiler_params=pltpu.CompilerParams(vmem_limit_bytes=32 * 1024 * 1024),
        )(*args)

    return run


def shift(array, axis, step):
    size = lax.axis_size(axis)
    return lax.ppermute(array, axis, [(i, (i + step) % size) for i in range(size)])


def shards(order_param, orientation, cell_slot, tile_grains):
    cz, cy, nx = order_param.shape
    slots = tile_grains.shape[-1]
    yb, xb = cy // ROWS, nx // COLS
    rows = cz * yb
    f32 = jnp.float32
    ids = tile_grains.reshape(1, slots).astype(f32)
    at_y = lax.axis_index("gy")
    edge = jnp.stack([at_y == 0, at_y == lax.axis_size("gy") - 1]).astype(jnp.int32)
    cells = (cz, ROWS, COLS, yb, xb)
    fields_out = [
        ((2,) + cells, f32),
        ((2,) + cells[1:], f32),
        ((2,) + cells[1:], f32),
        ((2 * cz * COLS, xb), f32),
        ((2 * cz * COLS, xb), f32),
    ]
    motion = pltpu.VMEM((8 * rows, xb), f32)
    prepare = call(prepare_kernel, "prepare", fields_out + [((rows, xb), f32)], [pltpu.VMEM((COLS, cz * cy, xb), f32)])
    onehots = call(onehot_kernel, "onehots", [((rows // 2, slots, 2 * xb), jnp.bfloat16)])
    terms = call(
        terms_kernel,
        "terms",
        [((8, slots), f32), ((2,) + cells, f32), ((6,) + cells, f32)],
        [
            pltpu.VMEM((6, cz + 2) + cells[1:], f32),
            pltpu.VMEM((2, 6, cz * COLS, xb), f32),
            pltpu.VMEM((16 * rows, xb), f32),
            pltpu.VMEM((16, slots), f32),
        ],
        scalars=1,
    )
    advance = call(advance_kernel, "advance", fields_out, [motion])
    finish = call(
        finish_kernel, "finish", [((cz, cy, nx), f32)] * 2, [motion, pltpu.VMEM((2, COLS, cz * cy, xb), f32)]
    )

    fields, below, above, first, last, block = prepare(order_param, orientation, cell_slot)
    (onehot,) = onehots(block)
    for step in range(STEPS):
        before_z = shift(above, "gz", 1)
        after_z = shift(below, "gz", -1)
        before_y = shift(last, "gy", 1)
        after_y = shift(first, "gy", -1)
        message, local, grads = terms(edge, fields, before_z, after_z, before_y, after_y, onehot, ids)
        before = shift(message, "gz", 1)
        after = shift(message, "gz", -1)
        operands = (message, before, after, onehot, local, grads)
        if step < STEPS - 1:
            fields, below, above, first, last = advance(*operands)
        else:
            return tuple(finish(*operands))


def solution(mesh):
    spec = P("gz", "gy", None)
    return jax.shard_map(shards, mesh=mesh, in_specs=(spec,) * 4, out_specs=(spec,) * 2, check_vma=False)
```

time: 2110 us -> 78.5 us (0.04)
  other arithmetic: 1210 us -> 0.76 us
  local copies, waits for them, and re-layouts: 829 us -> 2.84 us
    scatter-add x3 -> x0, other arithmetic: 1120 us -> none  [shards(): jax.ops.segment_sum(values, flat_slot, num_segments=slot_count)]
    gather x6 -> x0, local copies, waits for them, and re-layouts: 730 us -> none  [shards(): motion = jnp.take(velocity, cell_slot, axis=1)]
    another operation x24 -> x0, local copies, waits for them, and re-layouts: 95.9 us -> none  [the longest x21 95.5 us: cell_terms(): jnp.stack([weight * gradients[0][0], weight * gradients[1][0], weight * g...]
    add x8 -> x0, other arithmetic: 29.3 us -> none  [the longest x3 20.2 us: cell_terms(): torque = torque + other_phase * other_phase * jnp.sin(mismatch)]
    mul x15 -> x0, other arithmetic: 27.7 us -> none  [the longest x3 21.1 us: cell_terms(): weight * gradients[2][0]]
  transfers between devices with their start and end apart: 18 -> 18, of which waited for: 9 -> 10; matrix products, arithmetic and copies ran while one was open for 1% -> 1% of each run, Pallas kernels for 0% -> 1%
where the time goes in v1:
time: 78.5 us; the launch traced here: 78.3 us
  starting transfers between devices  33.2 us (42%)
  waiting for transfers between devices  25.2 us (32%)
  Pallas kernels  15.5 us (20%)
  local copies, waits for them, and re-layouts  2.84 us (4%)
    ppermute x18, starting transfers between devices, shift(): lax.ppermute(array, axis, [(i, (i + step) % size) for i in range(size)])  33.2 us
    ppermute x18, waiting for transfers between devices, shift(): lax.ppermute(array, axis, [(i, (i + step) % size) for i in range(size)])  25.2 us
    pallas_call x8, Pallas kernels, run(): pl.pallas_call(kernel, name=name, in_specs=[SMEM] * scalars + [VMEM] * (l...  15.5 us
    unnamed x6, local copies, waits for them, and re-layouts  2.84 us
  transfers between devices with their start and end apart: 18, of which 10 were waited for; matrix products, arithmetic and copies ran while one was open for 1% of the time, Pallas kernels for 1%

profile of v1, /device:TPU:0, one launch (start us, length us, event | category | flops | bytes accessed | tf_op | source)
XLA Modules:
  0.0 78.3 jit_solution(16186590324281333870)
XLA Ops:
  0.6 0.0 copy-start
  0.6 0.9 %copy-done = f32[4,32,512]{2,1,0:T(8,128)S(1)} copy-done((f32[4,32,512]{2,1,0:T(8,128)S(1)}, f32[4,32,512]{2,1,0:T(8,128)}, u32[]{:S(2)}) %copy-start) | copy-done | bytes 262168
  1.6 0.0 copy-start.1
  1.6 0.9 %copy-done.1 = f32[4,32,512]{2,1,0:T(8,128)S(1)} copy-done((f32[4,32,512]{2,1,0:T(8,128)S(1)}, f32[4,32,512]{2,1,0:T(8,128)}, u32[]{:S(2)}) %copy-start.1) | copy-done | bytes 262168
  2.5 0.0 copy-start.2
  2.5 0.9 %copy-done.2 = s32[4,32,512]{2,1,0:T(8,128)S(1)} copy-done((s32[4,32,512]{2,1,0:T(8,128)S(1)}, s32[4,32,512]{2,1,0:T(8,128)}, u32[]{:S(2)}) %copy-start.2) | copy-done | bytes 262168
  3.5 0.7 prepare.1
  4.2 0.5 collective-permute-start.2
  4.7 2.0 %collective-permute-start.3 = (f32[32,128]{1,0:T(8,128)S(1)}, f32[32,128]{1,0:T(8,128)S(1)}, u32[]{:S(2)}, u32[]{:S(2)}) collective-permute-start(f32[32,128]{1,0:T(8,128)S(1)} %get-tuple-element.31), channel_id=1, source_target_pairs={{0,3},{1,0},{2,1},{3,2},{4,7},{5,4},{6,5},{7,6},{8,11},{9,8},{10,9... | collective-permute-start | bytes 49160 | tf_op jit(solution)/shard_map/ppermute | solution.py:291
  6.7 2.3 %collective-permute-start = (f32[2,2,4,16,128]{4,3,2,1,0:T(8,128)S(1)}, f32[2,2,4,16,128]{4,3,2,1,0:T(8,128)S(1)}, u32[]{:S(2)}, u32[]{:S(2)}) collective-permute-start(f32[2,2,4,16,128]{4,3,2,1,0:T(8,128)S(1)} %get-tuple-element.28), channel_id=1, source_target_pairs={{0,4},{4,8},{8,12},{12,16},{16,20},{20,24},{24,28},{28,0},{1,5},{5... | collective-permute-start | bytes 393224 | tf_op jit(solution)/shard_map/ppermute | solution.py:291
  9.0 3.0 %collective-permute-start.1 = (f32[2,2,4,16,128]{4,3,2,1,0:T(8,128)S(1)}, f32[2,2,4,16,128]{4,3,2,1,0:T(8,128)S(1)}, u32[]{:S(2)}, u32[]{:S(2)}) collective-permute-start(f32[2,2,4,16,128]{4,3,2,1,0:T(8,128)S(1)} %get-tuple-element.29), channel_id=1, source_target_pairs={{0,28},{4,0},{8,4},{12,8},{16,12},{20,16},{24,20},{28,24},{1,29},{... | collective-permute-start | bytes 393224 | tf_op jit(solution)/shard_map/ppermute | solution.py:291
  12.0 0.7 convert_bitcast_fusion.ids_ref
  12.7 0.1 add_convert_fusion.edge_ref
  12.8 0.8 %onehots.1.onehot_ref = bf16[32,256,256]{2,1,0:T(8,128)(2,1)S(1)} custom-call(f32[64,128]{1,0:T(8,128)S(1)} %get-tuple-element.32.block_ref), custom_call_target="tpu_custom_call" | custom-call | tf_op jit(solution)/shard_map/onehots/pallas_call | solution.py:276
  13.6 0.0 collective-permute-done.2.before_y_ref
  13.6 0.0 collective-permute-done.3.after_y_ref
  13.6 2.0 %collective-permute-done.before_z_ref = f32[2,2,4,16,128]{4,3,2,1,0:T(8,128)S(1)} collective-permute-done((f32[2,2,4,16,128]{4,3,2,1,0:T(8,128)S(1)}, f32[2,2,4,16,128]{4,3,2,1,0:T(8,128)S(1)}, u32[]{:S(2)}, u32[]{:S(2)}) %collective-permute-start) | collective-permute-done | bytes 131104 | tf_op jit(solution)/shard_map/ppermute | solution.py:291
  15.6 1.1 %collective-permute-done.1.after_z_ref = f32[2,2,4,16,128]{4,3,2,1,0:T(8,128)S(1)} collective-permute-done((f32[2,2,4,16,128]{4,3,2,1,0:T(8,128)S(1)}, f32[2,2,4,16,128]{4,3,2,1,0:T(8,128)S(1)}, u32[]{:S(2)}, u32[]{:S(2)}) %collective-permute-start.1) | collective-permute-done | bytes 131104 | tf_op jit(solution)/shard_map/ppermute | solution.py:291
  16.8 3.0 %terms.3 = (f32[8,256]{1,0:T(8,128)S(1)}, f32[2,4,2,4,16,128]{5,4,3,2,1,0:T(8,128)S(1)}, f32[6,4,2,4,16,128]{5,4,3,2,1,0:T(8,128)S(1)}) custom-call(s32[2]{0:T(128)S(1)} %add_convert_fusion.edge_ref, f32[2,4,2,4,16,128]{5,4,3,2,1,0:T(8,128)S(1)} %get-tuple-element.27.fields_ref, f32[2,2,4,16,128]{4,3,2,1,0:T(8,128)S(1)} %collective-permute-done.before_z_ref, ...), custom_call_target="tpu_custom_call" | custom-call | tf_op jit(solution)/shard_map/terms/pallas_call | solution.py:276
  19.7 3.4 %collective-permute-start.5 = (f32[8,256]{1,0:T(8,128)S(1)}, f32[8,256]{1,0:T(8,128)S(1)}, u32[]{:S(2)}, u32[]{:S(2)}) collective-permute-start(f32[8,256]{1,0:T(8,128)S(1)} %get-tuple-element.33.message_ref), channel_id=1, source_target_pairs={{0,28},{4,0},{8,4},{12,8},{16,12},{20,16},{24,20},{28,24},{1,29},{... | collective-permute-start | bytes 24584 | tf_op jit(solution)/shard_map/ppermute | solution.py:291
  23.1 0.0 collective-permute-start.4
  23.1 1.4 %collective-permute-done.5.after_ref = f32[8,256]{1,0:T(8,128)S(1)} collective-permute-done((f32[8,256]{1,0:T(8,128)S(1)}, f32[8,256]{1,0:T(8,128)S(1)}, u32[]{:S(2)}, u32[]{:S(2)}) %collective-permute-start.5) | collective-permute-done | bytes 8224 | tf_op jit(solution)/shard_map/ppermute | solution.py:291
  24.5 5.0 %collective-permute-done.4.before_ref = f32[8,256]{1,0:T(8,128)S(1)} collective-permute-done((f32[8,256]{1,0:T(8,128)S(1)}, f32[8,256]{1,0:T(8,128)S(1)}, u32[]{:S(2)}, u32[]{:S(2)}) %collective-permute-start.4) | collective-permute-done | bytes 8224 | tf_op jit(solution)/shard_map/ppermute | solution.py:291
  29.4 1.2 %advance.2 = (f32[2,4,2,4,16,128]{5,4,3,2,1,0:T(8,128)S(1)}, f32[2,2,4,16,128]{4,3,2,1,0:T(8,128)S(1)}, f32[2,2,4,16,128]{4,3,2,1,0:T(8,128)S(1)}, f32[32,128]{1,0:T(8,128)S(1)}, f32[32,128]{1,0:T(8,128)S(1)}) custom-call(f32[8,256]{1,0:T(8,128)S(1)} %get-tuple-element.33.message_ref, f32[8,256]{1,0:T(8,128)S(1)} %collective-permute-done.4.before_ref, ...), custom_call_target="tpu_custom_call" | custom-call | tf_op jit(solution)/shard_map/advance/pallas_call | solution.py:276
  30.7 0.1 collective-permute-start.6
  30.7 4.7 %collective-permute-start.7 = (f32[2,2,4,16,128]{4,3,2,1,0:T(8,128)S(1)}, f32[2,2,4,16,128]{4,3,2,1,0:T(8,128)S(1)}, u32[]{:S(2)}, u32[]{:S(2)}) collective-permute-start(f32[2,2,4,16,128]{4,3,2,1,0:T(8,128)S(1)} %get-tuple-element.38), channel_id=1, source_target_pairs={{0,28},{4,0},{8,4},{12,8},{16,12},{20,16},{24,20},{28,24},{1,29},{... | collective-permute-start | bytes 393224 | tf_op jit(solution)/shard_map/ppermute | solution.py:291
  35.4 0.0 collective-permute-start.8
  35.5 1.7 %collective-permute-start.9 = (f32[32,128]{1,0:T(8,128)S(1)}, f32[32,128]{1,0:T(8,128)S(1)}, u32[]{:S(2)}, u32[]{:S(2)}) collective-permute-start(f32[32,128]{1,0:T(8,128)S(1)} %get-tuple-element.40), channel_id=1, source_target_pairs={{0,3},{1,0},{2,1},{3,2},{4,7},{5,4},{6,5},{7,6},{8,11},{9,8},{10,9... | collective-permute-start | bytes 49160 | tf_op jit(solution)/shard_map/ppermute | solution.py:291
  37.2 1.4 %collective-permute-done.8.before_y_ref = f32[32,128]{1,0:T(8,128)S(1)} collective-permute-done((f32[32,128]{1,0:T(8,128)S(1)}, f32[32,128]{1,0:T(8,128)S(1)}, u32[]{:S(2)}, u32[]{:S(2)}) %collective-permute-start.8) | collective-permute-done | bytes 16416 | tf_op jit(solution)/shard_map/ppermute | solution.py:291
  38.6 0.0 collective-permute-done.9.after_y_ref
  38.6 0.0 collective-permute-done.6.before_z_ref
  38.6 0.0 collective-permute-done.7.after_z_ref
  38.6 3.0 %terms.4 = (f32[8,256]{1,0:T(8,128)S(1)}, f32[2,4,2,4,16,128]{5,4,3,2,1,0:T(8,128)S(1)}, f32[6,4,2,4,16,128]{5,4,3,2,1,0:T(8,128)S(1)}) custom-call(s32[2]{0:T(128)S(1)} %add_convert_fusion.edge_ref, f32[2,4,2,4,16,128]{5,4,3,2,1,0:T(8,128)S(1)} %get-tuple-element.36.fields_ref, f32[2,2,4,16,128]{4,3,2,1,0:T(8,128)S(1)} %collective-permute-done.6.before_z_ref, ...), custom_call_target="tpu_custom_call" | custom-call | tf_op jit(solution)/shard_map/terms/pallas_call | solution.py:276
  41.6 4.5 %collective-permute-start.11 = (f32[8,256]{1,0:T(8,128)S(1)}, f32[8,256]{1,0:T(8,128)S(1)}, u32[]{:S(2)}, u32[]{:S(2)}) collective-permute-start(f32[8,256]{1,0:T(8,128)S(1)} %get-tuple-element.41.message_ref), channel_id=1, source_target_pairs={{0,28},{4,0},{8,4},{12,8},{16,12},{20,16},{24,20},{28,24},{1,29},{... | collective-permute-start | bytes 24584 | tf_op jit(solution)/shard_map/ppermute | solution.py:291
  46.2 0.0 collective-permute-start.10
  46.2 1.4 %collective-permute-done.11.after_ref = f32[8,256]{1,0:T(8,128)S(1)} collective-permute-done((f32[8,256]{1,0:T(8,128)S(1)}, f32[8,256]{1,0:T(8,128)S(1)}, u32[]{:S(2)}, u32[]{:S(2)}) %collective-permute-start.11) | collective-permute-done | bytes 8224 | tf_op jit(solution)/shard_map/ppermute | solution.py:291
  47.5 5.1 %collective-permute-done.10.before_ref = f32[8,256]{1,0:T(8,128)S(1)} collective-permute-done((f32[8,256]{1,0:T(8,128)S(1)}, f32[8,256]{1,0:T(8,128)S(1)}, u32[]{:S(2)}, u32[]{:S(2)}) %collective-permute-start.10) | collective-permute-done | bytes 8224 | tf_op jit(solution)/shard_map/ppermute | solution.py:291
  52.6 1.2 %advance.3 = (f32[2,4,2,4,16,128]{5,4,3,2,1,0:T(8,128)S(1)}, f32[2,2,4,16,128]{4,3,2,1,0:T(8,128)S(1)}, f32[2,2,4,16,128]{4,3,2,1,0:T(8,128)S(1)}, f32[32,128]{1,0:T(8,128)S(1)}, f32[32,128]{1,0:T(8,128)S(1)}) custom-call(f32[8,256]{1,0:T(8,128)S(1)} %get-tuple-element.41.message_ref, f32[8,256]{1,0:T(8,128)S(1)} %collective-permute-done.10.before_ref, ...), custom_call_target="tpu_custom_call" | custom-call | tf_op jit(solution)/shard_map/advance/pallas_call | solution.py:276
  53.9 0.1 collective-permute-start.12
  53.9 4.7 %collective-permute-start.13 = (f32[2,2,4,16,128]{4,3,2,1,0:T(8,128)S(1)}, f32[2,2,4,16,128]{4,3,2,1,0:T(8,128)S(1)}, u32[]{:S(2)}, u32[]{:S(2)}) collective-permute-start(f32[2,2,4,16,128]{4,3,2,1,0:T(8,128)S(1)} %get-tuple-element.46), channel_id=1, source_target_pairs={{0,28},{4,0},{8,4},{12,8},{16,12},{20,16},{24,20},{28,24},{1,29},{... | collective-permute-start | bytes 393224 | tf_op jit(solution)/shard_map/ppermute | solution.py:291
  58.6 0.0 collective-permute-start.14
  58.6 1.7 %collective-permute-start.15 = (f32[32,128]{1,0:T(8,128)S(1)}, f32[32,128]{1,0:T(8,128)S(1)}, u32[]{:S(2)}, u32[]{:S(2)}) collective-permute-start(f32[32,128]{1,0:T(8,128)S(1)} %get-tuple-element.48), channel_id=1, source_target_pairs={{0,3},{1,0},{2,1},{3,2},{4,7},{5,4},{6,5},{7,6},{8,11},{9,8},{10,9... | collective-permute-start | bytes 49160 | tf_op jit(solution)/shard_map/ppermute | solution.py:291
  60.4 1.4 %collective-permute-done.14.before_y_ref = f32[32,128]{1,0:T(8,128)S(1)} collective-permute-done((f32[32,128]{1,0:T(8,128)S(1)}, f32[32,128]{1,0:T(8,128)S(1)}, u32[]{:S(2)}, u32[]{:S(2)}) %collective-permute-start.14) | collective-permute-done | bytes 16416 | tf_op jit(solution)/shard_map/ppermute | solution.py:291
  61.8 0.0 collective-permute-done.15.after_y_ref
  61.8 0.0 collective-permute-done.12.before_z_ref
  61.8 0.0 collective-permute-done.13.after_z_ref
  61.8 3.0 %terms.5 = (f32[8,256]{1,0:T(8,128)S(1)}, f32[2,4,2,4,16,128]{5,4,3,2,1,0:T(8,128)S(1)}, f32[6,4,2,4,16,128]{5,4,3,2,1,0:T(8,128)S(1)}) custom-call(s32[2]{0:T(128)S(1)} %add_convert_fusion.edge_ref, f32[2,4,2,4,16,128]{5,4,3,2,1,0:T(8,128)S(1)} %get-tuple-element.44.fields_ref, f32[2,2,4,16,128]{4,3,2,1,0:T(8,128)S(1)} %collective-permute-done.12.before_z_ref, ...), custom_call_target="tpu_custom_call" | custom-call | tf_op jit(solution)/shard_map/terms/pallas_call | solution.py:276
  64.8 4.5 %collective-permute-start.17 = (f32[8,256]{1,0:T(8,128)S(1)}, f32[8,256]{1,0:T(8,128)S(1)}, u32[]{:S(2)}, u32[]{:S(2)}) collective-permute-start(f32[8,256]{1,0:T(8,128)S(1)} %get-tuple-element.49.message_ref), channel_id=1, source_target_pairs={{0,28},{4,0},{8,4},{12,8},{16,12},{20,16},{24,20},{28,24},{1,29},{... | collective-permute-start | bytes 24584 | tf_op jit(solution)/shard_map/ppermute | solution.py:291
  69.3 0.0 collective-permute-start.16
  69.3 1.4 %collective-permute-done.17.after_ref = f32[8,256]{1,0:T(8,128)S(1)} collective-permute-done((f32[8,256]{1,0:T(8,128)S(1)}, f32[8,256]{1,0:T(8,128)S(1)}, u32[]{:S(2)}, u32[]{:S(2)}) %collective-permute-start.17) | collective-permute-done | bytes 8224 | tf_op jit(solution)/shard_map/ppermute | solution.py:291
  70.7 5.0 %collective-permute-done.16.before_ref = f32[8,256]{1,0:T(8,128)S(1)} collective-permute-done((f32[8,256]{1,0:T(8,128)S(1)}, f32[8,256]{1,0:T(8,128)S(1)}, u32[]{:S(2)}, u32[]{:S(2)}) %collective-permute-start.16) | collective-permute-done | bytes 8224 | tf_op jit(solution)/shard_map/ppermute | solution.py:291
  75.7 2.6 %finish.1 = (f32[4,32,512]{2,1,0:T(8,128)}, f32[4,32,512]{2,1,0:T(8,128)}) custom-call(f32[8,256]{1,0:T(8,128)S(1)} %get-tuple-element.49.message_ref, f32[8,256]{1,0:T(8,128)S(1)} %collective-permute-done.16.before_ref, f32[8,256]{1,0:T(8,128)S(1)} %collective-permute-done.17.after_ref, bf16[32,256,256]{2,1,0:T(8,128)(2,1)S(1)} %onehots.1.onehot_ref, ...), custom_call_target="tpu_custom_call" | custom-call | tf_op jit(solution)/shard_map/finish/pallas_call | solution.py:276
Async XLA Ops:
  0.6 1.0 %copy-start = (f32[4,32,512]{2,1,0:T(8,128)S(1)}, f32[4,32,512]{2,1,0:T(8,128)}, u32[]{:S(2)}) copy-start(f32[4,32,512]{2,1,0:T(8,128)} %e_ref.1) | copy-start | bytes 786436
  1.6 0.9 %copy-start.1 = (f32[4,32,512]{2,1,0:T(8,128)S(1)}, f32[4,32,512]{2,1,0:T(8,128)}, u32[]{:S(2)}) copy-start(f32[4,32,512]{2,1,0:T(8,128)} %q_ref.1) | copy-start | bytes 786436
  2.5 0.9 %copy-start.2 = (s32[4,32,512]{2,1,0:T(8,128)S(1)}, s32[4,32,512]{2,1,0:T(8,128)}, u32[]{:S(2)}) copy-start(s32[4,32,512]{2,1,0:T(8,128)} %slot_ref.1) | copy-start | bytes 786436
  4.2 9.4 %collective-permute-start.2 = (f32[32,128]{1,0:T(8,128)S(1)}, f32[32,128]{1,0:T(8,128)S(1)}, u32[]{:S(2)}, u32[]{:S(2)}) collective-permute-start(f32[32,128]{1,0:T(8,128)S(1)} %get-tuple-element.30), channel_id=1, source_target_pairs={{0,1},{1,2},{2,3},{3,0},{4,5},{5,6},{6,7},{7,4},{8,9},{9,10},{10,1... | collective-permute-start | bytes 49160 | tf_op jit(solution)/shard_map/ppermute | solution.py:291
  4.7 8.9 %collective-permute-start.3 = (f32[32,128]{1,0:T(8,128)S(1)}, f32[32,128]{1,0:T(8,128)S(1)}, u32[]{:S(2)}, u32[]{:S(2)}) collective-permute-start(f32[32,128]{1,0:T(8,128)S(1)} %get-tuple-element.31), channel_id=1, source_target_pairs={{0,3},{1,0},{2,1},{3,2},{4,7},{5,4},{6,5},{7,6},{8,11},{9,8},{10,9... | collective-permute-start | bytes 49160 | tf_op jit(solution)/shard_map/ppermute | solution.py:291
  6.7 8.9 %collective-permute-start = (f32[2,2,4,16,128]{4,3,2,1,0:T(8,128)S(1)}, f32[2,2,4,16,128]{4,3,2,1,0:T(8,128)S(1)}, u32[]{:S(2)}, u32[]{:S(2)}) collective-permute-start(f32[2,2,4,16,128]{4,3,2,1,0:T(8,128)S(1)} %get-tuple-element.28), channel_id=1, source_target_pairs={{0,4},{4,8},{8,12},{12,16},{16,20},{20,24},{24,28},{28,0},{1,5},{5... | collective-permute-start | bytes 393224 | tf_op jit(solution)/shard_map/ppermute | solution.py:291
  9.0 7.8 %collective-permute-start.1 = (f32[2,2,4,16,128]{4,3,2,1,0:T(8,128)S(1)}, f32[2,2,4,16,128]{4,3,2,1,0:T(8,128)S(1)}, u32[]{:S(2)}, u32[]{:S(2)}) collective-permute-start(f32[2,2,4,16,128]{4,3,2,1,0:T(8,128)S(1)} %get-tuple-element.29), channel_id=1, source_target_pairs={{0,28},{4,0},{8,4},{12,8},{16,12},{20,16},{24,20},{28,24},{1,29},{... | collective-permute-start | bytes 393224 | tf_op jit(solution)/shard_map/ppermute | solution.py:291
  19.7 4.7 %collective-permute-start.5 = (f32[8,256]{1,0:T(8,128)S(1)}, f32[8,256]{1,0:T(8,128)S(1)}, u32[]{:S(2)}, u32[]{:S(2)}) collective-permute-start(f32[8,256]{1,0:T(8,128)S(1)} %get-tuple-element.33.message_ref), channel_id=1, source_target_pairs={{0,28},{4,0},{8,4},{12,8},{16,12},{20,16},{24,20},{28,24},{1,29},{... | collective-permute-start | bytes 24584 | tf_op jit(solution)/shard_map/ppermute | solution.py:291
  23.1 6.3 %collective-permute-start.4 = (f32[8,256]{1,0:T(8,128)S(1)}, f32[8,256]{1,0:T(8,128)S(1)}, u32[]{:S(2)}, u32[]{:S(2)}) collective-permute-start(f32[8,256]{1,0:T(8,128)S(1)} %get-tuple-element.33.message_ref), channel_id=1, source_target_pairs={{0,4},{4,8},{8,12},{12,16},{16,20},{20,24},{24,28},{28,0},{1,5},{5... | collective-permute-start | bytes 24584 | tf_op jit(solution)/shard_map/ppermute | solution.py:291
  30.7 8.0 %collective-permute-start.6 = (f32[2,2,4,16,128]{4,3,2,1,0:T(8,128)S(1)}, f32[2,2,4,16,128]{4,3,2,1,0:T(8,128)S(1)}, u32[]{:S(2)}, u32[]{:S(2)}) collective-permute-start(f32[2,2,4,16,128]{4,3,2,1,0:T(8,128)S(1)} %get-tuple-element.37), channel_id=1, source_target_pairs={{0,4},{4,8},{8,12},{12,16},{16,20},{20,24},{24,28},{28,0},{1,5},{5... | collective-permute-start | bytes 393224 | tf_op jit(solution)/shard_map/ppermute | solution.py:291
  30.7 7.9 %collective-permute-start.7 = (f32[2,2,4,16,128]{4,3,2,1,0:T(8,128)S(1)}, f32[2,2,4,16,128]{4,3,2,1,0:T(8,128)S(1)}, u32[]{:S(2)}, u32[]{:S(2)}) collective-permute-start(f32[2,2,4,16,128]{4,3,2,1,0:T(8,128)S(1)} %get-tuple-element.38), channel_id=1, source_target_pairs={{0,28},{4,0},{8,4},{12,8},{16,12},{20,16},{24,20},{28,24},{1,29},{... | collective-permute-start | bytes 393224 | tf_op jit(solution)/shard_map/ppermute | solution.py:291
  35.4 3.2 %collective-permute-start.8 = (f32[32,128]{1,0:T(8,128)S(1)}, f32[32,128]{1,0:T(8,128)S(1)}, u32[]{:S(2)}, u32[]{:S(2)}) collective-permute-start(f32[32,128]{1,0:T(8,128)S(1)} %get-tuple-element.39), channel_id=1, source_target_pairs={{0,1},{1,2},{2,3},{3,0},{4,5},{5,6},{6,7},{7,4},{8,9},{9,10},{10,1... | collective-permute-start | bytes 49160 | tf_op jit(solution)/shard_map/ppermute | solution.py:291
  35.5 3.2 %collective-permute-start.9 = (f32[32,128]{1,0:T(8,128)S(1)}, f32[32,128]{1,0:T(8,128)S(1)}, u32[]{:S(2)}, u32[]{:S(2)}) collective-permute-start(f32[32,128]{1,0:T(8,128)S(1)} %get-tuple-element.40), channel_id=1, source_target_pairs={{0,3},{1,0},{2,1},{3,2},{4,7},{5,4},{6,5},{7,6},{8,11},{9,8},{10,9... | collective-permute-start | bytes 49160 | tf_op jit(solution)/shard_map/ppermute | solution.py:291
  41.6 5.9 %collective-permute-start.11 = (f32[8,256]{1,0:T(8,128)S(1)}, f32[8,256]{1,0:T(8,128)S(1)}, u32[]{:S(2)}, u32[]{:S(2)}) collective-permute-start(f32[8,256]{1,0:T(8,128)S(1)} %get-tuple-element.41.message_ref), channel_id=1, source_target_pairs={{0,28},{4,0},{8,4},{12,8},{16,12},{20,16},{24,20},{28,24},{1,29},{... | collective-permute-start | bytes 24584 | tf_op jit(solution)/shard_map/ppermute | solution.py:291
  46.2 6.5 %collective-permute-start.10 = (f32[8,256]{1,0:T(8,128)S(1)}, f32[8,256]{1,0:T(8,128)S(1)}, u32[]{:S(2)}, u32[]{:S(2)}) collective-permute-start(f32[8,256]{1,0:T(8,128)S(1)} %get-tuple-element.41.message_ref), channel_id=1, source_target_pairs={{0,4},{4,8},{8,12},{12,16},{16,20},{20,24},{24,28},{28,0},{1,5},{5... | collective-permute-start | bytes 24584 | tf_op jit(solution)/shard_map/ppermute | solution.py:291
  53.9 8.0 %collective-permute-start.12 = (f32[2,2,4,16,128]{4,3,2,1,0:T(8,128)S(1)}, f32[2,2,4,16,128]{4,3,2,1,0:T(8,128)S(1)}, u32[]{:S(2)}, u32[]{:S(2)}) collective-permute-start(f32[2,2,4,16,128]{4,3,2,1,0:T(8,128)S(1)} %get-tuple-element.45), channel_id=1, source_target_pairs={{0,4},{4,8},{8,12},{12,16},{16,20},{20,24},{24,28},{28,0},{1,5},{5... | collective-permute-start | bytes 393224 | tf_op jit(solution)/shard_map/ppermute | solution.py:291
  53.9 7.9 %collective-permute-start.13 = (f32[2,2,4,16,128]{4,3,2,1,0:T(8,128)S(1)}, f32[2,2,4,16,128]{4,3,2,1,0:T(8,128)S(1)}, u32[]{:S(2)}, u32[]{:S(2)}) collective-permute-start(f32[2,2,4,16,128]{4,3,2,1,0:T(8,128)S(1)} %get-tuple-element.46), channel_id=1, source_target_pairs={{0,28},{4,0},{8,4},{12,8},{16,12},{20,16},{24,20},{28,24},{1,29},{... | collective-permute-start | bytes 393224 | tf_op jit(solution)/shard_map/ppermute | solution.py:291
  58.6 3.2 %collective-permute-start.14 = (f32[32,128]{1,0:T(8,128)S(1)}, f32[32,128]{1,0:T(8,128)S(1)}, u32[]{:S(2)}, u32[]{:S(2)}) collective-permute-start(f32[32,128]{1,0:T(8,128)S(1)} %get-tuple-element.47), channel_id=1, source_target_pairs={{0,1},{1,2},{2,3},{3,0},{4,5},{5,6},{6,7},{7,4},{8,9},{9,10},{10,1... | collective-permute-start | bytes 49160 | tf_op jit(solution)/shard_map/ppermute | solution.py:291
  58.6 3.2 %collective-permute-start.15 = (f32[32,128]{1,0:T(8,128)S(1)}, f32[32,128]{1,0:T(8,128)S(1)}, u32[]{:S(2)}, u32[]{:S(2)}) collective-permute-start(f32[32,128]{1,0:T(8,128)S(1)} %get-tuple-element.48), channel_id=1, source_target_pairs={{0,3},{1,0},{2,1},{3,2},{4,7},{5,4},{6,5},{7,6},{8,11},{9,8},{10,9... | collective-permute-start | bytes 49160 | tf_op jit(solution)/shard_map/ppermute | solution.py:291
  64.8 5.9 %collective-permute-start.17 = (f32[8,256]{1,0:T(8,128)S(1)}, f32[8,256]{1,0:T(8,128)S(1)}, u32[]{:S(2)}, u32[]{:S(2)}) collective-permute-start(f32[8,256]{1,0:T(8,128)S(1)} %get-tuple-element.49.message_ref), channel_id=1, source_target_pairs={{0,28},{4,0},{8,4},{12,8},{16,12},{20,16},{24,20},{28,24},{1,29},{... | collective-permute-start | bytes 24584 | tf_op jit(solution)/shard_map/ppermute | solution.py:291
  69.3 6.3 %collective-permute-start.16 = (f32[8,256]{1,0:T(8,128)S(1)}, f32[8,256]{1,0:T(8,128)S(1)}, u32[]{:S(2)}, u32[]{:S(2)}) collective-permute-start(f32[8,256]{1,0:T(8,128)S(1)} %get-tuple-element.49.message_ref), channel_id=1, source_target_pairs={{0,4},{4,8},{8,12},{12,16},{16,20},{20,24},{24,28},{28,0},{1,5},{5... | collective-permute-start | bytes 24584 | tf_op jit(solution)/shard_map/ppermute | solution.py:291

commit v2 on v0

v2 whole, which is shorter than its diff:
```python
import functools

import jax
import jax.numpy as jnp
from jax import lax
from jax.experimental import pallas as pl
from jax.experimental.pallas import tpu as pltpu
from jax.sharding import PartitionSpec as P

STEPS = 3

DIFFUSE = 0.1
BARRIER = 0.5
PENALTY = 0.05
TORSION = 0.1
TRANSLATE = 2.0
ROTATE = 2.0

ROWS = 2
COLS = 4


def split3(value):
    high = value.astype(jnp.bfloat16)
    rest = value - high.astype(jnp.float32)
    middle = rest.astype(jnp.bfloat16)
    low = (rest - middle.astype(jnp.float32)).astype(jnp.bfloat16)
    return high, middle, low


def exact_dot(value, chooser):
    return sum(jnp.dot(part, chooser, preferred_element_type=jnp.float32) for part in split3(value))


def sin_cos(angle):
    turns = jnp.floor(angle * 0.6366197723675814 + 0.5)
    rest = angle - turns * 1.5703125
    rest = rest - turns * 4.837512969970703125e-4
    rest = rest - turns * 7.54978995489188216e-8
    square = rest * rest
    sine = ((-1.9515295891e-4 * square + 8.3321608736e-3) * square - 1.6666654611e-1) * square * rest + rest
    cosine = ((2.443315711809948e-5 * square - 1.388731625493765e-3) * square + 4.166664568298827e-2) * square * square
    cosine = cosine - 0.5 * square + 1.0
    quarter = turns.astype(jnp.int32)
    odd = (quarter & 1) == 1
    sin_value = jnp.where(odd, cosine, sine)
    cos_value = jnp.where(odd, sine, cosine)
    sin_value = jnp.where((quarter & 2) == 2, -sin_value, sin_value)
    cos_value = jnp.where(((quarter + 1) & 2) == 2, -cos_value, cos_value)
    return sin_value, cos_value


def odd(axis):
    return (lax.axis_index(axis) & 1) == 1


def layer(outer_ref, inner_ref, k, z, p, j):
    cz = inner_ref.shape[1] + 2
    if z == 0:
        return outer_ref[k, 0, p, j]
    if z == cz - 1:
        return outer_ref[k, 1, p, j]
    return inner_ref[k, z - 1, p, j]


def put_z_edges(outer_ref, near_ref, far_ref):
    first_to_near = odd("gz").astype(jnp.int32)
    for f in range(2):
        for p in range(ROWS):
            for j in range(COLS):
                near_ref[f, p, j] = outer_ref[f, 1 - first_to_near, p, j]
                far_ref[f, p, j] = outer_ref[f, first_to_near, p, j]


def put_y_edges(outer_ref, inner_ref, near_ref, far_ref):
    cz, yb = inner_ref.shape[1] + 2, inner_ref.shape[4]
    first_to_near = odd("gy")
    for f in range(2):
        for z in range(cz):
            for j in range(COLS):
                at = (f * cz + z) * COLS + j
                first = layer(outer_ref, inner_ref, f, z, 0, j)[0:1]
                last = layer(outer_ref, inner_ref, f, z, ROWS - 1, j)[yb - 1 : yb]
                near_ref[at : at + 1, :] = jnp.where(first_to_near, first, last)
                far_ref[at : at + 1, :] = jnp.where(first_to_near, last, first)


def x_chooser(nx, xb, back=False):
    first = lax.broadcasted_iota(jnp.int32, (nx, nx), 1 if back else 0)
    second = lax.broadcasted_iota(jnp.int32, (nx, nx), 0 if back else 1)
    return jnp.where(first == COLS * (second % xb) + second // xb, 1.0, 0.0).astype(jnp.bfloat16)


def prepare_kernel(
    e_hbm, q_hbm,
    outer_ref, inner_ref, z_near_ref, z_far_ref, y_near_ref, y_far_ref,
    in_ref, rows_ref, sems,
):
    _, cz, cy, nx = in_ref.shape
    yb, xb = cy // ROWS, nx // COLS
    copies = [pltpu.make_async_copy(ref, in_ref.at[f], sems.at[f]) for f, ref in enumerate((e_hbm, q_hbm))]
    for copy in copies:
        copy.start()
    chooser = x_chooser(nx, xb)
    for f in range(2):
        copies[f].wait()
        moved = exact_dot(in_ref[f].reshape(cz * cy, nx), chooser)
        for j in range(COLS):
            rows_ref[j] = moved[:, j * xb : (j + 1) * xb]
        for z in range(cz):
            for p in range(ROWS):
                for j in range(COLS):
                    value = rows_ref[j, pl.ds(z * cy + p, yb, stride=ROWS), :]
                    if z == 0:
                        outer_ref[f, 0, p, j] = value
                    elif z == cz - 1:
                        outer_ref[f, 1, p, j] = value
                    else:
                        inner_ref[f, z - 1, p, j] = value
    put_z_edges(outer_ref, z_near_ref, z_far_ref)
    put_y_edges(outer_ref, inner_ref, y_near_ref, y_far_ref)


def onehot_kernel(slot_hbm, onehot_ref, slot_ref, rows_ref, sem):
    cz, cy, nx = slot_ref.shape
    yb, xb = cy // ROWS, nx // COLS
    slots = onehot_ref.shape[1]
    copy = pltpu.make_async_copy(slot_hbm, slot_ref, sem)
    copy.start()
    chooser = jnp.where(
        lax.broadcasted_iota(jnp.int32, (nx, xb), 0) == COLS * lax.broadcasted_iota(jnp.int32, (nx, xb), 1), 1.0, 0.0
    ).astype(jnp.bfloat16)
    slot = lax.broadcasted_iota(jnp.int32, (slots, xb), 0).astype(jnp.float32)
    copy.wait()
    values = slot_ref[...].reshape(cz * cy, nx).astype(jnp.float32).astype(jnp.bfloat16)
    rows_ref[...] = jnp.dot(values, chooser, preferred_element_type=jnp.float32)
    for r in range(cz * yb):
        hit = jnp.where(slot == rows_ref[ROWS * r : ROWS * r + 1, :], 1.0, 0.0).astype(jnp.bfloat16)
        onehot_ref[r // 2, :, (r % 2) * xb : (r % 2 + 1) * xb] = hit


def derived(e, q):
    sin_value, cos_value = sin_cos(q)
    square = e * e
    return cos_value, sin_value, square * cos_value, square * sin_value


def trig_kernel(outer_ref, inner_ref, trig_ref):
    _, cz, rows, cols, _, _ = trig_ref.shape
    for z in range(cz):
        for p in range(rows):
            for j in range(cols):
                e, q = (layer(outer_ref, inner_ref, f, z, p, j) for f in range(2))
                for k, value in enumerate(derived(e, q)):
                    trig_ref[k, z, p, j] = value


def cell_terms(get, rim_ref, z, p, j):
    yb, xb = get(0, z, p, j).shape
    row = lax.broadcasted_iota(jnp.int32, (yb, xb), 0)
    at = z * COLS + j

    def beside(k):
        x_plus = get(k, z, p, j + 1) if j + 1 < COLS else pltpu.roll(get(k, z, p, 0), xb - 1, 1)
        x_minus = get(k, z, p, j - 1) if j > 0 else pltpu.roll(get(k, z, p, COLS - 1), 1, 1)
        if p + 1 < ROWS:
            y_plus = get(k, z, p + 1, j)
        else:
            y_plus = jnp.where(row == yb - 1, rim_ref[1, k, at : at + 1, :], pltpu.roll(get(k, z, 0, j), yb - 1, 0))
        if p > 0:
            y_minus = get(k, z, p - 1, j)
        else:
            y_minus = jnp.where(row == 0, rim_ref[0, k, at : at + 1, :], pltpu.roll(get(k, z, ROWS - 1, j), 1, 0))
        return x_plus, x_minus, y_plus, y_minus, get(k, z + 1, p, j), get(k, z - 1, p, j)

    e_side, q_side = beside(0), beside(1)
    c_sum, s_sum, a_sum, b_sum = (sum(beside(k)) for k in range(2, 6))
    e, q, c, s = (get(k, z, p, j) for k in range(4))
    misfit = 6.0 - c * c_sum - s * s_sum
    torque = c * b_sum - s * a_sum
    grads = [(side[2 * d] - side[2 * d + 1]) * 0.5 for side in (e_side, q_side) for d in range(3)]
    laplace = sum(e_side) - 6.0 * e
    weight = e * misfit
    densities = [weight * g for g in grads[:3]] + [torque, 0.5 + e * e]
    e_local = e + DIFFUSE * laplace + BARRIER * e * (1.0 - e) * (e - 0.5) - PENALTY * weight
    return [e_local, q + TORSION * torque] + grads, densities


def layer_terms(get, rim_ref, z, local_ref, at, sums_ref):
    totals = None
    for p in range(ROWS):
        for j in range(COLS):
            local, densities = cell_terms(get, rim_ref, z, p, j)
            totals = densities if totals is None else [a + b for a, b in zip(totals, densities)]
            for k, value in enumerate(local):
                local_ref[k, at, p, j] = value
    rows = sums_ref.shape[0] // 16
    yb = rows // local_ref.shape[1]
    for k, value in enumerate(totals):
        for part, piece in enumerate(split3(value)):
            start = (part * 5 + k) * rows + at * yb
            sums_ref[start : start + yb, :] = piece.astype(jnp.float32)


def slot_sums(acc, sums_ref, onehot_ref, pairs):
    rows = sums_ref.shape[0] // 16
    for i, pair in enumerate(pairs):
        left = jnp.concatenate(
            [sums_ref[pl.ds(2 * i + h, 16, stride=rows), :] for h in range(2)], axis=1
        ).astype(jnp.bfloat16)
        acc = acc + lax.dot_general(
            left, onehot_ref[pair], (((1,), (1,)), ((), ())), preferred_element_type=jnp.float32
        )
    return acc


def inner_kernel(
    outer_ref, inner_ref, trig_ref, y_near_ref, y_far_ref, onehot_ref,
    rim_ref, local_ref, acc_ref,
    sums_ref,
):
    _, cz, _, _, yb, xb = trig_ref.shape
    n = cz * COLS
    last = lax.axis_size("gy") - 1
    for side in range(2):
        inside = lax.axis_index("gy") != (0, last)[side]
        from_near = odd("gy") if side == 0 else jnp.logical_not(odd("gy"))
        e, q = (
            jnp.where(inside, jnp.where(from_near, y_near_ref[f * n : f * n + n, :], y_far_ref[f * n : f * n + n, :]), 0.0)
            for f in range(2)
        )
        for k, value in enumerate((e, q) + derived(e, q)):
            rim_ref[side, k] = value

    def get(k, z, p, j):
        return layer(outer_ref, inner_ref, k, z, p, j) if k < 2 else trig_ref[k - 2, z, p, j]

    for z in range(1, cz - 1):
        layer_terms(get, rim_ref, z, local_ref, z - 1, sums_ref)
    rows = (cz - 2) * yb
    sums_ref[15 * rows : 16 * rows, :] = jnp.zeros((rows, xb), jnp.float32)
    pairs = [yb // 2 + i for i in range(rows // 2)]
    acc_ref[...] = slot_sums(jnp.zeros(acc_ref.shape, jnp.float32), sums_ref, onehot_ref, pairs)


def outer_kernel(
    outer_ref, inner_ref, trig_ref, rim_ref, z_near_ref, z_far_ref, onehot_ref, acc_ref, ids_ref,
    message_ref, local_ref,
    halo_ref, sums_ref, total_ref,
):
    _, cz, _, _, yb, xb = trig_ref.shape
    for side in range(2):
        from_near = odd("gz") if side == 0 else jnp.logical_not(odd("gz"))
        for p in range(ROWS):
            for j in range(COLS):
                e, q = (jnp.where(from_near, z_near_ref[f, p, j], z_far_ref[f, p, j]) for f in range(2))
                for k, value in enumerate((e, q) + derived(e, q)):
                    halo_ref[side, k, p, j] = value

    def get(k, z, p, j):
        if z < 0 or z == cz:
            return halo_ref[int(z == cz), k, p, j]
        return layer(outer_ref, inner_ref, k, z, p, j) if k < 2 else trig_ref[k - 2, z, p, j]

    for at, z in enumerate((0, cz - 1)):
        layer_terms(get, rim_ref, z, local_ref, at, sums_ref)
    rows = 2 * yb
    sums_ref[15 * rows : 16 * rows, :] = jnp.zeros((rows, xb), jnp.float32)
    half = yb // 2
    pairs = list(range(half)) + list(range((cz - 1) * half, cz * half))
    total_ref[...] = slot_sums(acc_ref[...], sums_ref, onehot_ref, pairs)
    message_ref[0:5, :] = total_ref[0:5, :] + total_ref[5:10, :] + total_ref[10:15, :]
    message_ref[5:6, :] = ids_ref[...].astype(jnp.float32)
    message_ref[6:8, :] = jnp.zeros((2, message_ref.shape[1]), jnp.float32)


def stacked(value):
    return jnp.concatenate([part.astype(jnp.float32) for part in split3(value)], axis=0).astype(jnp.bfloat16)


def unstacked(value):
    return value[0:8] + value[8:16] + value[16:24]


def slot_motion(message_ref, near_ref, far_ref):
    slots = message_ref.shape[1]
    totals = message_ref[...]
    own = jnp.broadcast_to(message_ref[5:6, :], (slots, slots))
    for ref in (near_ref, far_ref):
        other = jnp.transpose(jnp.broadcast_to(ref[5:6, :], (slots, slots)))
        matches = jnp.where(other == own, 1.0, 0.0).astype(jnp.bfloat16)
        totals = totals + unstacked(jnp.dot(stacked(ref[...]), matches, preferred_element_type=jnp.float32))
    inverse = 1.0 / totals[4:5, :]
    return stacked(TRANSLATE * totals * inverse)


def block_motion(velocity, onehot_ref, motion_ref, pairs):
    rows = motion_ref.shape[0] // 8
    xb = motion_ref.shape[1]
    for i, pair in enumerate(pairs):
        moved = unstacked(jnp.dot(velocity, onehot_ref[pair], preferred_element_type=jnp.float32))
        for h in range(2):
            motion_ref[pl.ds(2 * i + h, 8, stride=rows), :] = moved[:, h * xb : (h + 1) * xb]


def advanced(local_ref, motion_ref, at, p, j):
    layers, yb = local_ref.shape[1], local_ref.shape[4]
    rows = layers * yb
    vx, vy, vz, turn = (motion_ref[k * rows + at * yb : k * rows + (at + 1) * yb, :] for k in range(4))
    g = [local_ref[k, at, p, j] for k in range(2, 8)]
    e = local_ref[0, at, p, j] - (vx * g[0] + vy * g[1] + vz * g[2])
    q = local_ref[1, at, p, j] + turn - (vx * g[3] + vy * g[4] + vz * g[5])
    return e, q


def outer_pairs(cz, yb):
    half = yb // 2
    return list(range(half)) + list(range((cz - 1) * half, cz * half))


def inner_pairs(cz, yb):
    return list(range(yb // 2, (cz - 1) * yb // 2))


def advance_outer_kernel(
    message_ref, near_ref, far_ref, onehot_ref, local_ref,
    velocity_ref, outer_ref, z_near_ref, z_far_ref,
    motion_ref,
):
    yb = local_ref.shape[4]
    cz = 2 * onehot_ref.shape[0] // yb
    velocity = slot_motion(message_ref, near_ref, far_ref)
    velocity_ref[...] = velocity
    block_motion(velocity, onehot_ref, motion_ref, outer_pairs(cz, yb))
    for at in range(2):
        for p in range(ROWS):
            for j in range(COLS):
                outer_ref[0, at, p, j], outer_ref[1, at, p, j] = advanced(local_ref, motion_ref, at, p, j)
    put_z_edges(outer_ref, z_near_ref, z_far_ref)


def advance_inner_kernel(
    velocity_ref, onehot_ref, local_ref, outer_ref,
    inner_ref, y_near_ref, y_far_ref,
    motion_ref,
):
    _, layers, _, _, yb, _ = local_ref.shape
    block_motion(velocity_ref[...], onehot_ref, motion_ref, inner_pairs(layers + 2, yb))
    for at in range(layers):
        for p in range(ROWS):
            for j in range(COLS):
                inner_ref[0, at, p, j], inner_ref[1, at, p, j] = advanced(local_ref, motion_ref, at, p, j)
    put_y_edges(outer_ref, inner_ref, y_near_ref, y_far_ref)


def finish_kernel(
    message_ref, near_ref, far_ref, onehot_ref, outer_local_ref, inner_local_ref,
    e_hbm, q_hbm,
    outer_motion_ref, inner_motion_ref, rows_ref, out_ref, sems,
):
    yb, xb = outer_local_ref.shape[4:]
    _, cz, cy, nx = out_ref.shape
    velocity = slot_motion(message_ref, near_ref, far_ref)
    block_motion(velocity, onehot_ref, outer_motion_ref, outer_pairs(cz, yb))
    block_motion(velocity, onehot_ref, inner_motion_ref, inner_pairs(cz, yb))
    for z in range(cz):
        for p in range(ROWS):
            to = pl.ds(z * cy + p, yb, stride=ROWS)
            for j in range(COLS):
                if z in (0, cz - 1):
                    e, q = advanced(outer_local_ref, outer_motion_ref, int(z > 0), p, j)
                else:
                    e, q = advanced(inner_local_ref, inner_motion_ref, z - 1, p, j)
                rows_ref[0, j, to, :] = e
                rows_ref[1, j, to, :] = q
    chooser = x_chooser(nx, xb, back=True)
    copies = []
    for f, ref in enumerate((e_hbm, q_hbm)):
        moved = exact_dot(jnp.concatenate([rows_ref[f, j] for j in range(COLS)], axis=1), chooser)
        out_ref[f] = moved.reshape(out_ref.shape[1:])
        copies.append(pltpu.make_async_copy(out_ref.at[f], ref, sems.at[f]))
        copies[f].start()
    for copy in copies:
        copy.wait()


VMEM = pl.BlockSpec(memory_space=pltpu.VMEM)
HBM = pl.BlockSpec(memory_space=pltpu.HBM)


def call(kernel, name, outs, scratch=(), cycles=1000, in_spec=VMEM, out_spec=VMEM):
    def run(*args):
        return pl.pallas_call(
            kernel,
            name=name,
            in_specs=[in_spec] * len(args),
            out_specs=[out_spec] * len(outs),
            out_shape=[jax.ShapeDtypeStruct(shape, dtype) for shape, dtype in outs],
            scratch_shapes=list(scratch),
            compiler_params=pltpu.CompilerParams(vmem_limit_bytes=24 * 1024 * 1024),
            cost_estimate=pl.CostEstimate(flops=cycles * 4096, bytes_accessed=cycles * 1024, transcendentals=0),
        )(*args)

    return run


def swap(array, axis, far):
    size = lax.axis_size(axis)
    pairs = [(i, (((i + 1) ^ 1) - 1) % size if far else i ^ 1) for i in range(size)]
    return lax.ppermute(array, axis, pairs)


def both(near, far, axis):
    far = swap(far, axis, True)
    return swap(near, axis, False), far


def shards(order_param, orientation, cell_slot, tile_grains):
    cz, cy, nx = order_param.shape
    slots = tile_grains.shape[-1]
    yb, xb = cy // ROWS, nx // COLS
    rows = cz * yb
    f32, bf16 = jnp.float32, jnp.bfloat16
    ids = tile_grains.reshape(1, slots)
    block = (ROWS, COLS, yb, xb)
    outer_out, inner_out = ((2, 2) + block, f32), ((2, cz - 2) + block, f32)
    z_out, y_out = [((2,) + block, f32)] * 2, [((2 * cz * COLS, xb), f32)] * 2
    outer_motion = pltpu.VMEM((8 * 2 * yb, xb), f32)
    inner_motion = pltpu.VMEM((8 * (cz - 2) * yb, xb), f32)
    outer_sums = pltpu.VMEM((16 * 2 * yb, xb), f32)
    inner_sums = pltpu.VMEM((16 * (cz - 2) * yb, xb), f32)
    acc = pltpu.VMEM((16, slots), f32)
    tile2 = pltpu.VMEM((2, cz, cy, nx), f32)
    prepare = call(
        prepare_kernel, "prepare", [outer_out, inner_out] + z_out + y_out,
        [tile2, pltpu.VMEM((COLS, cz * cy, xb), f32), pltpu.SemaphoreType.DMA((2,))], in_spec=HBM,
    )
    onehots = call(
        onehot_kernel, "onehots", [((rows // 2, slots, 2 * xb), bf16)],
        [pltpu.VMEM((cz, cy, nx), jnp.int32), pltpu.VMEM((cz * cy, xb), f32), pltpu.SemaphoreType.DMA(())], in_spec=HBM,
    )
    trigs = call(trig_kernel, "trigs", [((4, cz) + block, f32)])
    inner_terms = call(
        inner_kernel, "inner_terms",
        [((2, 6, cz * COLS, xb), f32), ((8, cz - 2) + block, f32), ((16, slots), f32)], [inner_sums],
    )
    outer_terms = call(
        outer_kernel, "outer_terms", [((8, slots), f32), ((8, 2) + block, f32)],
        [pltpu.VMEM((2, 6) + block, f32), outer_sums, acc],
    )
    advance_outer = call(
        advance_outer_kernel, "advance_outer", [((24, slots), bf16), outer_out] + z_out, [outer_motion]
    )
    advance_inner = call(advance_inner_kernel, "advance_inner", [inner_out] + y_out, [inner_motion])
    finish = call(
        finish_kernel, "finish", [((cz, cy, nx), f32)] * 2,
        [outer_motion, inner_motion, pltpu.VMEM((2, COLS, cz * cy, xb), f32), tile2, pltpu.SemaphoreType.DMA((2,))],
        out_spec=HBM,
    )

    outer, inner, z_near, z_far, y_near, y_far = prepare(order_param, orientation)
    for step in range(STEPS):
        z_near, z_far = both(z_near, z_far, "gz")
        if step > 0:
            inner, y_near, y_far = advance_inner(velocity, onehot, inner_local, outer)
        y_near, y_far = both(y_near, y_far, "gy")
        if step == 0:
            (onehot,) = onehots(cell_slot)
        (trig,) = trigs(outer, inner)
        rim, inner_local, sums = inner_terms(outer, inner, trig, y_near, y_far, onehot)
        message, outer_local = outer_terms(outer, inner, trig, rim, z_near, z_far, onehot, sums, ids)
        near, far = both(message, message, "gz")
        if step < STEPS - 1:
            velocity, outer, z_near, z_far = advance_outer(message, near, far, onehot, outer_local)
    return tuple(finish(message, near, far, onehot, outer_local, inner_local))


def solution(mesh):
    spec = P("gz", "gy", None)
    return jax.shard_map(shards, mesh=mesh, in_specs=(spec,) * 4, out_specs=(spec,) * 2, check_vma=False)
```

time: 2110 us -> 58.4 us (0.03)
  other arithmetic: 1210 us -> 0 us
  local copies, waits for them, and re-layouts: 829 us -> 2.85 us
    scatter-add x3 -> x0, other arithmetic: 1120 us -> none  [shards(): jax.ops.segment_sum(values, flat_slot, num_segments=slot_count)]
    gather x6 -> x0, local copies, waits for them, and re-layouts: 730 us -> none  [shards(): motion = jnp.take(velocity, cell_slot, axis=1)]
    another operation x24 -> x0, local copies, waits for them, and re-layouts: 95.9 us -> none  [the longest x21 95.5 us: cell_terms(): jnp.stack([weight * gradients[0][0], weight * gradients[1][0], weight * g...]
    add x8 -> x0, other arithmetic: 29.3 us -> none  [the longest x3 20.2 us: cell_terms(): torque = torque + other_phase * other_phase * jnp.sin(mismatch)]
    mul x15 -> x0, other arithmetic: 27.7 us -> none  [the longest x3 21.1 us: cell_terms(): weight * gradients[2][0]]
  transfers between devices with their start and end apart: 18 -> 18, of which waited for: 9 -> 7; matrix products, arithmetic and copies ran while one was open for 1% -> 0% of each run, Pallas kernels for 0% -> 11%
where the time goes in v2:
time: 58.4 us; the launch traced here: 58.2 us
  starting transfers between devices  24.4 us (42%)
  Pallas kernels  15.4 us (26%)
  waiting for transfers between devices  14.7 us (25%)
  local copies, waits for them, and re-layouts  2.85 us (5%)
  between operations  0.8 us (1%)
    ppermute x18, starting transfers between devices, swap(): return lax.ppermute(array, axis, pairs)  24.4 us
    pallas_call x16, Pallas kernels, run(): pl.pallas_call(kernel, name=name, in_specs=[in_spec] * len(args), out_spe...  15.4 us
    ppermute x18, waiting for transfers between devices, swap(): return lax.ppermute(array, axis, pairs)  14.7 us
    unnamed x8, local copies, waits for them, and re-layouts  2.85 us
  transfers between devices with their start and end apart: 18, of which 7 were waited for; matrix products, arithmetic and copies ran while one was open for 0% of the time, Pallas kernels for 11%

profile of v2, /device:TPU:0, one launch (start us, length us, event | category | flops | bytes accessed | tf_op | source)
XLA Modules:
  0.0 58.2 jit_solution(1312121567039224399)
XLA Ops:
  0.6 0.0 copy-start.1
  0.6 0.9 %copy-done.1 = f32[4,32,512]{2,1,0:T(8,128)S(1)} copy-done((f32[4,32,512]{2,1,0:T(8,128)S(1)}, f32[4,32,512]{2,1,0:T(8,128)}, u32[]{:S(2)}) %copy-start.1) | copy-done | bytes 262168
  1.6 0.0 copy-start.2
  1.6 0.9 %copy-done.2 = f32[4,32,512]{2,1,0:T(8,128)S(1)} copy-done((f32[4,32,512]{2,1,0:T(8,128)S(1)}, f32[4,32,512]{2,1,0:T(8,128)}, u32[]{:S(2)}) %copy-start.2) | copy-done | bytes 262168
  2.5 1.0 %prepare.1 = (f32[2,2,2,4,16,128]{5,4,3,2,1,0:T(8,128)S(1)}, f32[2,2,2,4,16,128]{5,4,3,2,1,0:T(8,128)S(1)}, f32[2,2,4,16,128]{4,3,2,1,0:T(8,128)S(1)}, f32[2,2,4...) custom-call(f32[4,32,512]{2,1,0:T(8,128)S(1)} %copy-done.1, f32[4,32,512]{2,1,0:T(8,128)S(1)} %copy-done.2), custom_call_target="tpu_custom_call" | custom-call | flops 4096000 | bytes 1024000 | tf_op jit(solution)/shard_map/prepare/pallas_call | solution.py:393
  3.6 3.0 %collective-permute-start.2 = (f32[2,2,4,16,128]{4,3,2,1,0:T(8,128)S(1)}, f32[2,2,4,16,128]{4,3,2,1,0:T(8,128)S(1)}, u32[]{:S(2)}, u32[]{:S(2)}) collective-permute-start(f32[2,2,4,16,128]{4,3,2,1,0:T(8,128)S(1)} %get-tuple-element.42), channel_id=1, source_target_pairs={{0,4},{4,0},{8,12},{12,8},{16,20},{20,16},{24,28},{28,24},{1,5},{5... | collective-permute-start | bytes 393224 | tf_op jit(solution)/shard_map/ppermute | solution.py:410
  6.6 3.5 %collective-permute-start.3 = (f32[2,2,4,16,128]{4,3,2,1,0:T(8,128)S(1)}, f32[2,2,4,16,128]{4,3,2,1,0:T(8,128)S(1)}, u32[]{:S(2)}, u32[]{:S(2)}) collective-permute-start(f32[2,2,4,16,128]{4,3,2,1,0:T(8,128)S(1)} %get-tuple-element.43), channel_id=1, source_target_pairs={{0,28},{4,8},{8,4},{12,16},{16,12},{20,24},{24,20},{28,0},{1,29},{... | collective-permute-start | bytes 393224 | tf_op jit(solution)/shard_map/ppermute | solution.py:410
  10.2 0.0 collective-permute-start
  10.2 1.6 %collective-permute-start.1 = (f32[32,128]{1,0:T(8,128)S(1)}, f32[32,128]{1,0:T(8,128)S(1)}, u32[]{:S(2)}, u32[]{:S(2)}) collective-permute-start(f32[32,128]{1,0:T(8,128)S(1)} %get-tuple-element.40), channel_id=1, source_target_pairs={{0,3},{1,2},{2,1},{3,0},{4,7},{5,6},{6,5},{7,4},{8,11},{9,10},{10,... | collective-permute-start | bytes 49160 | tf_op jit(solution)/shard_map/ppermute | solution.py:410
  11.8 0.0 copy-start
  11.8 0.9 %copy-done = s32[4,32,512]{2,1,0:T(8,128)S(1)} copy-done((s32[4,32,512]{2,1,0:T(8,128)S(1)}, s32[4,32,512]{2,1,0:T(8,128)}, u32[]{:S(2)}) %copy-start) | copy-done | bytes 262168
  12.7 1.1 %onehots.1.onehot_ref = bf16[32,256,256]{2,1,0:T(8,128)(2,1)S(1)} custom-call(s32[4,32,512]{2,1,0:T(8,128)S(1)} %copy-done), custom_call_target="tpu_custom_call" | custom-call | flops 4096000 | bytes 1024000 | tf_op jit(solution)/shard_map/onehots/pallas_call | solution.py:393
  13.8 0.0 copy-start.3
  13.8 0.4 trigs.3.trig_ref
  14.2 0.0 collective-permute-done.y_near_ref
  14.2 0.0 collective-permute-done.1.y_far_ref
  14.2 1.1 %inner_terms.3 = (f32[2,6,16,128]{3,2,1,0:T(8,128)S(1)}, f32[8,2,2,4,16,128]{5,4,3,2,1,0:T(8,128)S(1)}, f32[16,256]{1,0:T(8,128)S(1)}) custom-call(f32[2,2,2,4,16,128]{5,4,3,2,1,0:T(8,128)S(1)} %get-tuple-element.37.outer_ref, f32[2,2,2,4,16,128]{5,4,3,2,1,0:T(8,128)S(1)} %get-tuple-element.38.inner_ref, f32[4,4,2,4,16,128]{5,4,3,2,1,0:T(8,128)S(1)} %trigs.3.trig_ref, ...), custom_call_target="tpu_custom_call" | custom-call | flops 4096000 | bytes 1024000 | tf_op jit(solution)/shard_map/inner_terms/pallas_call | solution.py:393
  15.3 0.0 collective-permute-done.2.z_near_ref
  15.3 0.0 collective-permute-done.3.z_far_ref
  15.3 0.0 copy-done.3
  15.3 1.2 %outer_terms.3 = (f32[8,256]{1,0:T(8,128)S(1)}, f32[8,2,2,4,16,128]{5,4,3,2,1,0:T(8,128)S(1)}) custom-call(f32[2,2,2,4,16,128]{5,4,3,2,1,0:T(8,128)S(1)} %get-tuple-element.37.outer_ref, f32[2,2,2,4,16,128]{5,4,3,2,1,0:T(8,128)S(1)} %get-tuple-element.38.inner_ref, f32[4,4,2,4,16,128]{5,4,3,2,1,0:T(8,128)S(1)} %trigs.3.trig_ref, ...), custom_call_target="tpu_custom_call" | custom-call | flops 4096000 | bytes 1024000 | tf_op jit(solution)/shard_map/outer_terms/pallas_call | solution.py:393
  16.6 2.5 %collective-permute-start.5 = (f32[8,256]{1,0:T(8,128)S(1)}, f32[8,256]{1,0:T(8,128)S(1)}, u32[]{:S(2)}, u32[]{:S(2)}) collective-permute-start(f32[8,256]{1,0:T(8,128)S(1)} %get-tuple-element.45.message_ref), channel_id=1, source_target_pairs={{0,28},{4,8},{8,4},{12,16},{16,12},{20,24},{24,20},{28,0},{1,29},{... | collective-permute-start | bytes 24584 | tf_op jit(solution)/shard_map/ppermute | solution.py:410
  19.1 0.0 collective-permute-start.4
  19.1 3.9 %collective-permute-done.5.far_ref = f32[8,256]{1,0:T(8,128)S(1)} collective-permute-done((f32[8,256]{1,0:T(8,128)S(1)}, f32[8,256]{1,0:T(8,128)S(1)}, u32[]{:S(2)}, u32[]{:S(2)}) %collective-permute-start.5) | collective-permute-done | bytes 8224 | tf_op jit(solution)/shard_map/ppermute | solution.py:410
  23.0 0.0 collective-permute-done.4.near_ref
  23.0 0.8 %advance_outer.2 = (bf16[24,256]{1,0:T(8,128)(2,1)S(1)}, f32[2,2,2,4,16,128]{5,4,3,2,1,0:T(8,128)S(1)}, f32[2,2,4,16,128]{4,3,2,1,0:T(8,128)S(1)}, f32[2,2,4,16,128]{4,3,2,1,0:T(8,128)S(1)}) custom-call(f32[8,256]{1,0:T(8,128)S(1)} %get-tuple-element.45.message_ref, f32[8,256]{1,0:T(8,128)S(1)} %collective-permute-done.4.near_ref, ...), custom_call_target="tpu_custom_call" | custom-call | flops 4096000 | bytes 1024000 | tf_op jit(solution)/shard_map/advance_outer/pallas_call | solution.py:393
  23.8 0.1 collective-permute-start.8
  23.9 2.5 %collective-permute-start.9 = (f32[2,2,4,16,128]{4,3,2,1,0:T(8,128)S(1)}, f32[2,2,4,16,128]{4,3,2,1,0:T(8,128)S(1)}, u32[]{:S(2)}, u32[]{:S(2)}) collective-permute-start(f32[2,2,4,16,128]{4,3,2,1,0:T(8,128)S(1)} %get-tuple-element.55), channel_id=1, source_target_pairs={{0,28},{4,8},{8,4},{12,16},{16,12},{20,24},{24,20},{28,0},{1,29},{... | collective-permute-start | bytes 393224 | tf_op jit(solution)/shard_map/ppermute | solution.py:410
  26.4 0.5 advance_inner.2
  27.0 0.1 collective-permute-start.6
  27.0 1.6 %collective-permute-start.7 = (f32[32,128]{1,0:T(8,128)S(1)}, f32[32,128]{1,0:T(8,128)S(1)}, u32[]{:S(2)}, u32[]{:S(2)}) collective-permute-start(f32[32,128]{1,0:T(8,128)S(1)} %get-tuple-element.52), channel_id=1, source_target_pairs={{0,3},{1,2},{2,1},{3,0},{4,7},{5,6},{6,5},{7,4},{8,11},{9,10},{10,... | collective-permute-start | bytes 49160 | tf_op jit(solution)/shard_map/ppermute | solution.py:410
  28.6 0.4 trigs.4.trig_ref
  29.0 0.0 collective-permute-done.6.y_near_ref
  29.0 1.2 %collective-permute-done.7.y_far_ref = f32[32,128]{1,0:T(8,128)S(1)} collective-permute-done((f32[32,128]{1,0:T(8,128)S(1)}, f32[32,128]{1,0:T(8,128)S(1)}, u32[]{:S(2)}, u32[]{:S(2)}) %collective-permute-start.7) | collective-permute-done | bytes 16416 | tf_op jit(solution)/shard_map/ppermute | solution.py:410
  30.3 1.1 %inner_terms.4 = (f32[2,6,16,128]{3,2,1,0:T(8,128)S(1)}, f32[8,2,2,4,16,128]{5,4,3,2,1,0:T(8,128)S(1)}, f32[16,256]{1,0:T(8,128)S(1)}) custom-call(f32[2,2,2,4,16,128]{5,4,3,2,1,0:T(8,128)S(1)} %get-tuple-element.47.outer_ref, f32[2,2,2,4,16,128]{5,4,3,2,1,0:T(8,128)S(1)} %get-tuple-element.50.inner_ref, f32[4,4,2,4,16,128]{5,4,3,2,1,0:T(8,128)S(1)} %trigs.4.trig_ref, ...), custom_call_target="tpu_custom_call" | custom-call | flops 4096000 | bytes 1024000 | tf_op jit(solution)/shard_map/inner_terms/pallas_call | solution.py:393
  31.3 0.0 collective-permute-done.8.z_near_ref
  31.3 0.3 collective-permute-done.9.z_far_ref
  31.6 1.3 %outer_terms.4 = (f32[8,256]{1,0:T(8,128)S(1)}, f32[8,2,2,4,16,128]{5,4,3,2,1,0:T(8,128)S(1)}) custom-call(f32[2,2,2,4,16,128]{5,4,3,2,1,0:T(8,128)S(1)} %get-tuple-element.47.outer_ref, f32[2,2,2,4,16,128]{5,4,3,2,1,0:T(8,128)S(1)} %get-tuple-element.50.inner_ref, f32[4,4,2,4,16,128]{5,4,3,2,1,0:T(8,128)S(1)} %trigs.4.trig_ref, ...), custom_call_target="tpu_custom_call" | custom-call | flops 4096000 | bytes 1024000 | tf_op jit(solution)/shard_map/outer_terms/pallas_call | solution.py:393
  32.9 2.5 %collective-permute-start.11 = (f32[8,256]{1,0:T(8,128)S(1)}, f32[8,256]{1,0:T(8,128)S(1)}, u32[]{:S(2)}, u32[]{:S(2)}) collective-permute-start(f32[8,256]{1,0:T(8,128)S(1)} %get-tuple-element.57.message_ref), channel_id=1, source_target_pairs={{0,28},{4,8},{8,4},{12,16},{16,12},{20,24},{24,20},{28,0},{1,29},{... | collective-permute-start | bytes 24584 | tf_op jit(solution)/shard_map/ppermute | solution.py:410
  35.5 0.0 collective-permute-start.10
  35.5 3.9 %collective-permute-done.11.far_ref = f32[8,256]{1,0:T(8,128)S(1)} collective-permute-done((f32[8,256]{1,0:T(8,128)S(1)}, f32[8,256]{1,0:T(8,128)S(1)}, u32[]{:S(2)}, u32[]{:S(2)}) %collective-permute-start.11) | collective-permute-done | bytes 8224 | tf_op jit(solution)/shard_map/ppermute | solution.py:410
  39.3 0.0 collective-permute-done.10.near_ref
  39.3 0.8 %advance_outer.3 = (bf16[24,256]{1,0:T(8,128)(2,1)S(1)}, f32[2,2,2,4,16,128]{5,4,3,2,1,0:T(8,128)S(1)}, f32[2,2,4,16,128]{4,3,2,1,0:T(8,128)S(1)}, f32[2,2,4,16,128]{4,3,2,1,0:T(8,128)S(1)}) custom-call(f32[8,256]{1,0:T(8,128)S(1)} %get-tuple-element.57.message_ref, f32[8,256]{1,0:T(8,128)S(1)} %collective-permute-done.10.near_ref, ...), custom_call_target="tpu_custom_call" | custom-call | flops 4096000 | bytes 1024000 | tf_op jit(solution)/shard_map/advance_outer/pallas_call | solution.py:393
  40.1 0.1 collective-permute-start.14
  40.2 2.5 %collective-permute-start.15 = (f32[2,2,4,16,128]{4,3,2,1,0:T(8,128)S(1)}, f32[2,2,4,16,128]{4,3,2,1,0:T(8,128)S(1)}, u32[]{:S(2)}, u32[]{:S(2)}) collective-permute-start(f32[2,2,4,16,128]{4,3,2,1,0:T(8,128)S(1)} %get-tuple-element.67), channel_id=1, source_target_pairs={{0,28},{4,8},{8,4},{12,16},{16,12},{20,24},{24,20},{28,0},{1,29},{... | collective-permute-start | bytes 393224 | tf_op jit(solution)/shard_map/ppermute | solution.py:410
  42.8 0.5 advance_inner.3
  43.3 0.1 collective-permute-start.12
  43.4 1.6 %collective-permute-start.13 = (f32[32,128]{1,0:T(8,128)S(1)}, f32[32,128]{1,0:T(8,128)S(1)}, u32[]{:S(2)}, u32[]{:S(2)}) collective-permute-start(f32[32,128]{1,0:T(8,128)S(1)} %get-tuple-element.64), channel_id=1, source_target_pairs={{0,3},{1,2},{2,1},{3,0},{4,7},{5,6},{6,5},{7,4},{8,11},{9,10},{10,... | collective-permute-start | bytes 49160 | tf_op jit(solution)/shard_map/ppermute | solution.py:410
  45.0 0.4 trigs.5.trig_ref
  45.3 0.0 collective-permute-done.12.y_near_ref
  45.4 1.2 %collective-permute-done.13.y_far_ref = f32[32,128]{1,0:T(8,128)S(1)} collective-permute-done((f32[32,128]{1,0:T(8,128)S(1)}, f32[32,128]{1,0:T(8,128)S(1)}, u32[]{:S(2)}, u32[]{:S(2)}) %collective-permute-start.13) | collective-permute-done | bytes 16416 | tf_op jit(solution)/shard_map/ppermute | solution.py:410
  46.6 1.1 %inner_terms.5 = (f32[2,6,16,128]{3,2,1,0:T(8,128)S(1)}, f32[8,2,2,4,16,128]{5,4,3,2,1,0:T(8,128)S(1)}, f32[16,256]{1,0:T(8,128)S(1)}) custom-call(f32[2,2,2,4,16,128]{5,4,3,2,1,0:T(8,128)S(1)} %get-tuple-element.59.outer_ref, f32[2,2,2,4,16,128]{5,4,3,2,1,0:T(8,128)S(1)} %get-tuple-element.62.inner_ref, f32[4,4,2,4,16,128]{5,4,3,2,1,0:T(8,128)S(1)} %trigs.5.trig_ref, ...), custom_call_target="tpu_custom_call" | custom-call | flops 4096000 | bytes 1024000 | tf_op jit(solution)/shard_map/inner_terms/pallas_call | solution.py:393
  47.7 0.0 collective-permute-done.14.z_near_ref
  47.7 0.3 collective-permute-done.15.z_far_ref
  48.0 1.3 %outer_terms.5 = (f32[8,256]{1,0:T(8,128)S(1)}, f32[8,2,2,4,16,128]{5,4,3,2,1,0:T(8,128)S(1)}) custom-call(f32[2,2,2,4,16,128]{5,4,3,2,1,0:T(8,128)S(1)} %get-tuple-element.59.outer_ref, f32[2,2,2,4,16,128]{5,4,3,2,1,0:T(8,128)S(1)} %get-tuple-element.62.inner_ref, f32[4,4,2,4,16,128]{5,4,3,2,1,0:T(8,128)S(1)} %trigs.5.trig_ref, ...), custom_call_target="tpu_custom_call" | custom-call | flops 4096000 | bytes 1024000 | tf_op jit(solution)/shard_map/outer_terms/pallas_call | solution.py:393
  49.2 2.5 %collective-permute-start.17 = (f32[8,256]{1,0:T(8,128)S(1)}, f32[8,256]{1,0:T(8,128)S(1)}, u32[]{:S(2)}, u32[]{:S(2)}) collective-permute-start(f32[8,256]{1,0:T(8,128)S(1)} %get-tuple-element.69.message_ref), channel_id=1, source_target_pairs={{0,28},{4,8},{8,4},{12,16},{16,12},{20,24},{24,20},{28,0},{1,29},{... | collective-permute-start | bytes 24584 | tf_op jit(solution)/shard_map/ppermute | solution.py:410
  51.8 0.0 collective-permute-start.16
  51.8 3.9 %collective-permute-done.17.far_ref = f32[8,256]{1,0:T(8,128)S(1)} collective-permute-done((f32[8,256]{1,0:T(8,128)S(1)}, f32[8,256]{1,0:T(8,128)S(1)}, u32[]{:S(2)}, u32[]{:S(2)}) %collective-permute-start.17) | collective-permute-done | bytes 8224 | tf_op jit(solution)/shard_map/ppermute | solution.py:410
  55.6 0.0 collective-permute-done.16.near_ref
  55.7 2.6 %finish.1 = (f32[4,32,512]{2,1,0:T(8,128)}, f32[4,32,512]{2,1,0:T(8,128)}) custom-call(f32[8,256]{1,0:T(8,128)S(1)} %get-tuple-element.69.message_ref, f32[8,256]{1,0:T(8,128)S(1)} %collective-permute-done.16.near_ref, f32[8,256]{1,0:T(8,128)S(1)} %collective-permute-done.17.far_ref, bf16[32,256,256]{2,1,0:T(8,128)(2,1)S(1)} %onehots.1.onehot_ref, ...), custom_call_target="tpu_custom_call" | custom-call | flops 4096000 | bytes 1024000 | tf_op jit(solution)/shard_map/finish/pallas_call | solution.py:393
Async XLA Ops:
  0.6 1.0 %copy-start.1 = (f32[4,32,512]{2,1,0:T(8,128)S(1)}, f32[4,32,512]{2,1,0:T(8,128)}, u32[]{:S(2)}) copy-start(f32[4,32,512]{2,1,0:T(8,128)} %e_hbm.1) | copy-start | bytes 786436
  1.6 0.9 %copy-start.2 = (f32[4,32,512]{2,1,0:T(8,128)S(1)}, f32[4,32,512]{2,1,0:T(8,128)}, u32[]{:S(2)}) copy-start(f32[4,32,512]{2,1,0:T(8,128)} %q_hbm.1) | copy-start | bytes 786436
  3.6 11.7 %collective-permute-start.2 = (f32[2,2,4,16,128]{4,3,2,1,0:T(8,128)S(1)}, f32[2,2,4,16,128]{4,3,2,1,0:T(8,128)S(1)}, u32[]{:S(2)}, u32[]{:S(2)}) collective-permute-start(f32[2,2,4,16,128]{4,3,2,1,0:T(8,128)S(1)} %get-tuple-element.42), channel_id=1, source_target_pairs={{0,4},{4,0},{8,12},{12,8},{16,20},{20,16},{24,28},{28,24},{1,5},{5... | collective-permute-start | bytes 393224 | tf_op jit(solution)/shard_map/ppermute | solution.py:410
  6.6 8.7 %collective-permute-start.3 = (f32[2,2,4,16,128]{4,3,2,1,0:T(8,128)S(1)}, f32[2,2,4,16,128]{4,3,2,1,0:T(8,128)S(1)}, u32[]{:S(2)}, u32[]{:S(2)}) collective-permute-start(f32[2,2,4,16,128]{4,3,2,1,0:T(8,128)S(1)} %get-tuple-element.43), channel_id=1, source_target_pairs={{0,28},{4,8},{8,4},{12,16},{16,12},{20,24},{24,20},{28,0},{1,29},{... | collective-permute-start | bytes 393224 | tf_op jit(solution)/shard_map/ppermute | solution.py:410
  10.2 4.1 %collective-permute-start = (f32[32,128]{1,0:T(8,128)S(1)}, f32[32,128]{1,0:T(8,128)S(1)}, u32[]{:S(2)}, u32[]{:S(2)}) collective-permute-start(f32[32,128]{1,0:T(8,128)S(1)} %get-tuple-element.39), channel_id=1, source_target_pairs={{0,1},{1,0},{2,3},{3,2},{4,5},{5,4},{6,7},{7,6},{8,9},{9,8},{10,11... | collective-permute-start | bytes 49160 | tf_op jit(solution)/shard_map/ppermute | solution.py:410
  10.2 4.1 %collective-permute-start.1 = (f32[32,128]{1,0:T(8,128)S(1)}, f32[32,128]{1,0:T(8,128)S(1)}, u32[]{:S(2)}, u32[]{:S(2)}) collective-permute-start(f32[32,128]{1,0:T(8,128)S(1)} %get-tuple-element.40), channel_id=1, source_target_pairs={{0,3},{1,2},{2,1},{3,0},{4,7},{5,6},{6,5},{7,4},{8,11},{9,10},{10,... | collective-permute-start | bytes 49160 | tf_op jit(solution)/shard_map/ppermute | solution.py:410
  11.8 0.9 %copy-start = (s32[4,32,512]{2,1,0:T(8,128)S(1)}, s32[4,32,512]{2,1,0:T(8,128)}, u32[]{:S(2)}) copy-start(s32[4,32,512]{2,1,0:T(8,128)} %slot_hbm.1) | copy-start | bytes 786436
  13.8 1.5 %copy-start.3 = (s32[1,1,256]{2,1,0:T(1,128)S(1)}, s32[1,1,256]{2,1,0:T(1,128)}, u32[]{:S(2)}) copy-start(s32[1,1,256]{2,1,0:T(1,128)} %param.7) | copy-start | bytes 3076
  16.6 6.4 %collective-permute-start.5 = (f32[8,256]{1,0:T(8,128)S(1)}, f32[8,256]{1,0:T(8,128)S(1)}, u32[]{:S(2)}, u32[]{:S(2)}) collective-permute-start(f32[8,256]{1,0:T(8,128)S(1)} %get-tuple-element.45.message_ref), channel_id=1, source_target_pairs={{0,28},{4,8},{8,4},{12,16},{16,12},{20,24},{24,20},{28,0},{1,29},{... | collective-permute-start | bytes 24584 | tf_op jit(solution)/shard_map/ppermute | solution.py:410
  19.1 3.9 %collective-permute-start.4 = (f32[8,256]{1,0:T(8,128)S(1)}, f32[8,256]{1,0:T(8,128)S(1)}, u32[]{:S(2)}, u32[]{:S(2)}) collective-permute-start(f32[8,256]{1,0:T(8,128)S(1)} %get-tuple-element.45.message_ref), channel_id=1, source_target_pairs={{0,4},{4,0},{8,12},{12,8},{16,20},{20,16},{24,28},{28,24},{1,5},{5... | collective-permute-start | bytes 24584 | tf_op jit(solution)/shard_map/ppermute | solution.py:410
  23.8 7.5 %collective-permute-start.8 = (f32[2,2,4,16,128]{4,3,2,1,0:T(8,128)S(1)}, f32[2,2,4,16,128]{4,3,2,1,0:T(8,128)S(1)}, u32[]{:S(2)}, u32[]{:S(2)}) collective-permute-start(f32[2,2,4,16,128]{4,3,2,1,0:T(8,128)S(1)} %get-tuple-element.54), channel_id=1, source_target_pairs={{0,4},{4,0},{8,12},{12,8},{16,20},{20,16},{24,28},{28,24},{1,5},{5... | collective-permute-start | bytes 393224 | tf_op jit(solution)/shard_map/ppermute | solution.py:410
  23.9 7.8 %collective-permute-start.9 = (f32[2,2,4,16,128]{4,3,2,1,0:T(8,128)S(1)}, f32[2,2,4,16,128]{4,3,2,1,0:T(8,128)S(1)}, u32[]{:S(2)}, u32[]{:S(2)}) collective-permute-start(f32[2,2,4,16,128]{4,3,2,1,0:T(8,128)S(1)} %get-tuple-element.55), channel_id=1, source_target_pairs={{0,28},{4,8},{8,4},{12,16},{16,12},{20,24},{24,20},{28,0},{1,29},{... | collective-permute-start | bytes 393224 | tf_op jit(solution)/shard_map/ppermute | solution.py:410
  27.0 2.1 %collective-permute-start.6 = (f32[32,128]{1,0:T(8,128)S(1)}, f32[32,128]{1,0:T(8,128)S(1)}, u32[]{:S(2)}, u32[]{:S(2)}) collective-permute-start(f32[32,128]{1,0:T(8,128)S(1)} %get-tuple-element.51), channel_id=1, source_target_pairs={{0,1},{1,0},{2,3},{3,2},{4,5},{5,4},{6,7},{7,6},{8,9},{9,8},{10,11... | collective-permute-start | bytes 49160 | tf_op jit(solution)/shard_map/ppermute | solution.py:410
  27.0 3.2 %collective-permute-start.7 = (f32[32,128]{1,0:T(8,128)S(1)}, f32[32,128]{1,0:T(8,128)S(1)}, u32[]{:S(2)}, u32[]{:S(2)}) collective-permute-start(f32[32,128]{1,0:T(8,128)S(1)} %get-tuple-element.52), channel_id=1, source_target_pairs={{0,3},{1,2},{2,1},{3,0},{4,7},{5,6},{6,5},{7,4},{8,11},{9,10},{10,... | collective-permute-start | bytes 49160 | tf_op jit(solution)/shard_map/ppermute | solution.py:410
  32.9 6.4 %collective-permute-start.11 = (f32[8,256]{1,0:T(8,128)S(1)}, f32[8,256]{1,0:T(8,128)S(1)}, u32[]{:S(2)}, u32[]{:S(2)}) collective-permute-start(f32[8,256]{1,0:T(8,128)S(1)} %get-tuple-element.57.message_ref), channel_id=1, source_target_pairs={{0,28},{4,8},{8,4},{12,16},{16,12},{20,24},{24,20},{28,0},{1,29},{... | collective-permute-start | bytes 24584 | tf_op jit(solution)/shard_map/ppermute | solution.py:410
  35.5 3.9 %collective-permute-start.10 = (f32[8,256]{1,0:T(8,128)S(1)}, f32[8,256]{1,0:T(8,128)S(1)}, u32[]{:S(2)}, u32[]{:S(2)}) collective-permute-start(f32[8,256]{1,0:T(8,128)S(1)} %get-tuple-element.57.message_ref), channel_id=1, source_target_pairs={{0,4},{4,0},{8,12},{12,8},{16,20},{20,16},{24,28},{28,24},{1,5},{5... | collective-permute-start | bytes 24584 | tf_op jit(solution)/shard_map/ppermute | solution.py:410
  40.1 7.5 %collective-permute-start.14 = (f32[2,2,4,16,128]{4,3,2,1,0:T(8,128)S(1)}, f32[2,2,4,16,128]{4,3,2,1,0:T(8,128)S(1)}, u32[]{:S(2)}, u32[]{:S(2)}) collective-permute-start(f32[2,2,4,16,128]{4,3,2,1,0:T(8,128)S(1)} %get-tuple-element.66), channel_id=1, source_target_pairs={{0,4},{4,0},{8,12},{12,8},{16,20},{20,16},{24,28},{28,24},{1,5},{5... | collective-permute-start | bytes 393224 | tf_op jit(solution)/shard_map/ppermute | solution.py:410
  40.2 7.8 %collective-permute-start.15 = (f32[2,2,4,16,128]{4,3,2,1,0:T(8,128)S(1)}, f32[2,2,4,16,128]{4,3,2,1,0:T(8,128)S(1)}, u32[]{:S(2)}, u32[]{:S(2)}) collective-permute-start(f32[2,2,4,16,128]{4,3,2,1,0:T(8,128)S(1)} %get-tuple-element.67), channel_id=1, source_target_pairs={{0,28},{4,8},{8,4},{12,16},{16,12},{20,24},{24,20},{28,0},{1,29},{... | collective-permute-start | bytes 393224 | tf_op jit(solution)/shard_map/ppermute | solution.py:410
  43.3 2.1 %collective-permute-start.12 = (f32[32,128]{1,0:T(8,128)S(1)}, f32[32,128]{1,0:T(8,128)S(1)}, u32[]{:S(2)}, u32[]{:S(2)}) collective-permute-start(f32[32,128]{1,0:T(8,128)S(1)} %get-tuple-element.63), channel_id=1, source_target_pairs={{0,1},{1,0},{2,3},{3,2},{4,5},{5,4},{6,7},{7,6},{8,9},{9,8},{10,11... | collective-permute-start | bytes 49160 | tf_op jit(solution)/shard_map/ppermute | solution.py:410
  43.4 3.2 %collective-permute-start.13 = (f32[32,128]{1,0:T(8,128)S(1)}, f32[32,128]{1,0:T(8,128)S(1)}, u32[]{:S(2)}, u32[]{:S(2)}) collective-permute-start(f32[32,128]{1,0:T(8,128)S(1)} %get-tuple-element.64), channel_id=1, source_target_pairs={{0,3},{1,2},{2,1},{3,0},{4,7},{5,6},{6,5},{7,4},{8,11},{9,10},{10,... | collective-permute-start | bytes 49160 | tf_op jit(solution)/shard_map/ppermute | solution.py:410
  49.2 6.4 %collective-permute-start.17 = (f32[8,256]{1,0:T(8,128)S(1)}, f32[8,256]{1,0:T(8,128)S(1)}, u32[]{:S(2)}, u32[]{:S(2)}) collective-permute-start(f32[8,256]{1,0:T(8,128)S(1)} %get-tuple-element.69.message_ref), channel_id=1, source_target_pairs={{0,28},{4,8},{8,4},{12,16},{16,12},{20,24},{24,20},{28,0},{1,29},{... | collective-permute-start | bytes 24584 | tf_op jit(solution)/shard_map/ppermute | solution.py:410
  51.8 3.9 %collective-permute-start.16 = (f32[8,256]{1,0:T(8,128)S(1)}, f32[8,256]{1,0:T(8,128)S(1)}, u32[]{:S(2)}, u32[]{:S(2)}) collective-permute-start(f32[8,256]{1,0:T(8,128)S(1)} %get-tuple-element.69.message_ref), channel_id=1, source_target_pairs={{0,4},{4,0},{8,12},{12,8},{16,20},{20,16},{24,28},{28,24},{1,5},{5... | collective-permute-start | bytes 24584 | tf_op jit(solution)/shard_map/ppermute | solution.py:410

commit v3 on v2

v3 whole, which is shorter than its diff:
```python
import functools

import jax
import jax.numpy as jnp
from jax import lax
from jax.experimental import pallas as pl
from jax.experimental.pallas import tpu as pltpu
from jax.sharding import PartitionSpec as P

STEPS = 3

DIFFUSE = 0.1
BARRIER = 0.5
PENALTY = 0.05
TORSION = 0.1
TRANSLATE = 2.0
ROTATE = 2.0

ROWS = 2
COLS = 4


def split3(value):
    high = value.astype(jnp.bfloat16)
    rest = value - high.astype(jnp.float32)
    middle = rest.astype(jnp.bfloat16)
    low = (rest - middle.astype(jnp.float32)).astype(jnp.bfloat16)
    return high, middle, low


def exact_dot(value, chooser):
    rows = value.shape[0]
    parts = jnp.dot(jnp.concatenate(split3(value), axis=0), chooser, preferred_element_type=jnp.float32)
    return parts[:rows] + parts[rows : 2 * rows] + parts[2 * rows :]


def sin_cos(angle):
    turns = jnp.floor(angle * 0.6366197723675814 + 0.5)
    rest = angle - turns * 1.5703125
    rest = rest - turns * 4.837512969970703125e-4
    rest = rest - turns * 7.54978995489188216e-8
    square = rest * rest
    sine = ((-1.9515295891e-4 * square + 8.3321608736e-3) * square - 1.6666654611e-1) * square * rest + rest
    cosine = ((2.443315711809948e-5 * square - 1.388731625493765e-3) * square + 4.166664568298827e-2) * square * square
    cosine = cosine - 0.5 * square + 1.0
    quarter = turns.astype(jnp.int32)
    odd = (quarter & 1) == 1
    sin_value = jnp.where(odd, cosine, sine)
    cos_value = jnp.where(odd, sine, cosine)
    sin_value = jnp.where((quarter & 2) == 2, -sin_value, sin_value)
    cos_value = jnp.where(((quarter + 1) & 2) == 2, -cos_value, cos_value)
    return sin_value, cos_value


def is_odd(axis):
    return lax.axis_index(axis) & 1


def place(layer, cz):
    odd = is_odd("gz")
    if layer == 0:
        return (1 - odd) * (cz - 1)
    if layer == 1:
        return odd * (cz - 1)
    return layer - 1


def facing(layer, layers):
    odd = is_odd("gz")
    return ((1 - odd) if layer == 0 else odd) * (layers - 1)


def upward(layer):
    half = 0.5 - is_odd("gz").astype(jnp.float32)
    return half if layer == 0 else -half


def tile(f, p, j):
    return (f * ROWS + p) * COLS + j


def put_y_edges(near_ref, far_ref, inner_ref, y_near_ref, y_far_ref):
    layers, yb = inner_ref.shape[1], inner_ref.shape[4]
    cz = layers + 2
    first_to_near = is_odd("gy") == 1
    for f in range(2):
        for layer in range(cz):
            for j in range(COLS):
                at = (f * cz + layer) * COLS + j
                if layer < 2:
                    ref = (near_ref, far_ref)[layer]
                    first, last = ref[tile(f, 0, j), 0:1], ref[tile(f, ROWS - 1, j), yb - 1 : yb]
                else:
                    first = inner_ref[f, layer - 2, 0, j, 0:1]
                    last = inner_ref[f, layer - 2, ROWS - 1, j, yb - 1 : yb]
                y_near_ref[at : at + 1, :] = jnp.where(first_to_near, first, last)
                y_far_ref[at : at + 1, :] = jnp.where(first_to_near, last, first)


def x_chooser(nx, xb, back=False):
    first = lax.broadcasted_iota(jnp.int32, (nx, nx), 1 if back else 0)
    second = lax.broadcasted_iota(jnp.int32, (nx, nx), 0 if back else 1)
    return jnp.where(first == COLS * (second % xb) + second // xb, 1.0, 0.0).astype(jnp.bfloat16)


def spread(in_ref, chooser, rows_ref, put):
    _, layers, cy, nx = in_ref.shape
    yb, xb = cy // ROWS, nx // COLS
    moved = exact_dot(in_ref[...].reshape(2 * layers * cy, nx), chooser)
    for j in range(COLS):
        rows_ref[j] = moved[:, j * xb : (j + 1) * xb]
    for f in range(2):
        for at in range(layers):
            for p in range(ROWS):
                for j in range(COLS):
                    start = (f * layers + at) * cy + p
                    put(f, at, p, j, rows_ref[j, pl.ds(start, yb, stride=ROWS), :])


def prepare_outer_kernel(
    e_hbm, q_hbm, slot_hbm, ids_hbm,
    near_ref, far_ref, raw_ref, slot_ref, ids_ref,
    in_ref, rows_ref, sems, raw_sems,
):
    cz = e_hbm.shape[0]
    _, _, cy, nx = in_ref.shape
    yb, xb = cy // ROWS, nx // COLS
    copies = [
        pltpu.make_async_copy(ref.at[place(at, cz)], in_ref.at[f, at], sems.at[f, at])
        for f, ref in enumerate((e_hbm, q_hbm))
        for at in range(2)
    ]
    copies.append(pltpu.make_async_copy(ids_hbm, ids_ref, raw_sems.at[0]))
    later = [
        pltpu.make_async_copy(e_hbm.at[1 : cz - 1], raw_ref.at[0], raw_sems.at[1]),
        pltpu.make_async_copy(q_hbm.at[1 : cz - 1], raw_ref.at[1], raw_sems.at[2]),
        pltpu.make_async_copy(slot_hbm, slot_ref, raw_sems.at[3]),
    ]
    for copy in copies + later:
        copy.start()
    chooser = x_chooser(nx, xb)
    for copy in copies:
        copy.wait()
    for ref in (near_ref, far_ref):
        ref[2 * ROWS * COLS] = jnp.zeros((yb, xb), jnp.float32)
        for half in range(ids_ref.shape[1] // xb):
            ref[2 * ROWS * COLS, half : half + 1, :] = ids_ref[:, half * xb : (half + 1) * xb].astype(jnp.float32)

    def put(f, at, p, j, value):
        (near_ref, far_ref)[at][tile(f, p, j)] = value

    spread(in_ref, chooser, rows_ref, put)
    for copy in later:
        copy.wait()


def prepare_inner_kernel(
    raw_ref, slot_ref, near_ref, far_ref,
    inner_ref, y_near_ref, y_far_ref, block_ref,
    rows_ref, slot_rows_ref,
):
    _, layers, cy, nx = raw_ref.shape
    cz = layers + 2
    yb, xb = cy // ROWS, nx // COLS
    chooser = x_chooser(nx, xb)

    def put(f, at, p, j, value):
        inner_ref[f, at, p, j] = value

    spread(raw_ref, chooser, rows_ref, put)
    put_y_edges(near_ref, far_ref, inner_ref, y_near_ref, y_far_ref)
    values = jnp.concatenate([slot_ref[place(layer, cz)] for layer in range(cz)], axis=0)
    values = values.astype(jnp.float32).astype(jnp.bfloat16)
    slot_rows_ref[...] = jnp.dot(values, chooser[:, :xb], preferred_element_type=jnp.float32)
    block_ref[...] = slot_rows_ref[pl.ds(0, cz * yb, stride=ROWS), :]


def onehot_kernel(block_ref, onehot_ref):
    rows, xb = block_ref.shape
    slots = onehot_ref.shape[1]
    slot = lax.broadcasted_iota(jnp.int32, (slots, xb), 0).astype(jnp.float32)
    for r in range(rows):
        hit = jnp.where(slot == block_ref[r : r + 1, :], 1.0, 0.0).astype(jnp.bfloat16)
        onehot_ref[r // 2, :, (r % 2) * xb : (r % 2 + 1) * xb] = hit


def derived(e, q):
    sin_value, cos_value = sin_cos(q)
    square = e * e
    return cos_value, sin_value, square * cos_value, square * sin_value


def trig_kernel(near_ref, far_ref, inner_ref, trig_ref):
    cz = trig_ref.shape[1]
    for layer in range(cz):
        for p in range(ROWS):
            for j in range(COLS):
                if layer < 2:
                    e, q = ((near_ref, far_ref)[layer][tile(f, p, j)] for f in range(2))
                else:
                    e, q = (inner_ref[f, layer - 2, p, j] for f in range(2))
                for k, value in enumerate(derived(e, q)):
                    trig_ref[k, layer, p, j] = value


def beside(get, up, down, rim_ref, layer, k, p, j):
    here = get(k, p, j)
    yb, xb = here.shape
    row = lax.broadcasted_iota(jnp.int32, (yb, xb), 0)
    at = layer * COLS + j
    x_plus = get(k, p, j + 1) if j + 1 < COLS else pltpu.roll(get(k, p, 0), xb - 1, 1)
    x_minus = get(k, p, j - 1) if j > 0 else pltpu.roll(get(k, p, COLS - 1), 1, 1)
    if p + 1 < ROWS:
        y_plus = get(k, p + 1, j)
    else:
        y_plus = jnp.where(row == yb - 1, rim_ref[1, k, at : at + 1, :], pltpu.roll(get(k, 0, j), yb - 1, 0))
    if p > 0:
        y_minus = get(k, p - 1, j)
    else:
        y_minus = jnp.where(row == 0, rim_ref[0, k, at : at + 1, :], pltpu.roll(get(k, ROWS - 1, j), 1, 0))
    return x_plus, x_minus, y_plus, y_minus, up(k, p, j), down(k, p, j)


def gradients(side, z_half):
    halves = (0.5, 0.5, z_half)
    return [(side[2 * d] - side[2 * d + 1]) * halves[d] for d in range(3)]


def cell_densities(get, up, down, rim_ref, layer, z_half, p, j):
    sides = [beside(get, up, down, rim_ref, layer, k, p, j) for k in (0, 2, 3, 4, 5)]
    e, c, s = get(0, p, j), get(2, p, j), get(3, p, j)
    c_sum, s_sum, a_sum, b_sum = (sum(side) for side in sides[1:])
    misfit = 6.0 - c * c_sum - s * s_sum
    torque = c * b_sum - s * a_sum
    weight = e * misfit
    grads = gradients(sides[0], z_half)
    return [weight * g for g in grads] + [torque, 0.5 + e * e], weight, torque


def cell_locals(get, up, down, rim_ref, layer, z_half, p, j, weight, torque):
    e_side, q_side = (beside(get, up, down, rim_ref, layer, k, p, j) for k in range(2))
    e, q = get(0, p, j), get(1, p, j)
    laplace = sum(e_side) - 6.0 * e
    e_local = e + DIFFUSE * laplace + BARRIER * e * (1.0 - e) * (e - 0.5) - PENALTY * weight
    return [e_local, q + TORSION * torque] + gradients(e_side, z_half) + gradients(q_side, z_half)


def put_sums(totals, at, yb, sums_ref):
    rows = sums_ref.shape[0] // 16
    for k, value in enumerate(totals):
        for part, piece in enumerate(split3(value)):
            start = (part * 5 + k) * rows + at * yb
            sums_ref[start : start + yb, :] = piece.astype(jnp.float32)


def slot_sums(sums_ref, onehot_ref, first_pair):
    rows = sums_ref.shape[0] // 16
    sums_ref[15 * rows : 16 * rows, :] = jnp.zeros((rows, sums_ref.shape[1]), jnp.float32)
    acc = jnp.zeros((16, onehot_ref.shape[1]), jnp.float32)
    for i in range(rows // 2):
        left = jnp.concatenate(
            [sums_ref[pl.ds(2 * i + h, 16, stride=rows), :] for h in range(2)], axis=1
        ).astype(jnp.bfloat16)
        acc = acc + lax.dot_general(
            left, onehot_ref[first_pair + i], (((1,), (1,)), ((), ())), preferred_element_type=jnp.float32
        )
    return acc


def inner_kernel(
    near_ref, far_ref, inner_ref, trig_ref, y_near_ref, y_far_ref, onehot_ref,
    rim_ref, local_ref, acc_ref,
    sums_ref,
):
    _, cz, _, _, yb, xb = trig_ref.shape
    n = cz * COLS
    last = lax.axis_size("gy") - 1
    for side in range(2):
        inside = lax.axis_index("gy") != (0, last)[side]
        from_near = is_odd("gy") == 1 - side
        e, q = (
            jnp.where(
                inside, jnp.where(from_near, y_near_ref[f * n : f * n + n, :], y_far_ref[f * n : f * n + n, :]), 0.0
            )
            for f in range(2)
        )
        for k, value in enumerate((e, q) + derived(e, q)):
            rim_ref[side, k] = value

    def inner(at, k, p, j):
        return inner_ref[k, at, p, j] if k < 2 else trig_ref[k - 2, at + 2, p, j]

    def outer(top, k, p, j):
        is_near = is_odd("gz") == (0 if top else 1)
        if k < 2:
            return jnp.where(is_near, near_ref[tile(k, p, j)], far_ref[tile(k, p, j)])
        return trig_ref[k - 2, jnp.where(is_near, 0, 1), p, j]

    for at in range(cz - 2):
        get = functools.partial(inner, at)
        up = functools.partial(inner, at + 1) if at + 1 < cz - 2 else functools.partial(outer, True)
        down = functools.partial(inner, at - 1) if at > 0 else functools.partial(outer, False)
        totals = None
        for p in range(ROWS):
            for j in range(COLS):
                densities, weight, torque = cell_densities(get, up, down, rim_ref, at + 2, 0.5, p, j)
                totals = densities if totals is None else [a + b for a, b in zip(totals, densities)]
                local = cell_locals(get, up, down, rim_ref, at + 2, 0.5, p, j, weight, torque)
                for k, value in enumerate(local):
                    local_ref[k, at, p, j] = value
        put_sums(totals, at, yb, sums_ref)
    acc_ref[...] = slot_sums(sums_ref, onehot_ref, yb)


def outer_getters(layer, own_ref, inner_ref, trig_ref, halo):
    beside_at = facing(layer, inner_ref.shape[1])

    def get(k, p, j):
        return own_ref[tile(k, p, j)] if k < 2 else trig_ref[k - 2, layer, p, j]

    def inward(k, p, j):
        return inner_ref[k, beside_at, p, j] if k < 2 else trig_ref[k - 2, beside_at + 2, p, j]

    return get, halo, inward


def outer_densities(layer, own_ref, inner_ref, trig_ref, rim_ref, halo_ref, onehot_ref, mixed_ref, trig_halo_ref, sums_ref):
    yb = trig_ref.shape[4]
    for p in range(ROWS):
        for j in range(COLS):
            for k, value in enumerate(derived(*(halo_ref[tile(f, p, j)] for f in range(2)))):
                trig_halo_ref[k, p, j] = value

    def halo(k, p, j):
        return halo_ref[tile(k, p, j)] if k < 2 else trig_halo_ref[k - 2, p, j]

    get, out, inward = outer_getters(layer, own_ref, inner_ref, trig_ref, halo)
    z_half = upward(layer)
    totals = None
    for p in range(ROWS):
        for j in range(COLS):
            densities, weight, torque = cell_densities(get, out, inward, rim_ref, layer, z_half, p, j)
            totals = densities if totals is None else [a + b for a, b in zip(totals, densities)]
            mixed_ref[0, p, j] = weight
            mixed_ref[1, p, j] = torque
    put_sums(totals, 0, yb, sums_ref)
    return slot_sums(sums_ref, onehot_ref, layer * yb // 2)


def near_kernel(
    near_ref, inner_ref, trig_ref, rim_ref, halo_ref, onehot_ref, before_ref,
    mixed_ref, acc_ref,
    trig_halo_ref, sums_ref,
):
    acc_ref[...] = before_ref[...] + outer_densities(
        0, near_ref, inner_ref, trig_ref, rim_ref, halo_ref, onehot_ref, mixed_ref, trig_halo_ref, sums_ref
    )


def far_kernel(
    far_ref, inner_ref, trig_ref, rim_ref, halo_ref, onehot_ref, before_ref,
    mixed_ref, message_ref,
    trig_halo_ref, sums_ref, acc_ref,
):
    acc_ref[...] = before_ref[...] + outer_densities(
        1, far_ref, inner_ref, trig_ref, rim_ref, halo_ref, onehot_ref, mixed_ref, trig_halo_ref, sums_ref
    )
    message_ref[0:5, :] = acc_ref[0:5, :] + acc_ref[5:10, :] + acc_ref[10:15, :]
    message_ref[5:8, :] = jnp.zeros((3, message_ref.shape[1]), jnp.float32)


def outer_local_kernel(
    near_ref, far_ref, inner_ref, trig_ref, rim_ref, near_halo_ref, far_halo_ref, near_mixed_ref, far_mixed_ref, local_ref
):
    for layer in range(2):
        halo_ref = (near_halo_ref, far_halo_ref)[layer]
        mixed_ref = (near_mixed_ref, far_mixed_ref)[layer]

        def halo(k, p, j, halo_ref=halo_ref):
            return halo_ref[tile(k, p, j)]

        get, out, inward = outer_getters(layer, (near_ref, far_ref)[layer], inner_ref, trig_ref, halo)
        z_half = upward(layer)
        for p in range(ROWS):
            for j in range(COLS):
                local = cell_locals(
                    get, out, inward, rim_ref, layer, z_half, p, j, mixed_ref[0, p, j], mixed_ref[1, p, j]
                )
                for k, value in enumerate(local):
                    local_ref[k, layer, p, j] = value


def match_kernel(ids_ref, near_halo_ref, far_halo_ref, match_ref):
    slots = ids_ref.shape[1]
    xb = near_halo_ref.shape[2]
    own = jnp.broadcast_to(ids_ref[...].astype(jnp.float32), (xb, slots))
    for side, ref in enumerate((near_halo_ref, far_halo_ref)):
        for half in range(slots // xb):
            line = ref[2 * ROWS * COLS, half : half + 1, :]
            other = jnp.transpose(jnp.broadcast_to(line, (xb, xb)))
            other = jnp.concatenate([other] * (slots // xb), axis=1)
            start = side * slots + half * xb
            match_ref[start : start + xb, :] = jnp.where(other == own, 1.0, 0.0).astype(jnp.bfloat16)


def stacked(value):
    return jnp.concatenate([part.astype(jnp.float32) for part in split3(value)], axis=0).astype(jnp.bfloat16)


def unstacked(value):
    return value[0:8] + value[8:16] + value[16:24]


def slot_motion(message_ref, near_ref, far_ref, match_ref):
    others = jnp.concatenate([stacked(near_ref[...]), stacked(far_ref[...])], axis=1)
    totals = message_ref[...] + unstacked(jnp.dot(others, match_ref[...], preferred_element_type=jnp.float32))
    inverse = 1.0 / totals[4:5, :]
    return stacked(TRANSLATE * totals * inverse)


def block_motion(velocity, onehot_ref, motion_ref, first_pair):
    rows = motion_ref.shape[0] // 8
    xb = motion_ref.shape[1]
    for i in range(rows // 2):
        moved = unstacked(jnp.dot(velocity, onehot_ref[first_pair + i], preferred_element_type=jnp.float32))
        for h in range(2):
            motion_ref[pl.ds(2 * i + h, 8, stride=rows), :] = moved[:, h * xb : (h + 1) * xb]


def advanced(local_ref, motion_ref, at, p, j):
    layers, yb = local_ref.shape[1], local_ref.shape[4]
    rows = layers * yb
    vx, vy, vz, turn = (motion_ref[k * rows + at * yb : k * rows + (at + 1) * yb, :] for k in range(4))
    g = [local_ref[k, at, p, j] for k in range(2, 8)]
    e = local_ref[0, at, p, j] - (vx * g[0] + vy * g[1] + vz * g[2])
    q = local_ref[1, at, p, j] + turn - (vx * g[3] + vy * g[4] + vz * g[5])
    return e, q


def advance_outer_kernel(
    message_ref, near_message_ref, far_message_ref, match_ref, onehot_ref, local_ref,
    velocity_ref, near_ref, far_ref,
    motion_ref,
):
    velocity = slot_motion(message_ref, near_message_ref, far_message_ref, match_ref)
    velocity_ref[...] = velocity
    block_motion(velocity, onehot_ref, motion_ref, 0)
    for layer, ref in enumerate((near_ref, far_ref)):
        for p in range(ROWS):
            for j in range(COLS):
                ref[tile(0, p, j)], ref[tile(1, p, j)] = advanced(local_ref, motion_ref, layer, p, j)


def advance_inner_kernel(
    velocity_ref, onehot_ref, local_ref, near_ref, far_ref,
    inner_ref, y_near_ref, y_far_ref,
    motion_ref,
):
    layers, yb = local_ref.shape[1], local_ref.shape[4]
    block_motion(velocity_ref[...], onehot_ref, motion_ref, yb)
    for at in range(layers):
        for p in range(ROWS):
            for j in range(COLS):
                inner_ref[0, at, p, j], inner_ref[1, at, p, j] = advanced(local_ref, motion_ref, at, p, j)
    put_y_edges(near_ref, far_ref, inner_ref, y_near_ref, y_far_ref)


def finish_kernel(
    message_ref, near_message_ref, far_message_ref, match_ref, onehot_ref, outer_local_ref, inner_local_ref,
    e_hbm, q_hbm,
    motion_ref, rows_ref, out_ref, sems,
):
    yb, xb = outer_local_ref.shape[4:]
    _, cz, cy, nx = out_ref.shape
    velocity = slot_motion(message_ref, near_message_ref, far_message_ref, match_ref)
    chooser = x_chooser(nx, xb, back=True)
    copies = []
    for part, local_ref in enumerate((outer_local_ref, inner_local_ref)):
        layers = local_ref.shape[1]
        block_motion(velocity, onehot_ref, motion_ref, part * yb)
        for at in range(layers):
            for p in range(ROWS):
                to = pl.ds(at * cy + p, yb, stride=ROWS)
                for j in range(COLS):
                    e, q = advanced(local_ref, motion_ref, at, p, j)
                    rows_ref[0, j, to, :] = e
                    rows_ref[1, j, to, :] = q
        moved = exact_dot(
            jnp.concatenate(
                [jnp.concatenate([rows_ref[f, j] for j in range(COLS)], axis=1) for f in range(2)], axis=0
            ),
            chooser,
        )
        for f, ref in enumerate((e_hbm, q_hbm)):
            for at in range(layers):
                layer = 2 * part + at
                start = (f * layers + at) * cy
                out_ref[f, layer] = moved[start : start + cy]
                copies.append(
                    pltpu.make_async_copy(out_ref.at[f, layer], ref.at[place(layer, cz)], sems.at[f, layer])
                )
                copies[-1].start()
    for copy in copies:
        copy.wait()


VMEM = pl.BlockSpec(memory_space=pltpu.VMEM)
HBM = pl.BlockSpec(memory_space=pltpu.HBM)
MIB = 1024 * 1024


def call(kernel, name, outs, scratch=(), hbm_in=0, hbm_out=False, limit=24):
    def run(*args):
        return pl.pallas_call(
            kernel,
            name=name,
            in_specs=[HBM] * hbm_in + [VMEM] * (len(args) - hbm_in),
            out_specs=[HBM if hbm_out else VMEM] * len(outs),
            out_shape=[jax.ShapeDtypeStruct(shape, dtype) for shape, dtype in outs],
            scratch_shapes=list(scratch),
            compiler_params=pltpu.CompilerParams(vmem_limit_bytes=limit * MIB),
            cost_estimate=pl.CostEstimate(flops=4 * MIB, bytes_accessed=MIB, transcendentals=0),
        )(*args)

    return run


def swap(array, axis, far):
    size = lax.axis_size(axis)
    pairs = [(i, (((i + 1) ^ 1) - 1) % size if far else i ^ 1) for i in range(size)]
    return lax.ppermute(array, axis, pairs)


def both(near, far, axis):
    far = swap(far, axis, True)
    return swap(near, axis, False), far


def shards(order_param, orientation, cell_slot, tile_grains):
    cz, cy, nx = order_param.shape
    slots = tile_grains.shape[-1]
    yb, xb = cy // ROWS, nx // COLS
    rows = cz * yb
    f32, bf16 = jnp.float32, jnp.bfloat16
    block = (ROWS, COLS, yb, xb)
    side_out = ((2 * ROWS * COLS, yb, xb), f32)
    first_side_out = ((2 * ROWS * COLS + 1, yb, xb), f32)
    inner_out = ((2, cz - 2) + block, f32)
    y_out = [((2 * cz * COLS, xb), f32)] * 2
    acc_out = ((16, slots), f32)
    mixed_out = ((2,) + block, f32)
    outer_motion = pltpu.VMEM((8 * 2 * yb, xb), f32)
    inner_motion = pltpu.VMEM((8 * (cz - 2) * yb, xb), f32)
    layer_scratch = [pltpu.VMEM((4,) + block, f32), pltpu.VMEM((16 * yb, xb), f32)]
    dma = pltpu.SemaphoreType.DMA
    prepare_outer = call(
        prepare_outer_kernel, "prepare_outer",
        [
            first_side_out, first_side_out, ((2, cz - 2, cy, nx), f32),
            ((cz, cy, nx), jnp.int32), ((1, slots), jnp.int32),
        ],
        [pltpu.VMEM((2, 2, cy, nx), f32), pltpu.VMEM((COLS, 4 * cy, xb), f32), dma((2, 2)), dma((4,))],
        hbm_in=4,
    )
    prepare_inner = call(
        prepare_inner_kernel, "prepare_inner", [inner_out] + y_out + [((rows, xb), f32)],
        [pltpu.VMEM((COLS, 2 * (cz - 2) * cy, xb), f32), pltpu.VMEM((cz * cy, xb), f32)],
    )
    onehots = call(onehot_kernel, "onehots", [((rows // 2, slots, 2 * xb), bf16)])
    trigs = call(trig_kernel, "trigs", [((4, cz) + block, f32)])
    inner_terms = call(
        inner_kernel, "inner_terms", [((2, 6, cz * COLS, xb), f32), ((8, cz - 2) + block, f32), acc_out],
        [pltpu.VMEM((16 * (cz - 2) * yb, xb), f32)],
    )
    near_terms = call(near_kernel, "near_terms", [mixed_out, acc_out], layer_scratch)
    far_terms = call(
        far_kernel, "far_terms", [mixed_out, ((8, slots), f32)], layer_scratch + [pltpu.VMEM((16, slots), f32)]
    )
    outer_locals = call(outer_local_kernel, "outer_locals", [((8, 2) + block, f32)])
    matches = call(match_kernel, "matches", [((2 * slots, slots), bf16)])
    advance_outer = call(
        advance_outer_kernel, "advance_outer", [((24, slots), bf16), side_out, side_out], [outer_motion]
    )
    advance_inner = call(advance_inner_kernel, "advance_inner", [inner_out] + y_out, [inner_motion])
    finish = call(
        finish_kernel, "finish", [((cz, cy, nx), f32)] * 2,
        [
            outer_motion, pltpu.VMEM((2, COLS, 2 * cy, xb), f32), pltpu.VMEM((2, cz, cy, nx), f32), dma((2, cz)),
        ],
        hbm_out=True,
    )

    inputs = (order_param, orientation, cell_slot, tile_grains.reshape(1, slots))
    near, far, raw, raw_slots, ids = prepare_outer(
        *(pltpu.with_memory_space_constraint(array, pltpu.HBM) for array in inputs)
    )
    for step in range(STEPS):
        near_halo, far_halo = both(near, far, "gz")
        if step == 0:
            inner, y_near, y_far, blocks = prepare_inner(raw, raw_slots, near, far)
        else:
            inner, y_near, y_far = advance_inner(velocity, onehot, inner_local, near, far)
        y_near, y_far = both(y_near, y_far, "gy")
        if step == 0:
            (onehot,) = onehots(blocks)
        (trig,) = trigs(near, far, inner)
        rim, inner_local, acc = inner_terms(near, far, inner, trig, y_near, y_far, onehot)
        near_mixed, acc = near_terms(near, inner, trig, rim, near_halo, onehot, acc)
        far_mixed, message = far_terms(far, inner, trig, rim, far_halo, onehot, acc)
        near_message, far_message = both(message, message, "gz")
        if step == 0:
            (match,) = matches(ids, near_halo, far_halo)
        (outer_local,) = outer_locals(near, far, inner, trig, rim, near_halo, far_halo, near_mixed, far_mixed)
        if step < STEPS - 1:
            velocity, near, far = advance_outer(message, near_message, far_message, match, onehot, outer_local)
    return tuple(finish(message, near_message, far_message, match, onehot, outer_local, inner_local))


def solution(mesh):
    spec = P("gz", "gy", None)
    return jax.shard_map(shards, mesh=mesh, in_specs=(spec,) * 4, out_specs=(spec,) * 2, check_vma=False)
```

time: 58.4 us -> 56.5 us (0.967)
  local copies, waits for them, and re-layouts: 2.85 us -> 0 us
  starting transfers between devices: 24.4 us -> 26.4 us
  waiting for transfers between devices: 14.7 us -> 12.9 us
  Pallas kernels: 15.4 us -> 16.2 us
    unnamed x8 -> x0, local copies, waits for them, and re-layouts: 2.85 us -> none
    ppermute x18, starting transfers between devices: 24.4 us -> 26.4 us  [swap(): return lax.ppermute(array, axis, pairs)]
    ppermute x18, waiting for transfers between devices: 14.7 us -> 12.9 us  [swap(): return lax.ppermute(array, axis, pairs)]
    pallas_call x16 -> x24, Pallas kernels: 15.4 us -> 16.2 us  [run(): pl.pallas_call(kernel, name=name, in_specs=[HBM] * hbm_in + [VMEM] * (len...]
  transfers between devices with their start and end apart: 18 -> 18, of which waited for: 7 -> 8; matrix products, arithmetic and copies ran while one was open for 0% -> 0% of each run, Pallas kernels for 11% -> 16%
where the time goes in v3:
time: 56.5 us; the launch traced here: 56.3 us
  starting transfers between devices  26.4 us (47%)
  Pallas kernels  16.2 us (29%)
  waiting for transfers between devices  12.9 us (23%)
  between operations  0.8 us (1%)
    ppermute x18, starting transfers between devices, swap(): return lax.ppermute(array, axis, pairs)  26.4 us
    pallas_call x24, Pallas kernels, run(): pl.pallas_call(kernel, name=name, in_specs=[HBM] * hbm_in + [VMEM] * (len...  16.2 us
    ppermute x18, waiting for transfers between devices, swap(): return lax.ppermute(array, axis, pairs)  12.9 us
  transfers between devices with their start and end apart: 18, of which 8 were waited for; matrix products, arithmetic and copies ran while one was open for 0% of the time, Pallas kernels for 16%

profile of v3, /device:TPU:0, one launch (start us, length us, event | category | flops | bytes accessed | tf_op | source)
XLA Modules:
  0.0 56.3 jit_solution(9905248291392958095)
XLA Ops:
  0.6 1.6 %prepare_outer.1 = (f32[17,16,128]{2,1,0:T(8,128)S(1)}, f32[17,16,128]{2,1,0:T(8,128)S(1)}, f32[2,2,32,512]{3,2,1,0:T(8,128)S(1)}, s32[4,32,512]{2,1,0:T(8,128)S(1)}, s32[1,256]{1,0:T(1,128)S(1)}) custom-call(f32[4,32,512]{2,1,0:T(8,128)} %e_hbm.1, f32[4,32,512]{2,1,0:T(8,128)} %q_hbm.1, s32[4,32,512]{2,1,0:T(8,128)} %slot_hbm.1, s32[1,256]{1,0:T(1,128)} %bitcast.1), custom_call_target="tpu_custom_call" | custom-call | flops 4194304 | bytes 1048576 | tf_op jit(solution)/shard_map/prepare_outer/pallas_call | solution.py:514
  2.2 3.0 %collective-permute-start.3 = (f32[17,16,128]{2,1,0:T(8,128)S(1)}, f32[17,16,128]{2,1,0:T(8,128)S(1)}, u32[]{:S(2)}, u32[]{:S(2)}) collective-permute-start(f32[17,16,128]{2,1,0:T(8,128)S(1)} %get-tuple-element.47.near_ref), channel_id=1, source_target_pairs={{0,4},{4,0},{8,12},{12,8},{16,20},{20,16},{24,28},{28,24},{1,5},{5... | collective-permute-start | bytes 417800 | tf_op jit(solution)/shard_map/ppermute | solution.py:531
  5.2 3.5 %collective-permute-start.2 = (f32[17,16,128]{2,1,0:T(8,128)S(1)}, f32[17,16,128]{2,1,0:T(8,128)S(1)}, u32[]{:S(2)}, u32[]{:S(2)}) collective-permute-start(f32[17,16,128]{2,1,0:T(8,128)S(1)} %get-tuple-element.44.far_ref), channel_id=1, source_target_pairs={{0,28},{4,8},{8,4},{12,16},{16,12},{20,24},{24,20},{28,0},{1,29},{... | collective-permute-start | bytes 417800 | tf_op jit(solution)/shard_map/ppermute | solution.py:531
  8.8 0.4 prepare_inner.1
  9.2 0.1 collective-permute-start
  9.3 1.6 %collective-permute-start.1 = (f32[32,128]{1,0:T(8,128)S(1)}, f32[32,128]{1,0:T(8,128)S(1)}, u32[]{:S(2)}, u32[]{:S(2)}) collective-permute-start(f32[32,128]{1,0:T(8,128)S(1)} %get-tuple-element.50), channel_id=1, source_target_pairs={{0,3},{1,2},{2,1},{3,0},{4,7},{5,6},{6,5},{7,4},{8,11},{9,10},{10,... | collective-permute-start | bytes 49160 | tf_op jit(solution)/shard_map/ppermute | solution.py:531
  10.9 0.4 trigs.3.trig_ref
  11.3 0.8 %onehots.1.onehot_ref = bf16[32,256,256]{2,1,0:T(8,128)(2,1)S(1)} custom-call(f32[64,128]{1,0:T(8,128)S(1)} %get-tuple-element.51.block_ref), custom_call_target="tpu_custom_call" | custom-call | flops 4194304 | bytes 1048576 | tf_op jit(solution)/shard_map/onehots/pallas_call | solution.py:514
  12.1 0.0 collective-permute-done.y_near_ref
  12.1 0.4 collective-permute-done.1.y_far_ref
  12.5 1.1 %inner_terms.3 = (f32[2,6,16,128]{3,2,1,0:T(8,128)S(1)}, f32[8,2,2,4,16,128]{5,4,3,2,1,0:T(8,128)S(1)}, f32[16,256]{1,0:T(8,128)S(1)}) custom-call(f32[17,16,128]{2,1,0:T(8,128)S(1)} %get-tuple-element.47.near_ref, f32[17,16,128]{2,1,0:T(8,128)S(1)} %get-tuple-element.44.far_ref, f32[2,2,2,4,16,128]{5,4,3,2,1,0:T(8,128)S(1)} %get-tuple-element.48.inner_ref, ...), custom_call_target="tpu_custom_call" | custom-call | flops 4194304 | bytes 1048576 | tf_op jit(solution)/shard_map/inner_terms/pallas_call | solution.py:514
  13.6 0.0 collective-permute-done.3.halo_ref.near_halo_ref
  13.6 0.6 %near_terms.3 = (f32[2,2,4,16,128]{4,3,2,1,0:T(8,128)S(1)}, f32[16,256]{1,0:T(8,128)S(1)}) custom-call(f32[17,16,128]{2,1,0:T(8,128)S(1)} %get-tuple-element.47.near_ref, f32[2,2,2,4,16,128]{5,4,3,2,1,0:T(8,128)S(1)} %get-tuple-element.48.inner_ref, f32[4,4,2,4,16,128]{5,4,3,2,1,0:T(8,128)S(1)} %trigs.3.trig_ref, ...), custom_call_target="tpu_custom_call" | custom-call | flops 4194304 | bytes 1048576 | tf_op jit(solution)/shard_map/near_terms/pallas_call | solution.py:514
  14.2 0.0 collective-permute-done.2.halo_ref.far_halo_ref
  14.2 0.6 %far_terms.3 = (f32[2,2,4,16,128]{4,3,2,1,0:T(8,128)S(1)}, f32[8,256]{1,0:T(8,128)S(1)}) custom-call(f32[17,16,128]{2,1,0:T(8,128)S(1)} %get-tuple-element.44.far_ref, f32[2,2,2,4,16,128]{5,4,3,2,1,0:T(8,128)S(1)} %get-tuple-element.48.inner_ref, f32[4,4,2,4,16,128]{5,4,3,2,1,0:T(8,128)S(1)} %trigs.3.trig_ref, ...), custom_call_target="tpu_custom_call" | custom-call | flops 4194304 | bytes 1048576 | tf_op jit(solution)/shard_map/far_terms/pallas_call | solution.py:514
  14.8 0.1 collective-permute-start.4
  14.9 3.5 %collective-permute-start.5 = (f32[8,256]{1,0:T(8,128)S(1)}, f32[8,256]{1,0:T(8,128)S(1)}, u32[]{:S(2)}, u32[]{:S(2)}) collective-permute-start(f32[8,256]{1,0:T(8,128)S(1)} %get-tuple-element.55.message_ref), channel_id=1, source_target_pairs={{0,28},{4,8},{8,4},{12,16},{16,12},{20,24},{24,20},{28,0},{1,29},{... | collective-permute-start | bytes 24584 | tf_op jit(solution)/shard_map/ppermute | solution.py:531
  18.4 0.1 matches.1.match_ref
  18.6 0.2 outer_locals.3.local_ref
  18.8 0.0 collective-permute-done.4.near_message_ref
  18.8 2.5 %collective-permute-done.5.far_message_ref = f32[8,256]{1,0:T(8,128)S(1)} collective-permute-done((f32[8,256]{1,0:T(8,128)S(1)}, f32[8,256]{1,0:T(8,128)S(1)}, u32[]{:S(2)}, u32[]{:S(2)}) %collective-permute-start.5) | collective-permute-done | bytes 8224 | tf_op jit(solution)/shard_map/ppermute | solution.py:531
  21.3 0.7 %advance_outer.2 = (bf16[24,256]{1,0:T(8,128)(2,1)S(1)}, f32[16,16,128]{2,1,0:T(8,128)S(1)}, f32[16,16,128]{2,1,0:T(8,128)S(1)}) custom-call(f32[8,256]{1,0:T(8,128)S(1)} %get-tuple-element.55.message_ref, f32[8,256]{1,0:T(8,128)S(1)} %collective-permute-done.4.near_message_ref, f32[8,256]{1,0:T(8,128)S(1)} %collective-permute-done.5.far_message_ref, ...), custom_call_target="tpu_custom_call" | custom-call | flops 4194304 | bytes 1048576 | tf_op jit(solution)/shard_map/advance_outer/pallas_call | solution.py:514
  22.0 0.2 collective-permute-start.9
  22.2 3.4 %collective-permute-start.8 = (f32[16,16,128]{2,1,0:T(8,128)S(1)}, f32[16,16,128]{2,1,0:T(8,128)S(1)}, u32[]{:S(2)}, u32[]{:S(2)}) collective-permute-start(f32[16,16,128]{2,1,0:T(8,128)S(1)} %get-tuple-element.59.far_ref), channel_id=1, source_target_pairs={{0,28},{4,8},{8,4},{12,16},{16,12},{20,24},{24,20},{28,0},{1,29},{... | collective-permute-start | bytes 393224 | tf_op jit(solution)/shard_map/ppermute | solution.py:531
  25.6 0.5 advance_inner.2
  26.1 0.1 collective-permute-start.6
  26.2 1.6 %collective-permute-start.7 = (f32[32,128]{1,0:T(8,128)S(1)}, f32[32,128]{1,0:T(8,128)S(1)}, u32[]{:S(2)}, u32[]{:S(2)}) collective-permute-start(f32[32,128]{1,0:T(8,128)S(1)} %get-tuple-element.65), channel_id=1, source_target_pairs={{0,3},{1,2},{2,1},{3,0},{4,7},{5,6},{6,5},{7,4},{8,11},{9,10},{10,... | collective-permute-start | bytes 49160 | tf_op jit(solution)/shard_map/ppermute | solution.py:531
  27.8 0.4 trigs.4.trig_ref
  28.2 0.0 collective-permute-done.6.y_near_ref
  28.2 1.2 %collective-permute-done.7.y_far_ref = f32[32,128]{1,0:T(8,128)S(1)} collective-permute-done((f32[32,128]{1,0:T(8,128)S(1)}, f32[32,128]{1,0:T(8,128)S(1)}, u32[]{:S(2)}, u32[]{:S(2)}) %collective-permute-start.7) | collective-permute-done | bytes 16416 | tf_op jit(solution)/shard_map/ppermute | solution.py:531
  29.4 1.0 %inner_terms.4 = (f32[2,6,16,128]{3,2,1,0:T(8,128)S(1)}, f32[8,2,2,4,16,128]{5,4,3,2,1,0:T(8,128)S(1)}, f32[16,256]{1,0:T(8,128)S(1)}) custom-call(f32[16,16,128]{2,1,0:T(8,128)S(1)} %get-tuple-element.62.near_ref, f32[16,16,128]{2,1,0:T(8,128)S(1)} %get-tuple-element.59.far_ref, f32[2,2,2,4,16,128]{5,4,3,2,1,0:T(8,128)S(1)} %get-tuple-element.63.inner_ref, ...), custom_call_target="tpu_custom_call" | custom-call | flops 4194304 | bytes 1048576 | tf_op jit(solution)/shard_map/inner_terms/pallas_call | solution.py:514
  30.5 0.0 collective-permute-done.9.halo_ref.near_halo_ref
  30.5 0.6 %near_terms.4 = (f32[2,2,4,16,128]{4,3,2,1,0:T(8,128)S(1)}, f32[16,256]{1,0:T(8,128)S(1)}) custom-call(f32[16,16,128]{2,1,0:T(8,128)S(1)} %get-tuple-element.62.near_ref, f32[2,2,2,4,16,128]{5,4,3,2,1,0:T(8,128)S(1)} %get-tuple-element.63.inner_ref, f32[4,4,2,4,16,128]{5,4,3,2,1,0:T(8,128)S(1)} %trigs.4.trig_ref, ...), custom_call_target="tpu_custom_call" | custom-call | flops 4194304 | bytes 1048576 | tf_op jit(solution)/shard_map/near_terms/pallas_call | solution.py:514
  31.1 0.0 collective-permute-done.8.halo_ref.far_halo_ref
  31.1 0.6 %far_terms.4 = (f32[2,2,4,16,128]{4,3,2,1,0:T(8,128)S(1)}, f32[8,256]{1,0:T(8,128)S(1)}) custom-call(f32[16,16,128]{2,1,0:T(8,128)S(1)} %get-tuple-element.59.far_ref, f32[2,2,2,4,16,128]{5,4,3,2,1,0:T(8,128)S(1)} %get-tuple-element.63.inner_ref, f32[4,4,2,4,16,128]{5,4,3,2,1,0:T(8,128)S(1)} %trigs.4.trig_ref, ...), custom_call_target="tpu_custom_call" | custom-call | flops 4194304 | bytes 1048576 | tf_op jit(solution)/shard_map/far_terms/pallas_call | solution.py:514
  31.7 0.1 collective-permute-start.10
  31.8 2.3 %collective-permute-start.11 = (f32[8,256]{1,0:T(8,128)S(1)}, f32[8,256]{1,0:T(8,128)S(1)}, u32[]{:S(2)}, u32[]{:S(2)}) collective-permute-start(f32[8,256]{1,0:T(8,128)S(1)} %get-tuple-element.69.message_ref), channel_id=1, source_target_pairs={{0,28},{4,8},{8,4},{12,16},{16,12},{20,24},{24,20},{28,0},{1,29},{... | collective-permute-start | bytes 24584 | tf_op jit(solution)/shard_map/ppermute | solution.py:531
  34.1 0.2 outer_locals.4.local_ref
  34.3 1.1 %collective-permute-done.10.near_message_ref = f32[8,256]{1,0:T(8,128)S(1)} collective-permute-done((f32[8,256]{1,0:T(8,128)S(1)}, f32[8,256]{1,0:T(8,128)S(1)}, u32[]{:S(2)}, u32[]{:S(2)}) %collective-permute-start.10) | collective-permute-done | bytes 8224 | tf_op jit(solution)/shard_map/ppermute | solution.py:531
  35.4 2.8 %collective-permute-done.11.far_message_ref = f32[8,256]{1,0:T(8,128)S(1)} collective-permute-done((f32[8,256]{1,0:T(8,128)S(1)}, f32[8,256]{1,0:T(8,128)S(1)}, u32[]{:S(2)}, u32[]{:S(2)}) %collective-permute-start.11) | collective-permute-done | bytes 8224 | tf_op jit(solution)/shard_map/ppermute | solution.py:531
  38.2 0.7 %advance_outer.3 = (bf16[24,256]{1,0:T(8,128)(2,1)S(1)}, f32[16,16,128]{2,1,0:T(8,128)S(1)}, f32[16,16,128]{2,1,0:T(8,128)S(1)}) custom-call(f32[8,256]{1,0:T(8,128)S(1)} %get-tuple-element.69.message_ref, f32[8,256]{1,0:T(8,128)S(1)} %collective-permute-done.10.near_message_ref, f32[8,256]{1,0:T(8,128)S(1)} %collective-permute-done.11.far_message_ref, ...), custom_call_target="tpu_custom_call" | custom-call | flops 4194304 | bytes 1048576 | tf_op jit(solution)/shard_map/advance_outer/pallas_call | solution.py:514
  38.9 0.2 collective-permute-start.15
  39.1 2.2 %collective-permute-start.14 = (f32[16,16,128]{2,1,0:T(8,128)S(1)}, f32[16,16,128]{2,1,0:T(8,128)S(1)}, u32[]{:S(2)}, u32[]{:S(2)}) collective-permute-start(f32[16,16,128]{2,1,0:T(8,128)S(1)} %get-tuple-element.72.far_ref), channel_id=1, source_target_pairs={{0,28},{4,8},{8,4},{12,16},{16,12},{20,24},{24,20},{28,0},{1,29},{... | collective-permute-start | bytes 393224 | tf_op jit(solution)/shard_map/ppermute | solution.py:531
  41.3 0.5 advance_inner.3
  41.8 0.1 collective-permute-start.12
  41.9 1.6 %collective-permute-start.13 = (f32[32,128]{1,0:T(8,128)S(1)}, f32[32,128]{1,0:T(8,128)S(1)}, u32[]{:S(2)}, u32[]{:S(2)}) collective-permute-start(f32[32,128]{1,0:T(8,128)S(1)} %get-tuple-element.78), channel_id=1, source_target_pairs={{0,3},{1,2},{2,1},{3,0},{4,7},{5,6},{6,5},{7,4},{8,11},{9,10},{10,... | collective-permute-start | bytes 49160 | tf_op jit(solution)/shard_map/ppermute | solution.py:531
  43.5 0.4 trigs.5.trig_ref
  43.9 0.0 collective-permute-done.12.y_near_ref
  43.9 1.2 %collective-permute-done.13.y_far_ref = f32[32,128]{1,0:T(8,128)S(1)} collective-permute-done((f32[32,128]{1,0:T(8,128)S(1)}, f32[32,128]{1,0:T(8,128)S(1)}, u32[]{:S(2)}, u32[]{:S(2)}) %collective-permute-start.13) | collective-permute-done | bytes 16416 | tf_op jit(solution)/shard_map/ppermute | solution.py:531
  45.1 1.0 %inner_terms.5 = (f32[2,6,16,128]{3,2,1,0:T(8,128)S(1)}, f32[8,2,2,4,16,128]{5,4,3,2,1,0:T(8,128)S(1)}, f32[16,256]{1,0:T(8,128)S(1)}) custom-call(f32[16,16,128]{2,1,0:T(8,128)S(1)} %get-tuple-element.75.near_ref, f32[16,16,128]{2,1,0:T(8,128)S(1)} %get-tuple-element.72.far_ref, f32[2,2,2,4,16,128]{5,4,3,2,1,0:T(8,128)S(1)} %get-tuple-element.76.inner_ref, ...), custom_call_target="tpu_custom_call" | custom-call | flops 4194304 | bytes 1048576 | tf_op jit(solution)/shard_map/inner_terms/pallas_call | solution.py:514
  46.2 0.0 collective-permute-done.15.halo_ref.near_halo_ref
  46.2 0.6 %near_terms.5 = (f32[2,2,4,16,128]{4,3,2,1,0:T(8,128)S(1)}, f32[16,256]{1,0:T(8,128)S(1)}) custom-call(f32[16,16,128]{2,1,0:T(8,128)S(1)} %get-tuple-element.75.near_ref, f32[2,2,2,4,16,128]{5,4,3,2,1,0:T(8,128)S(1)} %get-tuple-element.76.inner_ref, f32[4,4,2,4,16,128]{5,4,3,2,1,0:T(8,128)S(1)} %trigs.5.trig_ref, ...), custom_call_target="tpu_custom_call" | custom-call | flops 4194304 | bytes 1048576 | tf_op jit(solution)/shard_map/near_terms/pallas_call | solution.py:514
  46.8 0.0 collective-permute-done.14.halo_ref.far_halo_ref
  46.8 0.6 %far_terms.5 = (f32[2,2,4,16,128]{4,3,2,1,0:T(8,128)S(1)}, f32[8,256]{1,0:T(8,128)S(1)}) custom-call(f32[16,16,128]{2,1,0:T(8,128)S(1)} %get-tuple-element.72.far_ref, f32[2,2,2,4,16,128]{5,4,3,2,1,0:T(8,128)S(1)} %get-tuple-element.76.inner_ref, f32[4,4,2,4,16,128]{5,4,3,2,1,0:T(8,128)S(1)} %trigs.5.trig_ref, ...), custom_call_target="tpu_custom_call" | custom-call | flops 4194304 | bytes 1048576 | tf_op jit(solution)/shard_map/far_terms/pallas_call | solution.py:514
  47.4 0.2 collective-permute-start.16
  47.5 2.6 %collective-permute-start.17 = (f32[8,256]{1,0:T(8,128)S(1)}, f32[8,256]{1,0:T(8,128)S(1)}, u32[]{:S(2)}, u32[]{:S(2)}) collective-permute-start(f32[8,256]{1,0:T(8,128)S(1)} %get-tuple-element.82.message_ref), channel_id=1, source_target_pairs={{0,28},{4,8},{8,4},{12,16},{16,12},{20,24},{24,20},{28,0},{1,29},{... | collective-permute-start | bytes 24584 | tf_op jit(solution)/shard_map/ppermute | solution.py:531
  50.1 0.2 outer_locals.5.outer_local_ref
  50.3 0.8 %collective-permute-done.16.near_message_ref = f32[8,256]{1,0:T(8,128)S(1)} collective-permute-done((f32[8,256]{1,0:T(8,128)S(1)}, f32[8,256]{1,0:T(8,128)S(1)}, u32[]{:S(2)}, u32[]{:S(2)}) %collective-permute-start.16) | collective-permute-done | bytes 8224 | tf_op jit(solution)/shard_map/ppermute | solution.py:531
  51.1 2.8 %collective-permute-done.17.far_message_ref = f32[8,256]{1,0:T(8,128)S(1)} collective-permute-done((f32[8,256]{1,0:T(8,128)S(1)}, f32[8,256]{1,0:T(8,128)S(1)}, u32[]{:S(2)}, u32[]{:S(2)}) %collective-permute-start.17) | collective-permute-done | bytes 8224 | tf_op jit(solution)/shard_map/ppermute | solution.py:531
  53.9 2.4 %finish.1 = (f32[4,32,512]{2,1,0:T(8,128)}, f32[4,32,512]{2,1,0:T(8,128)}) custom-call(f32[8,256]{1,0:T(8,128)S(1)} %get-tuple-element.82.message_ref, f32[8,256]{1,0:T(8,128)S(1)} %collective-permute-done.16.near_message_ref, f32[8,256]{1,0:T(8,128)S(1)} %collective-permute-done.17.far_message_ref, bf16[512,256]{1,0:T(8,128)(2,1)S(1)} %matches.1.match_ref, ...), custom_call_target="tpu_custom_call" | custom-call | flops 4194304 | bytes 1048576 | tf_op jit(solution)/shard_map/finish/pallas_call | solution.py:514
Async XLA Ops:
  2.2 11.4 %collective-permute-start.3 = (f32[17,16,128]{2,1,0:T(8,128)S(1)}, f32[17,16,128]{2,1,0:T(8,128)S(1)}, u32[]{:S(2)}, u32[]{:S(2)}) collective-permute-start(f32[17,16,128]{2,1,0:T(8,128)S(1)} %get-tuple-element.47.near_ref), channel_id=1, source_target_pairs={{0,4},{4,0},{8,12},{12,8},{16,20},{20,16},{24,28},{28,24},{1,5},{5... | collective-permute-start | bytes 417800 | tf_op jit(solution)/shard_map/ppermute | solution.py:531
  5.2 9.0 %collective-permute-start.2 = (f32[17,16,128]{2,1,0:T(8,128)S(1)}, f32[17,16,128]{2,1,0:T(8,128)S(1)}, u32[]{:S(2)}, u32[]{:S(2)}) collective-permute-start(f32[17,16,128]{2,1,0:T(8,128)S(1)} %get-tuple-element.44.far_ref), channel_id=1, source_target_pairs={{0,28},{4,8},{8,4},{12,16},{16,12},{20,24},{24,20},{28,0},{1,29},{... | collective-permute-start | bytes 417800 | tf_op jit(solution)/shard_map/ppermute | solution.py:531
  9.2 2.9 %collective-permute-start = (f32[32,128]{1,0:T(8,128)S(1)}, f32[32,128]{1,0:T(8,128)S(1)}, u32[]{:S(2)}, u32[]{:S(2)}) collective-permute-start(f32[32,128]{1,0:T(8,128)S(1)} %get-tuple-element.49), channel_id=1, source_target_pairs={{0,1},{1,0},{2,3},{3,2},{4,5},{5,4},{6,7},{7,6},{8,9},{9,8},{10,11... | collective-permute-start | bytes 49160 | tf_op jit(solution)/shard_map/ppermute | solution.py:531
  9.3 3.2 %collective-permute-start.1 = (f32[32,128]{1,0:T(8,128)S(1)}, f32[32,128]{1,0:T(8,128)S(1)}, u32[]{:S(2)}, u32[]{:S(2)}) collective-permute-start(f32[32,128]{1,0:T(8,128)S(1)} %get-tuple-element.50), channel_id=1, source_target_pairs={{0,3},{1,2},{2,1},{3,0},{4,7},{5,6},{6,5},{7,4},{8,11},{9,10},{10,... | collective-permute-start | bytes 49160 | tf_op jit(solution)/shard_map/ppermute | solution.py:531
  14.8 4.0 %collective-permute-start.4 = (f32[8,256]{1,0:T(8,128)S(1)}, f32[8,256]{1,0:T(8,128)S(1)}, u32[]{:S(2)}, u32[]{:S(2)}) collective-permute-start(f32[8,256]{1,0:T(8,128)S(1)} %get-tuple-element.55.message_ref), channel_id=1, source_target_pairs={{0,4},{4,0},{8,12},{12,8},{16,20},{20,16},{24,28},{28,24},{1,5},{5... | collective-permute-start | bytes 24584 | tf_op jit(solution)/shard_map/ppermute | solution.py:531
  14.9 6.4 %collective-permute-start.5 = (f32[8,256]{1,0:T(8,128)S(1)}, f32[8,256]{1,0:T(8,128)S(1)}, u32[]{:S(2)}, u32[]{:S(2)}) collective-permute-start(f32[8,256]{1,0:T(8,128)S(1)} %get-tuple-element.55.message_ref), channel_id=1, source_target_pairs={{0,28},{4,8},{8,4},{12,16},{16,12},{20,24},{24,20},{28,0},{1,29},{... | collective-permute-start | bytes 24584 | tf_op jit(solution)/shard_map/ppermute | solution.py:531
  22.0 8.5 %collective-permute-start.9 = (f32[16,16,128]{2,1,0:T(8,128)S(1)}, f32[16,16,128]{2,1,0:T(8,128)S(1)}, u32[]{:S(2)}, u32[]{:S(2)}) collective-permute-start(f32[16,16,128]{2,1,0:T(8,128)S(1)} %get-tuple-element.62.near_ref), channel_id=1, source_target_pairs={{0,4},{4,0},{8,12},{12,8},{16,20},{20,16},{24,28},{28,24},{1,5},{5... | collective-permute-start | bytes 393224 | tf_op jit(solution)/shard_map/ppermute | solution.py:531
  22.2 8.9 %collective-permute-start.8 = (f32[16,16,128]{2,1,0:T(8,128)S(1)}, f32[16,16,128]{2,1,0:T(8,128)S(1)}, u32[]{:S(2)}, u32[]{:S(2)}) collective-permute-start(f32[16,16,128]{2,1,0:T(8,128)S(1)} %get-tuple-element.59.far_ref), channel_id=1, source_target_pairs={{0,28},{4,8},{8,4},{12,16},{16,12},{20,24},{24,20},{28,0},{1,29},{... | collective-permute-start | bytes 393224 | tf_op jit(solution)/shard_map/ppermute | solution.py:531
  26.1 2.1 %collective-permute-start.6 = (f32[32,128]{1,0:T(8,128)S(1)}, f32[32,128]{1,0:T(8,128)S(1)}, u32[]{:S(2)}, u32[]{:S(2)}) collective-permute-start(f32[32,128]{1,0:T(8,128)S(1)} %get-tuple-element.64), channel_id=1, source_target_pairs={{0,1},{1,0},{2,3},{3,2},{4,5},{5,4},{6,7},{7,6},{8,9},{9,8},{10,11... | collective-permute-start | bytes 49160 | tf_op jit(solution)/shard_map/ppermute | solution.py:531
  26.2 3.2 %collective-permute-start.7 = (f32[32,128]{1,0:T(8,128)S(1)}, f32[32,128]{1,0:T(8,128)S(1)}, u32[]{:S(2)}, u32[]{:S(2)}) collective-permute-start(f32[32,128]{1,0:T(8,128)S(1)} %get-tuple-element.65), channel_id=1, source_target_pairs={{0,3},{1,2},{2,1},{3,0},{4,7},{5,6},{6,5},{7,4},{8,11},{9,10},{10,... | collective-permute-start | bytes 49160 | tf_op jit(solution)/shard_map/ppermute | solution.py:531
  31.7 3.7 %collective-permute-start.10 = (f32[8,256]{1,0:T(8,128)S(1)}, f32[8,256]{1,0:T(8,128)S(1)}, u32[]{:S(2)}, u32[]{:S(2)}) collective-permute-start(f32[8,256]{1,0:T(8,128)S(1)} %get-tuple-element.69.message_ref), channel_id=1, source_target_pairs={{0,4},{4,0},{8,12},{12,8},{16,20},{20,16},{24,28},{28,24},{1,5},{5... | collective-permute-start | bytes 24584 | tf_op jit(solution)/shard_map/ppermute | solution.py:531
  31.8 6.4 %collective-permute-start.11 = (f32[8,256]{1,0:T(8,128)S(1)}, f32[8,256]{1,0:T(8,128)S(1)}, u32[]{:S(2)}, u32[]{:S(2)}) collective-permute-start(f32[8,256]{1,0:T(8,128)S(1)} %get-tuple-element.69.message_ref), channel_id=1, source_target_pairs={{0,28},{4,8},{8,4},{12,16},{16,12},{20,24},{24,20},{28,0},{1,29},{... | collective-permute-start | bytes 24584 | tf_op jit(solution)/shard_map/ppermute | solution.py:531
  38.9 7.3 %collective-permute-start.15 = (f32[16,16,128]{2,1,0:T(8,128)S(1)}, f32[16,16,128]{2,1,0:T(8,128)S(1)}, u32[]{:S(2)}, u32[]{:S(2)}) collective-permute-start(f32[16,16,128]{2,1,0:T(8,128)S(1)} %get-tuple-element.75.near_ref), channel_id=1, source_target_pairs={{0,4},{4,0},{8,12},{12,8},{16,20},{20,16},{24,28},{28,24},{1,5},{5... | collective-permute-start | bytes 393224 | tf_op jit(solution)/shard_map/ppermute | solution.py:531
  39.1 7.6 %collective-permute-start.14 = (f32[16,16,128]{2,1,0:T(8,128)S(1)}, f32[16,16,128]{2,1,0:T(8,128)S(1)}, u32[]{:S(2)}, u32[]{:S(2)}) collective-permute-start(f32[16,16,128]{2,1,0:T(8,128)S(1)} %get-tuple-element.72.far_ref), channel_id=1, source_target_pairs={{0,28},{4,8},{8,4},{12,16},{16,12},{20,24},{24,20},{28,0},{1,29},{... | collective-permute-start | bytes 393224 | tf_op jit(solution)/shard_map/ppermute | solution.py:531
  41.8 2.1 %collective-permute-start.12 = (f32[32,128]{1,0:T(8,128)S(1)}, f32[32,128]{1,0:T(8,128)S(1)}, u32[]{:S(2)}, u32[]{:S(2)}) collective-permute-start(f32[32,128]{1,0:T(8,128)S(1)} %get-tuple-element.77), channel_id=1, source_target_pairs={{0,1},{1,0},{2,3},{3,2},{4,5},{5,4},{6,7},{7,6},{8,9},{9,8},{10,11... | collective-permute-start | bytes 49160 | tf_op jit(solution)/shard_map/ppermute | solution.py:531
  41.9 3.2 %collective-permute-start.13 = (f32[32,128]{1,0:T(8,128)S(1)}, f32[32,128]{1,0:T(8,128)S(1)}, u32[]{:S(2)}, u32[]{:S(2)}) collective-permute-start(f32[32,128]{1,0:T(8,128)S(1)} %get-tuple-element.78), channel_id=1, source_target_pairs={{0,3},{1,2},{2,1},{3,0},{4,7},{5,6},{6,5},{7,4},{8,11},{9,10},{10,... | collective-permute-start | bytes 49160 | tf_op jit(solution)/shard_map/ppermute | solution.py:531
  47.4 3.7 %collective-permute-start.16 = (f32[8,256]{1,0:T(8,128)S(1)}, f32[8,256]{1,0:T(8,128)S(1)}, u32[]{:S(2)}, u32[]{:S(2)}) collective-permute-start(f32[8,256]{1,0:T(8,128)S(1)} %get-tuple-element.82.message_ref), channel_id=1, source_target_pairs={{0,4},{4,0},{8,12},{12,8},{16,20},{20,16},{24,28},{28,24},{1,5},{5... | collective-permute-start | bytes 24584 | tf_op jit(solution)/shard_map/ppermute | solution.py:531
  47.5 6.3 %collective-permute-start.17 = (f32[8,256]{1,0:T(8,128)S(1)}, f32[8,256]{1,0:T(8,128)S(1)}, u32[]{:S(2)}, u32[]{:S(2)}) collective-permute-start(f32[8,256]{1,0:T(8,128)S(1)} %get-tuple-element.82.message_ref), channel_id=1, source_target_pairs={{0,28},{4,8},{8,4},{12,16},{16,12},{20,24},{24,20},{28,0},{1,29},{... | collective-permute-start | bytes 24584 | tf_op jit(solution)/shard_map/ppermute | solution.py:531

commit v4 on v3

--- a/solution.py
+++ b/solution.py
@@ -100,7 +100,7 @@
 def x_chooser(nx, xb, back=False):
     first = lax.broadcasted_iota(jnp.int32, (nx, nx), 1 if back else 0)
     second = lax.broadcasted_iota(jnp.int32, (nx, nx), 0 if back else 1)
-    return jnp.where(first == COLS * (second % xb) + second // xb, 1.0, 0.0).astype(jnp.bfloat16)
+    return jnp.where(first == COLS * (second & (xb - 1)) + (second >> (xb.bit_length() - 1)), 1.0, 0.0).astype(jnp.bfloat16)
 
 
 def spread(in_ref, chooser, rows_ref, put):
@@ -175,13 +175,22 @@
     block_ref[...] = slot_rows_ref[pl.ds(0, cz * yb, stride=ROWS), :]
 
 
-def onehot_kernel(block_ref, onehot_ref):
+def onehot_kernel(block_ref, onehot_ref, chooser_ref):
     rows, xb = block_ref.shape
     slots = onehot_ref.shape[1]
-    slot = lax.broadcasted_iota(jnp.int32, (slots, xb), 0).astype(jnp.float32)
+    one, zero = jnp.ones((), jnp.bfloat16), jnp.zeros((), jnp.bfloat16)
+    down = lax.broadcasted_iota(jnp.int32, (slots, xb), 0).astype(jnp.float32).astype(jnp.bfloat16)
+    across = lax.broadcasted_iota(jnp.int32, (xb, xb), 1)
+    across = [(across + half * xb).astype(jnp.float32).astype(jnp.bfloat16) for half in range(slots // xb)]
+    turned = jnp.transpose(jnp.concatenate([block_ref[...], jnp.zeros((xb - rows, xb), jnp.float32)], axis=0))
     for r in range(rows):
-        hit = jnp.where(slot == block_ref[r : r + 1, :], 1.0, 0.0).astype(jnp.bfloat16)
-        onehot_ref[r // 2, :, (r % 2) * xb : (r % 2 + 1) * xb] = hit
+        at = (r % 2) * xb
+        line = jnp.broadcast_to(block_ref[r : r + 1, :], (16, xb)).astype(jnp.bfloat16)
+        line = jnp.concatenate([line] * (slots // 16), axis=0)
+        onehot_ref[r // 2, :, at : at + xb] = jnp.where(down == line, one, zero)
+        line = jnp.broadcast_to(turned[:, r : r + 1], (xb, xb)).astype(jnp.bfloat16)
+        for half in range(slots // xb):
+            chooser_ref[r // 2, at : at + xb, half * xb : (half + 1) * xb] = jnp.where(across[half] == line, one, zero)
 
 
 def derived(e, q):
@@ -253,22 +262,20 @@
             sums_ref[start : start + yb, :] = piece.astype(jnp.float32)
 
 
-def slot_sums(sums_ref, onehot_ref, first_pair):
+def slot_sums(sums_ref, chooser_ref, first_pair):
     rows = sums_ref.shape[0] // 16
     sums_ref[15 * rows : 16 * rows, :] = jnp.zeros((rows, sums_ref.shape[1]), jnp.float32)
-    acc = jnp.zeros((16, onehot_ref.shape[1]), jnp.float32)
+    acc = jnp.zeros((16, chooser_ref.shape[2]), jnp.float32)
     for i in range(rows // 2):
         left = jnp.concatenate(
             [sums_ref[pl.ds(2 * i + h, 16, stride=rows), :] for h in range(2)], axis=1
         ).astype(jnp.bfloat16)
-        acc = acc + lax.dot_general(
-            left, onehot_ref[first_pair + i], (((1,), (1,)), ((), ())), preferred_element_type=jnp.float32
-        )
+        acc = acc + jnp.dot(left, chooser_ref[first_pair + i], preferred_element_type=jnp.float32)
     return acc
 
 
 def inner_kernel(
-    near_ref, far_ref, inner_ref, trig_ref, y_near_ref, y_far_ref, onehot_ref,
+    near_ref, far_ref, inner_ref, trig_ref, y_near_ref, y_far_ref, chooser_ref,
     rim_ref, local_ref, acc_ref,
     sums_ref,
 ):
@@ -309,7 +316,7 @@
                 for k, value in enumerate(local):
                     local_ref[k, at, p, j] = value
         put_sums(totals, at, yb, sums_ref)
-    acc_ref[...] = slot_sums(sums_ref, onehot_ref, yb)
+    acc_ref[...] = slot_sums(sums_ref, chooser_ref, yb)
 
 
 def outer_getters(layer, own_ref, inner_ref, trig_ref, halo):
@@ -324,7 +331,7 @@
     return get, halo, inward
 
 
-def outer_densities(layer, own_ref, inner_ref, trig_ref, rim_ref, halo_ref, onehot_ref, mixed_ref, trig_halo_ref, sums_ref):
+def outer_densities(layer, own_ref, inner_ref, trig_ref, rim_ref, halo_ref, chooser_ref, mixed_ref, trig_halo_ref, sums_ref):
     yb = trig_ref.shape[4]
     for p in range(ROWS):
         for j in range(COLS):
@@ -344,26 +351,26 @@
             mixed_ref[0, p, j] = weight
             mixed_ref[1, p, j] = torque
     put_sums(totals, 0, yb, sums_ref)
-    return slot_sums(sums_ref, onehot_ref, layer * yb // 2)
+    return slot_sums(sums_ref, chooser_ref, layer * yb // 2)
 
 
 def near_kernel(
-    near_ref, inner_ref, trig_ref, rim_ref, halo_ref, onehot_ref, before_ref,
+    near_ref, inner_ref, trig_ref, rim_ref, halo_ref, chooser_ref, before_ref,
     mixed_ref, acc_ref,
     trig_halo_ref, sums_ref,
 ):
     acc_ref[...] = before_ref[...] + outer_densities(
-        0, near_ref, inner_ref, trig_ref, rim_ref, halo_ref, onehot_ref, mixed_ref, trig_halo_ref, sums_ref
+        0, near_ref, inner_ref, trig_ref, rim_ref, halo_ref, chooser_ref, mixed_ref, trig_halo_ref, sums_ref
     )
 
 
 def far_kernel(
-    far_ref, inner_ref, trig_ref, rim_ref, halo_ref, onehot_ref, before_ref,
+    far_ref, inner_ref, trig_ref, rim_ref, halo_ref, chooser_ref, before_ref,
     mixed_ref, message_ref,
     trig_halo_ref, sums_ref, acc_ref,
 ):
     acc_ref[...] = before_ref[...] + outer_densities(
-        1, far_ref, inner_ref, trig_ref, rim_ref, halo_ref, onehot_ref, mixed_ref, trig_halo_ref, sums_ref
+        1, far_ref, inner_ref, trig_ref, rim_ref, halo_ref, chooser_ref, mixed_ref, trig_halo_ref, sums_ref
     )
     message_ref[0:5, :] = acc_ref[0:5, :] + acc_ref[5:10, :] + acc_ref[10:15, :]
     message_ref[5:8, :] = jnp.zeros((3, message_ref.shape[1]), jnp.float32)
@@ -407,30 +414,35 @@
     return jnp.concatenate([part.astype(jnp.float32) for part in split3(value)], axis=0).astype(jnp.bfloat16)
 
 
-def unstacked(value):
-    return value[0:8] + value[8:16] + value[16:24]
-
-
-def slot_motion(message_ref, near_ref, far_ref, match_ref):
+def slot_motion(message_ref, near_ref, far_ref, match_ref, velocity_ref):
     others = jnp.concatenate([stacked(near_ref[...]), stacked(far_ref[...])], axis=1)
-    totals = message_ref[...] + unstacked(jnp.dot(others, match_ref[...], preferred_element_type=jnp.float32))
+    parts = jnp.dot(others, match_ref[...], preferred_element_type=jnp.float32)
+    totals = message_ref[...] + parts[0:8] + parts[8:16] + parts[16:24]
     inverse = 1.0 / totals[4:5, :]
-    return stacked(TRANSLATE * totals * inverse)
-
-
-def block_motion(velocity, onehot_ref, motion_ref, first_pair):
+    for part, piece in enumerate(split3(TRANSLATE * totals[0:4, :] * inverse)):
+        velocity_ref[4 * part : 4 * part + 4, :] = piece.astype(jnp.float32)
+    velocity_ref[12:16, :] = jnp.zeros((4, velocity_ref.shape[1]), jnp.float32)
+
+
+def block_motion(velocity_ref, onehot_ref, motion_ref, first_pair):
     rows = motion_ref.shape[0] // 8
     xb = motion_ref.shape[1]
+    velocity = velocity_ref[...].astype(jnp.bfloat16)
     for i in range(rows // 2):
-        moved = unstacked(jnp.dot(velocity, onehot_ref[first_pair + i], preferred_element_type=jnp.float32))
+        moved = jnp.dot(velocity, onehot_ref[first_pair + i], preferred_element_type=jnp.float32)
+        moved = moved[0:8] + moved[8:16]
         for h in range(2):
             motion_ref[pl.ds(2 * i + h, 8, stride=rows), :] = moved[:, h * xb : (h + 1) * xb]
 
 
-def advanced(local_ref, motion_ref, at, p, j):
-    layers, yb = local_ref.shape[1], local_ref.shape[4]
-    rows = layers * yb
-    vx, vy, vz, turn = (motion_ref[k * rows + at * yb : k * rows + (at + 1) * yb, :] for k in range(4))
+def layer_motion(motion_ref, at, yb):
+    rows = motion_ref.shape[0] // 8
+    parts = [motion_ref[k * rows + at * yb : k * rows + (at + 1) * yb, :] for k in range(8)]
+    return [parts[k] + parts[4 + k] for k in range(4)]
+
+
+def advanced(local_ref, motion, at, p, j):
+    vx, vy, vz, turn = motion
     g = [local_ref[k, at, p, j] for k in range(2, 8)]
     e = local_ref[0, at, p, j] - (vx * g[0] + vy * g[1] + vz * g[2])
     q = local_ref[1, at, p, j] + turn - (vx * g[3] + vy * g[4] + vz * g[5])
@@ -442,13 +454,13 @@
     velocity_ref, near_ref, far_ref,
     motion_ref,
 ):
-    velocity = slot_motion(message_ref, near_message_ref, far_message_ref, match_ref)
-    velocity_ref[...] = velocity
-    block_motion(velocity, onehot_ref, motion_ref, 0)
+    slot_motion(message_ref, near_message_ref, far_message_ref, match_ref, velocity_ref)
+    block_motion(velocity_ref, onehot_ref, motion_ref, 0)
     for layer, ref in enumerate((near_ref, far_ref)):
+        motion = layer_motion(motion_ref, layer, local_ref.shape[4])
         for p in range(ROWS):
             for j in range(COLS):
-                ref[tile(0, p, j)], ref[tile(1, p, j)] = advanced(local_ref, motion_ref, layer, p, j)
+                ref[tile(0, p, j)], ref[tile(1, p, j)] = advanced(local_ref, motion, layer, p, j)
 
 
 def advance_inner_kernel(
@@ -457,32 +469,34 @@
     motion_ref,
 ):
     layers, yb = local_ref.shape[1], local_ref.shape[4]
-    block_motion(velocity_ref[...], onehot_ref, motion_ref, yb)
+    block_motion(velocity_ref, onehot_ref, motion_ref, yb)
     for at in range(layers):
+        motion = layer_motion(motion_ref, at, yb)
         for p in range(ROWS):
             for j in range(COLS):
-                inner_ref[0, at, p, j], inner_ref[1, at, p, j] = advanced(local_ref, motion_ref, at, p, j)
+                inner_ref[0, at, p, j], inner_ref[1, at, p, j] = advanced(local_ref, motion, at, p, j)
     put_y_edges(near_ref, far_ref, inner_ref, y_near_ref, y_far_ref)
 
 
 def finish_kernel(
     message_ref, near_message_ref, far_message_ref, match_ref, onehot_ref, outer_local_ref, inner_local_ref,
     e_hbm, q_hbm,
-    motion_ref, rows_ref, out_ref, sems,
+    velocity_ref, motion_ref, rows_ref, out_ref, sems,
 ):
     yb, xb = outer_local_ref.shape[4:]
     _, cz, cy, nx = out_ref.shape
-    velocity = slot_motion(message_ref, near_message_ref, far_message_ref, match_ref)
+    slot_motion(message_ref, near_message_ref, far_message_ref, match_ref, velocity_ref)
     chooser = x_chooser(nx, xb, back=True)
     copies = []
     for part, local_ref in enumerate((outer_local_ref, inner_local_ref)):
         layers = local_ref.shape[1]
-        block_motion(velocity, onehot_ref, motion_ref, part * yb)
+        block_motion(velocity_ref, onehot_ref, motion_ref, part * yb)
         for at in range(layers):
+            motion = layer_motion(motion_ref, at, yb)
             for p in range(ROWS):
                 to = pl.ds(at * cy + p, yb, stride=ROWS)
                 for j in range(COLS):
-                    e, q = advanced(local_ref, motion_ref, at, p, j)
+                    e, q = advanced(local_ref, motion, at, p, j)
                     rows_ref[0, j, to, :] = e
                     rows_ref[1, j, to, :] = q
         moved = exact_dot(
@@ -566,7 +580,7 @@
         prepare_inner_kernel, "prepare_inner", [inner_out] + y_out + [((rows, xb), f32)],
         [pltpu.VMEM((COLS, 2 * (cz - 2) * cy, xb), f32), pltpu.VMEM((cz * cy, xb), f32)],
     )
-    onehots = call(onehot_kernel, "onehots", [((rows // 2, slots, 2 * xb), bf16)])
+    onehots = call(onehot_kernel, "onehots", [((rows // 2, slots, 2 * xb), bf16), ((rows // 2, 2 * xb, slots), bf16)])
     trigs = call(trig_kernel, "trigs", [((4, cz) + block, f32)])
     inner_terms = call(
         inner_kernel, "inner_terms", [((2, 6, cz * COLS, xb), f32), ((8, cz - 2) + block, f32), acc_out],
@@ -579,13 +593,13 @@
     outer_locals = call(outer_local_kernel, "outer_locals", [((8, 2) + block, f32)])
     matches = call(match_kernel, "matches", [((2 * slots, slots), bf16)])
     advance_outer = call(
-        advance_outer_kernel, "advance_outer", [((24, slots), bf16), side_out, side_out], [outer_motion]
+        advance_outer_kernel, "advance_outer", [((16, slots), f32), side_out, side_out], [outer_motion]
     )
     advance_inner = call(advance_inner_kernel, "advance_inner", [inner_out] + y_out, [inner_motion])
     finish = call(
         finish_kernel, "finish", [((cz, cy, nx), f32)] * 2,
         [
-            outer_motion, pltpu.VMEM((2, COLS, 2 * cy, xb), f32), pltpu.VMEM((2, cz, cy, nx), f32), dma((2, cz)),
+            pltpu.VMEM((16, slots), f32), outer_motion, pltpu.VMEM((2, COLS, 2 * cy, xb), f32), pltpu.VMEM((2, cz, cy, nx), f32), dma((2, cz)),
         ],
         hbm_out=True,
     )
@@ -602,11 +616,11 @@
             inner, y_near, y_far = advance_inner(velocity, onehot, inner_local, near, far)
         y_near, y_far = both(y_near, y_far, "gy")
         if step == 0:
-            (onehot,) = onehots(blocks)
+            onehot, chooser = onehots(blocks)
         (trig,) = trigs(near, far, inner)
-        rim, inner_local, acc = inner_terms(near, far, inner, trig, y_near, y_far, onehot)
-        near_mixed, acc = near_terms(near, inner, trig, rim, near_halo, onehot, acc)
-        far_mixed, message = far_terms(far, inner, trig, rim, far_halo, onehot, acc)
+        rim, inner_local, acc = inner_terms(near, far, inner, trig, y_near, y_far, chooser)
+        near_mixed, acc = near_terms(near, inner, trig, rim, near_halo, chooser, acc)
+        far_mixed, message = far_terms(far, inner, trig, rim, far_halo, chooser, acc)
         near_message, far_message = both(message, message, "gz")
         if step == 0:
             (match,) = matches(ids, near_halo, far_halo)

time: 56.5 us -> 55.9 us (0.989)
  Pallas kernels: 16.2 us -> 15.1 us
  starting transfers between devices: 26.4 us -> 27.3 us
    pallas_call x24, Pallas kernels: 16.2 us -> 15.1 us  [run(): pl.pallas_call(kernel, name=name, in_specs=[HBM] * hbm_in + [VMEM] * (len...]
    ppermute x18, starting transfers between devices: 26.4 us -> 27.3 us  [swap(): return lax.ppermute(array, axis, pairs)]
  transfers between devices with their start and end apart: 18 -> 18, of which waited for: 8 -> 7; matrix products, arithmetic and copies ran while one was open for 0% -> 0% of each run, Pallas kernels for 16% -> 15%
where the time goes in v4:
time: 55.9 us; the launch traced here: 55.8 us
  starting transfers between devices  27.3 us (49%)
  Pallas kernels  15.1 us (27%)
  waiting for transfers between devices  12.6 us (23%)
  between operations  0.81 us (1%)
    ppermute x18, starting transfers between devices, swap(): return lax.ppermute(array, axis, pairs)  27.3 us
    pallas_call x24, Pallas kernels, run(): pl.pallas_call(kernel, name=name, in_specs=[HBM] * hbm_in + [VMEM] * (len...  15.1 us
    ppermute x18, waiting for transfers between devices, swap(): return lax.ppermute(array, axis, pairs)  12.6 us
  transfers between devices with their start and end apart: 18, of which 7 were waited for; matrix products, arithmetic and copies ran while one was open for 0% of the time, Pallas kernels for 15%

profile of v4, /device:TPU:0, one launch (start us, length us, event | category | flops | bytes accessed | tf_op | source)
XLA Modules:
  0.0 55.8 jit_solution(2383953635743717951)
XLA Ops:
  0.6 1.6 %prepare_outer.1 = (f32[17,16,128]{2,1,0:T(8,128)S(1)}, f32[17,16,128]{2,1,0:T(8,128)S(1)}, f32[2,2,32,512]{3,2,1,0:T(8,128)S(1)}, s32[4,32,512]{2,1,0:T(8,128)S(1)}, s32[1,256]{1,0:T(1,128)S(1)}) custom-call(f32[4,32,512]{2,1,0:T(8,128)} %e_hbm.1, f32[4,32,512]{2,1,0:T(8,128)} %q_hbm.1, s32[4,32,512]{2,1,0:T(8,128)} %slot_hbm.1, s32[1,256]{1,0:T(1,128)} %bitcast.1), custom_call_target="tpu_custom_call" | custom-call | flops 4194304 | bytes 1048576 | tf_op jit(solution)/shard_map/prepare_outer/pallas_call | solution.py:528
  2.2 3.0 %collective-permute-start.3 = (f32[17,16,128]{2,1,0:T(8,128)S(1)}, f32[17,16,128]{2,1,0:T(8,128)S(1)}, u32[]{:S(2)}, u32[]{:S(2)}) collective-permute-start(f32[17,16,128]{2,1,0:T(8,128)S(1)} %get-tuple-element.49.near_ref), channel_id=1, source_target_pairs={{0,4},{4,0},{8,12},{12,8},{16,20},{20,16},{24,28},{28,24},{1,5},{5... | collective-permute-start | bytes 417800 | tf_op jit(solution)/shard_map/ppermute | solution.py:545
  5.2 3.5 %collective-permute-start.2 = (f32[17,16,128]{2,1,0:T(8,128)S(1)}, f32[17,16,128]{2,1,0:T(8,128)S(1)}, u32[]{:S(2)}, u32[]{:S(2)}) collective-permute-start(f32[17,16,128]{2,1,0:T(8,128)S(1)} %get-tuple-element.46.far_ref), channel_id=1, source_target_pairs={{0,28},{4,8},{8,4},{12,16},{16,12},{20,24},{24,20},{28,0},{1,29},{... | collective-permute-start | bytes 417800 | tf_op jit(solution)/shard_map/ppermute | solution.py:545
  8.8 0.4 prepare_inner.1
  9.2 0.1 collective-permute-start
  9.3 1.6 %collective-permute-start.1 = (f32[32,128]{1,0:T(8,128)S(1)}, f32[32,128]{1,0:T(8,128)S(1)}, u32[]{:S(2)}, u32[]{:S(2)}) collective-permute-start(f32[32,128]{1,0:T(8,128)S(1)} %get-tuple-element.52), channel_id=1, source_target_pairs={{0,3},{1,2},{2,1},{3,0},{4,7},{5,6},{6,5},{7,4},{8,11},{9,10},{10,... | collective-permute-start | bytes 49160 | tf_op jit(solution)/shard_map/ppermute | solution.py:545
  10.9 0.4 trigs.3.trig_ref
  11.3 1.5 %onehots.1 = (bf16[32,256,256]{2,1,0:T(8,128)(2,1)S(1)}, bf16[32,256,256]{2,1,0:T(8,128)(2,1)S(1)}) custom-call(f32[64,128]{1,0:T(8,128)S(1)} %get-tuple-element.53.block_ref), custom_call_target="tpu_custom_call" | custom-call | flops 4194304 | bytes 1048576 | tf_op jit(solution)/shard_map/onehots/pallas_call | solution.py:528
  12.8 0.0 collective-permute-done.y_near_ref
  12.8 0.0 collective-permute-done.1.y_far_ref
  12.8 0.8 %inner_terms.3 = (f32[2,6,16,128]{3,2,1,0:T(8,128)S(1)}, f32[8,2,2,4,16,128]{5,4,3,2,1,0:T(8,128)S(1)}, f32[16,256]{1,0:T(8,128)S(1)}) custom-call(f32[17,16,128]{2,1,0:T(8,128)S(1)} %get-tuple-element.49.near_ref, f32[17,16,128]{2,1,0:T(8,128)S(1)} %get-tuple-element.46.far_ref, f32[2,2,2,4,16,128]{5,4,3,2,1,0:T(8,128)S(1)} %get-tuple-element.50.inner_ref, ...), custom_call_target="tpu_custom_call" | custom-call | flops 4194304 | bytes 1048576 | tf_op jit(solution)/shard_map/inner_terms/pallas_call | solution.py:528
  13.6 0.0 collective-permute-done.3.halo_ref.near_halo_ref
  13.6 0.5 near_terms.3
  14.1 0.0 collective-permute-done.2.halo_ref.far_halo_ref
  14.1 0.5 far_terms.3
  14.6 0.1 collective-permute-start.4
  14.7 3.5 %collective-permute-start.5 = (f32[8,256]{1,0:T(8,128)S(1)}, f32[8,256]{1,0:T(8,128)S(1)}, u32[]{:S(2)}, u32[]{:S(2)}) collective-permute-start(f32[8,256]{1,0:T(8,128)S(1)} %get-tuple-element.58.message_ref), channel_id=1, source_target_pairs={{0,28},{4,8},{8,4},{12,16},{16,12},{20,24},{24,20},{28,0},{1,29},{... | collective-permute-start | bytes 24584 | tf_op jit(solution)/shard_map/ppermute | solution.py:545
  18.2 0.1 matches.1.match_ref
  18.4 0.2 outer_locals.3.local_ref
  18.5 0.0 collective-permute-done.4.near_message_ref
  18.6 2.5 %collective-permute-done.5.far_message_ref = f32[8,256]{1,0:T(8,128)S(1)} collective-permute-done((f32[8,256]{1,0:T(8,128)S(1)}, f32[8,256]{1,0:T(8,128)S(1)}, u32[]{:S(2)}, u32[]{:S(2)}) %collective-permute-start.5) | collective-permute-done | bytes 8224 | tf_op jit(solution)/shard_map/ppermute | solution.py:545
  21.1 0.6 %advance_outer.2 = (f32[16,256]{1,0:T(8,128)S(1)}, f32[16,16,128]{2,1,0:T(8,128)S(1)}, f32[16,16,128]{2,1,0:T(8,128)S(1)}) custom-call(f32[8,256]{1,0:T(8,128)S(1)} %get-tuple-element.58.message_ref, f32[8,256]{1,0:T(8,128)S(1)} %collective-permute-done.4.near_message_ref, f32[8,256]{1,0:T(8,128)S(1)} %collective-permute-done.5.far_message_ref, ...), custom_call_target="tpu_custom_call" | custom-call | flops 4194304 | bytes 1048576 | tf_op jit(solution)/shard_map/advance_outer/pallas_call | solution.py:528
  21.7 0.2 collective-permute-start.9
  21.9 3.4 %collective-permute-start.8 = (f32[16,16,128]{2,1,0:T(8,128)S(1)}, f32[16,16,128]{2,1,0:T(8,128)S(1)}, u32[]{:S(2)}, u32[]{:S(2)}) collective-permute-start(f32[16,16,128]{2,1,0:T(8,128)S(1)} %get-tuple-element.63.far_ref), channel_id=1, source_target_pairs={{0,28},{4,8},{8,4},{12,16},{16,12},{20,24},{24,20},{28,0},{1,29},{... | collective-permute-start | bytes 393224 | tf_op jit(solution)/shard_map/ppermute | solution.py:545
  25.4 0.4 advance_inner.2
  25.8 0.1 collective-permute-start.6
  25.9 1.6 %collective-permute-start.7 = (f32[32,128]{1,0:T(8,128)S(1)}, f32[32,128]{1,0:T(8,128)S(1)}, u32[]{:S(2)}, u32[]{:S(2)}) collective-permute-start(f32[32,128]{1,0:T(8,128)S(1)} %get-tuple-element.69), channel_id=1, source_target_pairs={{0,3},{1,2},{2,1},{3,0},{4,7},{5,6},{6,5},{7,4},{8,11},{9,10},{10,... | collective-permute-start | bytes 49160 | tf_op jit(solution)/shard_map/ppermute | solution.py:545
  27.5 0.4 trigs.4.trig_ref
  27.9 0.0 collective-permute-done.6.y_near_ref
  27.9 1.2 %collective-permute-done.7.y_far_ref = f32[32,128]{1,0:T(8,128)S(1)} collective-permute-done((f32[32,128]{1,0:T(8,128)S(1)}, f32[32,128]{1,0:T(8,128)S(1)}, u32[]{:S(2)}, u32[]{:S(2)}) %collective-permute-start.7) | collective-permute-done | bytes 16416 | tf_op jit(solution)/shard_map/ppermute | solution.py:545
  29.1 0.8 %inner_terms.4 = (f32[2,6,16,128]{3,2,1,0:T(8,128)S(1)}, f32[8,2,2,4,16,128]{5,4,3,2,1,0:T(8,128)S(1)}, f32[16,256]{1,0:T(8,128)S(1)}) custom-call(f32[16,16,128]{2,1,0:T(8,128)S(1)} %get-tuple-element.66.near_ref, f32[16,16,128]{2,1,0:T(8,128)S(1)} %get-tuple-element.63.far_ref, f32[2,2,2,4,16,128]{5,4,3,2,1,0:T(8,128)S(1)} %get-tuple-element.67.inner_ref, ...), custom_call_target="tpu_custom_call" | custom-call | flops 4194304 | bytes 1048576 | tf_op jit(solution)/shard_map/inner_terms/pallas_call | solution.py:528
  29.9 0.0 collective-permute-done.9.halo_ref.near_halo_ref
  29.9 0.5 near_terms.4
  30.4 0.0 collective-permute-done.8.halo_ref.far_halo_ref
  30.4 0.5 far_terms.4
  30.9 0.1 collective-permute-start.10
  31.0 2.7 %collective-permute-start.11 = (f32[8,256]{1,0:T(8,128)S(1)}, f32[8,256]{1,0:T(8,128)S(1)}, u32[]{:S(2)}, u32[]{:S(2)}) collective-permute-start(f32[8,256]{1,0:T(8,128)S(1)} %get-tuple-element.73.message_ref), channel_id=1, source_target_pairs={{0,28},{4,8},{8,4},{12,16},{16,12},{20,24},{24,20},{28,0},{1,29},{... | collective-permute-start | bytes 24584 | tf_op jit(solution)/shard_map/ppermute | solution.py:545
  33.7 0.2 outer_locals.4.local_ref
  33.9 0.7 %collective-permute-done.10.near_message_ref = f32[8,256]{1,0:T(8,128)S(1)} collective-permute-done((f32[8,256]{1,0:T(8,128)S(1)}, f32[8,256]{1,0:T(8,128)S(1)}, u32[]{:S(2)}, u32[]{:S(2)}) %collective-permute-start.10) | collective-permute-done | bytes 8224 | tf_op jit(solution)/shard_map/ppermute | solution.py:545
  34.6 2.8 %collective-permute-done.11.far_message_ref = f32[8,256]{1,0:T(8,128)S(1)} collective-permute-done((f32[8,256]{1,0:T(8,128)S(1)}, f32[8,256]{1,0:T(8,128)S(1)}, u32[]{:S(2)}, u32[]{:S(2)}) %collective-permute-start.11) | collective-permute-done | bytes 8224 | tf_op jit(solution)/shard_map/ppermute | solution.py:545
  37.4 0.6 %advance_outer.3 = (f32[16,256]{1,0:T(8,128)S(1)}, f32[16,16,128]{2,1,0:T(8,128)S(1)}, f32[16,16,128]{2,1,0:T(8,128)S(1)}) custom-call(f32[8,256]{1,0:T(8,128)S(1)} %get-tuple-element.73.message_ref, f32[8,256]{1,0:T(8,128)S(1)} %collective-permute-done.10.near_message_ref, f32[8,256]{1,0:T(8,128)S(1)} %collective-permute-done.11.far_message_ref, ...), custom_call_target="tpu_custom_call" | custom-call | flops 4194304 | bytes 1048576 | tf_op jit(solution)/shard_map/advance_outer/pallas_call | solution.py:528
  38.0 0.2 collective-permute-start.15
  38.2 2.6 %collective-permute-start.14 = (f32[16,16,128]{2,1,0:T(8,128)S(1)}, f32[16,16,128]{2,1,0:T(8,128)S(1)}, u32[]{:S(2)}, u32[]{:S(2)}) collective-permute-start(f32[16,16,128]{2,1,0:T(8,128)S(1)} %get-tuple-element.76.far_ref), channel_id=1, source_target_pairs={{0,28},{4,8},{8,4},{12,16},{16,12},{20,24},{24,20},{28,0},{1,29},{... | collective-permute-start | bytes 393224 | tf_op jit(solution)/shard_map/ppermute | solution.py:545
  40.8 0.4 advance_inner.3
  41.3 0.1 collective-permute-start.12
  41.4 1.6 %collective-permute-start.13 = (f32[32,128]{1,0:T(8,128)S(1)}, f32[32,128]{1,0:T(8,128)S(1)}, u32[]{:S(2)}, u32[]{:S(2)}) collective-permute-start(f32[32,128]{1,0:T(8,128)S(1)} %get-tuple-element.82), channel_id=1, source_target_pairs={{0,3},{1,2},{2,1},{3,0},{4,7},{5,6},{6,5},{7,4},{8,11},{9,10},{10,... | collective-permute-start | bytes 49160 | tf_op jit(solution)/shard_map/ppermute | solution.py:545
  43.0 0.4 trigs.5.trig_ref
  43.4 0.0 collective-permute-done.12.y_near_ref
  43.4 1.2 %collective-permute-done.13.y_far_ref = f32[32,128]{1,0:T(8,128)S(1)} collective-permute-done((f32[32,128]{1,0:T(8,128)S(1)}, f32[32,128]{1,0:T(8,128)S(1)}, u32[]{:S(2)}, u32[]{:S(2)}) %collective-permute-start.13) | collective-permute-done | bytes 16416 | tf_op jit(solution)/shard_map/ppermute | solution.py:545
  44.6 0.8 %inner_terms.5 = (f32[2,6,16,128]{3,2,1,0:T(8,128)S(1)}, f32[8,2,2,4,16,128]{5,4,3,2,1,0:T(8,128)S(1)}, f32[16,256]{1,0:T(8,128)S(1)}) custom-call(f32[16,16,128]{2,1,0:T(8,128)S(1)} %get-tuple-element.79.near_ref, f32[16,16,128]{2,1,0:T(8,128)S(1)} %get-tuple-element.76.far_ref, f32[2,2,2,4,16,128]{5,4,3,2,1,0:T(8,128)S(1)} %get-tuple-element.80.inner_ref, ...), custom_call_target="tpu_custom_call" | custom-call | flops 4194304 | bytes 1048576 | tf_op jit(solution)/shard_map/inner_terms/pallas_call | solution.py:528
  45.4 0.0 collective-permute-done.15.halo_ref.near_halo_ref
  45.4 0.5 near_terms.5
  45.9 0.0 collective-permute-done.14.halo_ref.far_halo_ref
  45.9 0.5 far_terms.5
  46.4 0.7 %collective-permute-start.16 = (f32[8,256]{1,0:T(8,128)S(1)}, f32[8,256]{1,0:T(8,128)S(1)}, u32[]{:S(2)}, u32[]{:S(2)}) collective-permute-start(f32[8,256]{1,0:T(8,128)S(1)} %get-tuple-element.86.message_ref), channel_id=1, source_target_pairs={{0,4},{4,0},{8,12},{12,8},{16,20},{20,16},{24,28},{28,24},{1,5},{5... | collective-permute-start | bytes 24584 | tf_op jit(solution)/shard_map/ppermute | solution.py:545
  47.1 2.1 %collective-permute-start.17 = (f32[8,256]{1,0:T(8,128)S(1)}, f32[8,256]{1,0:T(8,128)S(1)}, u32[]{:S(2)}, u32[]{:S(2)}) collective-permute-start(f32[8,256]{1,0:T(8,128)S(1)} %get-tuple-element.86.message_ref), channel_id=1, source_target_pairs={{0,28},{4,8},{8,4},{12,16},{16,12},{20,24},{24,20},{28,0},{1,29},{... | collective-permute-start | bytes 24584 | tf_op jit(solution)/shard_map/ppermute | solution.py:545
  49.2 0.2 outer_locals.5.outer_local_ref
  49.4 0.7 %collective-permute-done.16.near_message_ref = f32[8,256]{1,0:T(8,128)S(1)} collective-permute-done((f32[8,256]{1,0:T(8,128)S(1)}, f32[8,256]{1,0:T(8,128)S(1)}, u32[]{:S(2)}, u32[]{:S(2)}) %collective-permute-start.16) | collective-permute-done | bytes 8224 | tf_op jit(solution)/shard_map/ppermute | solution.py:545
  50.1 3.3 %collective-permute-done.17.far_message_ref = f32[8,256]{1,0:T(8,128)S(1)} collective-permute-done((f32[8,256]{1,0:T(8,128)S(1)}, f32[8,256]{1,0:T(8,128)S(1)}, u32[]{:S(2)}, u32[]{:S(2)}) %collective-permute-start.17) | collective-permute-done | bytes 8224 | tf_op jit(solution)/shard_map/ppermute | solution.py:545
  53.4 2.3 %finish.1 = (f32[4,32,512]{2,1,0:T(8,128)}, f32[4,32,512]{2,1,0:T(8,128)}) custom-call(f32[8,256]{1,0:T(8,128)S(1)} %get-tuple-element.86.message_ref, f32[8,256]{1,0:T(8,128)S(1)} %collective-permute-done.16.near_message_ref, f32[8,256]{1,0:T(8,128)S(1)} %collective-permute-done.17.far_message_ref, bf16[512,256]{1,0:T(8,128)(2,1)S(1)} %matches.1.match_ref, ...), custom_call_target="tpu_custom_call" | custom-call | flops 4194304 | bytes 1048576 | tf_op jit(solution)/shard_map/finish/pallas_call | solution.py:528
Async XLA Ops:
  2.2 11.4 %collective-permute-start.3 = (f32[17,16,128]{2,1,0:T(8,128)S(1)}, f32[17,16,128]{2,1,0:T(8,128)S(1)}, u32[]{:S(2)}, u32[]{:S(2)}) collective-permute-start(f32[17,16,128]{2,1,0:T(8,128)S(1)} %get-tuple-element.49.near_ref), channel_id=1, source_target_pairs={{0,4},{4,0},{8,12},{12,8},{16,20},{20,16},{24,28},{28,24},{1,5},{5... | collective-permute-start | bytes 417800 | tf_op jit(solution)/shard_map/ppermute | solution.py:545
  5.2 8.9 %collective-permute-start.2 = (f32[17,16,128]{2,1,0:T(8,128)S(1)}, f32[17,16,128]{2,1,0:T(8,128)S(1)}, u32[]{:S(2)}, u32[]{:S(2)}) collective-permute-start(f32[17,16,128]{2,1,0:T(8,128)S(1)} %get-tuple-element.46.far_ref), channel_id=1, source_target_pairs={{0,28},{4,8},{8,4},{12,16},{16,12},{20,24},{24,20},{28,0},{1,29},{... | collective-permute-start | bytes 417800 | tf_op jit(solution)/shard_map/ppermute | solution.py:545
  9.2 3.5 %collective-permute-start = (f32[32,128]{1,0:T(8,128)S(1)}, f32[32,128]{1,0:T(8,128)S(1)}, u32[]{:S(2)}, u32[]{:S(2)}) collective-permute-start(f32[32,128]{1,0:T(8,128)S(1)} %get-tuple-element.51), channel_id=1, source_target_pairs={{0,1},{1,0},{2,3},{3,2},{4,5},{5,4},{6,7},{7,6},{8,9},{9,8},{10,11... | collective-permute-start | bytes 49160 | tf_op jit(solution)/shard_map/ppermute | solution.py:545
  9.3 3.5 %collective-permute-start.1 = (f32[32,128]{1,0:T(8,128)S(1)}, f32[32,128]{1,0:T(8,128)S(1)}, u32[]{:S(2)}, u32[]{:S(2)}) collective-permute-start(f32[32,128]{1,0:T(8,128)S(1)} %get-tuple-element.52), channel_id=1, source_target_pairs={{0,3},{1,2},{2,1},{3,0},{4,7},{5,6},{6,5},{7,4},{8,11},{9,10},{10,... | collective-permute-start | bytes 49160 | tf_op jit(solution)/shard_map/ppermute | solution.py:545
  14.6 4.0 %collective-permute-start.4 = (f32[8,256]{1,0:T(8,128)S(1)}, f32[8,256]{1,0:T(8,128)S(1)}, u32[]{:S(2)}, u32[]{:S(2)}) collective-permute-start(f32[8,256]{1,0:T(8,128)S(1)} %get-tuple-element.58.message_ref), channel_id=1, source_target_pairs={{0,4},{4,0},{8,12},{12,8},{16,20},{20,16},{24,28},{28,24},{1,5},{5... | collective-permute-start | bytes 24584 | tf_op jit(solution)/shard_map/ppermute | solution.py:545
  14.7 6.4 %collective-permute-start.5 = (f32[8,256]{1,0:T(8,128)S(1)}, f32[8,256]{1,0:T(8,128)S(1)}, u32[]{:S(2)}, u32[]{:S(2)}) collective-permute-start(f32[8,256]{1,0:T(8,128)S(1)} %get-tuple-element.58.message_ref), channel_id=1, source_target_pairs={{0,28},{4,8},{8,4},{12,16},{16,12},{20,24},{24,20},{28,0},{1,29},{... | collective-permute-start | bytes 24584 | tf_op jit(solution)/shard_map/ppermute | solution.py:545
  21.7 8.2 %collective-permute-start.9 = (f32[16,16,128]{2,1,0:T(8,128)S(1)}, f32[16,16,128]{2,1,0:T(8,128)S(1)}, u32[]{:S(2)}, u32[]{:S(2)}) collective-permute-start(f32[16,16,128]{2,1,0:T(8,128)S(1)} %get-tuple-element.66.near_ref), channel_id=1, source_target_pairs={{0,4},{4,0},{8,12},{12,8},{16,20},{20,16},{24,28},{28,24},{1,5},{5... | collective-permute-start | bytes 393224 | tf_op jit(solution)/shard_map/ppermute | solution.py:545
  21.9 8.5 %collective-permute-start.8 = (f32[16,16,128]{2,1,0:T(8,128)S(1)}, f32[16,16,128]{2,1,0:T(8,128)S(1)}, u32[]{:S(2)}, u32[]{:S(2)}) collective-permute-start(f32[16,16,128]{2,1,0:T(8,128)S(1)} %get-tuple-element.63.far_ref), channel_id=1, source_target_pairs={{0,28},{4,8},{8,4},{12,16},{16,12},{20,24},{24,20},{28,0},{1,29},{... | collective-permute-start | bytes 393224 | tf_op jit(solution)/shard_map/ppermute | solution.py:545
  25.8 2.1 %collective-permute-start.6 = (f32[32,128]{1,0:T(8,128)S(1)}, f32[32,128]{1,0:T(8,128)S(1)}, u32[]{:S(2)}, u32[]{:S(2)}) collective-permute-start(f32[32,128]{1,0:T(8,128)S(1)} %get-tuple-element.68), channel_id=1, source_target_pairs={{0,1},{1,0},{2,3},{3,2},{4,5},{5,4},{6,7},{7,6},{8,9},{9,8},{10,11... | collective-permute-start | bytes 49160 | tf_op jit(solution)/shard_map/ppermute | solution.py:545
  25.9 3.2 %collective-permute-start.7 = (f32[32,128]{1,0:T(8,128)S(1)}, f32[32,128]{1,0:T(8,128)S(1)}, u32[]{:S(2)}, u32[]{:S(2)}) collective-permute-start(f32[32,128]{1,0:T(8,128)S(1)} %get-tuple-element.69), channel_id=1, source_target_pairs={{0,3},{1,2},{2,1},{3,0},{4,7},{5,6},{6,5},{7,4},{8,11},{9,10},{10,... | collective-permute-start | bytes 49160 | tf_op jit(solution)/shard_map/ppermute | solution.py:545
  30.9 3.7 %collective-permute-start.10 = (f32[8,256]{1,0:T(8,128)S(1)}, f32[8,256]{1,0:T(8,128)S(1)}, u32[]{:S(2)}, u32[]{:S(2)}) collective-permute-start(f32[8,256]{1,0:T(8,128)S(1)} %get-tuple-element.73.message_ref), channel_id=1, source_target_pairs={{0,4},{4,0},{8,12},{12,8},{16,20},{20,16},{24,28},{28,24},{1,5},{5... | collective-permute-start | bytes 24584 | tf_op jit(solution)/shard_map/ppermute | solution.py:545
  31.0 6.4 %collective-permute-start.11 = (f32[8,256]{1,0:T(8,128)S(1)}, f32[8,256]{1,0:T(8,128)S(1)}, u32[]{:S(2)}, u32[]{:S(2)}) collective-permute-start(f32[8,256]{1,0:T(8,128)S(1)} %get-tuple-element.73.message_ref), channel_id=1, source_target_pairs={{0,28},{4,8},{8,4},{12,16},{16,12},{20,24},{24,20},{28,0},{1,29},{... | collective-permute-start | bytes 24584 | tf_op jit(solution)/shard_map/ppermute | solution.py:545
  38.0 7.4 %collective-permute-start.15 = (f32[16,16,128]{2,1,0:T(8,128)S(1)}, f32[16,16,128]{2,1,0:T(8,128)S(1)}, u32[]{:S(2)}, u32[]{:S(2)}) collective-permute-start(f32[16,16,128]{2,1,0:T(8,128)S(1)} %get-tuple-element.79.near_ref), channel_id=1, source_target_pairs={{0,4},{4,0},{8,12},{12,8},{16,20},{20,16},{24,28},{28,24},{1,5},{5... | collective-permute-start | bytes 393224 | tf_op jit(solution)/shard_map/ppermute | solution.py:545
  38.2 7.7 %collective-permute-start.14 = (f32[16,16,128]{2,1,0:T(8,128)S(1)}, f32[16,16,128]{2,1,0:T(8,128)S(1)}, u32[]{:S(2)}, u32[]{:S(2)}) collective-permute-start(f32[16,16,128]{2,1,0:T(8,128)S(1)} %get-tuple-element.76.far_ref), channel_id=1, source_target_pairs={{0,28},{4,8},{8,4},{12,16},{16,12},{20,24},{24,20},{28,0},{1,29},{... | collective-permute-start | bytes 393224 | tf_op jit(solution)/shard_map/ppermute | solution.py:545
  41.3 2.1 %collective-permute-start.12 = (f32[32,128]{1,0:T(8,128)S(1)}, f32[32,128]{1,0:T(8,128)S(1)}, u32[]{:S(2)}, u32[]{:S(2)}) collective-permute-start(f32[32,128]{1,0:T(8,128)S(1)} %get-tuple-element.81), channel_id=1, source_target_pairs={{0,1},{1,0},{2,3},{3,2},{4,5},{5,4},{6,7},{7,6},{8,9},{9,8},{10,11... | collective-permute-start | bytes 49160 | tf_op jit(solution)/shard_map/ppermute | solution.py:545
  41.4 3.2 %collective-permute-start.13 = (f32[32,128]{1,0:T(8,128)S(1)}, f32[32,128]{1,0:T(8,128)S(1)}, u32[]{:S(2)}, u32[]{:S(2)}) collective-permute-start(f32[32,128]{1,0:T(8,128)S(1)} %get-tuple-element.82), channel_id=1, source_target_pairs={{0,3},{1,2},{2,1},{3,0},{4,7},{5,6},{6,5},{7,4},{8,11},{9,10},{10,... | collective-permute-start | bytes 49160 | tf_op jit(solution)/shard_map/ppermute | solution.py:545
  46.4 3.7 %collective-permute-start.16 = (f32[8,256]{1,0:T(8,128)S(1)}, f32[8,256]{1,0:T(8,128)S(1)}, u32[]{:S(2)}, u32[]{:S(2)}) collective-permute-start(f32[8,256]{1,0:T(8,128)S(1)} %get-tuple-element.86.message_ref), channel_id=1, source_target_pairs={{0,4},{4,0},{8,12},{12,8},{16,20},{20,16},{24,28},{28,24},{1,5},{5... | collective-permute-start | bytes 24584 | tf_op jit(solution)/shard_map/ppermute | solution.py:545
  47.1 6.3 %collective-permute-start.17 = (f32[8,256]{1,0:T(8,128)S(1)}, f32[8,256]{1,0:T(8,128)S(1)}, u32[]{:S(2)}, u32[]{:S(2)}) collective-permute-start(f32[8,256]{1,0:T(8,128)S(1)} %get-tuple-element.86.message_ref), channel_id=1, source_target_pairs={{0,28},{4,8},{8,4},{12,16},{16,12},{20,24},{24,20},{28,0},{1,29},{... | collective-permute-start | bytes 24584 | tf_op jit(solution)/shard_map/ppermute | solution.py:545

commit v5 on v4

--- a/solution.py
+++ b/solution.py
@@ -172,22 +172,19 @@
     values = jnp.concatenate([slot_ref[place(layer, cz)] for layer in range(cz)], axis=0)
     values = values.astype(jnp.float32).astype(jnp.bfloat16)
     slot_rows_ref[...] = jnp.dot(values, chooser[:, :xb], preferred_element_type=jnp.float32)
-    block_ref[...] = slot_rows_ref[pl.ds(0, cz * yb, stride=ROWS), :]
-
-
-def onehot_kernel(block_ref, onehot_ref, chooser_ref):
+    block_ref[...] = slot_rows_ref[pl.ds(0, cz * yb, stride=ROWS), :].astype(jnp.int32)
+
+
+def chooser_kernel(block_ref, chooser_ref):
     rows, xb = block_ref.shape
-    slots = onehot_ref.shape[1]
+    slots = chooser_ref.shape[2]
     one, zero = jnp.ones((), jnp.bfloat16), jnp.zeros((), jnp.bfloat16)
-    down = lax.broadcasted_iota(jnp.int32, (slots, xb), 0).astype(jnp.float32).astype(jnp.bfloat16)
     across = lax.broadcasted_iota(jnp.int32, (xb, xb), 1)
     across = [(across + half * xb).astype(jnp.float32).astype(jnp.bfloat16) for half in range(slots // xb)]
-    turned = jnp.transpose(jnp.concatenate([block_ref[...], jnp.zeros((xb - rows, xb), jnp.float32)], axis=0))
+    blocks = block_ref[...].astype(jnp.float32)
+    turned = jnp.transpose(jnp.concatenate([blocks, jnp.zeros((xb - rows, xb), jnp.float32)], axis=0))
     for r in range(rows):
         at = (r % 2) * xb
-        line = jnp.broadcast_to(block_ref[r : r + 1, :], (16, xb)).astype(jnp.bfloat16)
-        line = jnp.concatenate([line] * (slots // 16), axis=0)
-        onehot_ref[r // 2, :, at : at + xb] = jnp.where(down == line, one, zero)
         line = jnp.broadcast_to(turned[:, r : r + 1], (xb, xb)).astype(jnp.bfloat16)
         for half in range(slots // xb):
             chooser_ref[r // 2, at : at + xb, half * xb : (half + 1) * xb] = jnp.where(across[half] == line, one, zero)
@@ -419,26 +416,22 @@
     parts = jnp.dot(others, match_ref[...], preferred_element_type=jnp.float32)
     totals = message_ref[...] + parts[0:8] + parts[8:16] + parts[16:24]
     inverse = 1.0 / totals[4:5, :]
-    for part, piece in enumerate(split3(TRANSLATE * totals[0:4, :] * inverse)):
-        velocity_ref[4 * part : 4 * part + 4, :] = piece.astype(jnp.float32)
-    velocity_ref[12:16, :] = jnp.zeros((4, velocity_ref.shape[1]), jnp.float32)
-
-
-def block_motion(velocity_ref, onehot_ref, motion_ref, first_pair):
-    rows = motion_ref.shape[0] // 8
-    xb = motion_ref.shape[1]
-    velocity = velocity_ref[...].astype(jnp.bfloat16)
-    for i in range(rows // 2):
-        moved = jnp.dot(velocity, onehot_ref[first_pair + i], preferred_element_type=jnp.float32)
-        moved = moved[0:8] + moved[8:16]
-        for h in range(2):
-            motion_ref[pl.ds(2 * i + h, 8, stride=rows), :] = moved[:, h * xb : (h + 1) * xb]
-
-
-def layer_motion(motion_ref, at, yb):
-    rows = motion_ref.shape[0] // 8
-    parts = [motion_ref[k * rows + at * yb : k * rows + (at + 1) * yb, :] for k in range(8)]
-    return [parts[k] + parts[4 + k] for k in range(4)]
+    velocity_ref[...] = TRANSLATE * totals * inverse
+
+
+def layer_motion(velocity_ref, block_ref, layer, yb):
+    xb = block_ref.shape[1]
+    slot = block_ref[layer * yb : (layer + 1) * yb, :]
+    within = slot & (xb - 1)
+    motion = []
+    for k in range(4):
+        value = None
+        for part in range(velocity_ref.shape[1] // xb):
+            table = jnp.broadcast_to(velocity_ref[k : k + 1, part * xb : (part + 1) * xb], slot.shape)
+            found = jnp.take_along_axis(table, within, axis=1, mode="promise_in_bounds")
+            value = found if value is None else jnp.where(slot >= part * xb, found, value)
+        motion.append(value)
+    return motion
 
 
 def advanced(local_ref, motion, at, p, j):
@@ -450,28 +443,24 @@
 
 
 def advance_outer_kernel(
-    message_ref, near_message_ref, far_message_ref, match_ref, onehot_ref, local_ref,
+    message_ref, near_message_ref, far_message_ref, match_ref, block_ref, local_ref,
     velocity_ref, near_ref, far_ref,
-    motion_ref,
 ):
     slot_motion(message_ref, near_message_ref, far_message_ref, match_ref, velocity_ref)
-    block_motion(velocity_ref, onehot_ref, motion_ref, 0)
     for layer, ref in enumerate((near_ref, far_ref)):
-        motion = layer_motion(motion_ref, layer, local_ref.shape[4])
+        motion = layer_motion(velocity_ref, block_ref, layer, local_ref.shape[4])
         for p in range(ROWS):
             for j in range(COLS):
                 ref[tile(0, p, j)], ref[tile(1, p, j)] = advanced(local_ref, motion, layer, p, j)
 
 
 def advance_inner_kernel(
-    velocity_ref, onehot_ref, local_ref, near_ref, far_ref,
+    velocity_ref, block_ref, local_ref, near_ref, far_ref,
     inner_ref, y_near_ref, y_far_ref,
-    motion_ref,
 ):
     layers, yb = local_ref.shape[1], local_ref.shape[4]
-    block_motion(velocity_ref, onehot_ref, motion_ref, yb)
     for at in range(layers):
-        motion = layer_motion(motion_ref, at, yb)
+        motion = layer_motion(velocity_ref, block_ref, at + 2, yb)
         for p in range(ROWS):
             for j in range(COLS):
                 inner_ref[0, at, p, j], inner_ref[1, at, p, j] = advanced(local_ref, motion, at, p, j)
@@ -479,9 +468,9 @@
 
 
 def finish_kernel(
-    message_ref, near_message_ref, far_message_ref, match_ref, onehot_ref, outer_local_ref, inner_local_ref,
+    message_ref, near_message_ref, far_message_ref, match_ref, block_ref, outer_local_ref, inner_local_ref,
     e_hbm, q_hbm,
-    velocity_ref, motion_ref, rows_ref, out_ref, sems,
+    velocity_ref, rows_ref, out_ref, sems,
 ):
     yb, xb = outer_local_ref.shape[4:]
     _, cz, cy, nx = out_ref.shape
@@ -490,9 +479,8 @@
     copies = []
     for part, local_ref in enumerate((outer_local_ref, inner_local_ref)):
         layers = local_ref.shape[1]
-        block_motion(velocity_ref, onehot_ref, motion_ref, part * yb)
         for at in range(layers):
-            motion = layer_motion(motion_ref, at, yb)
+            motion = layer_motion(velocity_ref, block_ref, 2 * part + at, yb)
             for p in range(ROWS):
                 to = pl.ds(at * cy + p, yb, stride=ROWS)
                 for j in range(COLS):
@@ -563,8 +551,6 @@
     y_out = [((2 * cz * COLS, xb), f32)] * 2
     acc_out = ((16, slots), f32)
     mixed_out = ((2,) + block, f32)
-    outer_motion = pltpu.VMEM((8 * 2 * yb, xb), f32)
-    inner_motion = pltpu.VMEM((8 * (cz - 2) * yb, xb), f32)
     layer_scratch = [pltpu.VMEM((4,) + block, f32), pltpu.VMEM((16 * yb, xb), f32)]
     dma = pltpu.SemaphoreType.DMA
     prepare_outer = call(
@@ -577,10 +563,10 @@
         hbm_in=4,
     )
     prepare_inner = call(
-        prepare_inner_kernel, "prepare_inner", [inner_out] + y_out + [((rows, xb), f32)],
+        prepare_inner_kernel, "prepare_inner", [inner_out] + y_out + [((rows, xb), jnp.int32)],
         [pltpu.VMEM((COLS, 2 * (cz - 2) * cy, xb), f32), pltpu.VMEM((cz * cy, xb), f32)],
     )
-    onehots = call(onehot_kernel, "onehots", [((rows // 2, slots, 2 * xb), bf16), ((rows // 2, 2 * xb, slots), bf16)])
+    choosers = call(chooser_kernel, "choosers", [((rows // 2, 2 * xb, slots), bf16)])
     trigs = call(trig_kernel, "trigs", [((4, cz) + block, f32)])
     inner_terms = call(
         inner_kernel, "inner_terms", [((2, 6, cz * COLS, xb), f32), ((8, cz - 2) + block, f32), acc_out],
@@ -593,13 +579,13 @@
     outer_locals = call(outer_local_kernel, "outer_locals", [((8, 2) + block, f32)])
     matches = call(match_kernel, "matches", [((2 * slots, slots), bf16)])
     advance_outer = call(
-        advance_outer_kernel, "advance_outer", [((16, slots), f32), side_out, side_out], [outer_motion]
-    )
-    advance_inner = call(advance_inner_kernel, "advance_inner", [inner_out] + y_out, [inner_motion])
+        advance_outer_kernel, "advance_outer", [((8, slots), f32), side_out, side_out]
+    )
+    advance_inner = call(advance_inner_kernel, "advance_inner", [inner_out] + y_out)
     finish = call(
         finish_kernel, "finish", [((cz, cy, nx), f32)] * 2,
         [
-            pltpu.VMEM((16, slots), f32), outer_motion, pltpu.VMEM((2, COLS, 2 * cy, xb), f32), pltpu.VMEM((2, cz, cy, nx), f32), dma((2, cz)),
+            pltpu.VMEM((8, slots), f32), pltpu.VMEM((2, COLS, 2 * cy, xb), f32), pltpu.VMEM((2, cz, cy, nx), f32), dma((2, cz)),
         ],
         hbm_out=True,
     )
@@ -613,10 +599,10 @@
         if step == 0:
             inner, y_near, y_far, blocks = prepare_inner(raw, raw_slots, near, far)
         else:
-            inner, y_near, y_far = advance_inner(velocity, onehot, inner_local, near, far)
+            inner, y_near, y_far = advance_inner(velocity, blocks, inner_local, near, far)
         y_near, y_far = both(y_near, y_far, "gy")
         if step == 0:
-            onehot, chooser = onehots(blocks)
+            (chooser,) = choosers(blocks)
         (trig,) = trigs(near, far, inner)
         rim, inner_local, acc = inner_terms(near, far, inner, trig, y_near, y_far, chooser)
         near_mixed, acc = near_terms(near, inner, trig, rim, near_halo, chooser, acc)
@@ -626,8 +612,8 @@
             (match,) = matches(ids, near_halo, far_halo)
         (outer_local,) = outer_locals(near, far, inner, trig, rim, near_halo, far_halo, near_mixed, far_mixed)
         if step < STEPS - 1:
-            velocity, near, far = advance_outer(message, near_message, far_message, match, onehot, outer_local)
-    return tuple(finish(message, near_message, far_message, match, onehot, outer_local, inner_local))
+            velocity, near, far = advance_outer(message, near_message, far_message, match, blocks, outer_local)
+    return tuple(finish(message, near_message, far_message, match, blocks, outer_local, inner_local))
 
 
 def solution(mesh):

time: 55.9 us -> 54.5 us (0.975)
  Pallas kernels: 15.1 us -> 12.8 us
  starting transfers between devices: 27.3 us -> 28.5 us
    pallas_call x24, Pallas kernels: 15.1 us -> 12.8 us  [run(): pl.pallas_call(kernel, name=name, in_specs=[HBM] * hbm_in + [VMEM] * (len...]
    ppermute x18, starting transfers between devices: 27.3 us -> 28.5 us  [swap(): return lax.ppermute(array, axis, pairs)]
  transfers between devices with their start and end apart: 18 -> 18, of which waited for: 7 -> 8; matrix products, arithmetic and copies ran while one was open for 0% -> 0% of each run, Pallas kernels for 15% -> 14%
where the time goes in v5:
time: 54.5 us; the launch traced here: 54.4 us
  starting transfers between devices  28.5 us (52%)
  Pallas kernels  12.8 us (23%)
  waiting for transfers between devices  12.3 us (23%)
  between operations  0.81 us (1%)
    ppermute x18, starting transfers between devices, swap(): return lax.ppermute(array, axis, pairs)  28.5 us
    pallas_call x24, Pallas kernels, run(): pl.pallas_call(kernel, name=name, in_specs=[HBM] * hbm_in + [VMEM] * (len...  12.8 us
    ppermute x18, waiting for transfers between devices, swap(): return lax.ppermute(array, axis, pairs)  12.3 us
  transfers between devices with their start and end apart: 18, of which 8 were waited for; matrix products, arithmetic and copies ran while one was open for 0% of the time, Pallas kernels for 14%

profile of v5, /device:TPU:0, one launch (start us, length us, event | category | flops | bytes accessed | tf_op | source)
XLA Modules:
  0.0 54.4 jit_solution(13029667500514051787)
XLA Ops:
  0.6 1.6 %prepare_outer.1 = (f32[17,16,128]{2,1,0:T(8,128)S(1)}, f32[17,16,128]{2,1,0:T(8,128)S(1)}, f32[2,2,32,512]{3,2,1,0:T(8,128)S(1)}, s32[4,32,512]{2,1,0:T(8,128)S(1)}, s32[1,256]{1,0:T(1,128)S(1)}) custom-call(f32[4,32,512]{2,1,0:T(8,128)} %e_hbm.1, f32[4,32,512]{2,1,0:T(8,128)} %q_hbm.1, s32[4,32,512]{2,1,0:T(8,128)} %slot_hbm.1, s32[1,256]{1,0:T(1,128)} %bitcast.1), custom_call_target="tpu_custom_call" | custom-call | flops 4194304 | bytes 1048576 | tf_op jit(solution)/shard_map/prepare_outer/pallas_call | solution.py:516
  2.2 3.0 %collective-permute-start.3 = (f32[17,16,128]{2,1,0:T(8,128)S(1)}, f32[17,16,128]{2,1,0:T(8,128)S(1)}, u32[]{:S(2)}, u32[]{:S(2)}) collective-permute-start(f32[17,16,128]{2,1,0:T(8,128)S(1)} %get-tuple-element.47.near_ref), channel_id=1, source_target_pairs={{0,4},{4,0},{8,12},{12,8},{16,20},{20,16},{24,28},{28,24},{1,5},{5... | collective-permute-start | bytes 417800 | tf_op jit(solution)/shard_map/ppermute | solution.py:533
  5.2 3.5 %collective-permute-start.2 = (f32[17,16,128]{2,1,0:T(8,128)S(1)}, f32[17,16,128]{2,1,0:T(8,128)S(1)}, u32[]{:S(2)}, u32[]{:S(2)}) collective-permute-start(f32[17,16,128]{2,1,0:T(8,128)S(1)} %get-tuple-element.44.far_ref), channel_id=1, source_target_pairs={{0,28},{4,8},{8,4},{12,16},{16,12},{20,24},{24,20},{28,0},{1,29},{... | collective-permute-start | bytes 417800 | tf_op jit(solution)/shard_map/ppermute | solution.py:533
  8.8 0.4 prepare_inner.1
  9.2 0.1 collective-permute-start
  9.3 1.6 %collective-permute-start.1 = (f32[32,128]{1,0:T(8,128)S(1)}, f32[32,128]{1,0:T(8,128)S(1)}, u32[]{:S(2)}, u32[]{:S(2)}) collective-permute-start(f32[32,128]{1,0:T(8,128)S(1)} %get-tuple-element.50), channel_id=1, source_target_pairs={{0,3},{1,2},{2,1},{3,0},{4,7},{5,6},{6,5},{7,4},{8,11},{9,10},{10,... | collective-permute-start | bytes 49160 | tf_op jit(solution)/shard_map/ppermute | solution.py:533
  10.9 0.4 trigs.3.trig_ref
  11.3 0.9 %choosers.1.chooser_ref = bf16[32,256,256]{2,1,0:T(8,128)(2,1)S(1)} custom-call(s32[64,128]{1,0:T(8,128)S(1)} %get-tuple-element.51.block_ref), custom_call_target="tpu_custom_call" | custom-call | flops 4194304 | bytes 1048576 | tf_op jit(solution)/shard_map/choosers/pallas_call | solution.py:516
  12.2 0.0 collective-permute-done.y_near_ref
  12.2 0.3 collective-permute-done.1.y_far_ref
  12.5 0.8 %inner_terms.3 = (f32[2,6,16,128]{3,2,1,0:T(8,128)S(1)}, f32[8,2,2,4,16,128]{5,4,3,2,1,0:T(8,128)S(1)}, f32[16,256]{1,0:T(8,128)S(1)}) custom-call(f32[17,16,128]{2,1,0:T(8,128)S(1)} %get-tuple-element.47.near_ref, f32[17,16,128]{2,1,0:T(8,128)S(1)} %get-tuple-element.44.far_ref, f32[2,2,2,4,16,128]{5,4,3,2,1,0:T(8,128)S(1)} %get-tuple-element.48.inner_ref, ...), custom_call_target="tpu_custom_call" | custom-call | flops 4194304 | bytes 1048576 | tf_op jit(solution)/shard_map/inner_terms/pallas_call | solution.py:516
  13.3 0.0 collective-permute-done.3.halo_ref.near_halo_ref
  13.3 0.5 near_terms.3
  13.8 0.0 collective-permute-done.2.halo_ref.far_halo_ref
  13.8 0.5 far_terms.3
  14.3 0.3 collective-permute-start.4
  14.7 3.5 %collective-permute-start.5 = (f32[8,256]{1,0:T(8,128)S(1)}, f32[8,256]{1,0:T(8,128)S(1)}, u32[]{:S(2)}, u32[]{:S(2)}) collective-permute-start(f32[8,256]{1,0:T(8,128)S(1)} %get-tuple-element.55.message_ref), channel_id=1, source_target_pairs={{0,28},{4,8},{8,4},{12,16},{16,12},{20,24},{24,20},{28,0},{1,29},{... | collective-permute-start | bytes 24584 | tf_op jit(solution)/shard_map/ppermute | solution.py:533
  18.2 0.1 matches.1.match_ref
  18.3 0.2 outer_locals.3.local_ref
  18.5 0.0 collective-permute-done.4.near_message_ref
  18.5 2.5 %collective-permute-done.5.far_message_ref = f32[8,256]{1,0:T(8,128)S(1)} collective-permute-done((f32[8,256]{1,0:T(8,128)S(1)}, f32[8,256]{1,0:T(8,128)S(1)}, u32[]{:S(2)}, u32[]{:S(2)}) %collective-permute-start.5) | collective-permute-done | bytes 8224 | tf_op jit(solution)/shard_map/ppermute | solution.py:533
  21.0 0.3 advance_outer.2
  21.3 0.1 collective-permute-start.9
  21.4 3.6 %collective-permute-start.8 = (f32[16,16,128]{2,1,0:T(8,128)S(1)}, f32[16,16,128]{2,1,0:T(8,128)S(1)}, u32[]{:S(2)}, u32[]{:S(2)}) collective-permute-start(f32[16,16,128]{2,1,0:T(8,128)S(1)} %get-tuple-element.59.far_ref), channel_id=1, source_target_pairs={{0,28},{4,8},{8,4},{12,16},{16,12},{20,24},{24,20},{28,0},{1,29},{... | collective-permute-start | bytes 393224 | tf_op jit(solution)/shard_map/ppermute | solution.py:533
  25.0 0.2 advance_inner.2
  25.2 0.1 collective-permute-start.6
  25.3 1.6 %collective-permute-start.7 = (f32[32,128]{1,0:T(8,128)S(1)}, f32[32,128]{1,0:T(8,128)S(1)}, u32[]{:S(2)}, u32[]{:S(2)}) collective-permute-start(f32[32,128]{1,0:T(8,128)S(1)} %get-tuple-element.65), channel_id=1, source_target_pairs={{0,3},{1,2},{2,1},{3,0},{4,7},{5,6},{6,5},{7,4},{8,11},{9,10},{10,... | collective-permute-start | bytes 49160 | tf_op jit(solution)/shard_map/ppermute | solution.py:533
  26.9 0.4 trigs.4.trig_ref
  27.3 0.0 collective-permute-done.6.y_near_ref
  27.3 1.2 %collective-permute-done.7.y_far_ref = f32[32,128]{1,0:T(8,128)S(1)} collective-permute-done((f32[32,128]{1,0:T(8,128)S(1)}, f32[32,128]{1,0:T(8,128)S(1)}, u32[]{:S(2)}, u32[]{:S(2)}) %collective-permute-start.7) | collective-permute-done | bytes 16416 | tf_op jit(solution)/shard_map/ppermute | solution.py:533
  28.5 0.8 %inner_terms.4 = (f32[2,6,16,128]{3,2,1,0:T(8,128)S(1)}, f32[8,2,2,4,16,128]{5,4,3,2,1,0:T(8,128)S(1)}, f32[16,256]{1,0:T(8,128)S(1)}) custom-call(f32[16,16,128]{2,1,0:T(8,128)S(1)} %get-tuple-element.62.near_ref, f32[16,16,128]{2,1,0:T(8,128)S(1)} %get-tuple-element.59.far_ref, f32[2,2,2,4,16,128]{5,4,3,2,1,0:T(8,128)S(1)} %get-tuple-element.63.inner_ref, ...), custom_call_target="tpu_custom_call" | custom-call | flops 4194304 | bytes 1048576 | tf_op jit(solution)/shard_map/inner_terms/pallas_call | solution.py:516
  29.3 0.0 collective-permute-done.9.halo_ref.near_halo_ref
  29.3 0.5 near_terms.4
  29.8 0.0 collective-permute-done.8.halo_ref.far_halo_ref
  29.8 0.5 far_terms.4
  30.3 0.1 collective-permute-start.10
  30.4 3.0 %collective-permute-start.11 = (f32[8,256]{1,0:T(8,128)S(1)}, f32[8,256]{1,0:T(8,128)S(1)}, u32[]{:S(2)}, u32[]{:S(2)}) collective-permute-start(f32[8,256]{1,0:T(8,128)S(1)} %get-tuple-element.69.message_ref), channel_id=1, source_target_pairs={{0,28},{4,8},{8,4},{12,16},{16,12},{20,24},{24,20},{28,0},{1,29},{... | collective-permute-start | bytes 24584 | tf_op jit(solution)/shard_map/ppermute | solution.py:533
  33.4 0.2 outer_locals.4.local_ref
  33.6 0.4 collective-permute-done.10.near_message_ref
  34.0 2.8 %collective-permute-done.11.far_message_ref = f32[8,256]{1,0:T(8,128)S(1)} collective-permute-done((f32[8,256]{1,0:T(8,128)S(1)}, f32[8,256]{1,0:T(8,128)S(1)}, u32[]{:S(2)}, u32[]{:S(2)}) %collective-permute-start.11) | collective-permute-done | bytes 8224 | tf_op jit(solution)/shard_map/ppermute | solution.py:533
  36.8 0.3 advance_outer.3
  37.1 0.2 collective-permute-start.15
  37.4 2.9 %collective-permute-start.14 = (f32[16,16,128]{2,1,0:T(8,128)S(1)}, f32[16,16,128]{2,1,0:T(8,128)S(1)}, u32[]{:S(2)}, u32[]{:S(2)}) collective-permute-start(f32[16,16,128]{2,1,0:T(8,128)S(1)} %get-tuple-element.72.far_ref), channel_id=1, source_target_pairs={{0,28},{4,8},{8,4},{12,16},{16,12},{20,24},{24,20},{28,0},{1,29},{... | collective-permute-start | bytes 393224 | tf_op jit(solution)/shard_map/ppermute | solution.py:533
  40.2 0.2 advance_inner.3
  40.4 0.1 collective-permute-start.12
  40.5 1.6 %collective-permute-start.13 = (f32[32,128]{1,0:T(8,128)S(1)}, f32[32,128]{1,0:T(8,128)S(1)}, u32[]{:S(2)}, u32[]{:S(2)}) collective-permute-start(f32[32,128]{1,0:T(8,128)S(1)} %get-tuple-element.78), channel_id=1, source_target_pairs={{0,3},{1,2},{2,1},{3,0},{4,7},{5,6},{6,5},{7,4},{8,11},{9,10},{10,... | collective-permute-start | bytes 49160 | tf_op jit(solution)/shard_map/ppermute | solution.py:533
  42.1 0.4 trigs.5.trig_ref
  42.5 0.0 collective-permute-done.12.y_near_ref
  42.5 1.2 %collective-permute-done.13.y_far_ref = f32[32,128]{1,0:T(8,128)S(1)} collective-permute-done((f32[32,128]{1,0:T(8,128)S(1)}, f32[32,128]{1,0:T(8,128)S(1)}, u32[]{:S(2)}, u32[]{:S(2)}) %collective-permute-start.13) | collective-permute-done | bytes 16416 | tf_op jit(solution)/shard_map/ppermute | solution.py:533
  43.7 0.8 %inner_terms.5 = (f32[2,6,16,128]{3,2,1,0:T(8,128)S(1)}, f32[8,2,2,4,16,128]{5,4,3,2,1,0:T(8,128)S(1)}, f32[16,256]{1,0:T(8,128)S(1)}) custom-call(f32[16,16,128]{2,1,0:T(8,128)S(1)} %get-tuple-element.75.near_ref, f32[16,16,128]{2,1,0:T(8,128)S(1)} %get-tuple-element.72.far_ref, f32[2,2,2,4,16,128]{5,4,3,2,1,0:T(8,128)S(1)} %get-tuple-element.76.inner_ref, ...), custom_call_target="tpu_custom_call" | custom-call | flops 4194304 | bytes 1048576 | tf_op jit(solution)/shard_map/inner_terms/pallas_call | solution.py:516
  44.5 0.0 collective-permute-done.15.halo_ref.near_halo_ref
  44.5 0.5 near_terms.5
  45.0 0.0 collective-permute-done.14.halo_ref.far_halo_ref
  45.0 0.5 far_terms.5
  45.5 0.8 %collective-permute-start.16 = (f32[8,256]{1,0:T(8,128)S(1)}, f32[8,256]{1,0:T(8,128)S(1)}, u32[]{:S(2)}, u32[]{:S(2)}) collective-permute-start(f32[8,256]{1,0:T(8,128)S(1)} %get-tuple-element.82.message_ref), channel_id=1, source_target_pairs={{0,4},{4,0},{8,12},{12,8},{16,20},{20,16},{24,28},{28,24},{1,5},{5... | collective-permute-start | bytes 24584 | tf_op jit(solution)/shard_map/ppermute | solution.py:533
  46.3 2.3 %collective-permute-start.17 = (f32[8,256]{1,0:T(8,128)S(1)}, f32[8,256]{1,0:T(8,128)S(1)}, u32[]{:S(2)}, u32[]{:S(2)}) collective-permute-start(f32[8,256]{1,0:T(8,128)S(1)} %get-tuple-element.82.message_ref), channel_id=1, source_target_pairs={{0,28},{4,8},{8,4},{12,16},{16,12},{20,24},{24,20},{28,0},{1,29},{... | collective-permute-start | bytes 24584 | tf_op jit(solution)/shard_map/ppermute | solution.py:533
  48.6 0.2 outer_locals.5.outer_local_ref
  48.8 0.4 collective-permute-done.16.near_message_ref
  49.2 3.4 %collective-permute-done.17.far_message_ref = f32[8,256]{1,0:T(8,128)S(1)} collective-permute-done((f32[8,256]{1,0:T(8,128)S(1)}, f32[8,256]{1,0:T(8,128)S(1)}, u32[]{:S(2)}, u32[]{:S(2)}) %collective-permute-start.17) | collective-permute-done | bytes 8224 | tf_op jit(solution)/shard_map/ppermute | solution.py:533
  52.7 1.7 %finish.1 = (f32[4,32,512]{2,1,0:T(8,128)}, f32[4,32,512]{2,1,0:T(8,128)}) custom-call(f32[8,256]{1,0:T(8,128)S(1)} %get-tuple-element.82.message_ref, f32[8,256]{1,0:T(8,128)S(1)} %collective-permute-done.16.near_message_ref, f32[8,256]{1,0:T(8,128)S(1)} %collective-permute-done.17.far_message_ref, bf16[512,256]{1,0:T(8,128)(2,1)S(1)} %matches.1.match_ref, ...), custom_call_target="tpu_custom_call" | custom-call | flops 4194304 | bytes 1048576 | tf_op jit(solution)/shard_map/finish/pallas_call | solution.py:516
Async XLA Ops:
  2.2 11.1 %collective-permute-start.3 = (f32[17,16,128]{2,1,0:T(8,128)S(1)}, f32[17,16,128]{2,1,0:T(8,128)S(1)}, u32[]{:S(2)}, u32[]{:S(2)}) collective-permute-start(f32[17,16,128]{2,1,0:T(8,128)S(1)} %get-tuple-element.47.near_ref), channel_id=1, source_target_pairs={{0,4},{4,0},{8,12},{12,8},{16,20},{20,16},{24,28},{28,24},{1,5},{5... | collective-permute-start | bytes 417800 | tf_op jit(solution)/shard_map/ppermute | solution.py:533
  5.2 8.6 %collective-permute-start.2 = (f32[17,16,128]{2,1,0:T(8,128)S(1)}, f32[17,16,128]{2,1,0:T(8,128)S(1)}, u32[]{:S(2)}, u32[]{:S(2)}) collective-permute-start(f32[17,16,128]{2,1,0:T(8,128)S(1)} %get-tuple-element.44.far_ref), channel_id=1, source_target_pairs={{0,28},{4,8},{8,4},{12,16},{16,12},{20,24},{24,20},{28,0},{1,29},{... | collective-permute-start | bytes 417800 | tf_op jit(solution)/shard_map/ppermute | solution.py:533
  9.2 3.0 %collective-permute-start = (f32[32,128]{1,0:T(8,128)S(1)}, f32[32,128]{1,0:T(8,128)S(1)}, u32[]{:S(2)}, u32[]{:S(2)}) collective-permute-start(f32[32,128]{1,0:T(8,128)S(1)} %get-tuple-element.49), channel_id=1, source_target_pairs={{0,1},{1,0},{2,3},{3,2},{4,5},{5,4},{6,7},{7,6},{8,9},{9,8},{10,11... | collective-permute-start | bytes 49160 | tf_op jit(solution)/shard_map/ppermute | solution.py:533
  9.3 3.2 %collective-permute-start.1 = (f32[32,128]{1,0:T(8,128)S(1)}, f32[32,128]{1,0:T(8,128)S(1)}, u32[]{:S(2)}, u32[]{:S(2)}) collective-permute-start(f32[32,128]{1,0:T(8,128)S(1)} %get-tuple-element.50), channel_id=1, source_target_pairs={{0,3},{1,2},{2,1},{3,0},{4,7},{5,6},{6,5},{7,4},{8,11},{9,10},{10,... | collective-permute-start | bytes 49160 | tf_op jit(solution)/shard_map/ppermute | solution.py:533
  14.3 4.2 %collective-permute-start.4 = (f32[8,256]{1,0:T(8,128)S(1)}, f32[8,256]{1,0:T(8,128)S(1)}, u32[]{:S(2)}, u32[]{:S(2)}) collective-permute-start(f32[8,256]{1,0:T(8,128)S(1)} %get-tuple-element.55.message_ref), channel_id=1, source_target_pairs={{0,4},{4,0},{8,12},{12,8},{16,20},{20,16},{24,28},{28,24},{1,5},{5... | collective-permute-start | bytes 24584 | tf_op jit(solution)/shard_map/ppermute | solution.py:533
  14.7 6.3 %collective-permute-start.5 = (f32[8,256]{1,0:T(8,128)S(1)}, f32[8,256]{1,0:T(8,128)S(1)}, u32[]{:S(2)}, u32[]{:S(2)}) collective-permute-start(f32[8,256]{1,0:T(8,128)S(1)} %get-tuple-element.55.message_ref), channel_id=1, source_target_pairs={{0,28},{4,8},{8,4},{12,16},{16,12},{20,24},{24,20},{28,0},{1,29},{... | collective-permute-start | bytes 24584 | tf_op jit(solution)/shard_map/ppermute | solution.py:533
  21.3 8.0 %collective-permute-start.9 = (f32[16,16,128]{2,1,0:T(8,128)S(1)}, f32[16,16,128]{2,1,0:T(8,128)S(1)}, u32[]{:S(2)}, u32[]{:S(2)}) collective-permute-start(f32[16,16,128]{2,1,0:T(8,128)S(1)} %get-tuple-element.62.near_ref), channel_id=1, source_target_pairs={{0,4},{4,0},{8,12},{12,8},{16,20},{20,16},{24,28},{28,24},{1,5},{5... | collective-permute-start | bytes 393224 | tf_op jit(solution)/shard_map/ppermute | solution.py:533
  21.4 8.4 %collective-permute-start.8 = (f32[16,16,128]{2,1,0:T(8,128)S(1)}, f32[16,16,128]{2,1,0:T(8,128)S(1)}, u32[]{:S(2)}, u32[]{:S(2)}) collective-permute-start(f32[16,16,128]{2,1,0:T(8,128)S(1)} %get-tuple-element.59.far_ref), channel_id=1, source_target_pairs={{0,28},{4,8},{8,4},{12,16},{16,12},{20,24},{24,20},{28,0},{1,29},{... | collective-permute-start | bytes 393224 | tf_op jit(solution)/shard_map/ppermute | solution.py:533
  25.2 2.1 %collective-permute-start.6 = (f32[32,128]{1,0:T(8,128)S(1)}, f32[32,128]{1,0:T(8,128)S(1)}, u32[]{:S(2)}, u32[]{:S(2)}) collective-permute-start(f32[32,128]{1,0:T(8,128)S(1)} %get-tuple-element.64), channel_id=1, source_target_pairs={{0,1},{1,0},{2,3},{3,2},{4,5},{5,4},{6,7},{7,6},{8,9},{9,8},{10,11... | collective-permute-start | bytes 49160 | tf_op jit(solution)/shard_map/ppermute | solution.py:533
  25.3 3.2 %collective-permute-start.7 = (f32[32,128]{1,0:T(8,128)S(1)}, f32[32,128]{1,0:T(8,128)S(1)}, u32[]{:S(2)}, u32[]{:S(2)}) collective-permute-start(f32[32,128]{1,0:T(8,128)S(1)} %get-tuple-element.65), channel_id=1, source_target_pairs={{0,3},{1,2},{2,1},{3,0},{4,7},{5,6},{6,5},{7,4},{8,11},{9,10},{10,... | collective-permute-start | bytes 49160 | tf_op jit(solution)/shard_map/ppermute | solution.py:533
  30.3 3.7 %collective-permute-start.10 = (f32[8,256]{1,0:T(8,128)S(1)}, f32[8,256]{1,0:T(8,128)S(1)}, u32[]{:S(2)}, u32[]{:S(2)}) collective-permute-start(f32[8,256]{1,0:T(8,128)S(1)} %get-tuple-element.69.message_ref), channel_id=1, source_target_pairs={{0,4},{4,0},{8,12},{12,8},{16,20},{20,16},{24,28},{28,24},{1,5},{5... | collective-permute-start | bytes 24584 | tf_op jit(solution)/shard_map/ppermute | solution.py:533
  30.4 6.4 %collective-permute-start.11 = (f32[8,256]{1,0:T(8,128)S(1)}, f32[8,256]{1,0:T(8,128)S(1)}, u32[]{:S(2)}, u32[]{:S(2)}) collective-permute-start(f32[8,256]{1,0:T(8,128)S(1)} %get-tuple-element.69.message_ref), channel_id=1, source_target_pairs={{0,28},{4,8},{8,4},{12,16},{16,12},{20,24},{24,20},{28,0},{1,29},{... | collective-permute-start | bytes 24584 | tf_op jit(solution)/shard_map/ppermute | solution.py:533
  37.1 7.4 %collective-permute-start.15 = (f32[16,16,128]{2,1,0:T(8,128)S(1)}, f32[16,16,128]{2,1,0:T(8,128)S(1)}, u32[]{:S(2)}, u32[]{:S(2)}) collective-permute-start(f32[16,16,128]{2,1,0:T(8,128)S(1)} %get-tuple-element.75.near_ref), channel_id=1, source_target_pairs={{0,4},{4,0},{8,12},{12,8},{16,20},{20,16},{24,28},{28,24},{1,5},{5... | collective-permute-start | bytes 393224 | tf_op jit(solution)/shard_map/ppermute | solution.py:533
  37.4 7.7 %collective-permute-start.14 = (f32[16,16,128]{2,1,0:T(8,128)S(1)}, f32[16,16,128]{2,1,0:T(8,128)S(1)}, u32[]{:S(2)}, u32[]{:S(2)}) collective-permute-start(f32[16,16,128]{2,1,0:T(8,128)S(1)} %get-tuple-element.72.far_ref), channel_id=1, source_target_pairs={{0,28},{4,8},{8,4},{12,16},{16,12},{20,24},{24,20},{28,0},{1,29},{... | collective-permute-start | bytes 393224 | tf_op jit(solution)/shard_map/ppermute | solution.py:533
  40.4 2.1 %collective-permute-start.12 = (f32[32,128]{1,0:T(8,128)S(1)}, f32[32,128]{1,0:T(8,128)S(1)}, u32[]{:S(2)}, u32[]{:S(2)}) collective-permute-start(f32[32,128]{1,0:T(8,128)S(1)} %get-tuple-element.77), channel_id=1, source_target_pairs={{0,1},{1,0},{2,3},{3,2},{4,5},{5,4},{6,7},{7,6},{8,9},{9,8},{10,11... | collective-permute-start | bytes 49160 | tf_op jit(solution)/shard_map/ppermute | solution.py:533
  40.5 3.2 %collective-permute-start.13 = (f32[32,128]{1,0:T(8,128)S(1)}, f32[32,128]{1,0:T(8,128)S(1)}, u32[]{:S(2)}, u32[]{:S(2)}) collective-permute-start(f32[32,128]{1,0:T(8,128)S(1)} %get-tuple-element.78), channel_id=1, source_target_pairs={{0,3},{1,2},{2,1},{3,0},{4,7},{5,6},{6,5},{7,4},{8,11},{9,10},{10,... | collective-permute-start | bytes 49160 | tf_op jit(solution)/shard_map/ppermute | solution.py:533
  45.5 3.7 %collective-permute-start.16 = (f32[8,256]{1,0:T(8,128)S(1)}, f32[8,256]{1,0:T(8,128)S(1)}, u32[]{:S(2)}, u32[]{:S(2)}) collective-permute-start(f32[8,256]{1,0:T(8,128)S(1)} %get-tuple-element.82.message_ref), channel_id=1, source_target_pairs={{0,4},{4,0},{8,12},{12,8},{16,20},{20,16},{24,28},{28,24},{1,5},{5... | collective-permute-start | bytes 24584 | tf_op jit(solution)/shard_map/ppermute | solution.py:533
  46.3 6.3 %collective-permute-start.17 = (f32[8,256]{1,0:T(8,128)S(1)}, f32[8,256]{1,0:T(8,128)S(1)}, u32[]{:S(2)}, u32[]{:S(2)}) collective-permute-start(f32[8,256]{1,0:T(8,128)S(1)} %get-tuple-element.82.message_ref), channel_id=1, source_target_pairs={{0,28},{4,8},{8,4},{12,16},{16,12},{20,24},{24,20},{28,0},{1,29},{... | collective-permute-start | bytes 24584 | tf_op jit(solution)/shard_map/ppermute | solution.py:533

commit v6 on v5

--- a/solution.py
+++ b/solution.py
@@ -273,7 +273,7 @@
 
 def inner_kernel(
     near_ref, far_ref, inner_ref, trig_ref, y_near_ref, y_far_ref, chooser_ref,
-    rim_ref, local_ref, acc_ref,
+    rim_ref, local_ref, acc_ref, part_ref,
     sums_ref,
 ):
     _, cz, _, _, yb, xb = trig_ref.shape
@@ -315,6 +315,14 @@
         put_sums(totals, at, yb, sums_ref)
     acc_ref[...] = slot_sums(sums_ref, chooser_ref, yb)
 
+    get, _, inward = outer_getters(1, far_ref, inner_ref, trig_ref, None)
+    for p in range(ROWS):
+        for j in range(COLS):
+            sides = [beside(get, inward, inward, rim_ref, 1, k, p, j)[:5] for k in (2, 3, 4, 5, 0)]
+            grads = gradients(sides[4] + (sides[4][4],), 0.0)[:2]
+            for k, value in enumerate([sum(side) for side in sides[:4]] + grads):
+                part_ref[k, p, j] = value
+
 
 def outer_getters(layer, own_ref, inner_ref, trig_ref, halo):
     beside_at = facing(layer, inner_ref.shape[1])
@@ -362,13 +370,30 @@
 
 
 def far_kernel(
-    far_ref, inner_ref, trig_ref, rim_ref, halo_ref, chooser_ref, before_ref,
+    far_ref, inner_ref, trig_ref, part_ref, halo_ref, chooser_ref, before_ref,
     mixed_ref, message_ref,
-    trig_halo_ref, sums_ref, acc_ref,
-):
-    acc_ref[...] = before_ref[...] + outer_densities(
-        1, far_ref, inner_ref, trig_ref, rim_ref, halo_ref, chooser_ref, mixed_ref, trig_halo_ref, sums_ref
-    )
+    sums_ref, acc_ref,
+):
+    yb = trig_ref.shape[4]
+    get, _, inward = outer_getters(1, far_ref, inner_ref, trig_ref, None)
+    z_half = upward(1)
+    totals = None
+    for p in range(ROWS):
+        for j in range(COLS):
+            e_out, q_out = (halo_ref[tile(f, p, j)] for f in range(2))
+            c_sum, s_sum, a_sum, b_sum = (
+                part_ref[k, p, j] + value for k, value in enumerate(derived(e_out, q_out))
+            )
+            e, c, s = get(0, p, j), get(2, p, j), get(3, p, j)
+            weight = e * (6.0 - c * c_sum - s * s_sum)
+            torque = c * b_sum - s * a_sum
+            grads = [part_ref[4, p, j], part_ref[5, p, j], (e_out - inward(0, p, j)) * z_half]
+            densities = [weight * g for g in grads] + [torque, 0.5 + e * e]
+            totals = densities if totals is None else [x + y for x, y in zip(totals, densities)]
+            mixed_ref[0, p, j] = weight
+            mixed_ref[1, p, j] = torque
+    put_sums(totals, 0, yb, sums_ref)
+    acc_ref[...] = before_ref[...] + slot_sums(sums_ref, chooser_ref, yb // 2)
     message_ref[0:5, :] = acc_ref[0:5, :] + acc_ref[5:10, :] + acc_ref[10:15, :]
     message_ref[5:8, :] = jnp.zeros((3, message_ref.shape[1]), jnp.float32)
 
@@ -394,7 +419,7 @@
                     local_ref[k, layer, p, j] = value
 
 
-def match_kernel(ids_ref, near_halo_ref, far_halo_ref, match_ref):
+def match_kernel(ids_ref, near_halo_ref, far_halo_ref, match_ref, back_ref):
     slots = ids_ref.shape[1]
     xb = near_halo_ref.shape[2]
     own = jnp.broadcast_to(ids_ref[...].astype(jnp.float32), (xb, slots))
@@ -405,6 +430,7 @@
             other = jnp.concatenate([other] * (slots // xb), axis=1)
             start = side * slots + half * xb
             match_ref[start : start + xb, :] = jnp.where(other == own, 1.0, 0.0).astype(jnp.bfloat16)
+    back_ref[...] = x_chooser(back_ref.shape[0], xb, back=True)
 
 
 def stacked(value):
@@ -468,35 +494,40 @@
 
 
 def finish_kernel(
-    message_ref, near_message_ref, far_message_ref, match_ref, block_ref, outer_local_ref, inner_local_ref,
+    message_ref, near_message_ref, far_message_ref, match_ref, back_ref, block_ref, outer_local_ref, inner_local_ref,
     e_hbm, q_hbm,
     velocity_ref, rows_ref, out_ref, sems,
 ):
     yb, xb = outer_local_ref.shape[4:]
     _, cz, cy, nx = out_ref.shape
     slot_motion(message_ref, near_message_ref, far_message_ref, match_ref, velocity_ref)
-    chooser = x_chooser(nx, xb, back=True)
+    chooser = back_ref[...]
     copies = []
-    for part, local_ref in enumerate((outer_local_ref, inner_local_ref)):
-        layers = local_ref.shape[1]
-        for at in range(layers):
-            motion = layer_motion(velocity_ref, block_ref, 2 * part + at, yb)
+    for first, count in [(layer, 1) for layer in range(cz)]:
+        for at in range(count):
+            layer = first + at
+            motion = layer_motion(velocity_ref, block_ref, layer, yb)
+            local_ref, inside = (outer_local_ref, layer) if layer < 2 else (inner_local_ref, layer - 2)
             for p in range(ROWS):
                 to = pl.ds(at * cy + p, yb, stride=ROWS)
                 for j in range(COLS):
-                    e, q = advanced(local_ref, motion, at, p, j)
+                    e, q = advanced(local_ref, motion, inside, p, j)
                     rows_ref[0, j, to, :] = e
                     rows_ref[1, j, to, :] = q
         moved = exact_dot(
             jnp.concatenate(
-                [jnp.concatenate([rows_ref[f, j] for j in range(COLS)], axis=1) for f in range(2)], axis=0
+                [
+                    jnp.concatenate([rows_ref[f, j, : count * cy, :] for j in range(COLS)], axis=1)
+                    for f in range(2)
+                ],
+                axis=0,
             ),
             chooser,
         )
         for f, ref in enumerate((e_hbm, q_hbm)):
-            for at in range(layers):
-                layer = 2 * part + at
-                start = (f * layers + at) * cy
+            for at in range(count):
+                layer = first + at
+                start = (f * count + at) * cy
                 out_ref[f, layer] = moved[start : start + cy]
                 copies.append(
                     pltpu.make_async_copy(out_ref.at[f, layer], ref.at[place(layer, cz)], sems.at[f, layer])
@@ -569,15 +600,15 @@
     choosers = call(chooser_kernel, "choosers", [((rows // 2, 2 * xb, slots), bf16)])
     trigs = call(trig_kernel, "trigs", [((4, cz) + block, f32)])
     inner_terms = call(
-        inner_kernel, "inner_terms", [((2, 6, cz * COLS, xb), f32), ((8, cz - 2) + block, f32), acc_out],
+        inner_kernel, "inner_terms", [((2, 6, cz * COLS, xb), f32), ((8, cz - 2) + block, f32), acc_out, ((6,) + block, f32)],
         [pltpu.VMEM((16 * (cz - 2) * yb, xb), f32)],
     )
     near_terms = call(near_kernel, "near_terms", [mixed_out, acc_out], layer_scratch)
     far_terms = call(
-        far_kernel, "far_terms", [mixed_out, ((8, slots), f32)], layer_scratch + [pltpu.VMEM((16, slots), f32)]
+        far_kernel, "far_terms", [mixed_out, ((8, slots), f32)], [layer_scratch[1], pltpu.VMEM((16, slots), f32)]
     )
     outer_locals = call(outer_local_kernel, "outer_locals", [((8, 2) + block, f32)])
-    matches = call(match_kernel, "matches", [((2 * slots, slots), bf16)])
+    matches = call(match_kernel, "matches", [((2 * slots, slots), bf16), ((nx, nx), bf16)])
     advance_outer = call(
         advance_outer_kernel, "advance_outer", [((8, slots), f32), side_out, side_out]
     )
@@ -585,7 +616,7 @@
     finish = call(
         finish_kernel, "finish", [((cz, cy, nx), f32)] * 2,
         [
-            pltpu.VMEM((8, slots), f32), pltpu.VMEM((2, COLS, 2 * cy, xb), f32), pltpu.VMEM((2, cz, cy, nx), f32), dma((2, cz)),
+            pltpu.VMEM((8, slots), f32), pltpu.VMEM((2, COLS, cy, xb), f32), pltpu.VMEM((2, cz, cy, nx), f32), dma((2, cz)),
         ],
         hbm_out=True,
     )
@@ -604,16 +635,16 @@
         if step == 0:
             (chooser,) = choosers(blocks)
         (trig,) = trigs(near, far, inner)
-        rim, inner_local, acc = inner_terms(near, far, inner, trig, y_near, y_far, chooser)
+        rim, inner_local, acc, part = inner_terms(near, far, inner, trig, y_near, y_far, chooser)
         near_mixed, acc = near_terms(near, inner, trig, rim, near_halo, chooser, acc)
-        far_mixed, message = far_terms(far, inner, trig, rim, far_halo, chooser, acc)
+        far_mixed, message = far_terms(far, inner, trig, part, far_halo, chooser, acc)
         near_message, far_message = both(message, message, "gz")
         if step == 0:
-            (match,) = matches(ids, near_halo, far_halo)
+            match, back = matches(ids, near_halo, far_halo)
         (outer_local,) = outer_locals(near, far, inner, trig, rim, near_halo, far_halo, near_mixed, far_mixed)
         if step < STEPS - 1:
             velocity, near, far = advance_outer(message, near_message, far_message, match, blocks, outer_local)
-    return tuple(finish(message, near_message, far_message, match, blocks, outer_local, inner_local))
+    return tuple(finish(message, near_message, far_message, match, back, blocks, outer_local, inner_local))
 
 
 def solution(mesh):

time: 54.5 us -> 54.2 us (level)
  no operation moved by 1% of the time
where the time goes in v6:
time: 54.2 us; the launch traced here: 54.1 us
  starting transfers between devices  28.4 us (52%)
  Pallas kernels  12.7 us (23%)
  waiting for transfers between devices  12.1 us (22%)
  between operations  0.81 us (1%)
    ppermute x18, starting transfers between devices, swap(): return lax.ppermute(array, axis, pairs)  28.4 us
    pallas_call x24, Pallas kernels, run(): pl.pallas_call(kernel, name=name, in_specs=[HBM] * hbm_in + [VMEM] * (len...  12.7 us
    ppermute x18, waiting for transfers between devices, swap(): return lax.ppermute(array, axis, pairs)  12.1 us
  transfers between devices with their start and end apart: 18, of which 8 were waited for; matrix products, arithmetic and copies ran while one was open for 0% of the time, Pallas kernels for 14%

profile of v6, /device:TPU:0, one launch (start us, length us, event | category | flops | bytes accessed | tf_op | source)
XLA Modules:
  0.0 54.1 jit_solution(10098018508075068541)
XLA Ops:
  0.6 1.6 %prepare_outer.1 = (f32[17,16,128]{2,1,0:T(8,128)S(1)}, f32[17,16,128]{2,1,0:T(8,128)S(1)}, f32[2,2,32,512]{3,2,1,0:T(8,128)S(1)}, s32[4,32,512]{2,1,0:T(8,128)S(1)}, s32[1,256]{1,0:T(1,128)S(1)}) custom-call(f32[4,32,512]{2,1,0:T(8,128)} %e_hbm.1, f32[4,32,512]{2,1,0:T(8,128)} %q_hbm.1, s32[4,32,512]{2,1,0:T(8,128)} %slot_hbm.1, s32[1,256]{1,0:T(1,128)} %bitcast.1), custom_call_target="tpu_custom_call" | custom-call | flops 4194304 | bytes 1048576 | tf_op jit(solution)/shard_map/prepare_outer/pallas_call | solution.py:547
  2.2 3.0 %collective-permute-start.3 = (f32[17,16,128]{2,1,0:T(8,128)S(1)}, f32[17,16,128]{2,1,0:T(8,128)S(1)}, u32[]{:S(2)}, u32[]{:S(2)}) collective-permute-start(f32[17,16,128]{2,1,0:T(8,128)S(1)} %get-tuple-element.52.near_ref), channel_id=1, source_target_pairs={{0,4},{4,0},{8,12},{12,8},{16,20},{20,16},{24,28},{28,24},{1,5},{5... | collective-permute-start | bytes 417800 | tf_op jit(solution)/shard_map/ppermute | solution.py:564
  5.2 3.5 %collective-permute-start.2 = (f32[17,16,128]{2,1,0:T(8,128)S(1)}, f32[17,16,128]{2,1,0:T(8,128)S(1)}, u32[]{:S(2)}, u32[]{:S(2)}) collective-permute-start(f32[17,16,128]{2,1,0:T(8,128)S(1)} %get-tuple-element.49.far_ref), channel_id=1, source_target_pairs={{0,28},{4,8},{8,4},{12,16},{16,12},{20,24},{24,20},{28,0},{1,29},{... | collective-permute-start | bytes 417800 | tf_op jit(solution)/shard_map/ppermute | solution.py:564
  8.8 0.4 prepare_inner.1
  9.2 0.1 collective-permute-start
  9.3 1.6 %collective-permute-start.1 = (f32[32,128]{1,0:T(8,128)S(1)}, f32[32,128]{1,0:T(8,128)S(1)}, u32[]{:S(2)}, u32[]{:S(2)}) collective-permute-start(f32[32,128]{1,0:T(8,128)S(1)} %get-tuple-element.55), channel_id=1, source_target_pairs={{0,3},{1,2},{2,1},{3,0},{4,7},{5,6},{6,5},{7,4},{8,11},{9,10},{10,... | collective-permute-start | bytes 49160 | tf_op jit(solution)/shard_map/ppermute | solution.py:564
  10.9 0.4 trigs.3.trig_ref
  11.3 0.9 %choosers.1.chooser_ref = bf16[32,256,256]{2,1,0:T(8,128)(2,1)S(1)} custom-call(s32[64,128]{1,0:T(8,128)S(1)} %get-tuple-element.56.block_ref), custom_call_target="tpu_custom_call" | custom-call | flops 4194304 | bytes 1048576 | tf_op jit(solution)/shard_map/choosers/pallas_call | solution.py:547
  12.2 0.0 collective-permute-done.y_near_ref
  12.3 0.3 collective-permute-done.1.y_far_ref
  12.5 0.8 %inner_terms.3 = (f32[2,6,16,128]{3,2,1,0:T(8,128)S(1)}, f32[8,2,2,4,16,128]{5,4,3,2,1,0:T(8,128)S(1)}, f32[16,256]{1,0:T(8,128)S(1)}, f32[6,2,4,16,128]{4,3,2,1,0:T(8,128)S(1)}) custom-call(f32[17,16,128]{2,1,0:T(8,128)S(1)} %get-tuple-element.52.near_ref, f32[17,16,128]{2,1,0:T(8,128)S(1)} %get-tuple-element.49.far_ref, ...), custom_call_target="tpu_custom_call" | custom-call | flops 4194304 | bytes 1048576 | tf_op jit(solution)/shard_map/inner_terms/pallas_call | solution.py:547
  13.4 0.0 collective-permute-done.3.halo_ref.near_halo_ref
  13.4 0.5 near_terms.3
  13.8 0.0 collective-permute-done.2.halo_ref.far_halo_ref
  13.8 0.4 far_terms.3
  14.3 0.3 collective-permute-start.4
  14.6 3.5 %collective-permute-start.5 = (f32[8,256]{1,0:T(8,128)S(1)}, f32[8,256]{1,0:T(8,128)S(1)}, u32[]{:S(2)}, u32[]{:S(2)}) collective-permute-start(f32[8,256]{1,0:T(8,128)S(1)} %get-tuple-element.61.message_ref), channel_id=1, source_target_pairs={{0,28},{4,8},{8,4},{12,16},{16,12},{20,24},{24,20},{28,0},{1,29},{... | collective-permute-start | bytes 24584 | tf_op jit(solution)/shard_map/ppermute | solution.py:564
  18.1 0.4 matches.1
  18.5 0.2 outer_locals.3.local_ref
  18.7 0.0 collective-permute-done.4.near_message_ref
  18.7 2.2 %collective-permute-done.5.far_message_ref = f32[8,256]{1,0:T(8,128)S(1)} collective-permute-done((f32[8,256]{1,0:T(8,128)S(1)}, f32[8,256]{1,0:T(8,128)S(1)}, u32[]{:S(2)}, u32[]{:S(2)}) %collective-permute-start.5) | collective-permute-done | bytes 8224 | tf_op jit(solution)/shard_map/ppermute | solution.py:564
  20.9 0.3 advance_outer.2
  21.3 0.1 collective-permute-start.9
  21.4 3.6 %collective-permute-start.8 = (f32[16,16,128]{2,1,0:T(8,128)S(1)}, f32[16,16,128]{2,1,0:T(8,128)S(1)}, u32[]{:S(2)}, u32[]{:S(2)}) collective-permute-start(f32[16,16,128]{2,1,0:T(8,128)S(1)} %get-tuple-element.66.far_ref), channel_id=1, source_target_pairs={{0,28},{4,8},{8,4},{12,16},{16,12},{20,24},{24,20},{28,0},{1,29},{... | collective-permute-start | bytes 393224 | tf_op jit(solution)/shard_map/ppermute | solution.py:564
  25.0 0.2 advance_inner.2
  25.1 0.1 collective-permute-start.6
  25.2 1.6 %collective-permute-start.7 = (f32[32,128]{1,0:T(8,128)S(1)}, f32[32,128]{1,0:T(8,128)S(1)}, u32[]{:S(2)}, u32[]{:S(2)}) collective-permute-start(f32[32,128]{1,0:T(8,128)S(1)} %get-tuple-element.72), channel_id=1, source_target_pairs={{0,3},{1,2},{2,1},{3,0},{4,7},{5,6},{6,5},{7,4},{8,11},{9,10},{10,... | collective-permute-start | bytes 49160 | tf_op jit(solution)/shard_map/ppermute | solution.py:564
  26.8 0.4 trigs.4.trig_ref
  27.2 0.0 collective-permute-done.6.y_near_ref
  27.2 1.2 %collective-permute-done.7.y_far_ref = f32[32,128]{1,0:T(8,128)S(1)} collective-permute-done((f32[32,128]{1,0:T(8,128)S(1)}, f32[32,128]{1,0:T(8,128)S(1)}, u32[]{:S(2)}, u32[]{:S(2)}) %collective-permute-start.7) | collective-permute-done | bytes 16416 | tf_op jit(solution)/shard_map/ppermute | solution.py:564
  28.4 0.8 %inner_terms.4 = (f32[2,6,16,128]{3,2,1,0:T(8,128)S(1)}, f32[8,2,2,4,16,128]{5,4,3,2,1,0:T(8,128)S(1)}, f32[16,256]{1,0:T(8,128)S(1)}, f32[6,2,4,16,128]{4,3,2,1,0:T(8,128)S(1)}) custom-call(f32[16,16,128]{2,1,0:T(8,128)S(1)} %get-tuple-element.69.near_ref, f32[16,16,128]{2,1,0:T(8,128)S(1)} %get-tuple-element.66.far_ref, ...), custom_call_target="tpu_custom_call" | custom-call | flops 4194304 | bytes 1048576 | tf_op jit(solution)/shard_map/inner_terms/pallas_call | solution.py:547
  29.2 0.0 collective-permute-done.9.halo_ref.near_halo_ref
  29.2 0.5 near_terms.4
  29.7 0.0 collective-permute-done.8.halo_ref.far_halo_ref
  29.7 0.4 far_terms.4
  30.2 0.1 collective-permute-start.10
  30.2 3.0 %collective-permute-start.11 = (f32[8,256]{1,0:T(8,128)S(1)}, f32[8,256]{1,0:T(8,128)S(1)}, u32[]{:S(2)}, u32[]{:S(2)}) collective-permute-start(f32[8,256]{1,0:T(8,128)S(1)} %get-tuple-element.77.message_ref), channel_id=1, source_target_pairs={{0,28},{4,8},{8,4},{12,16},{16,12},{20,24},{24,20},{28,0},{1,29},{... | collective-permute-start | bytes 24584 | tf_op jit(solution)/shard_map/ppermute | solution.py:564
  33.3 0.2 outer_locals.4.local_ref
  33.4 0.4 collective-permute-done.10.near_message_ref
  33.9 2.8 %collective-permute-done.11.far_message_ref = f32[8,256]{1,0:T(8,128)S(1)} collective-permute-done((f32[8,256]{1,0:T(8,128)S(1)}, f32[8,256]{1,0:T(8,128)S(1)}, u32[]{:S(2)}, u32[]{:S(2)}) %collective-permute-start.11) | collective-permute-done | bytes 8224 | tf_op jit(solution)/shard_map/ppermute | solution.py:564
  36.7 0.3 advance_outer.3
  37.0 0.2 collective-permute-start.15
  37.2 2.9 %collective-permute-start.14 = (f32[16,16,128]{2,1,0:T(8,128)S(1)}, f32[16,16,128]{2,1,0:T(8,128)S(1)}, u32[]{:S(2)}, u32[]{:S(2)}) collective-permute-start(f32[16,16,128]{2,1,0:T(8,128)S(1)} %get-tuple-element.80.far_ref), channel_id=1, source_target_pairs={{0,28},{4,8},{8,4},{12,16},{16,12},{20,24},{24,20},{28,0},{1,29},{... | collective-permute-start | bytes 393224 | tf_op jit(solution)/shard_map/ppermute | solution.py:564
  40.1 0.2 advance_inner.3
  40.3 0.1 collective-permute-start.12
  40.4 1.6 %collective-permute-start.13 = (f32[32,128]{1,0:T(8,128)S(1)}, f32[32,128]{1,0:T(8,128)S(1)}, u32[]{:S(2)}, u32[]{:S(2)}) collective-permute-start(f32[32,128]{1,0:T(8,128)S(1)} %get-tuple-element.86), channel_id=1, source_target_pairs={{0,3},{1,2},{2,1},{3,0},{4,7},{5,6},{6,5},{7,4},{8,11},{9,10},{10,... | collective-permute-start | bytes 49160 | tf_op jit(solution)/shard_map/ppermute | solution.py:564
  42.0 0.4 trigs.5.trig_ref
  42.3 0.0 collective-permute-done.12.y_near_ref
  42.3 1.2 %collective-permute-done.13.y_far_ref = f32[32,128]{1,0:T(8,128)S(1)} collective-permute-done((f32[32,128]{1,0:T(8,128)S(1)}, f32[32,128]{1,0:T(8,128)S(1)}, u32[]{:S(2)}, u32[]{:S(2)}) %collective-permute-start.13) | collective-permute-done | bytes 16416 | tf_op jit(solution)/shard_map/ppermute | solution.py:564
  43.6 0.8 %inner_terms.5 = (f32[2,6,16,128]{3,2,1,0:T(8,128)S(1)}, f32[8,2,2,4,16,128]{5,4,3,2,1,0:T(8,128)S(1)}, f32[16,256]{1,0:T(8,128)S(1)}, f32[6,2,4,16,128]{4,3,2,1,0:T(8,128)S(1)}) custom-call(f32[16,16,128]{2,1,0:T(8,128)S(1)} %get-tuple-element.83.near_ref, f32[16,16,128]{2,1,0:T(8,128)S(1)} %get-tuple-element.80.far_ref, ...), custom_call_target="tpu_custom_call" | custom-call | flops 4194304 | bytes 1048576 | tf_op jit(solution)/shard_map/inner_terms/pallas_call | solution.py:547
  44.4 0.0 collective-permute-done.15.halo_ref.near_halo_ref
  44.4 0.5 near_terms.5
  44.9 0.0 collective-permute-done.14.halo_ref.far_halo_ref
  44.9 0.4 far_terms.5
  45.3 0.8 %collective-permute-start.16 = (f32[8,256]{1,0:T(8,128)S(1)}, f32[8,256]{1,0:T(8,128)S(1)}, u32[]{:S(2)}, u32[]{:S(2)}) collective-permute-start(f32[8,256]{1,0:T(8,128)S(1)} %get-tuple-element.91.message_ref), channel_id=1, source_target_pairs={{0,4},{4,0},{8,12},{12,8},{16,20},{20,16},{24,28},{28,24},{1,5},{5... | collective-permute-start | bytes 24584 | tf_op jit(solution)/shard_map/ppermute | solution.py:564
  46.1 2.3 %collective-permute-start.17 = (f32[8,256]{1,0:T(8,128)S(1)}, f32[8,256]{1,0:T(8,128)S(1)}, u32[]{:S(2)}, u32[]{:S(2)}) collective-permute-start(f32[8,256]{1,0:T(8,128)S(1)} %get-tuple-element.91.message_ref), channel_id=1, source_target_pairs={{0,28},{4,8},{8,4},{12,16},{16,12},{20,24},{24,20},{28,0},{1,29},{... | collective-permute-start | bytes 24584 | tf_op jit(solution)/shard_map/ppermute | solution.py:564
  48.4 0.2 outer_locals.5.outer_local_ref
  48.6 0.4 collective-permute-done.16.near_message_ref
  49.0 3.4 %collective-permute-done.17.far_message_ref = f32[8,256]{1,0:T(8,128)S(1)} collective-permute-done((f32[8,256]{1,0:T(8,128)S(1)}, f32[8,256]{1,0:T(8,128)S(1)}, u32[]{:S(2)}, u32[]{:S(2)}) %collective-permute-start.17) | collective-permute-done | bytes 8224 | tf_op jit(solution)/shard_map/ppermute | solution.py:564
  52.5 1.6 %finish.1 = (f32[4,32,512]{2,1,0:T(8,128)}, f32[4,32,512]{2,1,0:T(8,128)}) custom-call(f32[8,256]{1,0:T(8,128)S(1)} %get-tuple-element.91.message_ref, f32[8,256]{1,0:T(8,128)S(1)} %collective-permute-done.16.near_message_ref, f32[8,256]{1,0:T(8,128)S(1)} %collective-permute-done.17.far_message_ref, bf16[512,256]{1,0:T(8,128)(2,1)S(1)} %get-tuple-element.63.match_ref, ...), custom_call_target="tpu_custom_call" | custom-call | flops 4194304 | bytes 1048576 | tf_op jit(solution)/shard_map/finish/pallas_call | solution.py:547
Async XLA Ops:
  2.2 11.2 %collective-permute-start.3 = (f32[17,16,128]{2,1,0:T(8,128)S(1)}, f32[17,16,128]{2,1,0:T(8,128)S(1)}, u32[]{:S(2)}, u32[]{:S(2)}) collective-permute-start(f32[17,16,128]{2,1,0:T(8,128)S(1)} %get-tuple-element.52.near_ref), channel_id=1, source_target_pairs={{0,4},{4,0},{8,12},{12,8},{16,20},{20,16},{24,28},{28,24},{1,5},{5... | collective-permute-start | bytes 417800 | tf_op jit(solution)/shard_map/ppermute | solution.py:564
  5.2 8.6 %collective-permute-start.2 = (f32[17,16,128]{2,1,0:T(8,128)S(1)}, f32[17,16,128]{2,1,0:T(8,128)S(1)}, u32[]{:S(2)}, u32[]{:S(2)}) collective-permute-start(f32[17,16,128]{2,1,0:T(8,128)S(1)} %get-tuple-element.49.far_ref), channel_id=1, source_target_pairs={{0,28},{4,8},{8,4},{12,16},{16,12},{20,24},{24,20},{28,0},{1,29},{... | collective-permute-start | bytes 417800 | tf_op jit(solution)/shard_map/ppermute | solution.py:564
  9.2 3.0 %collective-permute-start = (f32[32,128]{1,0:T(8,128)S(1)}, f32[32,128]{1,0:T(8,128)S(1)}, u32[]{:S(2)}, u32[]{:S(2)}) collective-permute-start(f32[32,128]{1,0:T(8,128)S(1)} %get-tuple-element.54), channel_id=1, source_target_pairs={{0,1},{1,0},{2,3},{3,2},{4,5},{5,4},{6,7},{7,6},{8,9},{9,8},{10,11... | collective-permute-start | bytes 49160 | tf_op jit(solution)/shard_map/ppermute | solution.py:564
  9.3 3.2 %collective-permute-start.1 = (f32[32,128]{1,0:T(8,128)S(1)}, f32[32,128]{1,0:T(8,128)S(1)}, u32[]{:S(2)}, u32[]{:S(2)}) collective-permute-start(f32[32,128]{1,0:T(8,128)S(1)} %get-tuple-element.55), channel_id=1, source_target_pairs={{0,3},{1,2},{2,1},{3,0},{4,7},{5,6},{6,5},{7,4},{8,11},{9,10},{10,... | collective-permute-start | bytes 49160 | tf_op jit(solution)/shard_map/ppermute | solution.py:564
  14.3 4.4 %collective-permute-start.4 = (f32[8,256]{1,0:T(8,128)S(1)}, f32[8,256]{1,0:T(8,128)S(1)}, u32[]{:S(2)}, u32[]{:S(2)}) collective-permute-start(f32[8,256]{1,0:T(8,128)S(1)} %get-tuple-element.61.message_ref), channel_id=1, source_target_pairs={{0,4},{4,0},{8,12},{12,8},{16,20},{20,16},{24,28},{28,24},{1,5},{5... | collective-permute-start | bytes 24584 | tf_op jit(solution)/shard_map/ppermute | solution.py:564
  14.6 6.3 %collective-permute-start.5 = (f32[8,256]{1,0:T(8,128)S(1)}, f32[8,256]{1,0:T(8,128)S(1)}, u32[]{:S(2)}, u32[]{:S(2)}) collective-permute-start(f32[8,256]{1,0:T(8,128)S(1)} %get-tuple-element.61.message_ref), channel_id=1, source_target_pairs={{0,28},{4,8},{8,4},{12,16},{16,12},{20,24},{24,20},{28,0},{1,29},{... | collective-permute-start | bytes 24584 | tf_op jit(solution)/shard_map/ppermute | solution.py:564
  21.3 8.0 %collective-permute-start.9 = (f32[16,16,128]{2,1,0:T(8,128)S(1)}, f32[16,16,128]{2,1,0:T(8,128)S(1)}, u32[]{:S(2)}, u32[]{:S(2)}) collective-permute-start(f32[16,16,128]{2,1,0:T(8,128)S(1)} %get-tuple-element.69.near_ref), channel_id=1, source_target_pairs={{0,4},{4,0},{8,12},{12,8},{16,20},{20,16},{24,28},{28,24},{1,5},{5... | collective-permute-start | bytes 393224 | tf_op jit(solution)/shard_map/ppermute | solution.py:564
  21.4 8.4 %collective-permute-start.8 = (f32[16,16,128]{2,1,0:T(8,128)S(1)}, f32[16,16,128]{2,1,0:T(8,128)S(1)}, u32[]{:S(2)}, u32[]{:S(2)}) collective-permute-start(f32[16,16,128]{2,1,0:T(8,128)S(1)} %get-tuple-element.66.far_ref), channel_id=1, source_target_pairs={{0,28},{4,8},{8,4},{12,16},{16,12},{20,24},{24,20},{28,0},{1,29},{... | collective-permute-start | bytes 393224 | tf_op jit(solution)/shard_map/ppermute | solution.py:564
  25.1 2.1 %collective-permute-start.6 = (f32[32,128]{1,0:T(8,128)S(1)}, f32[32,128]{1,0:T(8,128)S(1)}, u32[]{:S(2)}, u32[]{:S(2)}) collective-permute-start(f32[32,128]{1,0:T(8,128)S(1)} %get-tuple-element.71), channel_id=1, source_target_pairs={{0,1},{1,0},{2,3},{3,2},{4,5},{5,4},{6,7},{7,6},{8,9},{9,8},{10,11... | collective-permute-start | bytes 49160 | tf_op jit(solution)/shard_map/ppermute | solution.py:564
  25.2 3.2 %collective-permute-start.7 = (f32[32,128]{1,0:T(8,128)S(1)}, f32[32,128]{1,0:T(8,128)S(1)}, u32[]{:S(2)}, u32[]{:S(2)}) collective-permute-start(f32[32,128]{1,0:T(8,128)S(1)} %get-tuple-element.72), channel_id=1, source_target_pairs={{0,3},{1,2},{2,1},{3,0},{4,7},{5,6},{6,5},{7,4},{8,11},{9,10},{10,... | collective-permute-start | bytes 49160 | tf_op jit(solution)/shard_map/ppermute | solution.py:564
  30.2 3.7 %collective-permute-start.10 = (f32[8,256]{1,0:T(8,128)S(1)}, f32[8,256]{1,0:T(8,128)S(1)}, u32[]{:S(2)}, u32[]{:S(2)}) collective-permute-start(f32[8,256]{1,0:T(8,128)S(1)} %get-tuple-element.77.message_ref), channel_id=1, source_target_pairs={{0,4},{4,0},{8,12},{12,8},{16,20},{20,16},{24,28},{28,24},{1,5},{5... | collective-permute-start | bytes 24584 | tf_op jit(solution)/shard_map/ppermute | solution.py:564
  30.2 6.4 %collective-permute-start.11 = (f32[8,256]{1,0:T(8,128)S(1)}, f32[8,256]{1,0:T(8,128)S(1)}, u32[]{:S(2)}, u32[]{:S(2)}) collective-permute-start(f32[8,256]{1,0:T(8,128)S(1)} %get-tuple-element.77.message_ref), channel_id=1, source_target_pairs={{0,28},{4,8},{8,4},{12,16},{16,12},{20,24},{24,20},{28,0},{1,29},{... | collective-permute-start | bytes 24584 | tf_op jit(solution)/shard_map/ppermute | solution.py:564
  37.0 7.4 %collective-permute-start.15 = (f32[16,16,128]{2,1,0:T(8,128)S(1)}, f32[16,16,128]{2,1,0:T(8,128)S(1)}, u32[]{:S(2)}, u32[]{:S(2)}) collective-permute-start(f32[16,16,128]{2,1,0:T(8,128)S(1)} %get-tuple-element.83.near_ref), channel_id=1, source_target_pairs={{0,4},{4,0},{8,12},{12,8},{16,20},{20,16},{24,28},{28,24},{1,5},{5... | collective-permute-start | bytes 393224 | tf_op jit(solution)/shard_map/ppermute | solution.py:564
  37.2 7.7 %collective-permute-start.14 = (f32[16,16,128]{2,1,0:T(8,128)S(1)}, f32[16,16,128]{2,1,0:T(8,128)S(1)}, u32[]{:S(2)}, u32[]{:S(2)}) collective-permute-start(f32[16,16,128]{2,1,0:T(8,128)S(1)} %get-tuple-element.80.far_ref), channel_id=1, source_target_pairs={{0,28},{4,8},{8,4},{12,16},{16,12},{20,24},{24,20},{28,0},{1,29},{... | collective-permute-start | bytes 393224 | tf_op jit(solution)/shard_map/ppermute | solution.py:564
  40.3 2.1 %collective-permute-start.12 = (f32[32,128]{1,0:T(8,128)S(1)}, f32[32,128]{1,0:T(8,128)S(1)}, u32[]{:S(2)}, u32[]{:S(2)}) collective-permute-start(f32[32,128]{1,0:T(8,128)S(1)} %get-tuple-element.85), channel_id=1, source_target_pairs={{0,1},{1,0},{2,3},{3,2},{4,5},{5,4},{6,7},{7,6},{8,9},{9,8},{10,11... | collective-permute-start | bytes 49160 | tf_op jit(solution)/shard_map/ppermute | solution.py:564
  40.4 3.2 %collective-permute-start.13 = (f32[32,128]{1,0:T(8,128)S(1)}, f32[32,128]{1,0:T(8,128)S(1)}, u32[]{:S(2)}, u32[]{:S(2)}) collective-permute-start(f32[32,128]{1,0:T(8,128)S(1)} %get-tuple-element.86), channel_id=1, source_target_pairs={{0,3},{1,2},{2,1},{3,0},{4,7},{5,6},{6,5},{7,4},{8,11},{9,10},{10,... | collective-permute-start | bytes 49160 | tf_op jit(solution)/shard_map/ppermute | solution.py:564
  45.3 3.7 %collective-permute-start.16 = (f32[8,256]{1,0:T(8,128)S(1)}, f32[8,256]{1,0:T(8,128)S(1)}, u32[]{:S(2)}, u32[]{:S(2)}) collective-permute-start(f32[8,256]{1,0:T(8,128)S(1)} %get-tuple-element.91.message_ref), channel_id=1, source_target_pairs={{0,4},{4,0},{8,12},{12,8},{16,20},{20,16},{24,28},{28,24},{1,5},{5... | collective-permute-start | bytes 24584 | tf_op jit(solution)/shard_map/ppermute | solution.py:564
  46.1 6.3 %collective-permute-start.17 = (f32[8,256]{1,0:T(8,128)S(1)}, f32[8,256]{1,0:T(8,128)S(1)}, u32[]{:S(2)}, u32[]{:S(2)}) collective-permute-start(f32[8,256]{1,0:T(8,128)S(1)} %get-tuple-element.91.message_ref), channel_id=1, source_target_pairs={{0,28},{4,8},{8,4},{12,16},{16,12},{20,24},{24,20},{28,0},{1,29},{... | collective-permute-start | bytes 24584 | tf_op jit(solution)/shard_map/ppermute | solution.py:564

commit v7 on v6

--- a/solution.py
+++ b/solution.py
@@ -423,26 +423,39 @@
     slots = ids_ref.shape[1]
     xb = near_halo_ref.shape[2]
     own = jnp.broadcast_to(ids_ref[...].astype(jnp.float32), (xb, slots))
+    number = lax.broadcasted_iota(jnp.int32, (xb, slots), 0)
     for side, ref in enumerate((near_halo_ref, far_halo_ref)):
+        where = jnp.full((1, slots), -1, jnp.int32)
         for half in range(slots // xb):
             line = ref[2 * ROWS * COLS, half : half + 1, :]
             other = jnp.transpose(jnp.broadcast_to(line, (xb, xb)))
             other = jnp.concatenate([other] * (slots // xb), axis=1)
-            start = side * slots + half * xb
-            match_ref[start : start + xb, :] = jnp.where(other == own, 1.0, 0.0).astype(jnp.bfloat16)
+            found = jnp.where(other == own, number + half * xb, -1)
+            where = jnp.maximum(where, jnp.max(found, axis=0, keepdims=True))
+        match_ref[side] = jnp.broadcast_to(where, (8, slots))
     back_ref[...] = x_chooser(back_ref.shape[0], xb, back=True)
 
 
-def stacked(value):
-    return jnp.concatenate([part.astype(jnp.float32) for part in split3(value)], axis=0).astype(jnp.bfloat16)
-
-
-def slot_motion(message_ref, near_ref, far_ref, match_ref, velocity_ref):
-    others = jnp.concatenate([stacked(near_ref[...]), stacked(far_ref[...])], axis=1)
-    parts = jnp.dot(others, match_ref[...], preferred_element_type=jnp.float32)
-    totals = message_ref[...] + parts[0:8] + parts[8:16] + parts[16:24]
-    inverse = 1.0 / totals[4:5, :]
-    velocity_ref[...] = TRANSLATE * totals * inverse
+def looked_up(tables, slot):
+    lanes = slot.shape[1]
+    within = slot & (lanes - 1)
+    value = None
+    for part, table in enumerate(tables):
+        found = jnp.take_along_axis(table, within, axis=1, mode="promise_in_bounds")
+        inside = (slot >= part * lanes) & (slot < (part + 1) * lanes)
+        value = jnp.where(inside, found, 0.0 if value is None else value)
+    return value
+
+
+def slot_motion(message_ref, near_ref, far_ref, match_ref, velocity_ref, lanes):
+    for start in range(0, message_ref.shape[1], lanes):
+        at = slice(start, start + lanes)
+        totals = message_ref[:, at]
+        for side, ref in enumerate((near_ref, far_ref)):
+            tables = [ref[:, part : part + lanes] for part in range(0, ref.shape[1], lanes)]
+            totals = totals + looked_up(tables, match_ref[side, :, at])
+        inverse = 1.0 / totals[4:5, :]
+        velocity_ref[:, at] = TRANSLATE * totals * inverse
 
 
 def layer_motion(velocity_ref, block_ref, layer, yb):
@@ -472,7 +485,7 @@
     message_ref, near_message_ref, far_message_ref, match_ref, block_ref, local_ref,
     velocity_ref, near_ref, far_ref,
 ):
-    slot_motion(message_ref, near_message_ref, far_message_ref, match_ref, velocity_ref)
+    slot_motion(message_ref, near_message_ref, far_message_ref, match_ref, velocity_ref, block_ref.shape[1])
     for layer, ref in enumerate((near_ref, far_ref)):
         motion = layer_motion(velocity_ref, block_ref, layer, local_ref.shape[4])
         for p in range(ROWS):
@@ -500,7 +513,7 @@
 ):
     yb, xb = outer_local_ref.shape[4:]
     _, cz, cy, nx = out_ref.shape
-    slot_motion(message_ref, near_message_ref, far_message_ref, match_ref, velocity_ref)
+    slot_motion(message_ref, near_message_ref, far_message_ref, match_ref, velocity_ref, xb)
     chooser = back_ref[...]
     copies = []
     for first, count in [(layer, 1) for layer in range(cz)]:
@@ -608,7 +621,7 @@
         far_kernel, "far_terms", [mixed_out, ((8, slots), f32)], [layer_scratch[1], pltpu.VMEM((16, slots), f32)]
     )
     outer_locals = call(outer_local_kernel, "outer_locals", [((8, 2) + block, f32)])
-    matches = call(match_kernel, "matches", [((2 * slots, slots), bf16), ((nx, nx), bf16)])
+    matches = call(match_kernel, "matches", [((2, 8, slots), jnp.int32), ((nx, nx), bf16)])
     advance_outer = call(
         advance_outer_kernel, "advance_outer", [((8, slots), f32), side_out, side_out]
     )

time: 54.2 us -> 54 us (level)
  no operation moved by 1% of the time
where the time goes in v7:
time: 54 us; the launch traced here: 53.9 us
  starting transfers between devices  28.4 us (53%)
  Pallas kernels  12.4 us (23%)
  waiting for transfers between devices  12.2 us (23%)
  between operations  0.81 us (2%)
    ppermute x18, starting transfers between devices, swap(): return lax.ppermute(array, axis, pairs)  28.4 us
    pallas_call x24, Pallas kernels, run(): pl.pallas_call(kernel, name=name, in_specs=[HBM] * hbm_in + [VMEM] * (len...  12.4 us
    ppermute x18, waiting for transfers between devices, swap(): return lax.ppermute(array, axis, pairs)  12.2 us
  transfers between devices with their start and end apart: 18, of which 8 were waited for; matrix products, arithmetic and copies ran while one was open for 0% of the time, Pallas kernels for 14%

profile of v7, /device:TPU:0, one launch (start us, length us, event | category | flops | bytes accessed | tf_op | source)
XLA Modules:
  0.0 53.9 jit_solution(11090175997151015435)
XLA Ops:
  0.6 1.6 %prepare_outer.1 = (f32[17,16,128]{2,1,0:T(8,128)S(1)}, f32[17,16,128]{2,1,0:T(8,128)S(1)}, f32[2,2,32,512]{3,2,1,0:T(8,128)S(1)}, s32[4,32,512]{2,1,0:T(8,128)S(1)}, s32[1,256]{1,0:T(1,128)S(1)}) custom-call(f32[4,32,512]{2,1,0:T(8,128)} %e_hbm.1, f32[4,32,512]{2,1,0:T(8,128)} %q_hbm.1, s32[4,32,512]{2,1,0:T(8,128)} %slot_hbm.1, s32[1,256]{1,0:T(1,128)} %bitcast.1), custom_call_target="tpu_custom_call" | custom-call | flops 4194304 | bytes 1048576 | tf_op jit(solution)/shard_map/prepare_outer/pallas_call | solution.py:560
  2.2 3.0 %collective-permute-start.3 = (f32[17,16,128]{2,1,0:T(8,128)S(1)}, f32[17,16,128]{2,1,0:T(8,128)S(1)}, u32[]{:S(2)}, u32[]{:S(2)}) collective-permute-start(f32[17,16,128]{2,1,0:T(8,128)S(1)} %get-tuple-element.52.near_ref), channel_id=1, source_target_pairs={{0,4},{4,0},{8,12},{12,8},{16,20},{20,16},{24,28},{28,24},{1,5},{5... | collective-permute-start | bytes 417800 | tf_op jit(solution)/shard_map/ppermute | solution.py:577
  5.2 3.5 %collective-permute-start.2 = (f32[17,16,128]{2,1,0:T(8,128)S(1)}, f32[17,16,128]{2,1,0:T(8,128)S(1)}, u32[]{:S(2)}, u32[]{:S(2)}) collective-permute-start(f32[17,16,128]{2,1,0:T(8,128)S(1)} %get-tuple-element.49.far_ref), channel_id=1, source_target_pairs={{0,28},{4,8},{8,4},{12,16},{16,12},{20,24},{24,20},{28,0},{1,29},{... | collective-permute-start | bytes 417800 | tf_op jit(solution)/shard_map/ppermute | solution.py:577
  8.8 0.4 prepare_inner.1
  9.2 0.1 collective-permute-start
  9.3 1.6 %collective-permute-start.1 = (f32[32,128]{1,0:T(8,128)S(1)}, f32[32,128]{1,0:T(8,128)S(1)}, u32[]{:S(2)}, u32[]{:S(2)}) collective-permute-start(f32[32,128]{1,0:T(8,128)S(1)} %get-tuple-element.55), channel_id=1, source_target_pairs={{0,3},{1,2},{2,1},{3,0},{4,7},{5,6},{6,5},{7,4},{8,11},{9,10},{10,... | collective-permute-start | bytes 49160 | tf_op jit(solution)/shard_map/ppermute | solution.py:577
  10.9 0.4 trigs.3.trig_ref
  11.3 0.9 %choosers.1.chooser_ref = bf16[32,256,256]{2,1,0:T(8,128)(2,1)S(1)} custom-call(s32[64,128]{1,0:T(8,128)S(1)} %get-tuple-element.56.block_ref), custom_call_target="tpu_custom_call" | custom-call | flops 4194304 | bytes 1048576 | tf_op jit(solution)/shard_map/choosers/pallas_call | solution.py:560
  12.2 0.0 collective-permute-done.y_near_ref
  12.3 0.3 collective-permute-done.1.y_far_ref
  12.5 0.8 %inner_terms.3 = (f32[2,6,16,128]{3,2,1,0:T(8,128)S(1)}, f32[8,2,2,4,16,128]{5,4,3,2,1,0:T(8,128)S(1)}, f32[16,256]{1,0:T(8,128)S(1)}, f32[6,2,4,16,128]{4,3,2,1,0:T(8,128)S(1)}) custom-call(f32[17,16,128]{2,1,0:T(8,128)S(1)} %get-tuple-element.52.near_ref, f32[17,16,128]{2,1,0:T(8,128)S(1)} %get-tuple-element.49.far_ref, ...), custom_call_target="tpu_custom_call" | custom-call | flops 4194304 | bytes 1048576 | tf_op jit(solution)/shard_map/inner_terms/pallas_call | solution.py:560
  13.4 0.0 collective-permute-done.3.halo_ref.near_halo_ref
  13.4 0.5 near_terms.3
  13.9 0.0 collective-permute-done.2.halo_ref.far_halo_ref
  13.9 0.4 far_terms.3
  14.3 0.3 collective-permute-start.4
  14.6 3.5 %collective-permute-start.5 = (f32[8,256]{1,0:T(8,128)S(1)}, f32[8,256]{1,0:T(8,128)S(1)}, u32[]{:S(2)}, u32[]{:S(2)}) collective-permute-start(f32[8,256]{1,0:T(8,128)S(1)} %get-tuple-element.61.message_ref), channel_id=1, source_target_pairs={{0,28},{4,8},{8,4},{12,16},{16,12},{20,24},{24,20},{28,0},{1,29},{... | collective-permute-start | bytes 24584 | tf_op jit(solution)/shard_map/ppermute | solution.py:577
  18.1 0.3 matches.1
  18.5 0.2 outer_locals.3.local_ref
  18.7 0.0 collective-permute-done.4.near_message_ref
  18.7 2.3 %collective-permute-done.5.far_message_ref = f32[8,256]{1,0:T(8,128)S(1)} collective-permute-done((f32[8,256]{1,0:T(8,128)S(1)}, f32[8,256]{1,0:T(8,128)S(1)}, u32[]{:S(2)}, u32[]{:S(2)}) %collective-permute-start.5) | collective-permute-done | bytes 8224 | tf_op jit(solution)/shard_map/ppermute | solution.py:577
  20.9 0.2 advance_outer.2
  21.2 0.1 collective-permute-start.9
  21.3 3.6 %collective-permute-start.8 = (f32[16,16,128]{2,1,0:T(8,128)S(1)}, f32[16,16,128]{2,1,0:T(8,128)S(1)}, u32[]{:S(2)}, u32[]{:S(2)}) collective-permute-start(f32[16,16,128]{2,1,0:T(8,128)S(1)} %get-tuple-element.66.far_ref), channel_id=1, source_target_pairs={{0,28},{4,8},{8,4},{12,16},{16,12},{20,24},{24,20},{28,0},{1,29},{... | collective-permute-start | bytes 393224 | tf_op jit(solution)/shard_map/ppermute | solution.py:577
  24.9 0.2 advance_inner.2
  25.0 0.1 collective-permute-start.6
  25.1 1.6 %collective-permute-start.7 = (f32[32,128]{1,0:T(8,128)S(1)}, f32[32,128]{1,0:T(8,128)S(1)}, u32[]{:S(2)}, u32[]{:S(2)}) collective-permute-start(f32[32,128]{1,0:T(8,128)S(1)} %get-tuple-element.72), channel_id=1, source_target_pairs={{0,3},{1,2},{2,1},{3,0},{4,7},{5,6},{6,5},{7,4},{8,11},{9,10},{10,... | collective-permute-start | bytes 49160 | tf_op jit(solution)/shard_map/ppermute | solution.py:577
  26.7 0.4 trigs.4.trig_ref
  27.1 0.0 collective-permute-done.6.y_near_ref
  27.1 1.2 %collective-permute-done.7.y_far_ref = f32[32,128]{1,0:T(8,128)S(1)} collective-permute-done((f32[32,128]{1,0:T(8,128)S(1)}, f32[32,128]{1,0:T(8,128)S(1)}, u32[]{:S(2)}, u32[]{:S(2)}) %collective-permute-start.7) | collective-permute-done | bytes 16416 | tf_op jit(solution)/shard_map/ppermute | solution.py:577
  28.4 0.8 %inner_terms.4 = (f32[2,6,16,128]{3,2,1,0:T(8,128)S(1)}, f32[8,2,2,4,16,128]{5,4,3,2,1,0:T(8,128)S(1)}, f32[16,256]{1,0:T(8,128)S(1)}, f32[6,2,4,16,128]{4,3,2,1,0:T(8,128)S(1)}) custom-call(f32[16,16,128]{2,1,0:T(8,128)S(1)} %get-tuple-element.69.near_ref, f32[16,16,128]{2,1,0:T(8,128)S(1)} %get-tuple-element.66.far_ref, ...), custom_call_target="tpu_custom_call" | custom-call | flops 4194304 | bytes 1048576 | tf_op jit(solution)/shard_map/inner_terms/pallas_call | solution.py:560
  29.2 0.0 collective-permute-done.9.halo_ref.near_halo_ref
  29.2 0.5 near_terms.4
  29.7 0.0 collective-permute-done.8.halo_ref.far_halo_ref
  29.7 0.4 far_terms.4
  30.1 0.1 collective-permute-start.10
  30.2 3.0 %collective-permute-start.11 = (f32[8,256]{1,0:T(8,128)S(1)}, f32[8,256]{1,0:T(8,128)S(1)}, u32[]{:S(2)}, u32[]{:S(2)}) collective-permute-start(f32[8,256]{1,0:T(8,128)S(1)} %get-tuple-element.77.message_ref), channel_id=1, source_target_pairs={{0,28},{4,8},{8,4},{12,16},{16,12},{20,24},{24,20},{28,0},{1,29},{... | collective-permute-start | bytes 24584 | tf_op jit(solution)/shard_map/ppermute | solution.py:577
  33.2 0.2 outer_locals.4.local_ref
  33.4 0.4 collective-permute-done.10.near_message_ref
  33.8 2.8 %collective-permute-done.11.far_message_ref = f32[8,256]{1,0:T(8,128)S(1)} collective-permute-done((f32[8,256]{1,0:T(8,128)S(1)}, f32[8,256]{1,0:T(8,128)S(1)}, u32[]{:S(2)}, u32[]{:S(2)}) %collective-permute-start.11) | collective-permute-done | bytes 8224 | tf_op jit(solution)/shard_map/ppermute | solution.py:577
  36.6 0.2 advance_outer.3
  36.8 0.2 collective-permute-start.15
  37.0 2.9 %collective-permute-start.14 = (f32[16,16,128]{2,1,0:T(8,128)S(1)}, f32[16,16,128]{2,1,0:T(8,128)S(1)}, u32[]{:S(2)}, u32[]{:S(2)}) collective-permute-start(f32[16,16,128]{2,1,0:T(8,128)S(1)} %get-tuple-element.80.far_ref), channel_id=1, source_target_pairs={{0,28},{4,8},{8,4},{12,16},{16,12},{20,24},{24,20},{28,0},{1,29},{... | collective-permute-start | bytes 393224 | tf_op jit(solution)/shard_map/ppermute | solution.py:577
  39.9 0.2 advance_inner.3
  40.1 0.1 collective-permute-start.12
  40.2 1.6 %collective-permute-start.13 = (f32[32,128]{1,0:T(8,128)S(1)}, f32[32,128]{1,0:T(8,128)S(1)}, u32[]{:S(2)}, u32[]{:S(2)}) collective-permute-start(f32[32,128]{1,0:T(8,128)S(1)} %get-tuple-element.86), channel_id=1, source_target_pairs={{0,3},{1,2},{2,1},{3,0},{4,7},{5,6},{6,5},{7,4},{8,11},{9,10},{10,... | collective-permute-start | bytes 49160 | tf_op jit(solution)/shard_map/ppermute | solution.py:577
  41.8 0.4 trigs.5.trig_ref
  42.1 0.0 collective-permute-done.12.y_near_ref
  42.2 1.2 %collective-permute-done.13.y_far_ref = f32[32,128]{1,0:T(8,128)S(1)} collective-permute-done((f32[32,128]{1,0:T(8,128)S(1)}, f32[32,128]{1,0:T(8,128)S(1)}, u32[]{:S(2)}, u32[]{:S(2)}) %collective-permute-start.13) | collective-permute-done | bytes 16416 | tf_op jit(solution)/shard_map/ppermute | solution.py:577
  43.4 0.8 %inner_terms.5 = (f32[2,6,16,128]{3,2,1,0:T(8,128)S(1)}, f32[8,2,2,4,16,128]{5,4,3,2,1,0:T(8,128)S(1)}, f32[16,256]{1,0:T(8,128)S(1)}, f32[6,2,4,16,128]{4,3,2,1,0:T(8,128)S(1)}) custom-call(f32[16,16,128]{2,1,0:T(8,128)S(1)} %get-tuple-element.83.near_ref, f32[16,16,128]{2,1,0:T(8,128)S(1)} %get-tuple-element.80.far_ref, ...), custom_call_target="tpu_custom_call" | custom-call | flops 4194304 | bytes 1048576 | tf_op jit(solution)/shard_map/inner_terms/pallas_call | solution.py:560
  44.2 0.0 collective-permute-done.15.halo_ref.near_halo_ref
  44.2 0.5 near_terms.5
  44.7 0.0 collective-permute-done.14.halo_ref.far_halo_ref
  44.7 0.4 far_terms.5
  45.1 0.8 %collective-permute-start.16 = (f32[8,256]{1,0:T(8,128)S(1)}, f32[8,256]{1,0:T(8,128)S(1)}, u32[]{:S(2)}, u32[]{:S(2)}) collective-permute-start(f32[8,256]{1,0:T(8,128)S(1)} %get-tuple-element.91.message_ref), channel_id=1, source_target_pairs={{0,4},{4,0},{8,12},{12,8},{16,20},{20,16},{24,28},{28,24},{1,5},{5... | collective-permute-start | bytes 24584 | tf_op jit(solution)/shard_map/ppermute | solution.py:577
  46.0 2.3 %collective-permute-start.17 = (f32[8,256]{1,0:T(8,128)S(1)}, f32[8,256]{1,0:T(8,128)S(1)}, u32[]{:S(2)}, u32[]{:S(2)}) collective-permute-start(f32[8,256]{1,0:T(8,128)S(1)} %get-tuple-element.91.message_ref), channel_id=1, source_target_pairs={{0,28},{4,8},{8,4},{12,16},{16,12},{20,24},{24,20},{28,0},{1,29},{... | collective-permute-start | bytes 24584 | tf_op jit(solution)/shard_map/ppermute | solution.py:577
  48.2 0.2 outer_locals.5.outer_local_ref
  48.4 0.4 collective-permute-done.16.near_message_ref
  48.8 3.5 %collective-permute-done.17.far_message_ref = f32[8,256]{1,0:T(8,128)S(1)} collective-permute-done((f32[8,256]{1,0:T(8,128)S(1)}, f32[8,256]{1,0:T(8,128)S(1)}, u32[]{:S(2)}, u32[]{:S(2)}) %collective-permute-start.17) | collective-permute-done | bytes 8224 | tf_op jit(solution)/shard_map/ppermute | solution.py:577
  52.3 1.6 %finish.1 = (f32[4,32,512]{2,1,0:T(8,128)}, f32[4,32,512]{2,1,0:T(8,128)}) custom-call(f32[8,256]{1,0:T(8,128)S(1)} %get-tuple-element.91.message_ref, f32[8,256]{1,0:T(8,128)S(1)} %collective-permute-done.16.near_message_ref, f32[8,256]{1,0:T(8,128)S(1)} %collective-permute-done.17.far_message_ref, s32[2,8,256]{2,1,0:T(8,128)S(1)} %get-tuple-element.63.match_ref, ...), custom_call_target="tpu_custom_call" | custom-call | flops 4194304 | bytes 1048576 | tf_op jit(solution)/shard_map/finish/pallas_call | solution.py:560
Async XLA Ops:
  2.2 11.2 %collective-permute-start.3 = (f32[17,16,128]{2,1,0:T(8,128)S(1)}, f32[17,16,128]{2,1,0:T(8,128)S(1)}, u32[]{:S(2)}, u32[]{:S(2)}) collective-permute-start(f32[17,16,128]{2,1,0:T(8,128)S(1)} %get-tuple-element.52.near_ref), channel_id=1, source_target_pairs={{0,4},{4,0},{8,12},{12,8},{16,20},{20,16},{24,28},{28,24},{1,5},{5... | collective-permute-start | bytes 417800 | tf_op jit(solution)/shard_map/ppermute | solution.py:577
  5.2 8.6 %collective-permute-start.2 = (f32[17,16,128]{2,1,0:T(8,128)S(1)}, f32[17,16,128]{2,1,0:T(8,128)S(1)}, u32[]{:S(2)}, u32[]{:S(2)}) collective-permute-start(f32[17,16,128]{2,1,0:T(8,128)S(1)} %get-tuple-element.49.far_ref), channel_id=1, source_target_pairs={{0,28},{4,8},{8,4},{12,16},{16,12},{20,24},{24,20},{28,0},{1,29},{... | collective-permute-start | bytes 417800 | tf_op jit(solution)/shard_map/ppermute | solution.py:577
  9.2 3.0 %collective-permute-start = (f32[32,128]{1,0:T(8,128)S(1)}, f32[32,128]{1,0:T(8,128)S(1)}, u32[]{:S(2)}, u32[]{:S(2)}) collective-permute-start(f32[32,128]{1,0:T(8,128)S(1)} %get-tuple-element.54), channel_id=1, source_target_pairs={{0,1},{1,0},{2,3},{3,2},{4,5},{5,4},{6,7},{7,6},{8,9},{9,8},{10,11... | collective-permute-start | bytes 49160 | tf_op jit(solution)/shard_map/ppermute | solution.py:577
  9.3 3.2 %collective-permute-start.1 = (f32[32,128]{1,0:T(8,128)S(1)}, f32[32,128]{1,0:T(8,128)S(1)}, u32[]{:S(2)}, u32[]{:S(2)}) collective-permute-start(f32[32,128]{1,0:T(8,128)S(1)} %get-tuple-element.55), channel_id=1, source_target_pairs={{0,3},{1,2},{2,1},{3,0},{4,7},{5,6},{6,5},{7,4},{8,11},{9,10},{10,... | collective-permute-start | bytes 49160 | tf_op jit(solution)/shard_map/ppermute | solution.py:577
  14.3 4.4 %collective-permute-start.4 = (f32[8,256]{1,0:T(8,128)S(1)}, f32[8,256]{1,0:T(8,128)S(1)}, u32[]{:S(2)}, u32[]{:S(2)}) collective-permute-start(f32[8,256]{1,0:T(8,128)S(1)} %get-tuple-element.61.message_ref), channel_id=1, source_target_pairs={{0,4},{4,0},{8,12},{12,8},{16,20},{20,16},{24,28},{28,24},{1,5},{5... | collective-permute-start | bytes 24584 | tf_op jit(solution)/shard_map/ppermute | solution.py:577
  14.6 6.3 %collective-permute-start.5 = (f32[8,256]{1,0:T(8,128)S(1)}, f32[8,256]{1,0:T(8,128)S(1)}, u32[]{:S(2)}, u32[]{:S(2)}) collective-permute-start(f32[8,256]{1,0:T(8,128)S(1)} %get-tuple-element.61.message_ref), channel_id=1, source_target_pairs={{0,28},{4,8},{8,4},{12,16},{16,12},{20,24},{24,20},{28,0},{1,29},{... | collective-permute-start | bytes 24584 | tf_op jit(solution)/shard_map/ppermute | solution.py:577
  21.2 8.0 %collective-permute-start.9 = (f32[16,16,128]{2,1,0:T(8,128)S(1)}, f32[16,16,128]{2,1,0:T(8,128)S(1)}, u32[]{:S(2)}, u32[]{:S(2)}) collective-permute-start(f32[16,16,128]{2,1,0:T(8,128)S(1)} %get-tuple-element.69.near_ref), channel_id=1, source_target_pairs={{0,4},{4,0},{8,12},{12,8},{16,20},{20,16},{24,28},{28,24},{1,5},{5... | collective-permute-start | bytes 393224 | tf_op jit(solution)/shard_map/ppermute | solution.py:577
  21.3 8.4 %collective-permute-start.8 = (f32[16,16,128]{2,1,0:T(8,128)S(1)}, f32[16,16,128]{2,1,0:T(8,128)S(1)}, u32[]{:S(2)}, u32[]{:S(2)}) collective-permute-start(f32[16,16,128]{2,1,0:T(8,128)S(1)} %get-tuple-element.66.far_ref), channel_id=1, source_target_pairs={{0,28},{4,8},{8,4},{12,16},{16,12},{20,24},{24,20},{28,0},{1,29},{... | collective-permute-start | bytes 393224 | tf_op jit(solution)/shard_map/ppermute | solution.py:577
  25.0 2.1 %collective-permute-start.6 = (f32[32,128]{1,0:T(8,128)S(1)}, f32[32,128]{1,0:T(8,128)S(1)}, u32[]{:S(2)}, u32[]{:S(2)}) collective-permute-start(f32[32,128]{1,0:T(8,128)S(1)} %get-tuple-element.71), channel_id=1, source_target_pairs={{0,1},{1,0},{2,3},{3,2},{4,5},{5,4},{6,7},{7,6},{8,9},{9,8},{10,11... | collective-permute-start | bytes 49160 | tf_op jit(solution)/shard_map/ppermute | solution.py:577
  25.1 3.2 %collective-permute-start.7 = (f32[32,128]{1,0:T(8,128)S(1)}, f32[32,128]{1,0:T(8,128)S(1)}, u32[]{:S(2)}, u32[]{:S(2)}) collective-permute-start(f32[32,128]{1,0:T(8,128)S(1)} %get-tuple-element.72), channel_id=1, source_target_pairs={{0,3},{1,2},{2,1},{3,0},{4,7},{5,6},{6,5},{7,4},{8,11},{9,10},{10,... | collective-permute-start | bytes 49160 | tf_op jit(solution)/shard_map/ppermute | solution.py:577
  30.1 3.7 %collective-permute-start.10 = (f32[8,256]{1,0:T(8,128)S(1)}, f32[8,256]{1,0:T(8,128)S(1)}, u32[]{:S(2)}, u32[]{:S(2)}) collective-permute-start(f32[8,256]{1,0:T(8,128)S(1)} %get-tuple-element.77.message_ref), channel_id=1, source_target_pairs={{0,4},{4,0},{8,12},{12,8},{16,20},{20,16},{24,28},{28,24},{1,5},{5... | collective-permute-start | bytes 24584 | tf_op jit(solution)/shard_map/ppermute | solution.py:577
  30.2 6.4 %collective-permute-start.11 = (f32[8,256]{1,0:T(8,128)S(1)}, f32[8,256]{1,0:T(8,128)S(1)}, u32[]{:S(2)}, u32[]{:S(2)}) collective-permute-start(f32[8,256]{1,0:T(8,128)S(1)} %get-tuple-element.77.message_ref), channel_id=1, source_target_pairs={{0,28},{4,8},{8,4},{12,16},{16,12},{20,24},{24,20},{28,0},{1,29},{... | collective-permute-start | bytes 24584 | tf_op jit(solution)/shard_map/ppermute | solution.py:577
  36.8 7.4 %collective-permute-start.15 = (f32[16,16,128]{2,1,0:T(8,128)S(1)}, f32[16,16,128]{2,1,0:T(8,128)S(1)}, u32[]{:S(2)}, u32[]{:S(2)}) collective-permute-start(f32[16,16,128]{2,1,0:T(8,128)S(1)} %get-tuple-element.83.near_ref), channel_id=1, source_target_pairs={{0,4},{4,0},{8,12},{12,8},{16,20},{20,16},{24,28},{28,24},{1,5},{5... | collective-permute-start | bytes 393224 | tf_op jit(solution)/shard_map/ppermute | solution.py:577
  37.0 7.7 %collective-permute-start.14 = (f32[16,16,128]{2,1,0:T(8,128)S(1)}, f32[16,16,128]{2,1,0:T(8,128)S(1)}, u32[]{:S(2)}, u32[]{:S(2)}) collective-permute-start(f32[16,16,128]{2,1,0:T(8,128)S(1)} %get-tuple-element.80.far_ref), channel_id=1, source_target_pairs={{0,28},{4,8},{8,4},{12,16},{16,12},{20,24},{24,20},{28,0},{1,29},{... | collective-permute-start | bytes 393224 | tf_op jit(solution)/shard_map/ppermute | solution.py:577
  40.1 2.1 %collective-permute-start.12 = (f32[32,128]{1,0:T(8,128)S(1)}, f32[32,128]{1,0:T(8,128)S(1)}, u32[]{:S(2)}, u32[]{:S(2)}) collective-permute-start(f32[32,128]{1,0:T(8,128)S(1)} %get-tuple-element.85), channel_id=1, source_target_pairs={{0,1},{1,0},{2,3},{3,2},{4,5},{5,4},{6,7},{7,6},{8,9},{9,8},{10,11... | collective-permute-start | bytes 49160 | tf_op jit(solution)/shard_map/ppermute | solution.py:577
  40.2 3.2 %collective-permute-start.13 = (f32[32,128]{1,0:T(8,128)S(1)}, f32[32,128]{1,0:T(8,128)S(1)}, u32[]{:S(2)}, u32[]{:S(2)}) collective-permute-start(f32[32,128]{1,0:T(8,128)S(1)} %get-tuple-element.86), channel_id=1, source_target_pairs={{0,3},{1,2},{2,1},{3,0},{4,7},{5,6},{6,5},{7,4},{8,11},{9,10},{10,... | collective-permute-start | bytes 49160 | tf_op jit(solution)/shard_map/ppermute | solution.py:577
  45.1 3.7 %collective-permute-start.16 = (f32[8,256]{1,0:T(8,128)S(1)}, f32[8,256]{1,0:T(8,128)S(1)}, u32[]{:S(2)}, u32[]{:S(2)}) collective-permute-start(f32[8,256]{1,0:T(8,128)S(1)} %get-tuple-element.91.message_ref), channel_id=1, source_target_pairs={{0,4},{4,0},{8,12},{12,8},{16,20},{20,16},{24,28},{28,24},{1,5},{5... | collective-permute-start | bytes 24584 | tf_op jit(solution)/shard_map/ppermute | solution.py:577
  46.0 6.3 %collective-permute-start.17 = (f32[8,256]{1,0:T(8,128)S(1)}, f32[8,256]{1,0:T(8,128)S(1)}, u32[]{:S(2)}, u32[]{:S(2)}) collective-permute-start(f32[8,256]{1,0:T(8,128)S(1)} %get-tuple-element.91.message_ref), channel_id=1, source_target_pairs={{0,28},{4,8},{8,4},{12,16},{16,12},{20,24},{24,20},{28,0},{1,29},{... | collective-permute-start | bytes 24584 | tf_op jit(solution)/shard_map/ppermute | solution.py:577

commit v8 on v7

--- a/solution.py
+++ b/solution.py
@@ -458,27 +458,33 @@
         velocity_ref[:, at] = TRANSLATE * totals * inverse
 
 
-def layer_motion(velocity_ref, block_ref, layer, yb):
-    xb = block_ref.shape[1]
-    slot = block_ref[layer * yb : (layer + 1) * yb, :]
-    within = slot & (xb - 1)
+def motion_at(velocity_ref, slot):
+    lanes = slot.shape[1]
+    within = slot & (lanes - 1)
     motion = []
     for k in range(4):
         value = None
-        for part in range(velocity_ref.shape[1] // xb):
-            table = jnp.broadcast_to(velocity_ref[k : k + 1, part * xb : (part + 1) * xb], slot.shape)
+        for start in range(0, velocity_ref.shape[1], lanes):
+            table = jnp.broadcast_to(velocity_ref[k : k + 1, start : start + lanes], slot.shape)
             found = jnp.take_along_axis(table, within, axis=1, mode="promise_in_bounds")
-            value = found if value is None else jnp.where(slot >= part * xb, found, value)
+            value = found if value is None else jnp.where(slot >= start, found, value)
         motion.append(value)
     return motion
 
 
+def layer_motion(velocity_ref, block_ref, layer, yb):
+    return motion_at(velocity_ref, block_ref[layer * yb : (layer + 1) * yb, :])
+
+
+def moved_on(local, motion):
+    vx, vy, vz, turn = motion
+    e = local[0] - (vx * local[2] + vy * local[3] + vz * local[4])
+    q = local[1] + turn - (vx * local[5] + vy * local[6] + vz * local[7])
+    return e, q
+
+
 def advanced(local_ref, motion, at, p, j):
-    vx, vy, vz, turn = motion
-    g = [local_ref[k, at, p, j] for k in range(2, 8)]
-    e = local_ref[0, at, p, j] - (vx * g[0] + vy * g[1] + vz * g[2])
-    q = local_ref[1, at, p, j] + turn - (vx * g[3] + vy * g[4] + vz * g[5])
-    return e, q
+    return moved_on([local_ref[k, at, p, j] for k in range(8)], motion)
 
 
 def advance_outer_kernel(
@@ -506,45 +512,54 @@
     put_y_edges(near_ref, far_ref, inner_ref, y_near_ref, y_far_ref)
 
 
+def natural_kernel(outer_local_ref, inner_local_ref, back_ref, natural_ref, widen_ref, rows_ref):
+    fields, cz, cy, nx = natural_ref.shape
+    yb, xb = outer_local_ref.shape[4:]
+    group = rows_ref.shape[0]
+    x = lax.broadcasted_iota(jnp.int32, (xb, nx), 1)
+    wide = jnp.where(x // COLS == lax.broadcasted_iota(jnp.int32, (xb, nx), 0), 1.0, 0.0).astype(jnp.bfloat16)
+    for part in range(3):
+        widen_ref[part * xb : (part + 1) * xb, :] = wide
+    for first in range(0, fields, group):
+        for f in range(group):
+            for layer in range(cz):
+                ref, inside = (outer_local_ref, layer) if layer < 2 else (inner_local_ref, layer - 2)
+                for p in range(ROWS):
+                    for j in range(COLS):
+                        rows_ref[f, j, pl.ds(layer * cy + p, yb, stride=ROWS), :] = ref[first + f, inside, p, j]
+        moved = exact_dot(
+            jnp.concatenate(
+                [jnp.concatenate([rows_ref[f, j] for j in range(COLS)], axis=1) for f in range(group)], axis=0
+            ),
+            back_ref[...],
+        )
+        for f in range(group):
+            natural_ref[first + f] = moved[f * cz * cy : (f + 1) * cz * cy].reshape(cz, cy, nx)
+
+
 def finish_kernel(
-    message_ref, near_message_ref, far_message_ref, match_ref, back_ref, block_ref, outer_local_ref, inner_local_ref,
+    message_ref, near_message_ref, far_message_ref, match_ref, block_ref, natural_ref, widen_ref,
     e_hbm, q_hbm,
     velocity_ref, rows_ref, out_ref, sems,
 ):
-    yb, xb = outer_local_ref.shape[4:]
     _, cz, cy, nx = out_ref.shape
+    xb = nx // COLS
     slot_motion(message_ref, near_message_ref, far_message_ref, match_ref, velocity_ref, xb)
-    chooser = back_ref[...]
+    for layer in range(cz):
+        for k, value in enumerate(layer_motion(velocity_ref, block_ref, layer, cy // ROWS)):
+            for p in range(ROWS):
+                rows_ref[pl.ds((layer * 4 + k) * cy + p, cy // ROWS, stride=ROWS), :] = value
     copies = []
-    for first, count in [(layer, 1) for layer in range(cz)]:
-        for at in range(count):
-            layer = first + at
-            motion = layer_motion(velocity_ref, block_ref, layer, yb)
-            local_ref, inside = (outer_local_ref, layer) if layer < 2 else (inner_local_ref, layer - 2)
-            for p in range(ROWS):
-                to = pl.ds(at * cy + p, yb, stride=ROWS)
-                for j in range(COLS):
-                    e, q = advanced(local_ref, motion, inside, p, j)
-                    rows_ref[0, j, to, :] = e
-                    rows_ref[1, j, to, :] = q
-        moved = exact_dot(
-            jnp.concatenate(
-                [
-                    jnp.concatenate([rows_ref[f, j, : count * cy, :] for j in range(COLS)], axis=1)
-                    for f in range(2)
-                ],
-                axis=0,
-            ),
-            chooser,
-        )
-        for f, ref in enumerate((e_hbm, q_hbm)):
-            for at in range(count):
-                layer = first + at
-                start = (f * count + at) * cy
-                out_ref[f, layer] = moved[start : start + cy]
-                copies.append(
-                    pltpu.make_async_copy(out_ref.at[f, layer], ref.at[place(layer, cz)], sems.at[f, layer])
-                )
+    group = 1
+    for first in range(0, cz, group):
+        rows = rows_ref[first * 4 * cy : (first + group) * 4 * cy, :]
+        wide = jnp.dot(jnp.concatenate(split3(rows), axis=1), widen_ref[...], preferred_element_type=jnp.float32)
+        for layer in range(first, first + group):
+            start = (layer - first) * 4
+            motion = [wide[(start + k) * cy : (start + k + 1) * cy] for k in range(4)]
+            out_ref[0, layer], out_ref[1, layer] = moved_on([natural_ref[k, layer] for k in range(8)], motion)
+            for f, ref in enumerate((e_hbm, q_hbm)):
+                copies.append(pltpu.make_async_copy(out_ref.at[f, layer], ref.at[place(layer, cz)], sems.at[f, layer]))
                 copies[-1].start()
     for copy in copies:
         copy.wait()
@@ -626,11 +641,12 @@
         advance_outer_kernel, "advance_outer", [((8, slots), f32), side_out, side_out]
     )
     advance_inner = call(advance_inner_kernel, "advance_inner", [inner_out] + y_out)
+    naturals = call(
+        natural_kernel, "naturals", [((8, cz, cy, nx), f32), ((3 * xb, nx), bf16)], [pltpu.VMEM((2, COLS, cz * cy, xb), f32)]
+    )
     finish = call(
         finish_kernel, "finish", [((cz, cy, nx), f32)] * 2,
-        [
-            pltpu.VMEM((8, slots), f32), pltpu.VMEM((2, COLS, cy, xb), f32), pltpu.VMEM((2, cz, cy, nx), f32), dma((2, cz)),
-        ],
+        [pltpu.VMEM((8, slots), f32), pltpu.VMEM((4 * cz * cy, xb), f32), pltpu.VMEM((2, cz, cy, nx), f32), dma((2, cz))],
         hbm_out=True,
     )
 
@@ -657,7 +673,8 @@
         (outer_local,) = outer_locals(near, far, inner, trig, rim, near_halo, far_halo, near_mixed, far_mixed)
         if step < STEPS - 1:
             velocity, near, far = advance_outer(message, near_message, far_message, match, blocks, outer_local)
-    return tuple(finish(message, near_message, far_message, match, back, blocks, outer_local, inner_local))
+    natural, widen = naturals(outer_local, inner_local, back)
+    return tuple(finish(message, near_message, far_message, match, blocks, natural, widen))
 
 
 def solution(mesh):

time: 54 us -> 53.8 us (level)
  waiting for transfers between devices: 12.2 us -> 10.3 us
  Pallas kernels: 12.4 us -> 14.1 us
    ppermute x18, waiting for transfers between devices: 12.2 us -> 10.3 us  [swap(): return lax.ppermute(array, axis, pairs)]
    pallas_call x24 -> x25, Pallas kernels: 12.4 us -> 14.1 us  [run(): pl.pallas_call(kernel, name=name, in_specs=[HBM] * hbm_in + [VMEM] * (len...]
  transfers between devices with their start and end apart: 18 -> 18, of which waited for: 8 -> 7; matrix products, arithmetic and copies ran while one was open for 0% -> 0% of each run, Pallas kernels for 14% -> 18%
where the time goes in v8:
time: 53.8 us; the launch traced here: 53.7 us
  starting transfers between devices  28.4 us (53%)
  Pallas kernels  14.1 us (26%)
  waiting for transfers between devices  10.3 us (19%)
  between operations  0.83 us (2%)
    ppermute x18, starting transfers between devices, swap(): return lax.ppermute(array, axis, pairs)  28.4 us
    pallas_call x25, Pallas kernels, run(): pl.pallas_call(kernel, name=name, in_specs=[HBM] * hbm_in + [VMEM] * (len...  14.1 us
    ppermute x18, waiting for transfers between devices, swap(): return lax.ppermute(array, axis, pairs)  10.3 us
  transfers between devices with their start and end apart: 18, of which 7 were waited for; matrix products, arithmetic and copies ran while one was open for 0% of the time, Pallas kernels for 18%

profile of v8, /device:TPU:0, one launch (start us, length us, event | category | flops | bytes accessed | tf_op | source)
XLA Modules:
  0.0 53.7 jit_solution(8145791041855600369)
XLA Ops:
  0.6 1.6 %prepare_outer.1 = (f32[17,16,128]{2,1,0:T(8,128)S(1)}, f32[17,16,128]{2,1,0:T(8,128)S(1)}, f32[2,2,32,512]{3,2,1,0:T(8,128)S(1)}, s32[4,32,512]{2,1,0:T(8,128)S(1)}, s32[1,256]{1,0:T(1,128)S(1)}) custom-call(f32[4,32,512]{2,1,0:T(8,128)} %e_hbm.1, f32[4,32,512]{2,1,0:T(8,128)} %q_hbm.1, s32[4,32,512]{2,1,0:T(8,128)} %slot_hbm.1, s32[1,256]{1,0:T(1,128)} %bitcast.1), custom_call_target="tpu_custom_call" | custom-call | flops 4194304 | bytes 1048576 | tf_op jit(solution)/shard_map/prepare_outer/pallas_call | solution.py:575
  2.2 3.0 %collective-permute-start.3 = (f32[17,16,128]{2,1,0:T(8,128)S(1)}, f32[17,16,128]{2,1,0:T(8,128)S(1)}, u32[]{:S(2)}, u32[]{:S(2)}) collective-permute-start(f32[17,16,128]{2,1,0:T(8,128)S(1)} %get-tuple-element.54.near_ref), channel_id=1, source_target_pairs={{0,4},{4,0},{8,12},{12,8},{16,20},{20,16},{24,28},{28,24},{1,5},{5... | collective-permute-start | bytes 417800 | tf_op jit(solution)/shard_map/ppermute | solution.py:592
  5.2 3.5 %collective-permute-start.2 = (f32[17,16,128]{2,1,0:T(8,128)S(1)}, f32[17,16,128]{2,1,0:T(8,128)S(1)}, u32[]{:S(2)}, u32[]{:S(2)}) collective-permute-start(f32[17,16,128]{2,1,0:T(8,128)S(1)} %get-tuple-element.51.far_ref), channel_id=1, source_target_pairs={{0,28},{4,8},{8,4},{12,16},{16,12},{20,24},{24,20},{28,0},{1,29},{... | collective-permute-start | bytes 417800 | tf_op jit(solution)/shard_map/ppermute | solution.py:592
  8.8 0.4 prepare_inner.1
  9.2 0.1 collective-permute-start
  9.3 1.6 %collective-permute-start.1 = (f32[32,128]{1,0:T(8,128)S(1)}, f32[32,128]{1,0:T(8,128)S(1)}, u32[]{:S(2)}, u32[]{:S(2)}) collective-permute-start(f32[32,128]{1,0:T(8,128)S(1)} %get-tuple-element.57), channel_id=1, source_target_pairs={{0,3},{1,2},{2,1},{3,0},{4,7},{5,6},{6,5},{7,4},{8,11},{9,10},{10,... | collective-permute-start | bytes 49160 | tf_op jit(solution)/shard_map/ppermute | solution.py:592
  10.9 0.4 trigs.3.trig_ref
  11.3 0.9 %choosers.1.chooser_ref = bf16[32,256,256]{2,1,0:T(8,128)(2,1)S(1)} custom-call(s32[64,128]{1,0:T(8,128)S(1)} %get-tuple-element.58.block_ref), custom_call_target="tpu_custom_call" | custom-call | flops 4194304 | bytes 1048576 | tf_op jit(solution)/shard_map/choosers/pallas_call | solution.py:575
  12.2 0.0 collective-permute-done.y_near_ref
  12.3 0.3 collective-permute-done.1.y_far_ref
  12.5 0.8 %inner_terms.3 = (f32[2,6,16,128]{3,2,1,0:T(8,128)S(1)}, f32[8,2,2,4,16,128]{5,4,3,2,1,0:T(8,128)S(1)}, f32[16,256]{1,0:T(8,128)S(1)}, f32[6,2,4,16,128]{4,3,2,1,0:T(8,128)S(1)}) custom-call(f32[17,16,128]{2,1,0:T(8,128)S(1)} %get-tuple-element.54.near_ref, f32[17,16,128]{2,1,0:T(8,128)S(1)} %get-tuple-element.51.far_ref, ...), custom_call_target="tpu_custom_call" | custom-call | flops 4194304 | bytes 1048576 | tf_op jit(solution)/shard_map/inner_terms/pallas_call | solution.py:575
  13.4 0.0 collective-permute-done.3.halo_ref.near_halo_ref
  13.4 0.5 near_terms.3
  13.9 0.0 collective-permute-done.2.halo_ref.far_halo_ref
  13.9 0.4 far_terms.3
  14.3 0.3 collective-permute-start.4
  14.6 3.5 %collective-permute-start.5 = (f32[8,256]{1,0:T(8,128)S(1)}, f32[8,256]{1,0:T(8,128)S(1)}, u32[]{:S(2)}, u32[]{:S(2)}) collective-permute-start(f32[8,256]{1,0:T(8,128)S(1)} %get-tuple-element.63.message_ref), channel_id=1, source_target_pairs={{0,28},{4,8},{8,4},{12,16},{16,12},{20,24},{24,20},{28,0},{1,29},{... | collective-permute-start | bytes 24584 | tf_op jit(solution)/shard_map/ppermute | solution.py:592
  18.1 0.3 matches.1
  18.5 0.2 outer_locals.3.local_ref
  18.7 0.0 collective-permute-done.4.near_message_ref
  18.7 2.3 %collective-permute-done.5.far_message_ref = f32[8,256]{1,0:T(8,128)S(1)} collective-permute-done((f32[8,256]{1,0:T(8,128)S(1)}, f32[8,256]{1,0:T(8,128)S(1)}, u32[]{:S(2)}, u32[]{:S(2)}) %collective-permute-start.5) | collective-permute-done | bytes 8224 | tf_op jit(solution)/shard_map/ppermute | solution.py:592
  20.9 0.2 advance_outer.2
  21.2 0.1 collective-permute-start.9
  21.3 3.6 %collective-permute-start.8 = (f32[16,16,128]{2,1,0:T(8,128)S(1)}, f32[16,16,128]{2,1,0:T(8,128)S(1)}, u32[]{:S(2)}, u32[]{:S(2)}) collective-permute-start(f32[16,16,128]{2,1,0:T(8,128)S(1)} %get-tuple-element.68.far_ref), channel_id=1, source_target_pairs={{0,28},{4,8},{8,4},{12,16},{16,12},{20,24},{24,20},{28,0},{1,29},{... | collective-permute-start | bytes 393224 | tf_op jit(solution)/shard_map/ppermute | solution.py:592
  24.9 0.2 advance_inner.2
  25.0 0.1 collective-permute-start.6
  25.1 1.6 %collective-permute-start.7 = (f32[32,128]{1,0:T(8,128)S(1)}, f32[32,128]{1,0:T(8,128)S(1)}, u32[]{:S(2)}, u32[]{:S(2)}) collective-permute-start(f32[32,128]{1,0:T(8,128)S(1)} %get-tuple-element.74), channel_id=1, source_target_pairs={{0,3},{1,2},{2,1},{3,0},{4,7},{5,6},{6,5},{7,4},{8,11},{9,10},{10,... | collective-permute-start | bytes 49160 | tf_op jit(solution)/shard_map/ppermute | solution.py:592
  26.7 0.4 trigs.4.trig_ref
  27.1 0.0 collective-permute-done.6.y_near_ref
  27.1 1.2 %collective-permute-done.7.y_far_ref = f32[32,128]{1,0:T(8,128)S(1)} collective-permute-done((f32[32,128]{1,0:T(8,128)S(1)}, f32[32,128]{1,0:T(8,128)S(1)}, u32[]{:S(2)}, u32[]{:S(2)}) %collective-permute-start.7) | collective-permute-done | bytes 16416 | tf_op jit(solution)/shard_map/ppermute | solution.py:592
  28.4 0.8 %inner_terms.4 = (f32[2,6,16,128]{3,2,1,0:T(8,128)S(1)}, f32[8,2,2,4,16,128]{5,4,3,2,1,0:T(8,128)S(1)}, f32[16,256]{1,0:T(8,128)S(1)}, f32[6,2,4,16,128]{4,3,2,1,0:T(8,128)S(1)}) custom-call(f32[16,16,128]{2,1,0:T(8,128)S(1)} %get-tuple-element.71.near_ref, f32[16,16,128]{2,1,0:T(8,128)S(1)} %get-tuple-element.68.far_ref, ...), custom_call_target="tpu_custom_call" | custom-call | flops 4194304 | bytes 1048576 | tf_op jit(solution)/shard_map/inner_terms/pallas_call | solution.py:575
  29.2 0.0 collective-permute-done.9.halo_ref.near_halo_ref
  29.2 0.5 near_terms.4
  29.7 0.0 collective-permute-done.8.halo_ref.far_halo_ref
  29.7 0.4 far_terms.4
  30.1 0.1 collective-permute-start.10
  30.2 3.0 %collective-permute-start.11 = (f32[8,256]{1,0:T(8,128)S(1)}, f32[8,256]{1,0:T(8,128)S(1)}, u32[]{:S(2)}, u32[]{:S(2)}) collective-permute-start(f32[8,256]{1,0:T(8,128)S(1)} %get-tuple-element.79.message_ref), channel_id=1, source_target_pairs={{0,28},{4,8},{8,4},{12,16},{16,12},{20,24},{24,20},{28,0},{1,29},{... | collective-permute-start | bytes 24584 | tf_op jit(solution)/shard_map/ppermute | solution.py:592
  33.2 0.2 outer_locals.4.local_ref
  33.4 0.4 collective-permute-done.10.near_message_ref
  33.8 2.8 %collective-permute-done.11.far_message_ref = f32[8,256]{1,0:T(8,128)S(1)} collective-permute-done((f32[8,256]{1,0:T(8,128)S(1)}, f32[8,256]{1,0:T(8,128)S(1)}, u32[]{:S(2)}, u32[]{:S(2)}) %collective-permute-start.11) | collective-permute-done | bytes 8224 | tf_op jit(solution)/shard_map/ppermute | solution.py:592
  36.6 0.2 advance_outer.3
  36.8 0.2 collective-permute-start.15
  37.0 2.9 %collective-permute-start.14 = (f32[16,16,128]{2,1,0:T(8,128)S(1)}, f32[16,16,128]{2,1,0:T(8,128)S(1)}, u32[]{:S(2)}, u32[]{:S(2)}) collective-permute-start(f32[16,16,128]{2,1,0:T(8,128)S(1)} %get-tuple-element.82.far_ref), channel_id=1, source_target_pairs={{0,28},{4,8},{8,4},{12,16},{16,12},{20,24},{24,20},{28,0},{1,29},{... | collective-permute-start | bytes 393224 | tf_op jit(solution)/shard_map/ppermute | solution.py:592
  39.9 0.2 advance_inner.3
  40.1 0.1 collective-permute-start.12
  40.2 1.6 %collective-permute-start.13 = (f32[32,128]{1,0:T(8,128)S(1)}, f32[32,128]{1,0:T(8,128)S(1)}, u32[]{:S(2)}, u32[]{:S(2)}) collective-permute-start(f32[32,128]{1,0:T(8,128)S(1)} %get-tuple-element.88), channel_id=1, source_target_pairs={{0,3},{1,2},{2,1},{3,0},{4,7},{5,6},{6,5},{7,4},{8,11},{9,10},{10,... | collective-permute-start | bytes 49160 | tf_op jit(solution)/shard_map/ppermute | solution.py:592
  41.8 0.4 trigs.5.trig_ref
  42.1 0.0 collective-permute-done.12.y_near_ref
  42.2 1.2 %collective-permute-done.13.y_far_ref = f32[32,128]{1,0:T(8,128)S(1)} collective-permute-done((f32[32,128]{1,0:T(8,128)S(1)}, f32[32,128]{1,0:T(8,128)S(1)}, u32[]{:S(2)}, u32[]{:S(2)}) %collective-permute-start.13) | collective-permute-done | bytes 16416 | tf_op jit(solution)/shard_map/ppermute | solution.py:592
  43.4 0.8 %inner_terms.5 = (f32[2,6,16,128]{3,2,1,0:T(8,128)S(1)}, f32[8,2,2,4,16,128]{5,4,3,2,1,0:T(8,128)S(1)}, f32[16,256]{1,0:T(8,128)S(1)}, f32[6,2,4,16,128]{4,3,2,1,0:T(8,128)S(1)}) custom-call(f32[16,16,128]{2,1,0:T(8,128)S(1)} %get-tuple-element.85.near_ref, f32[16,16,128]{2,1,0:T(8,128)S(1)} %get-tuple-element.82.far_ref, ...), custom_call_target="tpu_custom_call" | custom-call | flops 4194304 | bytes 1048576 | tf_op jit(solution)/shard_map/inner_terms/pallas_call | solution.py:575
  44.2 0.0 collective-permute-done.15.halo_ref.near_halo_ref
  44.2 0.5 near_terms.5
  44.7 0.0 collective-permute-done.14.halo_ref.far_halo_ref
  44.7 0.4 far_terms.5
  45.1 0.8 %collective-permute-start.16 = (f32[8,256]{1,0:T(8,128)S(1)}, f32[8,256]{1,0:T(8,128)S(1)}, u32[]{:S(2)}, u32[]{:S(2)}) collective-permute-start(f32[8,256]{1,0:T(8,128)S(1)} %get-tuple-element.93.message_ref), channel_id=1, source_target_pairs={{0,4},{4,0},{8,12},{12,8},{16,20},{20,16},{24,28},{28,24},{1,5},{5... | collective-permute-start | bytes 24584 | tf_op jit(solution)/shard_map/ppermute | solution.py:592
  45.9 2.3 %collective-permute-start.17 = (f32[8,256]{1,0:T(8,128)S(1)}, f32[8,256]{1,0:T(8,128)S(1)}, u32[]{:S(2)}, u32[]{:S(2)}) collective-permute-start(f32[8,256]{1,0:T(8,128)S(1)} %get-tuple-element.93.message_ref), channel_id=1, source_target_pairs={{0,28},{4,8},{8,4},{12,16},{16,12},{20,24},{24,20},{28,0},{1,29},{... | collective-permute-start | bytes 24584 | tf_op jit(solution)/shard_map/ppermute | solution.py:592
  48.2 0.2 outer_locals.5.outer_local_ref
  48.4 1.9 %naturals.1 = (f32[8,4,32,512]{3,2,1,0:T(8,128)S(1)}, bf16[384,512]{1,0:T(8,128)(2,1)S(1)}) custom-call(f32[8,2,2,4,16,128]{5,4,3,2,1,0:T(8,128)S(1)} %outer_locals.5.outer_local_ref, f32[8,2,2,4,16,128]{5,4,3,2,1,0:T(8,128)S(1)} %get-tuple-element.96.inner_local_ref, bf16[512,512]{1,0:T(8,128)(2,1)S(1)} %get-tuple-element.97.back_ref), custom_call_target="tpu_custom_call" | custom-call | flops 4194304 | bytes 1048576 | tf_op jit(solution)/shard_map/naturals/pallas_call | solution.py:575
  50.3 0.0 collective-permute-done.16.near_message_ref
  50.3 2.0 %collective-permute-done.17.far_message_ref = f32[8,256]{1,0:T(8,128)S(1)} collective-permute-done((f32[8,256]{1,0:T(8,128)S(1)}, f32[8,256]{1,0:T(8,128)S(1)}, u32[]{:S(2)}, u32[]{:S(2)}) %collective-permute-start.17) | collective-permute-done | bytes 8224 | tf_op jit(solution)/shard_map/ppermute | solution.py:592
  52.3 1.4 %finish.1 = (f32[4,32,512]{2,1,0:T(8,128)}, f32[4,32,512]{2,1,0:T(8,128)}) custom-call(f32[8,256]{1,0:T(8,128)S(1)} %get-tuple-element.93.message_ref, f32[8,256]{1,0:T(8,128)S(1)} %collective-permute-done.16.near_message_ref, f32[8,256]{1,0:T(8,128)S(1)} %collective-permute-done.17.far_message_ref, s32[2,8,256]{2,1,0:T(8,128)S(1)} %get-tuple-element.65.match_ref, ...), custom_call_target="tpu_custom_call" | custom-call | flops 4194304 | bytes 1048576 | tf_op jit(solution)/shard_map/finish/pallas_call | solution.py:575
Async XLA Ops:
  2.2 11.2 %collective-permute-start.3 = (f32[17,16,128]{2,1,0:T(8,128)S(1)}, f32[17,16,128]{2,1,0:T(8,128)S(1)}, u32[]{:S(2)}, u32[]{:S(2)}) collective-permute-start(f32[17,16,128]{2,1,0:T(8,128)S(1)} %get-tuple-element.54.near_ref), channel_id=1, source_target_pairs={{0,4},{4,0},{8,12},{12,8},{16,20},{20,16},{24,28},{28,24},{1,5},{5... | collective-permute-start | bytes 417800 | tf_op jit(solution)/shard_map/ppermute | solution.py:592
  5.2 8.6 %collective-permute-start.2 = (f32[17,16,128]{2,1,0:T(8,128)S(1)}, f32[17,16,128]{2,1,0:T(8,128)S(1)}, u32[]{:S(2)}, u32[]{:S(2)}) collective-permute-start(f32[17,16,128]{2,1,0:T(8,128)S(1)} %get-tuple-element.51.far_ref), channel_id=1, source_target_pairs={{0,28},{4,8},{8,4},{12,16},{16,12},{20,24},{24,20},{28,0},{1,29},{... | collective-permute-start | bytes 417800 | tf_op jit(solution)/shard_map/ppermute | solution.py:592
  9.2 3.0 %collective-permute-start = (f32[32,128]{1,0:T(8,128)S(1)}, f32[32,128]{1,0:T(8,128)S(1)}, u32[]{:S(2)}, u32[]{:S(2)}) collective-permute-start(f32[32,128]{1,0:T(8,128)S(1)} %get-tuple-element.56), channel_id=1, source_target_pairs={{0,1},{1,0},{2,3},{3,2},{4,5},{5,4},{6,7},{7,6},{8,9},{9,8},{10,11... | collective-permute-start | bytes 49160 | tf_op jit(solution)/shard_map/ppermute | solution.py:592
  9.3 3.2 %collective-permute-start.1 = (f32[32,128]{1,0:T(8,128)S(1)}, f32[32,128]{1,0:T(8,128)S(1)}, u32[]{:S(2)}, u32[]{:S(2)}) collective-permute-start(f32[32,128]{1,0:T(8,128)S(1)} %get-tuple-element.57), channel_id=1, source_target_pairs={{0,3},{1,2},{2,1},{3,0},{4,7},{5,6},{6,5},{7,4},{8,11},{9,10},{10,... | collective-permute-start | bytes 49160 | tf_op jit(solution)/shard_map/ppermute | solution.py:592
  14.3 4.4 %collective-permute-start.4 = (f32[8,256]{1,0:T(8,128)S(1)}, f32[8,256]{1,0:T(8,128)S(1)}, u32[]{:S(2)}, u32[]{:S(2)}) collective-permute-start(f32[8,256]{1,0:T(8,128)S(1)} %get-tuple-element.63.message_ref), channel_id=1, source_target_pairs={{0,4},{4,0},{8,12},{12,8},{16,20},{20,16},{24,28},{28,24},{1,5},{5... | collective-permute-start | bytes 24584 | tf_op jit(solution)/shard_map/ppermute | solution.py:592
  14.6 6.3 %collective-permute-start.5 = (f32[8,256]{1,0:T(8,128)S(1)}, f32[8,256]{1,0:T(8,128)S(1)}, u32[]{:S(2)}, u32[]{:S(2)}) collective-permute-start(f32[8,256]{1,0:T(8,128)S(1)} %get-tuple-element.63.message_ref), channel_id=1, source_target_pairs={{0,28},{4,8},{8,4},{12,16},{16,12},{20,24},{24,20},{28,0},{1,29},{... | collective-permute-start | bytes 24584 | tf_op jit(solution)/shard_map/ppermute | solution.py:592
  21.2 8.0 %collective-permute-start.9 = (f32[16,16,128]{2,1,0:T(8,128)S(1)}, f32[16,16,128]{2,1,0:T(8,128)S(1)}, u32[]{:S(2)}, u32[]{:S(2)}) collective-permute-start(f32[16,16,128]{2,1,0:T(8,128)S(1)} %get-tuple-element.71.near_ref), channel_id=1, source_target_pairs={{0,4},{4,0},{8,12},{12,8},{16,20},{20,16},{24,28},{28,24},{1,5},{5... | collective-permute-start | bytes 393224 | tf_op jit(solution)/shard_map/ppermute | solution.py:592
  21.3 8.4 %collective-permute-start.8 = (f32[16,16,128]{2,1,0:T(8,128)S(1)}, f32[16,16,128]{2,1,0:T(8,128)S(1)}, u32[]{:S(2)}, u32[]{:S(2)}) collective-permute-start(f32[16,16,128]{2,1,0:T(8,128)S(1)} %get-tuple-element.68.far_ref), channel_id=1, source_target_pairs={{0,28},{4,8},{8,4},{12,16},{16,12},{20,24},{24,20},{28,0},{1,29},{... | collective-permute-start | bytes 393224 | tf_op jit(solution)/shard_map/ppermute | solution.py:592
  25.0 2.1 %collective-permute-start.6 = (f32[32,128]{1,0:T(8,128)S(1)}, f32[32,128]{1,0:T(8,128)S(1)}, u32[]{:S(2)}, u32[]{:S(2)}) collective-permute-start(f32[32,128]{1,0:T(8,128)S(1)} %get-tuple-element.73), channel_id=1, source_target_pairs={{0,1},{1,0},{2,3},{3,2},{4,5},{5,4},{6,7},{7,6},{8,9},{9,8},{10,11... | collective-permute-start | bytes 49160 | tf_op jit(solution)/shard_map/ppermute | solution.py:592
  25.1 3.2 %collective-permute-start.7 = (f32[32,128]{1,0:T(8,128)S(1)}, f32[32,128]{1,0:T(8,128)S(1)}, u32[]{:S(2)}, u32[]{:S(2)}) collective-permute-start(f32[32,128]{1,0:T(8,128)S(1)} %get-tuple-element.74), channel_id=1, source_target_pairs={{0,3},{1,2},{2,1},{3,0},{4,7},{5,6},{6,5},{7,4},{8,11},{9,10},{10,... | collective-permute-start | bytes 49160 | tf_op jit(solution)/shard_map/ppermute | solution.py:592
  30.1 3.7 %collective-permute-start.10 = (f32[8,256]{1,0:T(8,128)S(1)}, f32[8,256]{1,0:T(8,128)S(1)}, u32[]{:S(2)}, u32[]{:S(2)}) collective-permute-start(f32[8,256]{1,0:T(8,128)S(1)} %get-tuple-element.79.message_ref), channel_id=1, source_target_pairs={{0,4},{4,0},{8,12},{12,8},{16,20},{20,16},{24,28},{28,24},{1,5},{5... | collective-permute-start | bytes 24584 | tf_op jit(solution)/shard_map/ppermute | solution.py:592
  30.2 6.4 %collective-permute-start.11 = (f32[8,256]{1,0:T(8,128)S(1)}, f32[8,256]{1,0:T(8,128)S(1)}, u32[]{:S(2)}, u32[]{:S(2)}) collective-permute-start(f32[8,256]{1,0:T(8,128)S(1)} %get-tuple-element.79.message_ref), channel_id=1, source_target_pairs={{0,28},{4,8},{8,4},{12,16},{16,12},{20,24},{24,20},{28,0},{1,29},{... | collective-permute-start | bytes 24584 | tf_op jit(solution)/shard_map/ppermute | solution.py:592
  36.8 7.4 %collective-permute-start.15 = (f32[16,16,128]{2,1,0:T(8,128)S(1)}, f32[16,16,128]{2,1,0:T(8,128)S(1)}, u32[]{:S(2)}, u32[]{:S(2)}) collective-permute-start(f32[16,16,128]{2,1,0:T(8,128)S(1)} %get-tuple-element.85.near_ref), channel_id=1, source_target_pairs={{0,4},{4,0},{8,12},{12,8},{16,20},{20,16},{24,28},{28,24},{1,5},{5... | collective-permute-start | bytes 393224 | tf_op jit(solution)/shard_map/ppermute | solution.py:592
  37.0 7.7 %collective-permute-start.14 = (f32[16,16,128]{2,1,0:T(8,128)S(1)}, f32[16,16,128]{2,1,0:T(8,128)S(1)}, u32[]{:S(2)}, u32[]{:S(2)}) collective-permute-start(f32[16,16,128]{2,1,0:T(8,128)S(1)} %get-tuple-element.82.far_ref), channel_id=1, source_target_pairs={{0,28},{4,8},{8,4},{12,16},{16,12},{20,24},{24,20},{28,0},{1,29},{... | collective-permute-start | bytes 393224 | tf_op jit(solution)/shard_map/ppermute | solution.py:592
  40.1 2.1 %collective-permute-start.12 = (f32[32,128]{1,0:T(8,128)S(1)}, f32[32,128]{1,0:T(8,128)S(1)}, u32[]{:S(2)}, u32[]{:S(2)}) collective-permute-start(f32[32,128]{1,0:T(8,128)S(1)} %get-tuple-element.87), channel_id=1, source_target_pairs={{0,1},{1,0},{2,3},{3,2},{4,5},{5,4},{6,7},{7,6},{8,9},{9,8},{10,11... | collective-permute-start | bytes 49160 | tf_op jit(solution)/shard_map/ppermute | solution.py:592
  40.2 3.2 %collective-permute-start.13 = (f32[32,128]{1,0:T(8,128)S(1)}, f32[32,128]{1,0:T(8,128)S(1)}, u32[]{:S(2)}, u32[]{:S(2)}) collective-permute-start(f32[32,128]{1,0:T(8,128)S(1)} %get-tuple-element.88), channel_id=1, source_target_pairs={{0,3},{1,2},{2,1},{3,0},{4,7},{5,6},{6,5},{7,4},{8,11},{9,10},{10,... | collective-permute-start | bytes 49160 | tf_op jit(solution)/shard_map/ppermute | solution.py:592
  45.1 5.2 %collective-permute-start.16 = (f32[8,256]{1,0:T(8,128)S(1)}, f32[8,256]{1,0:T(8,128)S(1)}, u32[]{:S(2)}, u32[]{:S(2)}) collective-permute-start(f32[8,256]{1,0:T(8,128)S(1)} %get-tuple-element.93.message_ref), channel_id=1, source_target_pairs={{0,4},{4,0},{8,12},{12,8},{16,20},{20,16},{24,28},{28,24},{1,5},{5... | collective-permute-start | bytes 24584 | tf_op jit(solution)/shard_map/ppermute | solution.py:592
  45.9 6.3 %collective-permute-start.17 = (f32[8,256]{1,0:T(8,128)S(1)}, f32[8,256]{1,0:T(8,128)S(1)}, u32[]{:S(2)}, u32[]{:S(2)}) collective-permute-start(f32[8,256]{1,0:T(8,128)S(1)} %get-tuple-element.93.message_ref), channel_id=1, source_target_pairs={{0,28},{4,8},{8,4},{12,16},{16,12},{20,24},{24,20},{28,0},{1,29},{... | collective-permute-start | bytes 24584 | tf_op jit(solution)/shard_map/ppermute | solution.py:592

commit v9 on v8

--- a/solution.py
+++ b/solution.py
@@ -136,8 +136,10 @@
         pltpu.make_async_copy(q_hbm.at[1 : cz - 1], raw_ref.at[1], raw_sems.at[2]),
         pltpu.make_async_copy(slot_hbm, slot_ref, raw_sems.at[3]),
     ]
-    for copy in copies + later:
+    for copy in copies:
         copy.start()
+    for copy in later:
+        copy.start(priority=1)
     chooser = x_chooser(nx, xb)
     for copy in copies:
         copy.wait()

time: 53.8 us -> 53.7 us (level)
  no operation moved by 1% of the time
where the time goes in v9:
time: 53.7 us; the launch traced here: 53.6 us
  starting transfers between devices  28.4 us (53%)
  Pallas kernels  14 us (26%)
  waiting for transfers between devices  10.3 us (19%)
  between operations  0.83 us (2%)
    ppermute x18, starting transfers between devices, swap(): return lax.ppermute(array, axis, pairs)  28.4 us
    pallas_call x25, Pallas kernels, run(): pl.pallas_call(kernel, name=name, in_specs=[HBM] * hbm_in + [VMEM] * (len...  14 us
    ppermute x18, waiting for transfers between devices, swap(): return lax.ppermute(array, axis, pairs)  10.3 us
  transfers between devices with their start and end apart: 18, of which 7 were waited for; matrix products, arithmetic and copies ran while one was open for 0% of the time, Pallas kernels for 18%

profile of v9, /device:TPU:0, one launch (start us, length us, event | category | flops | bytes accessed | tf_op | source)
XLA Modules:
  0.0 53.6 jit_solution(12791848773397239120)
XLA Ops:
  0.6 1.5 %prepare_outer.1 = (f32[17,16,128]{2,1,0:T(8,128)S(1)}, f32[17,16,128]{2,1,0:T(8,128)S(1)}, f32[2,2,32,512]{3,2,1,0:T(8,128)S(1)}, s32[4,32,512]{2,1,0:T(8,128)S(1)}, s32[1,256]{1,0:T(1,128)S(1)}) custom-call(f32[4,32,512]{2,1,0:T(8,128)} %e_hbm.1, f32[4,32,512]{2,1,0:T(8,128)} %q_hbm.1, s32[4,32,512]{2,1,0:T(8,128)} %slot_hbm.1, s32[1,256]{1,0:T(1,128)} %bitcast.1), custom_call_target="tpu_custom_call" | custom-call | flops 4194304 | bytes 1048576 | tf_op jit(solution)/shard_map/prepare_outer/pallas_call | solution.py:577
  2.1 3.0 %collective-permute-start.3 = (f32[17,16,128]{2,1,0:T(8,128)S(1)}, f32[17,16,128]{2,1,0:T(8,128)S(1)}, u32[]{:S(2)}, u32[]{:S(2)}) collective-permute-start(f32[17,16,128]{2,1,0:T(8,128)S(1)} %get-tuple-element.54.near_ref), channel_id=1, source_target_pairs={{0,4},{4,0},{8,12},{12,8},{16,20},{20,16},{24,28},{28,24},{1,5},{5... | collective-permute-start | bytes 417800 | tf_op jit(solution)/shard_map/ppermute | solution.py:594
  5.1 3.5 %collective-permute-start.2 = (f32[17,16,128]{2,1,0:T(8,128)S(1)}, f32[17,16,128]{2,1,0:T(8,128)S(1)}, u32[]{:S(2)}, u32[]{:S(2)}) collective-permute-start(f32[17,16,128]{2,1,0:T(8,128)S(1)} %get-tuple-element.51.far_ref), channel_id=1, source_target_pairs={{0,28},{4,8},{8,4},{12,16},{16,12},{20,24},{24,20},{28,0},{1,29},{... | collective-permute-start | bytes 417800 | tf_op jit(solution)/shard_map/ppermute | solution.py:594
  8.7 0.4 prepare_inner.1
  9.1 0.1 collective-permute-start
  9.2 1.6 %collective-permute-start.1 = (f32[32,128]{1,0:T(8,128)S(1)}, f32[32,128]{1,0:T(8,128)S(1)}, u32[]{:S(2)}, u32[]{:S(2)}) collective-permute-start(f32[32,128]{1,0:T(8,128)S(1)} %get-tuple-element.57), channel_id=1, source_target_pairs={{0,3},{1,2},{2,1},{3,0},{4,7},{5,6},{6,5},{7,4},{8,11},{9,10},{10,... | collective-permute-start | bytes 49160 | tf_op jit(solution)/shard_map/ppermute | solution.py:594
  10.8 0.4 trigs.3.trig_ref
  11.2 0.9 %choosers.1.chooser_ref = bf16[32,256,256]{2,1,0:T(8,128)(2,1)S(1)} custom-call(s32[64,128]{1,0:T(8,128)S(1)} %get-tuple-element.58.block_ref), custom_call_target="tpu_custom_call" | custom-call | flops 4194304 | bytes 1048576 | tf_op jit(solution)/shard_map/choosers/pallas_call | solution.py:577
  12.1 0.0 collective-permute-done.y_near_ref
  12.2 0.3 collective-permute-done.1.y_far_ref
  12.4 0.8 %inner_terms.3 = (f32[2,6,16,128]{3,2,1,0:T(8,128)S(1)}, f32[8,2,2,4,16,128]{5,4,3,2,1,0:T(8,128)S(1)}, f32[16,256]{1,0:T(8,128)S(1)}, f32[6,2,4,16,128]{4,3,2,1,0:T(8,128)S(1)}) custom-call(f32[17,16,128]{2,1,0:T(8,128)S(1)} %get-tuple-element.54.near_ref, f32[17,16,128]{2,1,0:T(8,128)S(1)} %get-tuple-element.51.far_ref, ...), custom_call_target="tpu_custom_call" | custom-call | flops 4194304 | bytes 1048576 | tf_op jit(solution)/shard_map/inner_terms/pallas_call | solution.py:577
  13.3 0.0 collective-permute-done.3.halo_ref.near_halo_ref
  13.3 0.5 near_terms.3
  13.8 0.0 collective-permute-done.2.halo_ref.far_halo_ref
  13.8 0.4 far_terms.3
  14.2 0.3 collective-permute-start.4
  14.5 3.5 %collective-permute-start.5 = (f32[8,256]{1,0:T(8,128)S(1)}, f32[8,256]{1,0:T(8,128)S(1)}, u32[]{:S(2)}, u32[]{:S(2)}) collective-permute-start(f32[8,256]{1,0:T(8,128)S(1)} %get-tuple-element.63.message_ref), channel_id=1, source_target_pairs={{0,28},{4,8},{8,4},{12,16},{16,12},{20,24},{24,20},{28,0},{1,29},{... | collective-permute-start | bytes 24584 | tf_op jit(solution)/shard_map/ppermute | solution.py:594
  18.1 0.3 matches.1
  18.4 0.2 outer_locals.3.local_ref
  18.6 0.0 collective-permute-done.4.near_message_ref
  18.6 2.3 %collective-permute-done.5.far_message_ref = f32[8,256]{1,0:T(8,128)S(1)} collective-permute-done((f32[8,256]{1,0:T(8,128)S(1)}, f32[8,256]{1,0:T(8,128)S(1)}, u32[]{:S(2)}, u32[]{:S(2)}) %collective-permute-start.5) | collective-permute-done | bytes 8224 | tf_op jit(solution)/shard_map/ppermute | solution.py:594
  20.9 0.2 advance_outer.2
  21.1 0.1 collective-permute-start.9
  21.2 3.6 %collective-permute-start.8 = (f32[16,16,128]{2,1,0:T(8,128)S(1)}, f32[16,16,128]{2,1,0:T(8,128)S(1)}, u32[]{:S(2)}, u32[]{:S(2)}) collective-permute-start(f32[16,16,128]{2,1,0:T(8,128)S(1)} %get-tuple-element.68.far_ref), channel_id=1, source_target_pairs={{0,28},{4,8},{8,4},{12,16},{16,12},{20,24},{24,20},{28,0},{1,29},{... | collective-permute-start | bytes 393224 | tf_op jit(solution)/shard_map/ppermute | solution.py:594
  24.8 0.2 advance_inner.2
  25.0 0.1 collective-permute-start.6
  25.0 1.6 %collective-permute-start.7 = (f32[32,128]{1,0:T(8,128)S(1)}, f32[32,128]{1,0:T(8,128)S(1)}, u32[]{:S(2)}, u32[]{:S(2)}) collective-permute-start(f32[32,128]{1,0:T(8,128)S(1)} %get-tuple-element.74), channel_id=1, source_target_pairs={{0,3},{1,2},{2,1},{3,0},{4,7},{5,6},{6,5},{7,4},{8,11},{9,10},{10,... | collective-permute-start | bytes 49160 | tf_op jit(solution)/shard_map/ppermute | solution.py:594
  26.6 0.4 trigs.4.trig_ref
  27.0 0.0 collective-permute-done.6.y_near_ref
  27.0 1.2 %collective-permute-done.7.y_far_ref = f32[32,128]{1,0:T(8,128)S(1)} collective-permute-done((f32[32,128]{1,0:T(8,128)S(1)}, f32[32,128]{1,0:T(8,128)S(1)}, u32[]{:S(2)}, u32[]{:S(2)}) %collective-permute-start.7) | collective-permute-done | bytes 16416 | tf_op jit(solution)/shard_map/ppermute | solution.py:594
  28.3 0.8 %inner_terms.4 = (f32[2,6,16,128]{3,2,1,0:T(8,128)S(1)}, f32[8,2,2,4,16,128]{5,4,3,2,1,0:T(8,128)S(1)}, f32[16,256]{1,0:T(8,128)S(1)}, f32[6,2,4,16,128]{4,3,2,1,0:T(8,128)S(1)}) custom-call(f32[16,16,128]{2,1,0:T(8,128)S(1)} %get-tuple-element.71.near_ref, f32[16,16,128]{2,1,0:T(8,128)S(1)} %get-tuple-element.68.far_ref, ...), custom_call_target="tpu_custom_call" | custom-call | flops 4194304 | bytes 1048576 | tf_op jit(solution)/shard_map/inner_terms/pallas_call | solution.py:577
  29.1 0.0 collective-permute-done.9.halo_ref.near_halo_ref
  29.1 0.5 near_terms.4
  29.6 0.0 collective-permute-done.8.halo_ref.far_halo_ref
  29.6 0.4 far_terms.4
  30.0 0.1 collective-permute-start.10
  30.1 3.0 %collective-permute-start.11 = (f32[8,256]{1,0:T(8,128)S(1)}, f32[8,256]{1,0:T(8,128)S(1)}, u32[]{:S(2)}, u32[]{:S(2)}) collective-permute-start(f32[8,256]{1,0:T(8,128)S(1)} %get-tuple-element.79.message_ref), channel_id=1, source_target_pairs={{0,28},{4,8},{8,4},{12,16},{16,12},{20,24},{24,20},{28,0},{1,29},{... | collective-permute-start | bytes 24584 | tf_op jit(solution)/shard_map/ppermute | solution.py:594
  33.1 0.2 outer_locals.4.local_ref
  33.3 0.4 collective-permute-done.10.near_message_ref
  33.7 2.8 %collective-permute-done.11.far_message_ref = f32[8,256]{1,0:T(8,128)S(1)} collective-permute-done((f32[8,256]{1,0:T(8,128)S(1)}, f32[8,256]{1,0:T(8,128)S(1)}, u32[]{:S(2)}, u32[]{:S(2)}) %collective-permute-start.11) | collective-permute-done | bytes 8224 | tf_op jit(solution)/shard_map/ppermute | solution.py:594
  36.5 0.2 advance_outer.3
  36.7 0.2 collective-permute-start.15
  37.0 2.9 %collective-permute-start.14 = (f32[16,16,128]{2,1,0:T(8,128)S(1)}, f32[16,16,128]{2,1,0:T(8,128)S(1)}, u32[]{:S(2)}, u32[]{:S(2)}) collective-permute-start(f32[16,16,128]{2,1,0:T(8,128)S(1)} %get-tuple-element.82.far_ref), channel_id=1, source_target_pairs={{0,28},{4,8},{8,4},{12,16},{16,12},{20,24},{24,20},{28,0},{1,29},{... | collective-permute-start | bytes 393224 | tf_op jit(solution)/shard_map/ppermute | solution.py:594
  39.8 0.2 advance_inner.3
  40.0 0.1 collective-permute-start.12
  40.1 1.6 %collective-permute-start.13 = (f32[32,128]{1,0:T(8,128)S(1)}, f32[32,128]{1,0:T(8,128)S(1)}, u32[]{:S(2)}, u32[]{:S(2)}) collective-permute-start(f32[32,128]{1,0:T(8,128)S(1)} %get-tuple-element.88), channel_id=1, source_target_pairs={{0,3},{1,2},{2,1},{3,0},{4,7},{5,6},{6,5},{7,4},{8,11},{9,10},{10,... | collective-permute-start | bytes 49160 | tf_op jit(solution)/shard_map/ppermute | solution.py:594
  41.7 0.4 trigs.5.trig_ref
  42.1 0.0 collective-permute-done.12.y_near_ref
  42.1 1.2 %collective-permute-done.13.y_far_ref = f32[32,128]{1,0:T(8,128)S(1)} collective-permute-done((f32[32,128]{1,0:T(8,128)S(1)}, f32[32,128]{1,0:T(8,128)S(1)}, u32[]{:S(2)}, u32[]{:S(2)}) %collective-permute-start.13) | collective-permute-done | bytes 16416 | tf_op jit(solution)/shard_map/ppermute | solution.py:594
  43.3 0.8 %inner_terms.5 = (f32[2,6,16,128]{3,2,1,0:T(8,128)S(1)}, f32[8,2,2,4,16,128]{5,4,3,2,1,0:T(8,128)S(1)}, f32[16,256]{1,0:T(8,128)S(1)}, f32[6,2,4,16,128]{4,3,2,1,0:T(8,128)S(1)}) custom-call(f32[16,16,128]{2,1,0:T(8,128)S(1)} %get-tuple-element.85.near_ref, f32[16,16,128]{2,1,0:T(8,128)S(1)} %get-tuple-element.82.far_ref, ...), custom_call_target="tpu_custom_call" | custom-call | flops 4194304 | bytes 1048576 | tf_op jit(solution)/shard_map/inner_terms/pallas_call | solution.py:577
  44.1 0.0 collective-permute-done.15.halo_ref.near_halo_ref
  44.1 0.5 near_terms.5
  44.6 0.0 collective-permute-done.14.halo_ref.far_halo_ref
  44.6 0.4 far_terms.5
  45.0 0.8 %collective-permute-start.16 = (f32[8,256]{1,0:T(8,128)S(1)}, f32[8,256]{1,0:T(8,128)S(1)}, u32[]{:S(2)}, u32[]{:S(2)}) collective-permute-start(f32[8,256]{1,0:T(8,128)S(1)} %get-tuple-element.93.message_ref), channel_id=1, source_target_pairs={{0,4},{4,0},{8,12},{12,8},{16,20},{20,16},{24,28},{28,24},{1,5},{5... | collective-permute-start | bytes 24584 | tf_op jit(solution)/shard_map/ppermute | solution.py:594
  45.9 2.3 %collective-permute-start.17 = (f32[8,256]{1,0:T(8,128)S(1)}, f32[8,256]{1,0:T(8,128)S(1)}, u32[]{:S(2)}, u32[]{:S(2)}) collective-permute-start(f32[8,256]{1,0:T(8,128)S(1)} %get-tuple-element.93.message_ref), channel_id=1, source_target_pairs={{0,28},{4,8},{8,4},{12,16},{16,12},{20,24},{24,20},{28,0},{1,29},{... | collective-permute-start | bytes 24584 | tf_op jit(solution)/shard_map/ppermute | solution.py:594
  48.1 0.2 outer_locals.5.outer_local_ref
  48.3 1.9 %naturals.1 = (f32[8,4,32,512]{3,2,1,0:T(8,128)S(1)}, bf16[384,512]{1,0:T(8,128)(2,1)S(1)}) custom-call(f32[8,2,2,4,16,128]{5,4,3,2,1,0:T(8,128)S(1)} %outer_locals.5.outer_local_ref, f32[8,2,2,4,16,128]{5,4,3,2,1,0:T(8,128)S(1)} %get-tuple-element.96.inner_local_ref, bf16[512,512]{1,0:T(8,128)(2,1)S(1)} %get-tuple-element.97.back_ref), custom_call_target="tpu_custom_call" | custom-call | flops 4194304 | bytes 1048576 | tf_op jit(solution)/shard_map/naturals/pallas_call | solution.py:577
  50.2 0.0 collective-permute-done.16.near_message_ref
  50.2 2.0 %collective-permute-done.17.far_message_ref = f32[8,256]{1,0:T(8,128)S(1)} collective-permute-done((f32[8,256]{1,0:T(8,128)S(1)}, f32[8,256]{1,0:T(8,128)S(1)}, u32[]{:S(2)}, u32[]{:S(2)}) %collective-permute-start.17) | collective-permute-done | bytes 8224 | tf_op jit(solution)/shard_map/ppermute | solution.py:594
  52.2 1.4 %finish.1 = (f32[4,32,512]{2,1,0:T(8,128)}, f32[4,32,512]{2,1,0:T(8,128)}) custom-call(f32[8,256]{1,0:T(8,128)S(1)} %get-tuple-element.93.message_ref, f32[8,256]{1,0:T(8,128)S(1)} %collective-permute-done.16.near_message_ref, f32[8,256]{1,0:T(8,128)S(1)} %collective-permute-done.17.far_message_ref, s32[2,8,256]{2,1,0:T(8,128)S(1)} %get-tuple-element.65.match_ref, ...), custom_call_target="tpu_custom_call" | custom-call | flops 4194304 | bytes 1048576 | tf_op jit(solution)/shard_map/finish/pallas_call | solution.py:577
Async XLA Ops:
  2.1 11.2 %collective-permute-start.3 = (f32[17,16,128]{2,1,0:T(8,128)S(1)}, f32[17,16,128]{2,1,0:T(8,128)S(1)}, u32[]{:S(2)}, u32[]{:S(2)}) collective-permute-start(f32[17,16,128]{2,1,0:T(8,128)S(1)} %get-tuple-element.54.near_ref), channel_id=1, source_target_pairs={{0,4},{4,0},{8,12},{12,8},{16,20},{20,16},{24,28},{28,24},{1,5},{5... | collective-permute-start | bytes 417800 | tf_op jit(solution)/shard_map/ppermute | solution.py:594
  5.1 8.6 %collective-permute-start.2 = (f32[17,16,128]{2,1,0:T(8,128)S(1)}, f32[17,16,128]{2,1,0:T(8,128)S(1)}, u32[]{:S(2)}, u32[]{:S(2)}) collective-permute-start(f32[17,16,128]{2,1,0:T(8,128)S(1)} %get-tuple-element.51.far_ref), channel_id=1, source_target_pairs={{0,28},{4,8},{8,4},{12,16},{16,12},{20,24},{24,20},{28,0},{1,29},{... | collective-permute-start | bytes 417800 | tf_op jit(solution)/shard_map/ppermute | solution.py:594
  9.1 3.0 %collective-permute-start = (f32[32,128]{1,0:T(8,128)S(1)}, f32[32,128]{1,0:T(8,128)S(1)}, u32[]{:S(2)}, u32[]{:S(2)}) collective-permute-start(f32[32,128]{1,0:T(8,128)S(1)} %get-tuple-element.56), channel_id=1, source_target_pairs={{0,1},{1,0},{2,3},{3,2},{4,5},{5,4},{6,7},{7,6},{8,9},{9,8},{10,11... | collective-permute-start | bytes 49160 | tf_op jit(solution)/shard_map/ppermute | solution.py:594
  9.2 3.2 %collective-permute-start.1 = (f32[32,128]{1,0:T(8,128)S(1)}, f32[32,128]{1,0:T(8,128)S(1)}, u32[]{:S(2)}, u32[]{:S(2)}) collective-permute-start(f32[32,128]{1,0:T(8,128)S(1)} %get-tuple-element.57), channel_id=1, source_target_pairs={{0,3},{1,2},{2,1},{3,0},{4,7},{5,6},{6,5},{7,4},{8,11},{9,10},{10,... | collective-permute-start | bytes 49160 | tf_op jit(solution)/shard_map/ppermute | solution.py:594
  14.2 4.4 %collective-permute-start.4 = (f32[8,256]{1,0:T(8,128)S(1)}, f32[8,256]{1,0:T(8,128)S(1)}, u32[]{:S(2)}, u32[]{:S(2)}) collective-permute-start(f32[8,256]{1,0:T(8,128)S(1)} %get-tuple-element.63.message_ref), channel_id=1, source_target_pairs={{0,4},{4,0},{8,12},{12,8},{16,20},{20,16},{24,28},{28,24},{1,5},{5... | collective-permute-start | bytes 24584 | tf_op jit(solution)/shard_map/ppermute | solution.py:594
  14.5 6.3 %collective-permute-start.5 = (f32[8,256]{1,0:T(8,128)S(1)}, f32[8,256]{1,0:T(8,128)S(1)}, u32[]{:S(2)}, u32[]{:S(2)}) collective-permute-start(f32[8,256]{1,0:T(8,128)S(1)} %get-tuple-element.63.message_ref), channel_id=1, source_target_pairs={{0,28},{4,8},{8,4},{12,16},{16,12},{20,24},{24,20},{28,0},{1,29},{... | collective-permute-start | bytes 24584 | tf_op jit(solution)/shard_map/ppermute | solution.py:594
  21.1 8.0 %collective-permute-start.9 = (f32[16,16,128]{2,1,0:T(8,128)S(1)}, f32[16,16,128]{2,1,0:T(8,128)S(1)}, u32[]{:S(2)}, u32[]{:S(2)}) collective-permute-start(f32[16,16,128]{2,1,0:T(8,128)S(1)} %get-tuple-element.71.near_ref), channel_id=1, source_target_pairs={{0,4},{4,0},{8,12},{12,8},{16,20},{20,16},{24,28},{28,24},{1,5},{5... | collective-permute-start | bytes 393224 | tf_op jit(solution)/shard_map/ppermute | solution.py:594
  21.2 8.4 %collective-permute-start.8 = (f32[16,16,128]{2,1,0:T(8,128)S(1)}, f32[16,16,128]{2,1,0:T(8,128)S(1)}, u32[]{:S(2)}, u32[]{:S(2)}) collective-permute-start(f32[16,16,128]{2,1,0:T(8,128)S(1)} %get-tuple-element.68.far_ref), channel_id=1, source_target_pairs={{0,28},{4,8},{8,4},{12,16},{16,12},{20,24},{24,20},{28,0},{1,29},{... | collective-permute-start | bytes 393224 | tf_op jit(solution)/shard_map/ppermute | solution.py:594
  25.0 2.1 %collective-permute-start.6 = (f32[32,128]{1,0:T(8,128)S(1)}, f32[32,128]{1,0:T(8,128)S(1)}, u32[]{:S(2)}, u32[]{:S(2)}) collective-permute-start(f32[32,128]{1,0:T(8,128)S(1)} %get-tuple-element.73), channel_id=1, source_target_pairs={{0,1},{1,0},{2,3},{3,2},{4,5},{5,4},{6,7},{7,6},{8,9},{9,8},{10,11... | collective-permute-start | bytes 49160 | tf_op jit(solution)/shard_map/ppermute | solution.py:594
  25.0 3.2 %collective-permute-start.7 = (f32[32,128]{1,0:T(8,128)S(1)}, f32[32,128]{1,0:T(8,128)S(1)}, u32[]{:S(2)}, u32[]{:S(2)}) collective-permute-start(f32[32,128]{1,0:T(8,128)S(1)} %get-tuple-element.74), channel_id=1, source_target_pairs={{0,3},{1,2},{2,1},{3,0},{4,7},{5,6},{6,5},{7,4},{8,11},{9,10},{10,... | collective-permute-start | bytes 49160 | tf_op jit(solution)/shard_map/ppermute | solution.py:594
  30.0 3.7 %collective-permute-start.10 = (f32[8,256]{1,0:T(8,128)S(1)}, f32[8,256]{1,0:T(8,128)S(1)}, u32[]{:S(2)}, u32[]{:S(2)}) collective-permute-start(f32[8,256]{1,0:T(8,128)S(1)} %get-tuple-element.79.message_ref), channel_id=1, source_target_pairs={{0,4},{4,0},{8,12},{12,8},{16,20},{20,16},{24,28},{28,24},{1,5},{5... | collective-permute-start | bytes 24584 | tf_op jit(solution)/shard_map/ppermute | solution.py:594
  30.1 6.4 %collective-permute-start.11 = (f32[8,256]{1,0:T(8,128)S(1)}, f32[8,256]{1,0:T(8,128)S(1)}, u32[]{:S(2)}, u32[]{:S(2)}) collective-permute-start(f32[8,256]{1,0:T(8,128)S(1)} %get-tuple-element.79.message_ref), channel_id=1, source_target_pairs={{0,28},{4,8},{8,4},{12,16},{16,12},{20,24},{24,20},{28,0},{1,29},{... | collective-permute-start | bytes 24584 | tf_op jit(solution)/shard_map/ppermute | solution.py:594
  36.7 7.4 %collective-permute-start.15 = (f32[16,16,128]{2,1,0:T(8,128)S(1)}, f32[16,16,128]{2,1,0:T(8,128)S(1)}, u32[]{:S(2)}, u32[]{:S(2)}) collective-permute-start(f32[16,16,128]{2,1,0:T(8,128)S(1)} %get-tuple-element.85.near_ref), channel_id=1, source_target_pairs={{0,4},{4,0},{8,12},{12,8},{16,20},{20,16},{24,28},{28,24},{1,5},{5... | collective-permute-start | bytes 393224 | tf_op jit(solution)/shard_map/ppermute | solution.py:594
  37.0 7.7 %collective-permute-start.14 = (f32[16,16,128]{2,1,0:T(8,128)S(1)}, f32[16,16,128]{2,1,0:T(8,128)S(1)}, u32[]{:S(2)}, u32[]{:S(2)}) collective-permute-start(f32[16,16,128]{2,1,0:T(8,128)S(1)} %get-tuple-element.82.far_ref), channel_id=1, source_target_pairs={{0,28},{4,8},{8,4},{12,16},{16,12},{20,24},{24,20},{28,0},{1,29},{... | collective-permute-start | bytes 393224 | tf_op jit(solution)/shard_map/ppermute | solution.py:594
  40.0 2.1 %collective-permute-start.12 = (f32[32,128]{1,0:T(8,128)S(1)}, f32[32,128]{1,0:T(8,128)S(1)}, u32[]{:S(2)}, u32[]{:S(2)}) collective-permute-start(f32[32,128]{1,0:T(8,128)S(1)} %get-tuple-element.87), channel_id=1, source_target_pairs={{0,1},{1,0},{2,3},{3,2},{4,5},{5,4},{6,7},{7,6},{8,9},{9,8},{10,11... | collective-permute-start | bytes 49160 | tf_op jit(solution)/shard_map/ppermute | solution.py:594
  40.1 3.2 %collective-permute-start.13 = (f32[32,128]{1,0:T(8,128)S(1)}, f32[32,128]{1,0:T(8,128)S(1)}, u32[]{:S(2)}, u32[]{:S(2)}) collective-permute-start(f32[32,128]{1,0:T(8,128)S(1)} %get-tuple-element.88), channel_id=1, source_target_pairs={{0,3},{1,2},{2,1},{3,0},{4,7},{5,6},{6,5},{7,4},{8,11},{9,10},{10,... | collective-permute-start | bytes 49160 | tf_op jit(solution)/shard_map/ppermute | solution.py:594
  45.0 5.2 %collective-permute-start.16 = (f32[8,256]{1,0:T(8,128)S(1)}, f32[8,256]{1,0:T(8,128)S(1)}, u32[]{:S(2)}, u32[]{:S(2)}) collective-permute-start(f32[8,256]{1,0:T(8,128)S(1)} %get-tuple-element.93.message_ref), channel_id=1, source_target_pairs={{0,4},{4,0},{8,12},{12,8},{16,20},{20,16},{24,28},{28,24},{1,5},{5... | collective-permute-start | bytes 24584 | tf_op jit(solution)/shard_map/ppermute | solution.py:594
  45.9 6.3 %collective-permute-start.17 = (f32[8,256]{1,0:T(8,128)S(1)}, f32[8,256]{1,0:T(8,128)S(1)}, u32[]{:S(2)}, u32[]{:S(2)}) collective-permute-start(f32[8,256]{1,0:T(8,128)S(1)} %get-tuple-element.93.message_ref), channel_id=1, source_target_pairs={{0,28},{4,8},{8,4},{12,16},{16,12},{20,24},{24,20},{28,0},{1,29},{... | collective-permute-start | bytes 24584 | tf_op jit(solution)/shard_map/ppermute | solution.py:594
